TPU v7x, 32 devices: a whole 2x2x4 slice. The times are simulated.
32 devices in a mesh: fsdp: 4 (over z), ctx: 4 (over y, core), tp: 2 (over x).
Axes of the slice: x: 2, y: 2, z: 4, core: 2. Of those that a mesh axis runs over, the one named last changes fastest.
Arguments:
- prompt_input: bfloat16 [4, 1024, 2048], P('fsdp', 'ctx'), may hold values from -6 to 6
- continuation_input: bfloat16 [4, 8, 128, 2048], P('fsdp', 'ctx'), may hold values from -6 to 6
- prompt_lengths: int32 [4], P('fsdp'), may hold values from 769 to 1024, as said below
- continuation_lengths: int32 [4, 8], P('fsdp', 'ctx'), may hold values from 32 to 128, as said below
- query_weight: bfloat16 [2048, 2048], P('fsdp', 'tp'), may hold values from -0.1875 to 0.1875
- key_weight: bfloat16 [2048, 2048], P('fsdp', 'tp'), may hold values from -0.1875 to 0.1875
- value_weight: bfloat16 [2048, 2048], P('fsdp', 'tp'), may hold values from -0.125 to 0.125
- query_bias: bfloat16 [16, 128], P('tp', 'fsdp'), may hold values from -2 to 2
- value_bias: bfloat16 [16, 128], P('tp', 'fsdp'), may hold values from -0.59765625 to 0.59765625
- output_weight: bfloat16 [2048, 2048], P('tp', 'fsdp'), may hold values from -1 to 1
- output_bias: bfloat16 [2048], P('fsdp'), may hold values from -2 to 2
- first_gain: bfloat16 [2048], P('fsdp'), may hold values from 0.5 to 1.5
- first_shift: bfloat16 [2048], P('fsdp'), may hold values from -2 to 2
- second_gain: bfloat16 [2048], P('fsdp'), may hold values from 0.5 to 1.5
- second_shift: bfloat16 [2048], P('fsdp'), may hold values from -2 to 2
- up_weight: bfloat16 [2048, 8192], P('fsdp', 'tp'), may hold values from -0.125 to 0.125
- up_bias: bfloat16 [64, 128], P('tp', 'fsdp'), may hold values from -3 to 3
- down_weight: bfloat16 [8192, 2048], P('tp', 'fsdp'), may hold values from -0.09375 to 0.09375
- down_bias: bfloat16 [2048], P('fsdp'), may hold values from -2 to 2
- prompt_cotangent: bfloat16 [4, 1024, 2048], P('fsdp', 'ctx'), may hold values from -6 to 6
- continuation_cotangent: bfloat16 [4, 8, 128, 2048], P('fsdp', 'ctx'), may hold values from -6 to 6
Outputs:
- prompt_output: bfloat16 [4, 1024, 2048], P('fsdp', 'ctx')
- continuation_output: bfloat16 [4, 8, 128, 2048], P('fsdp', 'ctx')
- prompt_input_grad: bfloat16 [4, 1024, 2048], P('fsdp', 'ctx')
- continuation_input_grad: bfloat16 [4, 8, 128, 2048], P('fsdp', 'ctx')
- query_weight_grad: float32 [2048, 2048], P('fsdp', 'tp')
- key_weight_grad: float32 [2048, 2048], P('fsdp', 'tp')
- value_weight_grad: float32 [2048, 2048], P('fsdp', 'tp')
- query_bias_grad: float32 [16, 128], P('tp', 'fsdp')
- value_bias_grad: float32 [16, 128], P('tp', 'fsdp')
- output_weight_grad: float32 [2048, 2048], P('tp', 'fsdp')
- output_bias_grad: float32 [2048], P('fsdp')
- first_gain_grad: float32 [2048], P('fsdp')
- first_shift_grad: float32 [2048], P('fsdp')
- second_gain_grad: float32 [2048], P('fsdp')
- second_shift_grad: float32 [2048], P('fsdp')
- up_weight_grad: float32 [2048, 8192], P('fsdp', 'tp')
- up_bias_grad: float32 [64, 128], P('tp', 'fsdp')
- down_weight_grad: float32 [8192, 2048], P('tp', 'fsdp')
- down_bias_grad: float32 [2048], P('fsdp')
Inputs may be any that keep to these rules, and one draw needn't show every extreme that they name: `prompt_lengths`: valid prompt tokens of each group; some group has all 1024. `continuation_lengths`: valid tokens of each continuation; every group has a continuation of all 128 tokens.
All inputs are finite; a program needn't handle non-finite values.
Results may differ from a plain program's by a relative error of at most 0.02.
Values may be sent and summed in bfloat16 or wider, within the bound.
No kernel may reach another device: no remote copies, remote signals or barrier semaphores. Data moves between devices by JAX's collectives and lax.ppermute only.
A program may use at most 512 MiB of HBM per device.

v0:
```python
from functools import partial
import math

import jax
import jax.numpy as jnp
from jax import lax
from jax.sharding import PartitionSpec as P

HD = 128


norm_epsilon = 1e-05


def normalize(values):
    centre = jnp.mean(values, axis=-1, keepdims=True)
    centered = values - centre
    inverse = lax.rsqrt(jnp.mean(centered * centered, axis=-1, keepdims=True) + norm_epsilon)
    return (centered * inverse, inverse)


def norm_backward(incoming, normed, inverse, gain_vec):
    scaled = incoming * gain_vec
    return inverse * (
        scaled
        - jnp.mean(scaled, axis=-1, keepdims=True)
        - normed * jnp.mean(scaled * normed, axis=-1, keepdims=True)
    )


def attention_weights(
    query_weight,
    key_weight,
    value_weight,
    query_bias,
    value_bias,
    output_weight,
    output_bias,
    first_gain,
    first_shift,
):
    return (
        lax.all_gather(query_weight, "fsdp", axis=0, tiled=True),
        lax.all_gather(key_weight, "fsdp", axis=0, tiled=True),
        lax.all_gather(value_weight, "fsdp", axis=0, tiled=True),
        lax.all_gather(query_bias, "fsdp", axis=1, tiled=True),
        lax.all_gather(value_bias, "fsdp", axis=1, tiled=True),
        lax.all_gather(output_weight, "fsdp", axis=1, tiled=True),
        lax.all_gather(output_bias, "fsdp", axis=0, tiled=True),
        lax.all_gather(first_gain, "fsdp", axis=0, tiled=True),
        lax.all_gather(first_shift, "fsdp", axis=0, tiled=True),
    )


def sum_heads(partial_sum):
    return lax.psum(partial_sum.astype(jnp.bfloat16), "tp").astype(jnp.float32)


def sum_features(partial_sum):
    return lax.psum(partial_sum.astype(jnp.bfloat16), "tp").astype(jnp.float32)


def score_block(query_heads, key_heads, visible, score_scale):
    raw_scores = (
        jnp.einsum("qhd,khd->hqk", query_heads, key_heads, preferred_element_type=jnp.float32)
        * score_scale
    )
    return jnp.where(visible[None, :, :], raw_scores, -1e30)


def body(
    prompt_input,
    continuation_input,
    prompt_lengths,
    continuation_lengths,
    query_weight,
    key_weight,
    value_weight,
    query_bias,
    value_bias,
    output_weight,
    output_bias,
    first_gain,
    first_shift,
    second_gain,
    second_shift,
    up_weight,
    up_bias,
    down_weight,
    down_bias,
    prompt_cotangent,
    continuation_cotangent,
):
    prompt_dev = prompt_input.shape[1]
    cont_dev = continuation_input.shape[1]
    cont_len = continuation_input.shape[2]
    model_width = prompt_input.shape[2]
    row_total = prompt_dev + cont_dev * cont_len
    ctx_size = lax.axis_size("ctx")
    prompt_total = prompt_dev * ctx_size
    key_total = prompt_total + cont_dev * cont_len
    score_scale = 1.0 / math.sqrt(HD)
    stacked = jnp.concatenate(
        [prompt_input[0], continuation_input[0].reshape(cont_dev * cont_len, model_width)], axis=0
    ).astype(jnp.float32)
    row_ids = jnp.arange(row_total, dtype=jnp.int32)
    query_prompt = row_ids < prompt_dev
    query_seq = jnp.where(query_prompt, -1, (row_ids - prompt_dev) // cont_len)
    query_pos = jnp.where(
        query_prompt,
        lax.axis_index("ctx") * prompt_dev + row_ids,
        (row_ids - prompt_dev) % cont_len,
    )
    key_ids = jnp.arange(key_total, dtype=jnp.int32)
    key_prompt = key_ids < prompt_total
    key_seq = jnp.where(key_prompt, -1, (key_ids - prompt_total) // cont_len)
    key_pos = jnp.where(key_prompt, key_ids, (key_ids - prompt_total) % cont_len)
    seq_lengths = jnp.sum(
        jnp.where(
            key_seq[:, None] == jnp.arange(cont_dev, dtype=jnp.int32)[None, :],
            continuation_lengths[0][None, :],
            0,
        ),
        axis=1,
    )
    key_limit = jnp.where(key_prompt, prompt_lengths[0], seq_lengths)
    cross = key_prompt[None, :] & jnp.logical_not(query_prompt[:, None])
    causal = (key_seq[None, :] == query_seq[:, None]) & (key_pos[None, :] <= query_pos[:, None])
    visible = (key_pos < key_limit)[None, :] & (cross | causal)
    (
        full_query,
        full_key,
        full_value,
        full_qbias,
        full_vbias,
        full_output,
        full_obias,
        gain_one,
        shift_one,
    ) = attention_weights(
        query_weight,
        key_weight,
        value_weight,
        query_bias,
        value_bias,
        output_weight,
        output_bias,
        first_gain,
        first_shift,
    )
    normed_one, inverse_one = normalize(stacked)
    act_one = (normed_one * gain_one.astype(jnp.float32) + shift_one.astype(jnp.float32)).astype(
        jnp.bfloat16
    )
    queries = (
        jnp.dot(act_one, full_query, preferred_element_type=jnp.float32)
        + full_qbias.reshape(-1).astype(jnp.float32)
    ).astype(jnp.bfloat16)
    keys_local = jnp.dot(act_one, full_key, preferred_element_type=jnp.float32).astype(jnp.bfloat16)
    values_local = (
        jnp.dot(act_one, full_value, preferred_element_type=jnp.float32)
        + full_vbias.reshape(-1).astype(jnp.float32)
    ).astype(jnp.bfloat16)
    prompt_keys, prompt_values = (
        lax.all_gather(keys_local[:prompt_dev], "ctx", axis=0, tiled=True),
        lax.all_gather(values_local[:prompt_dev], "ctx", axis=0, tiled=True),
    )
    key_rows = jnp.concatenate([prompt_keys, keys_local[prompt_dev:]], axis=0)
    value_rows = jnp.concatenate([prompt_values, values_local[prompt_dev:]], axis=0)
    heads_local = queries.shape[1] // HD
    query_heads = queries.reshape(row_total, heads_local, HD)
    key_heads = key_rows.reshape(key_total, heads_local, HD)
    value_heads = value_rows.reshape(key_total, heads_local, HD)
    masked = score_block(query_heads, key_heads, visible, score_scale)
    row_top = jnp.max(masked, axis=-1, keepdims=True)
    log_total = row_top + jnp.log(jnp.sum(jnp.exp(masked - row_top), axis=-1, keepdims=True))
    prob_low = jnp.exp(masked - log_total).astype(jnp.bfloat16)
    attended = (
        jnp.einsum("hqk,khd->qhd", prob_low, value_heads, preferred_element_type=jnp.float32)
        .reshape(row_total, -1)
        .astype(jnp.bfloat16)
    )
    attn_sum = sum_heads(jnp.dot(attended, full_output, preferred_element_type=jnp.float32))
    middle = stacked + (attn_sum + full_obias.astype(jnp.float32))
    up_full, ubias_full, down_full, dbias_full, gain_two, shift_two = (
        lax.all_gather(up_weight, "fsdp", axis=0, tiled=True),
        lax.all_gather(up_bias, "fsdp", axis=1, tiled=True),
        lax.all_gather(down_weight, "fsdp", axis=1, tiled=True),
        lax.all_gather(down_bias, "fsdp", axis=0, tiled=True),
        lax.all_gather(second_gain, "fsdp", axis=0, tiled=True),
        lax.all_gather(second_shift, "fsdp", axis=0, tiled=True),
    )
    normed_two, inverse_two = normalize(middle)
    act_two = (normed_two * gain_two.astype(jnp.float32) + shift_two.astype(jnp.float32)).astype(
        jnp.bfloat16
    )
    pre_act = jnp.dot(act_two, up_full, preferred_element_type=jnp.float32) + ubias_full.reshape(
        -1
    ).astype(jnp.float32)
    hidden = jax.nn.gelu(pre_act, approximate=False).astype(jnp.bfloat16)
    mlp_sum = sum_heads(jnp.dot(hidden, down_full, preferred_element_type=jnp.float32))
    result = middle + (mlp_sum + dbias_full.astype(jnp.float32))
    prompt_output = result[:prompt_dev][None].astype(jnp.bfloat16)
    continuation_output = (
        result[prompt_dev:].reshape(1, cont_dev, cont_len, model_width).astype(jnp.bfloat16)
    )
    upstream = jnp.concatenate(
        [prompt_cotangent[0], continuation_cotangent[0].reshape(cont_dev * cont_len, model_width)],
        axis=0,
    ).astype(jnp.float32)
    upstream_low = upstream.astype(jnp.bfloat16)
    grad_hidden = jnp.einsum(
        "rd,fd->rf", upstream_low, down_full, preferred_element_type=jnp.float32
    )
    gelu_pull = jax.vjp(partial(jax.nn.gelu, approximate=False), pre_act)[1]
    grad_pre = gelu_pull(grad_hidden)[0].astype(jnp.bfloat16)
    grad_act_two = sum_features(
        jnp.einsum("rf,df->rd", grad_pre, up_full, preferred_element_type=jnp.float32)
    )
    grad_middle = upstream + norm_backward(
        grad_act_two, normed_two, inverse_two, gain_two.astype(jnp.float32)
    )
    middle_low = grad_middle.astype(jnp.bfloat16)
    (
        full_query,
        full_key,
        full_value,
        full_qbias,
        full_vbias,
        full_output,
        full_obias,
        gain_one,
        shift_one,
    ) = attention_weights(
        query_weight,
        key_weight,
        value_weight,
        query_bias,
        value_bias,
        output_weight,
        output_bias,
        first_gain,
        first_shift,
    )
    grad_attended = jnp.einsum(
        "rd,kd->rk", middle_low, full_output, preferred_element_type=jnp.float32
    ).astype(jnp.bfloat16)
    grad_att_heads = grad_attended.reshape(row_total, heads_local, HD)
    masked = score_block(query_heads, key_heads, visible, score_scale)
    prob_full = jnp.exp(masked - log_total)
    prob_low = prob_full.astype(jnp.bfloat16)
    grad_values = jnp.einsum(
        "hqk,qhd->khd", prob_low, grad_att_heads, preferred_element_type=jnp.float32
    ).reshape(key_total, -1)
    grad_probs = jnp.einsum(
        "qhd,khd->hqk", grad_att_heads, value_heads, preferred_element_type=jnp.float32
    )
    grad_scores = (
        prob_full * (grad_probs - jnp.sum(prob_full * grad_probs, axis=-1, keepdims=True))
    ).astype(jnp.bfloat16)
    grad_queries = (
        (
            jnp.einsum("hqk,khd->qhd", grad_scores, key_heads, preferred_element_type=jnp.float32)
            * score_scale
        )
        .reshape(row_total, -1)
        .astype(jnp.bfloat16)
    )
    grad_keys = (
        jnp.einsum(
            "hqk,qhd->khd", grad_scores, query_heads, preferred_element_type=jnp.float32
        ).reshape(key_total, -1)
        * score_scale
    )
    prompt_dkeys, prompt_dvalues = (
        lax.psum_scatter(
            grad_keys[:prompt_total].astype(jnp.bfloat16), "ctx", scatter_dimension=0, tiled=True
        ).astype(jnp.float32),
        lax.psum_scatter(
            grad_values[:prompt_total].astype(jnp.bfloat16), "ctx", scatter_dimension=0, tiled=True
        ).astype(jnp.float32),
    )
    grad_key_rows = jnp.concatenate([prompt_dkeys, grad_keys[prompt_total:]], axis=0).astype(
        jnp.bfloat16
    )
    grad_value_rows = jnp.concatenate([prompt_dvalues, grad_values[prompt_total:]], axis=0).astype(
        jnp.bfloat16
    )
    grad_act_one = sum_features(
        jnp.einsum("rk,dk->rd", grad_queries, full_query, preferred_element_type=jnp.float32)
        + jnp.einsum("rk,dk->rd", grad_key_rows, full_key, preferred_element_type=jnp.float32)
        + jnp.einsum("rk,dk->rd", grad_value_rows, full_value, preferred_element_type=jnp.float32)
    )
    grad_stacked = grad_middle + norm_backward(
        grad_act_one, normed_one, inverse_one, gain_one.astype(jnp.float32)
    )
    prompt_input_grad = grad_stacked[:prompt_dev][None].astype(jnp.bfloat16)
    continuation_input_grad = (
        grad_stacked[prompt_dev:].reshape(1, cont_dev, cont_len, model_width).astype(jnp.bfloat16)
    )
    qkv_grads = jnp.concatenate([grad_queries, grad_key_rows, grad_value_rows], axis=1)
    qbias_term = jnp.sum(grad_queries, axis=0, dtype=jnp.float32).reshape(-1, HD)
    vbias_term = jnp.sum(grad_value_rows, axis=0, dtype=jnp.float32).reshape(-1, HD)
    ubias_term = jnp.sum(grad_pre, axis=0, dtype=jnp.float32).reshape(-1, HD)
    obias_term = jnp.sum(middle_low, axis=0, dtype=jnp.float32)
    gain_one_term = jnp.sum(grad_act_one * normed_one, axis=0)
    shift_one_term = jnp.sum(grad_act_one, axis=0)
    gain_two_term = jnp.sum(grad_act_two * normed_two, axis=0)
    shift_two_term = jnp.sum(grad_act_two, axis=0)
    dbias_term = jnp.sum(upstream_low, axis=0, dtype=jnp.float32)
    matrix_piece = lax.psum_scatter(
        jnp.concatenate(
            [
                jnp.einsum("rc,rk->ck", act_one, qkv_grads, preferred_element_type=jnp.float32),
                jnp.einsum("rc,rk->ck", middle_low, attended, preferred_element_type=jnp.float32),
                jnp.einsum("rc,rk->ck", act_two, grad_pre, preferred_element_type=jnp.float32),
                jnp.einsum("rc,rk->ck", upstream_low, hidden, preferred_element_type=jnp.float32),
            ],
            axis=1,
        ).astype(jnp.bfloat16),
        "fsdp",
        scatter_dimension=0,
        tiled=True,
    )
    (
        qbias_piece,
        vbias_piece,
        ubias_piece,
        obias_piece,
        gain_one_piece,
        shift_one_piece,
        gain_two_piece,
        shift_two_piece,
        dbias_piece,
    ) = (
        lax.psum_scatter(
            qbias_term.astype(jnp.bfloat16), "fsdp", scatter_dimension=1, tiled=True
        ).astype(jnp.float32),
        lax.psum_scatter(
            vbias_term.astype(jnp.bfloat16), "fsdp", scatter_dimension=1, tiled=True
        ).astype(jnp.float32),
        lax.psum_scatter(
            ubias_term.astype(jnp.bfloat16), "fsdp", scatter_dimension=1, tiled=True
        ).astype(jnp.float32),
        lax.psum_scatter(
            obias_term.astype(jnp.bfloat16), "fsdp", scatter_dimension=0, tiled=True
        ).astype(jnp.float32),
        lax.psum_scatter(
            gain_one_term.astype(jnp.bfloat16), "fsdp", scatter_dimension=0, tiled=True
        ).astype(jnp.float32),
        lax.psum_scatter(
            shift_one_term.astype(jnp.bfloat16), "fsdp", scatter_dimension=0, tiled=True
        ).astype(jnp.float32),
        lax.psum_scatter(
            gain_two_term.astype(jnp.bfloat16), "fsdp", scatter_dimension=0, tiled=True
        ).astype(jnp.float32),
        lax.psum_scatter(
            shift_two_term.astype(jnp.bfloat16), "fsdp", scatter_dimension=0, tiled=True
        ).astype(jnp.float32),
        lax.psum_scatter(
            dbias_term.astype(jnp.bfloat16), "fsdp", scatter_dimension=0, tiled=True
        ).astype(jnp.float32),
    )
    (
        matrix_block,
        qbias_grad,
        vbias_grad,
        ubias_grad,
        obias_grad,
        gain_one_grad,
        shift_one_grad,
        gain_two_grad,
        shift_two_grad,
        dbias_grad,
    ) = (
        lax.psum(matrix_piece, "ctx").astype(jnp.float32),
        lax.psum(qbias_piece.astype(jnp.bfloat16), "ctx").astype(jnp.float32),
        lax.psum(vbias_piece.astype(jnp.bfloat16), "ctx").astype(jnp.float32),
        lax.psum(ubias_piece.astype(jnp.bfloat16), "ctx").astype(jnp.float32),
        lax.psum(obias_piece.astype(jnp.bfloat16), "ctx").astype(jnp.float32),
        lax.psum(gain_one_piece.astype(jnp.bfloat16), "ctx").astype(jnp.float32),
        lax.psum(shift_one_piece.astype(jnp.bfloat16), "ctx").astype(jnp.float32),
        lax.psum(gain_two_piece.astype(jnp.bfloat16), "ctx").astype(jnp.float32),
        lax.psum(shift_two_piece.astype(jnp.bfloat16), "ctx").astype(jnp.float32),
        lax.psum(dbias_piece.astype(jnp.bfloat16), "ctx").astype(jnp.float32),
    )
    local_width = full_query.shape[1]
    local_units = up_full.shape[1]
    query_grad = matrix_block[:, :local_width]
    key_grad = matrix_block[:, local_width : 2 * local_width]
    value_grad = matrix_block[:, 2 * local_width : 3 * local_width]
    output_grad = matrix_block[:, 3 * local_width : 4 * local_width].T
    up_grad = matrix_block[:, 4 * local_width : 4 * local_width + local_units]
    down_grad = matrix_block[:, 4 * local_width + local_units :].T
    return (
        prompt_output,
        continuation_output,
        prompt_input_grad,
        continuation_input_grad,
        query_grad,
        key_grad,
        value_grad,
        qbias_grad,
        vbias_grad,
        output_grad,
        obias_grad,
        gain_one_grad,
        shift_one_grad,
        gain_two_grad,
        shift_two_grad,
        up_grad,
        ubias_grad,
        down_grad,
        dbias_grad,
    )


def solution(mesh):
    return jax.shard_map(
        body,
        mesh=mesh,
        in_specs=(
            P("fsdp", "ctx", None),
            P("fsdp", "ctx", None, None),
            P("fsdp"),
            P("fsdp", "ctx"),
            P("fsdp", "tp"),
            P("fsdp", "tp"),
            P("fsdp", "tp"),
            P("tp", "fsdp"),
            P("tp", "fsdp"),
            P("tp", "fsdp"),
            P("fsdp"),
            P("fsdp"),
            P("fsdp"),
            P("fsdp"),
            P("fsdp"),
            P("fsdp", "tp"),
            P("tp", "fsdp"),
            P("tp", "fsdp"),
            P("fsdp"),
            P("fsdp", "ctx", None),
            P("fsdp", "ctx", None, None),
        ),
        out_specs=(
            P("fsdp", "ctx", None),
            P("fsdp", "ctx", None, None),
            P("fsdp", "ctx", None),
            P("fsdp", "ctx", None, None),
            P("fsdp", "tp"),
            P("fsdp", "tp"),
            P("fsdp", "tp"),
            P("tp", "fsdp"),
            P("tp", "fsdp"),
            P("tp", "fsdp"),
            P("fsdp"),
            P("fsdp"),
            P("fsdp"),
            P("fsdp"),
            P("fsdp"),
            P("fsdp", "tp"),
            P("tp", "fsdp"),
            P("tp", "fsdp"),
            P("fsdp"),
        ),
        check_vma=False,
    )
```

profile of v0, /device:TPU:0, one launch (start us, length us, event | category | flops | bytes accessed | tf_op | source)
XLA Modules:
  0.0 2561.5 jit_solution(17474665477025225468)
XLA Ops:
  10.2 13.5 all-gather.1
  24.4 12.0 all-gather
  39.1 54.1 %all-gather.23.cloned.1.call-done = bf16[2048,1024]{1,0:T(8,128)(2,1)} async-done(((bf16[512,1024]{1,0:T(8,128)(2,1)}), bf16[2048,1024]{1,0:T(8,128)(2,1)}) %all-gather.23.cloned.1.call-update) | async-done | bytes 4194320 | tf_op jit(solution)/shard_map/all_gather | solution.py:44
  93.2 4.6 convolution_convert_fusion.9
  98.8 12.0 all-gather.2
  110.9 63.2 %all-gather.17.cloned.1.call-done = bf16[2048,1024]{1,0:T(8,128)(2,1)} async-done(((bf16[512,1024]{1,0:T(8,128)(2,1)}), bf16[2048,1024]{1,0:T(8,128)(2,1)}) %all-gather.17.cloned.1.call-update) | async-done | bytes 4194320 | tf_op jit(solution)/shard_map/all_gather | solution.py:45
  174.1 4.6 add_convert_fusion.5
  180.3 12.6 all-gather.3
  195.6 59.5 %all-gather.21.cloned.1.call-done = bf16[2048,1024]{1,0:T(8,128)(2,1)} async-done(((bf16[512,1024]{1,0:T(8,128)(2,1)}), bf16[2048,1024]{1,0:T(8,128)(2,1)}) %all-gather.21.cloned.1.call-update) | async-done | bytes 4194320 | tf_op jit(solution)/shard_map/all_gather | solution.py:43
  255.1 5.6 add_convert_fusion.4
  263.0 15.2 all-gather.25.cloned.1.call-done
  278.2 3.3 pad_maximum_fusion.1
  281.5 4.4 copy.115
  285.9 6.9 fusion.101
  292.8 3.8 exponential_reduce_fusion
  296.6 3.2 copy-done
  302.8 9.6 fusion.50
  312.4 72.6 %all-gather.27.cloned.1.call-done = bf16[1024,2048]{1,0:T(8,128)(2,1)} async-done(((bf16[1024,512]{1,0:T(8,128)(2,1)}), bf16[1024,2048]{1,0:T(8,128)(2,1)}) %all-gather.27.cloned.1.call-update) | async-done | bytes 4194320 | tf_op jit(solution)/shard_map/all_gather | solution.py:48
  385.0 5.9 convolution_convert_fusion.5
  392.6 13.1 all_gather.70
  405.9 11.9 all-gather.6
  417.8 11.9 all-gather.5
  429.7 11.9 all-gather.4
  441.6 11.0 all-reduce.14.cloned.1.call-done
  456.1 284.9 %all-gather.29.cloned.1.call-done = bf16[2048,4096]{1,0:T(8,128)(2,1)} async-done(((bf16[512,4096]{1,0:T(8,128)(2,1)}), bf16[2048,4096]{1,0:T(8,128)(2,1)}) %all-gather.29.cloned.1.call-update) | async-done | bytes 16777232 | tf_op jit(solution)/shard_map/all_gather | solution.py:186
  741.0 35.0 %multiply_convert_fusion.1 = (bf16[512,4096]{1,0:T(8,128)(2,1)}, f32[512,4096]{1,0:T(8,128)}, f32[512,4096]{1,0:T(8,128)}) fusion(f32[4096]{0:T(1024)S(1)} %bitcast_convert_fusion, bf16[2048,4096]{1,0:T(8,128)(2,1)} %all-gather.29.cloned.1.call-done, f32[2048]{0:T(1024)S(1)} %bitcast.195, f32[2048]{0:T(1024)S(1)} %bitcast.183, f32[512]{0:T(512)S(1)} %add_rsqrt_fusion, ...), kind=kOutput, calls=%fused_computation.14 | convolution fusion | flops 8740929536 | bytes 41988096 | tf_op jit(solution)/shard_map/dot_general | solution.py:197
  776.1 251.6 %all-gather.31.cloned.1.call-done = bf16[4096,2048]{1,0:T(8,128)(2,1)} async-done(((bf16[4096,512]{1,0:T(8,128)(2,1)}), bf16[4096,2048]{1,0:T(8,128)(2,1)}) %all-gather.31.cloned.1.call-update) | async-done | bytes 16777232 | tf_op jit(solution)/shard_map/all_gather | solution.py:188
  1027.7 18.5 fusion.103
  1048.2 13.4 convolution_convert_fusion.6
  1061.7 61.2 %all-reduce.16.cloned.1.call-done = bf16[512,2048]{1,0:T(8,128)(2,1)} async-done(((bf16[512,2048]{1,0:T(8,128)(2,1)}), bf16[512,2048]{1,0:T(8,128)(2,1)}) %all-reduce.16.cloned.1.call-update) | async-done | bytes 2097168 | tf_op jit(solution)/shard_map/psum | solution.py:60
  1122.9 6.1 fusion.28
  1129.0 5.0 convert_reduce_fusion.1
  1136.0 3.4 convolution_convert_fusion.8
  1141.6 16.0 multiply_reduce_fusion
  1157.6 14.2 multiply_convert_fusion
  1178.2 11.5 fusion.31
  1192.9 15.4 convolution_convert_fusion
  1208.3 15.3 convolution_convert_fusion.1
  1224.7 4.4 convolution_convert_fusion.3
  1229.1 6.7 copy.105
  1237.1 9.5 fusion.102
  1246.7 11.8 convolution_convert_fusion.2
  1258.5 33.0 %pad_maximum_fusion = bf16[2048,12288]{1,0:T(8,128)(2,1)} fusion(bf16[2048,4096]{1,0:T(8,128)(2,1)} %convolution_convert_fusion, bf16[2048,4096]{1,0:T(8,128)(2,1)} %convolution_convert_fusion.1, bf16[2048,1024]{1,0:T(8,128)(2,1)} %copy.105, bf16[2048,3072]{1,0:T(8,128)(2,1)} %convolution_convert_fusion.2), kind=kLoop, calls=%fused_computation | loop fusion | flops 201326592 | bytes 100663296 | tf_op jit(solution)/shard_map/concatenate | solution.py:312
  1293.0 14.9 convolution_convert_fusion.7
  1309.2 7.0 fusion.104
  1317.2 5.0 fusion.56
  1322.3 3.7 add_convert_fusion.1
  1326.1 785.8 %reduce-scatter.17.cloned.1.call-done = bf16[512,12288]{1,0:T(8,128)(2,1)} async-done(((bf16[2048,12288]{1,0:T(8,128)(2,1)}), bf16[512,12288]{1,0:T(8,128)(2,1)}) %reduce-scatter.17.cloned.1.call-update) | async-done | bytes 12582928 | tf_op jit(solution)/shard_map/reduce_scatter | solution.py:311
  2114.8 14.0 all-gather.7
  2130.2 5.5 reduce-scatter.23.cloned.1.call-done
  2136.5 19.0 reduce-scatter.19.cloned.1.call-done
  2156.3 19.1 reduce-scatter.21.cloned.1.call-done
  2176.1 109.1 %all-reduce.20.cloned.1.call-done = (bf16[512,2048]{1,0:T(8,128)(2,1)}, bf16[512,2048]{1,0:T(8,128)(2,1)}) async-done(((bf16[512,2048]{1,0:T(8,128)(2,1)}, bf16[512,2048]{1,0:T(8,128)(2,1)}), (bf16[512,2048]{1,0:T(8,128)(2,1)}, bf16[512,2048]{1,0:T(8,128)(2,1)})) %all-reduce.20.cloned.1.call-update) | async-done | bytes 4194320 | tf_op jit(solution)/shard_map/psum | solution.py:56
  2287.1 3.8 fusion.30
  2290.9 18.9 all-reduce.7
  2310.3 12.5 all-reduce.6
  2328.1 5.9 fusion.22
  2337.1 171.8 %all-reduce.18.cloned.1.call-done = bf16[512,12288]{1,0:T(8,128)(2,1)} async-done(((bf16[512,12288]{1,0:T(8,128)(2,1)}), bf16[512,12288]{1,0:T(8,128)(2,1)}) %all-reduce.18.cloned.1.call-update) | async-done | bytes 12582928 | tf_op jit(solution)/shard_map/psum | solution.py:376
  2508.9 7.2 convert_element_type.298
  2516.1 8.3 copy-done.8
  2524.5 7.8 slice_bitcast_fusion
  2534.1 8.9 copy.107
  2543.0 4.8 fusion.96
  2547.8 6.7 slice.106
  (211 shorter events, 62.0 us)
Async XLA Ops:
  7.2 31.2 %copy-start.2 = (bf16[1,2,128,2048]{3,2,1,0:T(8,128)(2,1)S(1)}, bf16[1,2,128,2048]{3,2,1,0:T(8,128)(2,1)}, u32[]{:S(2)}) copy-start(bf16[1,2,128,2048]{3,2,1,0:T(8,128)(2,1)} %param.22) | copy-start | bytes 3145732
  7.2 31.2 %copy-start.3 = (bf16[1,256,2048]{2,1,0:T(8,128)(2,1)S(1)}, bf16[1,256,2048]{2,1,0:T(8,128)(2,1)}, u32[]{:S(2)}) copy-start(bf16[1,256,2048]{2,1,0:T(8,128)(2,1)} %param.21) | copy-start | bytes 3145732
  7.2 86.0 %all-gather.23.cloned.1.call-start = ((), (), s32[]{:S(2)}) async-start(), calls=%async_computation.9 | async-start | bytes 5242880 | tf_op jit(solution)/shard_map/all_gather | solution.py:44
  7.9 166.2 %all-gather.17.cloned.1.call-start = ((), (), s32[]{:S(2)}) async-start(), calls=%async_computation.6 | async-start | bytes 5242880 | tf_op jit(solution)/shard_map/all_gather | solution.py:45
  8.7 246.4 %all-gather.21.cloned.1.call-start = ((), (), s32[]{:S(2)}) async-start(), calls=%async_computation.8 | async-start | bytes 5242880 | tf_op jit(solution)/shard_map/all_gather | solution.py:43
  9.4 268.8 %all-gather.25.cloned.1.call-start = ((), (), s32[]{:S(2)}) async-start(), calls=%async_computation.10 | async-start | bytes 2621440 | tf_op jit(solution)/shard_map/all_gather | solution.py:165
  23.7 231.4 %copy-start.33 = (f32[4,1,512]{2,1,0:T(1,128)}, f32[4,1,512]{2,1,0:T(1,128)S(1)}, u32[]{:S(2)}) copy-start(f32[4,1,512]{2,1,0:T(1,128)S(1)} %convert_element_type.316) | copy-start | bytes 24580
  36.5 218.7 %copy-start.22 = (f32[4,1,512]{2,1,0:T(1,128)}, f32[4,1,512]{2,1,0:T(1,128)S(1)}, u32[]{:S(2)}) copy-start(f32[4,1,512]{2,1,0:T(1,128)S(1)} %convert_element_type.315) | copy-start | bytes 24580
  38.4 216.7 %copy-start.24 = (f32[512]{0:T(512)}, f32[512]{0:T(512)S(1)}, u32[]{:S(2)}) copy-start(f32[512]{0:T(512)S(1)} %broadcast_multiply_fusion.5) | copy-start | bytes 6148
  39.1 216.0 %copy-start.26 = (f32[512]{0:T(512)}, f32[512]{0:T(512)S(1)}, u32[]{:S(2)}) copy-start(f32[512]{0:T(512)S(1)} %add_rsqrt_fusion.1) | copy-start | bytes 6148
  93.2 5.5 copy-start.35
  98.7 204.1 %all-gather.19.cloned.1.call-start = ((), (), s32[]{:S(2)}) async-start(), calls=%async_computation.7 | async-start | bytes 2621440 | tf_op jit(solution)/shard_map/all_gather | solution.py:166
  174.1 6.2 copy-start.36
  174.1 19.6 copy-start.41
  179.7 205.4 %all-gather.27.cloned.1.call-start = ((), (), s32[]{:S(2)}) async-start(), calls=%async_computation.11 | async-start | bytes 5242880 | tf_op jit(solution)/shard_map/all_gather | solution.py:48
  180.2 272.3 %all-reduce.14.cloned.1.call-start = ((), (), s32[]{:S(2)}) async-start(), calls=%async_computation.12 | async-start | bytes 4194304 | tf_op jit(solution)/shard_map/psum | solution.py:56
  292.8 7.0 copy-start
  312.4 78.5 %copy-start.17 = (bf16[8,128,512]{2,1,0:T(8,128)(2,1)}, bf16[8,128,512]{2,1,0:T(8,128)(2,1)S(1)}, u32[]{:S(2)}) copy-start(bf16[8,128,512]{2,1,0:T(8,128)(2,1)S(1)} %fusion.50) | copy-start | bytes 3145732
  390.9 1.6 copy-start.32
  391.0 14.9 copy-start.37
  391.0 26.8 %copy-start.38 = (bf16[512]{0:T(512)(128)(2,1)S(1)}, bf16[512]{0:T(512)(128)(2,1)}, u32[]{:S(2)}) copy-start(bf16[512]{0:T(512)(128)(2,1)} %param.34) | copy-start | bytes 3076
  391.0 38.7 %copy-start.39 = (bf16[512]{0:T(512)(128)(2,1)S(1)}, bf16[512]{0:T(512)(128)(2,1)}, u32[]{:S(2)}) copy-start(bf16[512]{0:T(512)(128)(2,1)} %param.31) | copy-start | bytes 3076
  391.0 61.6 %copy-start.4 = (bf16[1,256,2048]{2,1,0:T(8,128)(2,1)S(1)}, bf16[1,256,2048]{2,1,0:T(8,128)(2,1)}, u32[]{:S(2)}) copy-start(bf16[1,256,2048]{2,1,0:T(8,128)(2,1)} %param.21) | copy-start | bytes 3145732
  391.0 350.0 %all-gather.29.cloned.1.call-start = ((), (), s32[]{:S(2)}) async-start(), calls=%async_computation.13 | async-start | bytes 20971520 | tf_op jit(solution)/shard_map/all_gather | solution.py:186
  391.8 635.9 %all-gather.31.cloned.1.call-start = ((), (), s32[]{:S(2)}) async-start(), calls=%async_computation.14 | async-start | bytes 20971520 | tf_op jit(solution)/shard_map/all_gather | solution.py:188
  392.5 730.4 %all-reduce.16.cloned.1.call-start = ((), (), s32[]{:S(2)}) async-start(), calls=%async_computation.15 | async-start | bytes 4194304 | tf_op jit(solution)/shard_map/psum | solution.py:60
  452.6 2.5 copy-start.5
  1046.2 2.0 copy-start.46
  1061.6 185.0 %reduce-scatter.13.cloned.1.call-start = ((), (), s32[]{:S(2)}) async-start(), calls=%async_computation.16 | async-start | bytes 2621440 | tf_op jit(solution)/shard_map/reduce_scatter | solution.py:276
  1122.9 6.1 copy-start.6
  1122.9 6.1 copy-start.14
  1122.9 6.1 copy-start.15
  1122.9 6.1 copy-start.16
  1129.0 7.0 copy-start.43
  1134.0 2.0 copy-start.10
  1157.6 14.2 copy-start.9
  1171.8 4.0 copy-start.1
  1175.8 2.2 copy-start.12
  1178.0 68.6 %reduce-scatter.15.cloned.1.call-start = ((), (), s32[]{:S(2)}) async-start(), calls=%async_computation.17 | async-start | bytes 2621440 | tf_op jit(solution)/shard_map/reduce_scatter | solution.py:279
  1189.7 1.5 copy-start.13
  1192.8 919.1 %reduce-scatter.17.cloned.1.call-start = ((), (), s32[]{:S(2)}) async-start(), calls=%async_computation.18 | async-start | bytes 62914560 | tf_op jit(solution)/shard_map/reduce_scatter | solution.py:311
  1192.9 15.4 copy-start.7
  1208.3 16.4 copy-start.11
  1208.3 16.4 copy-start.18
  1237.1 9.6 copy-start.20
  1237.1 9.6 copy-start.23
  1237.1 9.6 copy-start.25
  1237.1 9.6 copy-start.27
  1237.1 9.6 copy-start.34
  1291.6 844.2 %reduce-scatter.23.cloned.1.call-start = ((), (), s32[]{:S(2)}) async-start(), calls=%async_computation.22 | async-start | bytes 40960
  1293.0 862.5 %reduce-scatter.19.cloned.1.call-start = ((), (), s32[]{:S(2)}) async-start(), calls=%async_computation.20 | async-start | bytes 40960
  1308.7 7.4 copy-start.19
  1308.7 866.6 %reduce-scatter.21.cloned.1.call-start = ((), (), s32[]{:S(2)}) async-start(), calls=%async_computation.21 | async-start | bytes 40960
  1317.1 968.0 %all-reduce.20.cloned.1.call-start = ((), (), s32[]{:S(2)}) async-start(), calls=%async_computation.23 | async-start | bytes 8388608 | tf_op jit(solution)/shard_map/psum | solution.py:56
  1317.2 5.0 copy-start.21
  1317.2 5.0 copy-start.42
  1317.2 5.2 copy-start.45
  1326.1 1182.8 %all-reduce.18.cloned.1.call-start = ((), (), s32[]{:S(2)}) async-start(), calls=%async_computation.19 | async-start | bytes 25165824 | tf_op jit(solution)/shard_map/psum | solution.py:376
  2112.0 2.9 copy-start.40
  2112.0 17.0 copy-start.44
  2112.0 178.9 %copy-start.28 = (bf16[2048]{0:T(1024)(128)(2,1)S(1)}, bf16[2048]{0:T(1024)(128)(2,1)}, u32[]{:S(2)}) copy-start(bf16[2048]{0:T(1024)(128)(2,1)} %get-tuple-element.137) | copy-start | bytes 12292
  2112.0 178.9 %copy-start.29 = (bf16[2048]{0:T(1024)(128)(2,1)S(1)}, bf16[2048]{0:T(1024)(128)(2,1)}, u32[]{:S(2)}) copy-start(bf16[2048]{0:T(1024)(128)(2,1)} %get-tuple-element.146) | copy-start | bytes 12292
  2112.0 178.9 %copy-start.30 = (bf16[2048]{0:T(1024)(128)(2,1)S(1)}, bf16[2048]{0:T(1024)(128)(2,1)}, u32[]{:S(2)}) copy-start(bf16[2048]{0:T(1024)(128)(2,1)} %get-tuple-element.114) | copy-start | bytes 12292
  2516.1 8.3 copy-start.8
  (1 other events, 0.7 us)
Sparse Core Ops, SparseCore 0:
  9.6 83.5 all-gather.22
  94.8 79.2 all-gather.16
  175.7 79.3 all-gather.20
  257.1 21.0 all-gather.24
  280.2 22.5 all-gather.18
  304.2 80.7 all-gather.26
  391.1 61.4 all-reduce.13
  454.2 286.7 all-gather.28
  742.7 284.9 all-gather.30
  1061.8 61.0 all-reduce.15
  1178.1 31.4 reduce-scatter.12
  1212.7 31.3 reduce-scatter.14
  1291.7 820.2 reduce-scatter.16
  2114.7 20.9 reduce-scatter.22
  2138.4 17.0 reduce-scatter.18
  2158.2 17.0 reduce-scatter.20
  2178.8 106.3 all-reduce.19
  2287.6 221.1 all-reduce.17
where the time goes:
time: 2570 us; the launch traced here: 2560 us
  waiting for transfers between devices  1990 us (77%)
  matrix products  224 us (9%)
  blocking collectives  144 us (6%)
  other arithmetic  102 us (4%)
  local copies, waits for them, and re-layouts  83.1 us (3%)
    reduce_scatter x1, waiting for transfers between devices, body(): lax.psum_scatter(jnp.concatenate([jnp.einsum('rc,rk->ck', act_one, qkv_gr...  786 us
    all_gather x1, waiting for transfers between devices, body(): lax.all_gather(up_weight, 'fsdp', axis=0, tiled=True)  285 us
    all_gather x1, waiting for transfers between devices, body(): lax.all_gather(down_weight, 'fsdp', axis=1, tiled=True)  252 us
    psum x1, waiting for transfers between devices, body(): lax.psum(matrix_piece, 'ctx').astype(jnp.float32)  172 us
    psum x2, waiting for transfers between devices, sum_heads(): return lax.psum(partial_sum.astype(jnp.bfloat16), 'tp').astype(jnp.float32)  120 us
    all_gather x1, waiting for transfers between devices, attention_weights(): lax.all_gather(output_weight, 'fsdp', axis=1, tiled=True)  72.6 us
    all_gather x1, waiting for transfers between devices, attention_weights(): lax.all_gather(value_weight, 'fsdp', axis=0, tiled=True)  63.2 us
    psum x1, waiting for transfers between devices, sum_features(): return lax.psum(partial_sum.astype(jnp.bfloat16), 'tp').astype(jnp.float32)  61.2 us
  transfers between devices with their start and end apart: 18, of which 16 were waited for; matrix products, arithmetic and copies ran while one was open for 8% of the time, Pallas kernels for 0%

commit v1 on v0

v1 whole, which is shorter than its diff:
```python
from functools import partial
import math

import jax
import jax.numpy as jnp
from jax import lax
from jax.experimental import pallas as pl
from jax.experimental.pallas import tpu as pltpu
from jax.sharding import PartitionSpec as P

HD = 128
BF = jnp.bfloat16
F32 = jnp.float32


norm_epsilon = 1e-05


def normalize(values):
    centre = jnp.mean(values, axis=-1, keepdims=True)
    centered = values - centre
    inverse = lax.rsqrt(jnp.mean(centered * centered, axis=-1, keepdims=True) + norm_epsilon)
    return (centered * inverse, inverse)


def norm_backward(incoming, normed, inverse, gain_vec):
    scaled = incoming * gain_vec
    return inverse * (
        scaled
        - jnp.mean(scaled, axis=-1, keepdims=True)
        - normed * jnp.mean(scaled * normed, axis=-1, keepdims=True)
    )


def swap_tp(value):
    return lax.ppermute(value, "tp", [(0, 1), (1, 0)])


def swap_low(value):
    return lax.ppermute(value, "ctx", [(0, 1), (1, 0), (2, 3), (3, 2)])


def swap_high(value):
    return lax.ppermute(value, "ctx", [(0, 2), (2, 0), (1, 3), (3, 1)])


def gather_blocks(own):
    half = own.shape[0] // 2
    across = swap_tp(own)
    along = swap_high(own)
    corner = jnp.concatenate([swap_high(across[:half]), swap_tp(along[half:])], axis=0)
    return [
        own,
        across,
        swap_low(own),
        swap_low(across),
        along,
        corner,
        swap_low(along),
        swap_low(corner),
    ]


def scatter_blocks(parts):
    half = parts[0].shape[0] // 2
    kept = {p: parts[p].astype(F32) + swap_low(parts[p ^ 2]).astype(F32) for p in (5, 1, 4, 0)}
    corner = kept[5].astype(BF)
    via_high = swap_high(corner[:half]).astype(F32)
    via_tp = swap_tp(corner[half:]).astype(F32)
    across = jnp.concatenate([kept[1][:half] + via_high, kept[1][half:]], axis=0).astype(BF)
    along = jnp.concatenate([kept[4][:half], kept[4][half:] + via_tp], axis=0).astype(BF)
    return kept[0] + swap_tp(across).astype(F32) + swap_high(along).astype(F32)


def gather_ctx(pair):
    low = swap_low(pair)
    high = swap_high(pair)
    return jnp.concatenate([pair, low, high, swap_low(high)], axis=0)


def pair_mask(rows, limits, split):
    row = lax.broadcasted_iota(jnp.int32, (rows, rows), 0)
    col = lax.broadcasted_iota(jnp.int32, (rows, rows), 1)
    mask = col <= row
    for seq in range(rows // split):
        inside = (row >= seq * split) & (row < (seq + 1) * split)
        limit = jnp.where(inside, limits[seq] + seq * split, 0)
        lower = jnp.where(inside, seq * split, 0)
        ok = (col >= lower) & (col < limit)
        mask = mask & (jnp.logical_not(inside) | ok)
    return mask


def attention_tiles(info_ref, tiles, rows, cont_len):
    me = info_ref[0]
    prompt_len = info_ref[1]
    per_block = rows // cont_len
    col = lax.broadcasted_iota(jnp.int32, (rows, rows), 1)
    row = lax.broadcasted_iota(jnp.int32, (rows, rows), 0)
    plan = []
    for t in range(tiles):
        keys = []
        for j in range(t + 1):
            mask = (col + j * rows) < prompt_len
            if j == t:
                mask = mask & (col <= row)
            keys.append((2 * j, mask))
        plan.append((2 * t, keys))
    for t in range(tiles):
        keys = []
        for j in range(tiles):
            keys.append((2 * j, (col + j * rows) < prompt_len))
        base = 2 + ((2 * t) ^ (me & (2 * tiles - 2))) // 2 * per_block
        limits = [info_ref[base + s] for s in range(per_block)]
        keys.append((2 * t + 1, pair_mask(rows, limits, cont_len)))
        plan.append((2 * t + 1, keys))
    return me, plan


def dot_nt(a, b):
    return lax.dot_general(a, b, (((1,), (1,)), ((), ())), preferred_element_type=F32)


def dot_nn(a, b):
    return lax.dot_general(a, b, (((1,), (0,)), ((), ())), preferred_element_type=F32)


def dot_tn(a, b):
    return lax.dot_general(a, b, (((0,), (0,)), ((), ())), preferred_element_type=F32)


def softmax_tiles(query, keys, scale):
    scores = [jnp.where(mask, dot_nt(query, key) * scale, -1e30) for key, mask in keys]
    top = jnp.max(scores[0], axis=-1, keepdims=True)
    for s in scores[1:]:
        top = jnp.maximum(top, jnp.max(s, axis=-1, keepdims=True))
    weights = [jnp.exp(s - top) for s in scores]
    total = jnp.sum(weights[0], axis=-1, keepdims=True)
    for w in weights[1:]:
        total = total + jnp.sum(w, axis=-1, keepdims=True)
    inverse = 1.0 / total
    return [w * inverse for w in weights]


def attention_forward_kernel(tiles, rows, cont_len, heads, info_ref, qkv_ref, out_ref):
    h = pl.program_id(0)
    scale = 1.0 / math.sqrt(HD)
    me, plan = attention_tiles(info_ref, tiles, rows, cont_len)

    def load(kind, block):
        cols = pl.ds(pl.multiple_of((kind * heads + h) * HD, HD), HD)
        return qkv_ref[block ^ me, :, cols]

    for block, keys in plan:
        query = load(0, block)
        probs = softmax_tiles(query, [(load(1, kb), mask) for kb, mask in keys], scale)
        total = None
        for p, (kb, _) in zip(probs, keys):
            term = dot_nn(p.astype(BF), load(2, kb))
            total = term if total is None else total + term
        cols = pl.ds(pl.multiple_of(h * HD, HD), HD)
        out_ref[block ^ me, :, cols] = total.astype(BF)


def attention_backward_kernel(
    tiles, rows, cont_len, heads, info_ref, qkv_ref, grad_ref, out_ref, dkey_ref, dvalue_ref
):
    h = pl.program_id(0)
    scale = 1.0 / math.sqrt(HD)
    me, plan = attention_tiles(info_ref, tiles, rows, cont_len)

    def columns(kind):
        return pl.ds(pl.multiple_of((kind * heads + h) * HD, HD), HD)

    def load(kind, block):
        return qkv_ref[block ^ me, :, columns(kind)]

    seen = set()
    for block, keys in plan:
        query = load(0, block)
        grad = grad_ref[block ^ me, :, columns(0)]
        probs = softmax_tiles(query, [(load(1, kb), mask) for kb, mask in keys], scale)
        gprobs = [dot_nt(grad, load(2, kb)) for kb, _ in keys]
        delta = jnp.sum(probs[0] * gprobs[0], axis=-1, keepdims=True)
        for p, g in zip(probs[1:], gprobs[1:]):
            delta = delta + jnp.sum(p * g, axis=-1, keepdims=True)
        dquery = None
        for p, g, (kb, _) in zip(probs, gprobs, keys):
            dscore = (p * (g - delta)).astype(BF)
            term = dot_nn(dscore, load(1, kb))
            dquery = term if dquery is None else dquery + term
            dkey = dot_tn(dscore, query)
            dvalue = dot_tn(p.astype(BF), grad)
            if kb in seen:
                dkey_ref[kb] += dkey
                dvalue_ref[kb] += dvalue
            else:
                dkey_ref[kb] = dkey
                dvalue_ref[kb] = dvalue
                seen.add(kb)
        out_ref[block ^ me, :, columns(0)] = (dquery * scale).astype(BF)
    for kb in sorted(seen):
        out_ref[kb ^ me, :, columns(1)] = (dkey_ref[kb] * scale).astype(BF)
        out_ref[kb ^ me, :, columns(2)] = dvalue_ref[kb].astype(BF)


def attention_cost(blocks, rows, heads, matmuls):
    tiles = blocks // 2
    pairs = (tiles * (tiles + 1)) // 2 + tiles * (tiles + 1)
    return pl.CostEstimate(
        flops=2 * matmuls * pairs * heads * rows * rows * HD,
        transcendentals=pairs * heads * rows * rows,
        bytes_accessed=2 * blocks * rows * heads * HD * (4 if matmuls == 2 else 7),
    )


def attention_forward(info, qkv, cont_len):
    blocks, rows, width = qkv.shape
    heads = width // (3 * HD)
    return pl.pallas_call(
        partial(attention_forward_kernel, blocks // 2, rows, cont_len, heads),
        grid=(heads,),
        in_specs=[
            pl.BlockSpec(memory_space=pltpu.SMEM),
            pl.BlockSpec((blocks, rows, width), lambda h: (0, 0, 0)),
        ],
        out_specs=pl.BlockSpec((blocks, rows, heads * HD), lambda h: (0, 0, 0)),
        out_shape=jax.ShapeDtypeStruct((blocks, rows, heads * HD), BF),
        compiler_params=pltpu.CompilerParams(vmem_limit_bytes=40 << 20),
        cost_estimate=attention_cost(blocks, rows, heads, 2),
        name="attention_forward",
    )(info, qkv)


def attention_backward(info, qkv, grad, cont_len):
    blocks, rows, width = qkv.shape
    heads = width // (3 * HD)
    return pl.pallas_call(
        partial(attention_backward_kernel, blocks // 2, rows, cont_len, heads),
        grid=(heads,),
        in_specs=[
            pl.BlockSpec(memory_space=pltpu.SMEM),
            pl.BlockSpec((blocks, rows, width), lambda h: (0, 0, 0)),
            pl.BlockSpec((blocks, rows, heads * HD), lambda h: (0, 0, 0)),
        ],
        out_specs=pl.BlockSpec((blocks, rows, width), lambda h: (0, 0, 0)),
        out_shape=jax.ShapeDtypeStruct((blocks, rows, width), BF),
        scratch_shapes=[
            pltpu.VMEM((blocks, rows, HD), F32),
            pltpu.VMEM((blocks, rows, HD), F32),
        ],
        compiler_params=pltpu.CompilerParams(vmem_limit_bytes=40 << 20),
        cost_estimate=attention_cost(blocks, rows, heads, 7),
        name="attention_backward",
    )(info, qkv, grad)


def gather_small(packed, size):
    index = lax.axis_index("fsdp")
    out = lax.dynamic_update_slice(
        jnp.zeros((size,) + packed.shape, packed.dtype), packed[None], (index, 0)
    )
    for step in range(1, size):
        moved = lax.ppermute(packed, "fsdp", [(i, (i + step) % size) for i in range(size)])
        out = lax.dynamic_update_slice(out, moved[None], ((index + size - step) % size, 0))
    return out


def body(
    prompt_input,
    continuation_input,
    prompt_lengths,
    continuation_lengths,
    query_weight,
    key_weight,
    value_weight,
    query_bias,
    value_bias,
    output_weight,
    output_bias,
    first_gain,
    first_shift,
    second_gain,
    second_shift,
    up_weight,
    up_bias,
    down_weight,
    down_bias,
    prompt_cotangent,
    continuation_cotangent,
):
    prompt_dev = prompt_input.shape[1]
    cont_dev = continuation_input.shape[1]
    cont_len = continuation_input.shape[2]
    width = prompt_input.shape[2]
    rows = prompt_dev
    fsdp_size = lax.axis_size("fsdp")
    ctx_size = lax.axis_size("ctx")
    tp_size = lax.axis_size("tp")
    assert ctx_size == 4 and tp_size == 2 and cont_dev * cont_len == rows
    blocks = ctx_size * tp_size
    total_rows = blocks * rows
    z = lax.axis_index("fsdp")
    ctx = lax.axis_index("ctx")
    tp = lax.axis_index("tp")
    me = 2 * ctx + tp

    heads_tp = query_bias.shape[0]
    heads = heads_tp // ctx_size
    head_width = heads * HD
    units = up_weight.shape[1] // ctx_size
    unit_rows = units // HD
    d_local = query_weight.shape[0]

    def cols(weight, count):
        return lax.dynamic_slice_in_dim(weight, ctx * count, count, axis=1)

    def rws(weight, count):
        return lax.dynamic_slice_in_dim(weight, ctx * count, count, axis=0)

    attn_shard = jnp.concatenate(
        [
            cols(query_weight, head_width),
            cols(key_weight, head_width),
            cols(value_weight, head_width),
            rws(output_weight, head_width).T,
        ],
        axis=1,
    )
    attn_full = lax.all_gather(attn_shard, "fsdp", axis=0, tiled=True)
    w_qkv = attn_full[:, : 3 * head_width]
    w_out = attn_full[:, 3 * head_width :]
    w_up = lax.all_gather(cols(up_weight, units), "fsdp", axis=0, tiled=True)
    w_down = lax.all_gather(rws(down_weight, units).T, "fsdp", axis=0, tiled=True)

    packed = jnp.concatenate(
        [
            output_bias,
            first_gain,
            first_shift,
            second_gain,
            second_shift,
            down_bias,
            rws(query_bias, heads).reshape(-1),
            rws(value_bias, heads).reshape(-1),
            rws(up_bias, unit_rows).reshape(-1),
        ]
    )
    small = gather_small(packed, fsdp_size).astype(F32)
    vectors = [small[:, i * d_local : (i + 1) * d_local].reshape(-1) for i in range(6)]
    obias, gain_one, shift_one, gain_two, shift_two, dbias = vectors
    hd_local = HD // fsdp_size

    def head_vector(start, count):
        piece = small[:, start : start + count * hd_local].reshape(fsdp_size, count, hd_local)
        return piece.transpose(1, 0, 2).reshape(-1)

    start = 6 * d_local
    qbias = head_vector(start, heads)
    vbias = head_vector(start + heads * hd_local, heads)
    ubias = head_vector(start + 2 * heads * hd_local, unit_rows)
    qkv_bias = jnp.concatenate([qbias, jnp.zeros_like(qbias), vbias])

    lens = continuation_lengths[0]
    lens_high = swap_high(lens)
    info = jnp.concatenate(
        [me[None].astype(jnp.int32), prompt_lengths, lens, swap_low(lens), lens_high, swap_low(lens_high)]
    )

    def own_pair(first, second):
        a = first[0]
        b = second[0].reshape(rows, width)
        return jnp.where(tp == 0, a, b), jnp.where(tp == 0, b, a)

    in_own, in_other = own_pair(prompt_input, continuation_input)
    up_own, up_other = own_pair(prompt_cotangent, continuation_cotangent)
    stacked = jnp.concatenate([in_own, in_other], axis=0).astype(F32)
    normed_pair, inverse_pair = normalize(stacked)
    act_pair = (normed_pair * gain_one + shift_one).astype(BF)
    act_one = gather_ctx(act_pair)
    normed_one = normed_pair[:rows]
    inverse_one = inverse_pair[:rows]
    x_own = stacked[:rows]

    qkv = (jnp.dot(act_one, w_qkv, preferred_element_type=F32) + qkv_bias).astype(BF)
    qkv = qkv.reshape(blocks, rows, 3 * head_width)
    attended = attention_forward(info, qkv, cont_len)

    def scatter_matmul(left, right):
        parts = {}
        for group in ((2, 3), (6, 7), (4, 5), (0, 1)):
            lhs = left[group[0] : group[0] + 2].reshape(2 * rows, -1)
            res = dot_nt(lhs, right).astype(BF)
            parts[group[0]] = res[:rows]
            parts[group[1]] = res[rows:]
        return scatter_blocks(parts)

    attn_sum = scatter_matmul(attended, w_out)
    middle = x_own + (attn_sum + obias)
    normed_two, inverse_two = normalize(middle)
    act_two_own = (normed_two * gain_two + shift_two).astype(BF)
    act_two = jnp.concatenate(gather_blocks(act_two_own), axis=0)
    upstream_low = gather_ctx(jnp.concatenate([up_own, up_other], axis=0))

    pre_act = jnp.dot(act_two, w_up, preferred_element_type=F32) + ubias
    hidden = jax.nn.gelu(pre_act, approximate=False).astype(BF)
    down_term = dot_tn(upstream_low, hidden).astype(BF)
    down_piece = lax.psum_scatter(down_term, "fsdp", scatter_dimension=0, tiled=True)
    grad_hidden = jnp.dot(upstream_low, w_down, preferred_element_type=F32)
    gelu_pull = jax.vjp(partial(jax.nn.gelu, approximate=False), pre_act)[1]
    grad_pre = gelu_pull(grad_hidden)[0].astype(BF)
    up_term = dot_tn(act_two, grad_pre).astype(BF)
    up_piece = lax.psum_scatter(up_term, "fsdp", scatter_dimension=0, tiled=True)
    grad_act_two = scatter_matmul(grad_pre.reshape(blocks, rows, units), w_up)
    grad_middle = up_own.astype(F32) + norm_backward(
        grad_act_two, normed_two, inverse_two, gain_two
    )
    middle_low_own = grad_middle.astype(BF)
    middle_low = jnp.concatenate(gather_blocks(middle_low_own), axis=0)

    mlp_sum = scatter_matmul(hidden.reshape(blocks, rows, units), w_down)
    result = (middle + (mlp_sum + dbias)).astype(BF)
    result_other = swap_tp(result)

    out_term = dot_tn(middle_low, attended.reshape(total_rows, head_width)).astype(BF)
    grad_attended = jnp.dot(middle_low, w_out, preferred_element_type=F32).astype(BF)
    dqkv = attention_backward(info, qkv, grad_attended.reshape(blocks, rows, head_width), cont_len)
    dqkv_flat = dqkv.reshape(total_rows, 3 * head_width)
    qkv_term = dot_tn(act_one, dqkv_flat).astype(BF)
    attn_piece = lax.psum_scatter(
        jnp.concatenate([qkv_term, out_term], axis=1), "fsdp", scatter_dimension=0, tiled=True
    )
    grad_act_one = scatter_matmul(dqkv, w_qkv)
    grad_stacked = (
        grad_middle + norm_backward(grad_act_one, normed_one, inverse_one, gain_one)
    ).astype(BF)
    stacked_other = swap_tp(grad_stacked)

    def to_outputs(own, other):
        first = jnp.where(tp == 0, own, other)
        second = jnp.where(tp == 0, other, own)
        return first[None], second.reshape(1, cont_dev, cont_len, width)

    prompt_output, continuation_output = to_outputs(result, result_other)
    prompt_input_grad, continuation_input_grad = to_outputs(grad_stacked, stacked_other)

    def colsum(value):
        return jnp.sum(value, axis=0, dtype=F32)

    d_vectors = jnp.stack(
        [
            colsum(middle_low_own),
            colsum(grad_act_one * normed_one),
            colsum(grad_act_one),
            colsum(grad_act_two * normed_two),
            colsum(grad_act_two),
            colsum(up_own),
        ]
    )
    summed = lax.psum(d_vectors, ("fsdp", "ctx", "tp"))
    summed = lax.dynamic_slice_in_dim(summed, z * d_local, d_local, axis=1)
    obias_grad, gain_one_grad, shift_one_grad, gain_two_grad, shift_two_grad, dbias_grad = [
        summed[i] for i in range(6)
    ]
    colsum_qkv = colsum(dqkv_flat)
    head_terms = jnp.concatenate(
        [
            colsum_qkv[:head_width].reshape(heads, HD),
            colsum_qkv[2 * head_width :].reshape(heads, HD),
            colsum(grad_pre).reshape(unit_rows, HD),
        ]
    )
    head_slots = jnp.where(
        lax.broadcasted_iota(jnp.int32, (ctx_size, 1, 1), 0) == ctx, head_terms[None], 0.0
    )
    head_sums = lax.psum(head_slots, ("fsdp", "ctx"))
    head_sums = lax.dynamic_slice_in_dim(head_sums, z * hd_local, hd_local, axis=2)
    qbias_grad = head_sums[:, :heads].reshape(heads_tp, hd_local)
    vbias_grad = head_sums[:, heads : 2 * heads].reshape(heads_tp, hd_local)
    ubias_grad = head_sums[:, 2 * heads :].reshape(ctx_size * unit_rows, hd_local)

    def spread(piece, axis):
        count = piece.shape[axis]
        shape = list(piece.shape)
        shape[axis] = count * ctx_size
        low = swap_low(piece)
        high = swap_high(piece)
        both = swap_low(high)
        out = jnp.zeros(shape, F32)
        for offset, part in ((0, piece), (1, low), (2, high), (3, both)):
            position = [0, 0]
            position[axis] = (ctx ^ offset) * count
            out = lax.dynamic_update_slice(out, part.astype(F32), tuple(position))
        return out

    down_grad = spread(down_piece.T, 0)
    up_grad = spread(up_piece, 1)
    query_grad = spread(attn_piece[:, :head_width], 1)
    key_grad = spread(attn_piece[:, head_width : 2 * head_width], 1)
    value_grad = spread(attn_piece[:, 2 * head_width : 3 * head_width], 1)
    output_grad = spread(attn_piece[:, 3 * head_width :].T, 0)
    return (
        prompt_output,
        continuation_output,
        prompt_input_grad,
        continuation_input_grad,
        query_grad,
        key_grad,
        value_grad,
        qbias_grad,
        vbias_grad,
        output_grad,
        obias_grad,
        gain_one_grad,
        shift_one_grad,
        gain_two_grad,
        shift_two_grad,
        up_grad,
        ubias_grad,
        down_grad,
        dbias_grad,
    )


def solution(mesh):
    return jax.shard_map(
        body,
        mesh=mesh,
        in_specs=(
            P("fsdp", "ctx", None),
            P("fsdp", "ctx", None, None),
            P("fsdp"),
            P("fsdp", "ctx"),
            P("fsdp", "tp"),
            P("fsdp", "tp"),
            P("fsdp", "tp"),
            P("tp", "fsdp"),
            P("tp", "fsdp"),
            P("tp", "fsdp"),
            P("fsdp"),
            P("fsdp"),
            P("fsdp"),
            P("fsdp"),
            P("fsdp"),
            P("fsdp", "tp"),
            P("tp", "fsdp"),
            P("tp", "fsdp"),
            P("fsdp"),
            P("fsdp", "ctx", None),
            P("fsdp", "ctx", None, None),
        ),
        out_specs=(
            P("fsdp", "ctx", None),
            P("fsdp", "ctx", None, None),
            P("fsdp", "ctx", None),
            P("fsdp", "ctx", None, None),
            P("fsdp", "tp"),
            P("fsdp", "tp"),
            P("fsdp", "tp"),
            P("tp", "fsdp"),
            P("tp", "fsdp"),
            P("tp", "fsdp"),
            P("fsdp"),
            P("fsdp"),
            P("fsdp"),
            P("fsdp"),
            P("fsdp"),
            P("fsdp", "tp"),
            P("tp", "fsdp"),
            P("tp", "fsdp"),
            P("fsdp"),
        ),
        check_vma=False,
    )
```

time: 2570 us -> 812 us (0.32)
  waiting for transfers between devices: 1990 us -> 252 us
  matrix products: 224 us -> 138 us
  starting transfers between devices: 1.3 us -> 58.2 us
  Pallas kernels: 0 us -> 32.5 us
    reduce_scatter x3, waiting for transfers between devices: 786 us -> 0.02 us  [the longest x1 0.01 us: body(): lax.psum_scatter(up_term, 'fsdp', scatter_dimension=0, tiled=True)]
    all_gather x8 -> x3, waiting for transfers between devices: 804 us -> 32.7 us  [the longest x1 21.7 us: body(): lax.all_gather(rws(down_weight, units).T, 'fsdp', axis=0, tiled=True)]
    psum x4 -> x0, waiting for transfers between devices: 353 us -> none  [the longest x1 172 us: body(): lax.psum(matrix_piece, 'ctx').astype(jnp.float32)]
    ppermute x0 -> x80, waiting for transfers between devices: none -> 220 us  [the longest x21 109 us: swap_high(): return lax.ppermute(value, 'ctx', [(0, 2), (2, 0), (1, 3), (3, 1)])]
    all_gather x9 -> x0, blocking collectives: 113 us -> none  [the longest x1 14 us: body(): lax.all_gather(down_bias, 'fsdp', axis=0, tiled=True)]
    psum x1 -> x2, blocking collectives: 12.5 us -> 123 us  [the longest x1 72.6 us: body(): head_sums = lax.psum(head_slots, ('fsdp', 'ctx'))]
    dot_general x22 -> x24, matrix products: 224 us -> 138 us  [the longest x4 38.6 us: dot_tn(): lax.dot_general(a, b, (((0,), (0,)), ((), ())), preferred_element_type=F32)]
    ppermute x0 -> x80, starting transfers between devices: none -> 57.6 us  [the longest x21 26.5 us: swap_high(): return lax.ppermute(value, 'ctx', [(0, 2), (2, 0), (1, 3), (3, 1)])]
  transfers between devices with their start and end apart: 18 -> 86, of which waited for: 16 -> 26; matrix products, arithmetic and copies ran while one was open for 8% -> 31% of each run, Pallas kernels for 0% -> 4%
where the time goes in v1:
time: 812 us; the launch traced here: 806 us
  waiting for transfers between devices  252 us (31%)
  matrix products  138 us (17%)
  blocking collectives  123 us (15%)
  local copies, waits for them, and re-layouts  108 us (13%)
  other arithmetic  76.5 us (9%)
  starting transfers between devices  58.2 us (7%)
  Pallas kernels  32.5 us (4%)
  between operations  17.1 us (2%)
    ppermute x21, waiting for transfers between devices, swap_high(): return lax.ppermute(value, 'ctx', [(0, 2), (2, 0), (1, 3), (3, 1)])  109 us
    ppermute x14, waiting for transfers between devices, swap_tp(): return lax.ppermute(value, 'tp', [(0, 1), (1, 0)])  108 us
    psum x1, blocking collectives, body(): head_sums = lax.psum(head_slots, ('fsdp', 'ctx'))  72.6 us
    psum x1, blocking collectives, body(): summed = lax.psum(d_vectors, ('fsdp', 'ctx', 'tp'))  50.8 us
    dot_general x4, matrix products, dot_tn(): lax.dot_general(a, b, (((0,), (0,)), ((), ())), preferred_element_type=F32)  38.6 us
    dot_general x1, matrix products, body(): grad_hidden = jnp.dot(upstream_low, w_down, preferred_element_type=F32)  34.2 us
    dot_general x16, matrix products, dot_nt(): lax.dot_general(a, b, (((1,), (1,)), ((), ())), preferred_element_type=F32)  34.1 us
    unnamed x120, local copies, waits for them, and re-layouts  27.8 us
  transfers between devices with their start and end apart: 86, of which 26 were waited for; matrix products, arithmetic and copies ran while one was open for 31% of the time, Pallas kernels for 4%

profile of v1, /device:TPU:0, one launch (start us, length us, event | category | flops | bytes accessed | tf_op | source)
XLA Modules:
  0.0 805.6 jit_solution(364729361884290957)
XLA Ops:
  9.1 4.2 concatenate.79
  13.3 3.0 collective-permute-start.3
  16.3 2.6 collective-permute-start.4
  26.2 4.5 bitcast_select_fusion.3
  33.2 3.6 subtract_multiply_fusion
  38.3 45.3 %collective-permute-done.7 = bf16[512,2048]{1,0:T(8,128)(2,1)} collective-permute-done((bf16[512,2048]{1,0:T(8,128)(2,1)}, bf16[512,2048]{1,0:T(8,128)(2,1)}, u32[]{:S(2)}, u32[]{:S(2)}) %collective-permute-start.7) | collective-permute-done | bytes 2097184 | tf_op jit(solution)/shard_map/ppermute | solution.py:44
  87.3 2.3 constant_dynamic-slice_fusion.3
  92.2 11.0 %all-gather.4.cloned.1.call-done = bf16[2048,1024]{0,1:T(8,128)(2,1)} async-done(((bf16[512,1024]{0,1:T(8,128)(2,1)}), bf16[2048,1024]{0,1:T(8,128)(2,1)}) %all-gather.4.cloned.1.call-update) | async-done | bytes 4194320 | tf_op jit(solution)/shard_map/all_gather | solution.py:330
  103.2 13.5 %add_convert_fusion.1 = bf16[2048,768]{1,0:T(8,128)(2,1)S(1)} fusion(f32[768]{0:T(1024)S(1)} %pad_maximum_fusion.18, bf16[2048,1024]{0,1:T(8,128)(2,1)} %all-gather.4.cloned.1.call-done, bf16[512,2048]{1,0:T(8,128)(2,1)} %collective-permute-done.8, bf16[512,2048]{1,0:T(8,128)(2,1)} %collective-permute-done.7, bf16[512,2048]{1,0:T(8,128)(2,1)} %collective-permute-done.6, ...), kind=kOutput, calls=%fused_computation.20 | convolution fusion | flops 6479151104 | bytes 14683136 | tf_op jit(solution)/shard_map/dot_general | solution.py:385
  116.7 11.0 %attention_forward.1 = bf16[8,256,256]{2,1,0:T(8,128)(2,1)S(1)} custom-call(s32[10]{0:T(128)S(1)} %concatenate.78.info_ref, bf16[8,256,768]{2,1,0:T(8,128)(2,1)S(1)} %bitcast.116), custom_call_target="tpu_custom_call" | custom-call | flops 2013265920 | bytes 4194304 | tf_op jit(solution)/shard_map/attention_forward/pallas_call | solution.py:220
  138.0 10.0 %collective-permute-done.12 = bf16[128,2048]{1,0:T(8,128)(2,1)S(1)} collective-permute-done((bf16[128,2048]{1,0:T(8,128)(2,1)S(1)}, bf16[128,2048]{1,0:T(8,128)(2,1)S(1)}, u32[]{:S(2)}, u32[]{:S(2)}) %collective-permute-start.12) | collective-permute-done | bytes 524320 | tf_op jit(solution)/shard_map/ppermute | solution.py:44
  153.3 2.3 dynamic-slice_bitcast_fusion
  156.8 17.0 %collective-permute-done.13 = bf16[256,2048]{1,0:T(8,128)(2,1)} collective-permute-done((bf16[256,2048]{1,0:T(8,128)(2,1)}, bf16[256,2048]{1,0:T(8,128)(2,1)}, u32[]{:S(2)}, u32[]{:S(2)}) %collective-permute-start.13) | collective-permute-done | bytes 1048608 | tf_op jit(solution)/shard_map/ppermute | solution.py:36
  173.9 2.5 collective-permute-done.16
  176.4 2.4 fusion.36
  184.6 3.2 constant_dynamic-update-slice_fusion.11
  187.8 17.0 %collective-permute-done.17 = bf16[256,2048]{1,0:T(8,128)(2,1)S(1)} collective-permute-done((bf16[256,2048]{1,0:T(8,128)(2,1)S(1)}, bf16[256,2048]{1,0:T(8,128)(2,1)S(1)}, u32[]{:S(2)}, u32[]{:S(2)}) %collective-permute-start.17) | collective-permute-done | bytes 1048608 | tf_op jit(solution)/shard_map/ppermute | solution.py:36
  204.8 3.2 constant_dynamic-update-slice_fusion.10
  211.4 3.2 constant_dynamic-update-slice_fusion.9
  216.7 5.8 collective-permute-done.21
  229.7 14.7 %fusion.53 = f32[2048,1024]{1,0:T(8,128)} fusion(bf16[2048,2048]{1,0:T(8,128)(2,1)} %constant_dynamic-update-slice_fusion, bf16[2048,1024]{1,0:T(8,128)(2,1)} %all-gather.6.cloned.1.call-done), kind=kOutput, calls=%fused_computation.244 | convolution fusion | flops 8589934592 | bytes 20971520 | tf_op jit(solution)/shard_map/dot_general | solution.py:405
  244.4 21.7 %all-gather.8.cloned.1.call-done = bf16[2048,1024]{0,1:T(8,128)(2,1)} async-done(((bf16[512,1024]{0,1:T(8,128)(2,1)}), bf16[2048,1024]{0,1:T(8,128)(2,1)}) %all-gather.8.cloned.1.call-update) | async-done | bytes 4194320 | tf_op jit(solution)/shard_map/all_gather | solution.py:334
  266.1 34.2 %convert_reduce_fusion = (f32[1024]{0:T(1024)}, bf16[2048,1024]{1,0:T(8,128)(2,1)}, f32[2048,1024]{1,0:T(8,128)}) fusion(f32[2048,1024]{1,0:T(8,128)} %fusion.53, f32[1024]{0:T(1024)S(1)} %add.335, bf16[2048,2048]{1,0:T(8,128)(2,1)} %constant_dynamic-update-slice_fusion.9, bf16[2048,1024]{0,1:T(8,128)(2,1)} %all-gather.8.cloned.1.call-done), kind=kOutput, calls=%fused_computation.3 | convolution fusion | flops 8747219968 | bytes 33562624 | tf_op jit(solution)/shard_map/dot_general | solution.py:409
  300.4 8.1 %multiply_convert_fusion = bf16[2048,1024]{1,0:T(8,128)(2,1)S(1)} fusion(f32[2048,1024]{1,0:T(8,128)} %get-tuple-element.34, f32[2048,1024]{1,0:T(8,128)} %fusion.53, f32[1024]{0:T(1024)S(1)} %add.335), kind=kLoop, calls=%fused_computation.5 | loop fusion | flops 8388608 | bytes 20975616 | tf_op jit(solution)/shard_map/convert_element_type | solution.py:406
  310.5 12.8 %convolution_convert_fusion = bf16[2048,1024]{1,0:T(8,128)(2,1)} fusion(bf16[2048,2048]{1,0:T(8,128)(2,1)} %constant_dynamic-update-slice_fusion.9, bf16[2048,1024]{1,0:T(8,128)(2,1)S(1)} %multiply_convert_fusion), kind=kOutput, calls=%fused_computation.25 | convolution fusion | flops 8592031744 | bytes 16777216 | tf_op jit(solution)/shard_map/dot_general | solution.py:129
  323.6 5.0 convolution_convert_fusion.9
  330.8 2.4 convolution_convert_fusion.7
  335.4 2.4 convolution_convert_fusion.5
  338.1 2.4 convolution_convert_fusion.10
  340.5 2.4 convolution_convert_fusion.8
  342.9 2.4 convolution_convert_fusion.6
  345.3 2.6 convolution_convert_fusion.3
  347.9 2.4 convolution_convert_fusion.4
  359.3 19.3 %collective-permute-done.40 = bf16[128,2048]{1,0:T(8,128)(2,1)S(1)} collective-permute-done((bf16[128,2048]{1,0:T(8,128)(2,1)S(1)}, bf16[128,2048]{1,0:T(8,128)(2,1)S(1)}, u32[]{:S(2)}, u32[]{:S(2)}) %collective-permute-start.40) | collective-permute-done | bytes 524320 | tf_op jit(solution)/shard_map/ppermute | solution.py:44
  380.5 11.6 %collective-permute-done.43 = bf16[128,2048]{1,0:T(8,128)(2,1)S(1)} collective-permute-done((bf16[128,2048]{1,0:T(8,128)(2,1)S(1)}, bf16[128,2048]{1,0:T(8,128)(2,1)S(1)}, u32[]{:S(2)}, u32[]{:S(2)}) %collective-permute-start.43) | collective-permute-done | bytes 524320 | tf_op jit(solution)/shard_map/ppermute | solution.py:36
  397.2 21.1 %collective-permute-done.41 = bf16[256,2048]{1,0:T(8,128)(2,1)S(1)} collective-permute-done((bf16[256,2048]{1,0:T(8,128)(2,1)S(1)}, bf16[256,2048]{1,0:T(8,128)(2,1)S(1)}, u32[]{:S(2)}, u32[]{:S(2)}) %collective-permute-start.41) | collective-permute-done | bytes 1048608 | tf_op jit(solution)/shard_map/ppermute | solution.py:36
  421.7 16.9 %collective-permute-done.29 = bf16[256,2048]{1,0:T(8,128)(2,1)S(1)} collective-permute-done((bf16[256,2048]{1,0:T(8,128)(2,1)S(1)}, bf16[256,2048]{1,0:T(8,128)(2,1)S(1)}, u32[]{:S(2)}, u32[]{:S(2)}) %collective-permute-start.29) | collective-permute-done | bytes 1048608 | tf_op jit(solution)/shard_map/ppermute | solution.py:36
  440.3 3.4 convert_reduce_fusion.4
  445.7 20.7 %collective-permute-done.45 = bf16[256,2048]{1,0:T(8,128)(2,1)S(1)} collective-permute-done((bf16[256,2048]{1,0:T(8,128)(2,1)S(1)}, bf16[256,2048]{1,0:T(8,128)(2,1)S(1)}, u32[]{:S(2)}, u32[]{:S(2)}) %collective-permute-start.45) | collective-permute-done | bytes 1048608 | tf_op jit(solution)/shard_map/ppermute | solution.py:36
  466.4 14.0 %convolution_convert_fusion.1 = bf16[2048,1024]{1,0:T(8,128)(2,1)} fusion(bf16[2048,2048]{1,0:T(8,128)(2,1)} %constant_dynamic-update-slice_fusion, bf16[2048,1024]{1,0:T(8,128)(2,1)} %get-tuple-element.33), kind=kOutput, calls=%fused_computation.26 | convolution fusion | flops 8592031744 | bytes 16777216 | tf_op jit(solution)/shard_map/dot_general | solution.py:129
  486.1 8.8 %collective-permute-done.49 = bf16[128,2048]{1,0:T(8,128)(2,1)S(1)} collective-permute-done((bf16[128,2048]{1,0:T(8,128)(2,1)S(1)}, bf16[128,2048]{1,0:T(8,128)(2,1)S(1)}, u32[]{:S(2)}, u32[]{:S(2)}) %collective-permute-start.49) | collective-permute-done | bytes 524320 | tf_op jit(solution)/shard_map/ppermute | solution.py:44
  494.9 2.0 collective-permute-done.50
  500.7 2.5 convolution_convert_fusion.20
  503.3 21.5 %attention_backward.1 = bf16[8,256,768]{2,1,0:T(8,128)(2,1)S(1)} custom-call(s32[10]{0:T(128)S(1)} %copy-done.5, bf16[8,256,768]{2,1,0:T(8,128)(2,1)S(1)} %bitcast.117, bf16[8,256,256]{2,1,0:T(8,128)(2,1)S(1)} %bitcast.118), custom_call_target="tpu_custom_call" | custom-call | flops 7046430720 | bytes 7340032 | tf_op jit(solution)/shard_map/attention_backward/pallas_call | solution.py:238
  533.8 2.4 convolution_convert_fusion.19
  536.2 9.4 %convolution_convert_fusion.2 = bf16[2048,768]{0,1:T(8,128)(2,1)S(1)} fusion(bf16[2048,768]{1,0:T(8,128)(2,1)S(1)} %bitcast.114, bf16[512,2048]{1,0:T(8,128)(2,1)} %collective-permute-done.8, bf16[512,2048]{1,0:T(8,128)(2,1)} %collective-permute-done.7, bf16[512,2048]{1,0:T(8,128)(2,1)} %collective-permute-done.6, bf16[512,2048]{1,0:T(8,128)(2,1)} %get-tuple-element.46), kind=kOutput, calls=%fused_computation.27 | convolution fusion | flops 6477578240 | bytes 14680064 | tf_op jit(solution)/shard_map/dot_general | solution.py:129
  545.6 2.5 pad_maximum_fusion.1
  548.2 4.1 convolution_convert_fusion.18
  554.1 2.3 add_convert_fusion.4
  559.2 11.8 %collective-permute-done.56 = bf16[128,2048]{1,0:T(8,128)(2,1)S(1)} collective-permute-done((bf16[128,2048]{1,0:T(8,128)(2,1)S(1)}, bf16[128,2048]{1,0:T(8,128)(2,1)S(1)}, u32[]{:S(2)}, u32[]{:S(2)}) %collective-permute-start.56) | collective-permute-done | bytes 524320 | tf_op jit(solution)/shard_map/ppermute | solution.py:44
  575.7 3.0 broadcast_select_fusion.1
  579.3 72.6 %psum.14 = f32[4,12,128]{2,1,0:T(8,128)S(1)} all-reduce(f32[4,12,128]{2,1,0:T(8,128)S(1)} %broadcast_select_fusion.2), channel_id=1, replica_groups=mesh['fsdp'=4,'ctx'=4,'tp'=2] {'fsdp','ctx'}, use_global_device_ids=true, to_apply=%region_11.12 | all-reduce | flops 6144 | bytes 49152 | tf_op jit(solution)/shard_map/psum | solution.py:476
  652.0 4.0 multiply_reduce_fusion.2
  660.3 50.8 %psum.15 = f32[6,2048]{1,0:T(8,128)S(1)} all-reduce(f32[6,2048]{1,0:T(8,128)S(1)} %stack.27), channel_id=1, replica_groups=mesh['fsdp'=4,'ctx'=4,'tp'=2] {'fsdp','ctx','tp'}, use_global_device_ids=true, to_apply=%region_18.19 | all-reduce | flops 12288 | bytes 98304 | tf_op jit(solution)/shard_map/psum | solution.py:460
  711.8 2.3 collective-permute-start.75
  715.8 4.4 broadcast_in_dim.79
  723.6 4.5 broadcast_in_dim.80
  730.0 2.7 broadcast_select_fusion
  734.2 2.6 copy.97
  738.2 3.1 constant_dynamic-update-slice_fusion.25
  742.8 2.8 convert_dynamic-update-slice_fusion.2
  745.6 2.8 convert_dynamic-update-slice_fusion.1
  752.9 2.2 slice_bitcast_fusion
  796.2 2.0 convert_dynamic-update-slice_fusion.4
  (438 shorter events, 173.6 us)
Async XLA Ops:
  7.2 96.0 %all-gather.4.cloned.1.call-start = ((), (), s32[]{:S(2)}) async-start(), calls=%async_computation.3 | async-start | bytes 5242880 | tf_op jit(solution)/shard_map/all_gather | solution.py:330
  13.3 18.7 %collective-permute-start.3 = (bf16[3456]{0:T(1024)(128)(2,1)S(1)}, bf16[3456]{0:T(1024)(128)(2,1)S(1)}, u32[]{:S(2)}, u32[]{:S(2)}) collective-permute-start(bf16[3456]{0:T(1024)(128)(2,1)S(1)} %concatenate.79), channel_id=1, source_target_pairs={{0,8},{8,16},{16,24},{24,0},{1,9},{9,17},{17,25},{25,1},{2,10},{10... | collective-permute-start | bytes 20744 | tf_op jit(solution)/shard_map/ppermute | solution.py:264
  16.3 15.9 %collective-permute-start.4 = (bf16[3456]{0:T(1024)(128)(2,1)S(1)}, bf16[3456]{0:T(1024)(128)(2,1)S(1)}, u32[]{:S(2)}, u32[]{:S(2)}) collective-permute-start(bf16[3456]{0:T(1024)(128)(2,1)S(1)} %concatenate.79), channel_id=1, source_target_pairs={{0,16},{8,24},{16,0},{24,8},{1,17},{9,25},{17,1},{25,9},{2,18},{10... | collective-permute-start | bytes 20744 | tf_op jit(solution)/shard_map/ppermute | solution.py:264
  24.0 205.8 %all-gather.6.cloned.1.call-start = ((), (), s32[]{:S(2)}) async-start(), calls=%async_computation.4 | async-start | bytes 5242880 | tf_op jit(solution)/shard_map/all_gather | solution.py:333
  36.7 46.8 %collective-permute-start.7 = (bf16[512,2048]{1,0:T(8,128)(2,1)}, bf16[512,2048]{1,0:T(8,128)(2,1)}, u32[]{:S(2)}, u32[]{:S(2)}) collective-permute-start(bf16[512,2048]{1,0:T(8,128)(2,1)} %get-tuple-element.46), channel_id=1, source_target_pairs={{0,4},{4,0},{2,6},{6,2},{1,5},{5,1},{3,7},{7,3},{8,12},{12,8},{10,... | collective-permute-start | bytes 6291464 | tf_op jit(solution)/shard_map/ppermute | solution.py:44
  38.3 53.9 %collective-permute-start.6 = (bf16[512,2048]{1,0:T(8,128)(2,1)}, bf16[512,2048]{1,0:T(8,128)(2,1)}, u32[]{:S(2)}, u32[]{:S(2)}) collective-permute-start(bf16[512,2048]{1,0:T(8,128)(2,1)} %get-tuple-element.46), channel_id=1, source_target_pairs={{0,2},{2,0},{4,6},{6,4},{1,3},{3,1},{5,7},{7,5},{8,10},{10,8},{12,... | collective-permute-start | bytes 6291464 | tf_op jit(solution)/shard_map/ppermute | solution.py:40
  86.8 69.5 %collective-permute-start.35 = (bf16[512,2048]{1,0:T(8,128)(2,1)}, bf16[512,2048]{1,0:T(8,128)(2,1)}, u32[]{:S(2)}, u32[]{:S(2)}) collective-permute-start(bf16[512,2048]{1,0:T(8,128)(2,1)} %pad_maximum_fusion.3), channel_id=1, source_target_pairs={{0,4},{4,0},{2,6},{6,2},{1,5},{5,1},{3,7},{7,3},{8,12},{12,8},{10,... | collective-permute-start | bytes 6291464 | tf_op jit(solution)/shard_map/ppermute | solution.py:44
  89.6 176.5 %all-gather.8.cloned.1.call-start = ((), (), s32[]{:S(2)}) async-start(), calls=%async_computation.5 | async-start | bytes 5242880 | tf_op jit(solution)/shard_map/all_gather | solution.py:334
  131.2 25.7 %collective-permute-start.9 = (bf16[256,2048]{1,0:T(8,128)(2,1)}, bf16[256,2048]{1,0:T(8,128)(2,1)S(1)}, u32[]{:S(2)}, u32[]{:S(2)}) collective-permute-start(bf16[256,2048]{1,0:T(8,128)(2,1)} %get-tuple-element.70), channel_id=1, source_target_pairs={{0,2},{2,0},{4,6},{6,4},{1,3},{3,1},{5,7},{7,5},{8,10},{10,8},{12,... | collective-permute-start | bytes 3145736 | tf_op jit(solution)/shard_map/ppermute | solution.py:40
  134.0 14.0 %collective-permute-start.12 = (bf16[128,2048]{1,0:T(8,128)(2,1)S(1)}, bf16[128,2048]{1,0:T(8,128)(2,1)S(1)}, u32[]{:S(2)}, u32[]{:S(2)}) collective-permute-start(bf16[128,2048]{1,0:T(8,128)(2,1)S(1)} %get-tuple-element.91), channel_id=1, source_target_pairs={{0,4},{4,0},{2,6},{6,2},{1,5},{5,1},{3,7},{7,3},{8,12},{12,8},{10,... | collective-permute-start | bytes 1572872 | tf_op jit(solution)/shard_map/ppermute | solution.py:44
  136.3 14.3 %collective-permute-start.15 = (bf16[128,2048]{1,0:T(8,128)(2,1)S(1)}, bf16[128,2048]{1,0:T(8,128)(2,1)S(1)}, u32[]{:S(2)}, u32[]{:S(2)}) collective-permute-start(bf16[128,2048]{1,0:T(8,128)(2,1)S(1)} %get-tuple-element.92), channel_id=1, source_target_pairs={{0,1},{1,0},{2,3},{3,2},{4,5},{5,4},{6,7},{7,6},{8,9},{9,8},{10,11... | collective-permute-start | bytes 1572872 | tf_op jit(solution)/shard_map/ppermute | solution.py:36
  149.2 24.7 %collective-permute-start.13 = (bf16[256,2048]{1,0:T(8,128)(2,1)}, bf16[256,2048]{1,0:T(8,128)(2,1)}, u32[]{:S(2)}, u32[]{:S(2)}) collective-permute-start(bf16[256,2048]{1,0:T(8,128)(2,1)} %pad_maximum_fusion.7), channel_id=1, source_target_pairs={{0,1},{1,0},{2,3},{3,2},{4,5},{5,4},{6,7},{7,6},{8,9},{9,8},{10,11... | collective-permute-start | bytes 3145736 | tf_op jit(solution)/shard_map/ppermute | solution.py:36
  151.9 24.5 %collective-permute-start.16 = (bf16[256,2048]{1,0:T(8,128)(2,1)}, bf16[256,2048]{1,0:T(8,128)(2,1)}, u32[]{:S(2)}, u32[]{:S(2)}) collective-permute-start(bf16[256,2048]{1,0:T(8,128)(2,1)} %pad_maximum_fusion.8), channel_id=1, source_target_pairs={{0,4},{4,0},{2,6},{6,2},{1,5},{5,1},{3,7},{7,3},{8,12},{12,8},{10,... | collective-permute-start | bytes 3145736 | tf_op jit(solution)/shard_map/ppermute | solution.py:44
  153.3 31.3 %collective-permute-start.34 = (bf16[512,2048]{1,0:T(8,128)(2,1)}, bf16[512,2048]{1,0:T(8,128)(2,1)}, u32[]{:S(2)}, u32[]{:S(2)}) collective-permute-start(bf16[512,2048]{1,0:T(8,128)(2,1)} %pad_maximum_fusion.3), channel_id=1, source_target_pairs={{0,2},{2,0},{4,6},{6,4},{1,3},{3,1},{5,7},{7,5},{8,10},{10,8},{12,... | collective-permute-start | bytes 6291464 | tf_op jit(solution)/shard_map/ppermute | solution.py:40
  155.6 503.2 %reduce-scatter.8.cloned.1.call-start = ((), (), s32[]{:S(2)}) async-start(), calls=%async_computation.8 | async-start | bytes 5242880 | tf_op jit(solution)/shard_map/reduce_scatter | solution.py:408
  156.3 55.1 %collective-permute-start.36 = (bf16[512,2048]{1,0:T(8,128)(2,1)}, bf16[512,2048]{1,0:T(8,128)(2,1)}, u32[]{:S(2)}, u32[]{:S(2)}) collective-permute-start(bf16[512,2048]{1,0:T(8,128)(2,1)} %collective-permute-done.35), channel_id=1, source_target_pairs={{0,2},{2,0},{4,6},{6,4},{1,3},{3,1},{5,7},{7,5},{8,10},{10,8},{12,... | collective-permute-start | bytes 6291464 | tf_op jit(solution)/shard_map/ppermute | solution.py:40
  181.5 23.3 %collective-permute-start.17 = (bf16[256,2048]{1,0:T(8,128)(2,1)S(1)}, bf16[256,2048]{1,0:T(8,128)(2,1)S(1)}, u32[]{:S(2)}, u32[]{:S(2)}) collective-permute-start(bf16[256,2048]{1,0:T(8,128)(2,1)S(1)} %get-tuple-element.38), channel_id=1, source_target_pairs={{0,1},{1,0},{2,3},{3,2},{4,5},{5,4},{6,7},{7,6},{8,9},{9,8},{10,11... | collective-permute-start | bytes 3145736 | tf_op jit(solution)/shard_map/ppermute | solution.py:36
  183.0 26.6 %collective-permute-start.20 = (bf16[256,2048]{1,0:T(8,128)(2,1)S(1)}, bf16[256,2048]{1,0:T(8,128)(2,1)S(1)}, u32[]{:S(2)}, u32[]{:S(2)}) collective-permute-start(bf16[256,2048]{1,0:T(8,128)(2,1)S(1)} %get-tuple-element.38), channel_id=1, source_target_pairs={{0,4},{4,0},{2,6},{6,2},{1,5},{5,1},{3,7},{7,3},{8,12},{12,8},{10,... | collective-permute-start | bytes 3145736 | tf_op jit(solution)/shard_map/ppermute | solution.py:44
  184.6 31.0 %collective-permute-start.18 = (bf16[256,2048]{1,0:T(8,128)(2,1)S(1)}, bf16[256,2048]{1,0:T(8,128)(2,1)S(1)}, u32[]{:S(2)}, u32[]{:S(2)}) collective-permute-start(bf16[256,2048]{1,0:T(8,128)(2,1)S(1)} %get-tuple-element.38), channel_id=1, source_target_pairs={{0,2},{2,0},{4,6},{6,4},{1,3},{3,1},{5,7},{7,5},{8,10},{10,8},{12,... | collective-permute-start | bytes 3145736 | tf_op jit(solution)/shard_map/ppermute | solution.py:40
  204.8 19.1 %collective-permute-start.19 = (bf16[256,2048]{1,0:T(8,128)(2,1)S(1)}, bf16[256,2048]{1,0:T(8,128)(2,1)S(1)}, u32[]{:S(2)}, u32[]{:S(2)}) collective-permute-start(bf16[256,2048]{1,0:T(8,128)(2,1)S(1)} %collective-permute-done.17), channel_id=1, source_target_pairs={{0,2},{2,0},{4,6},{6,4},{1,3},{3,1},{5,7},{7,5},{8,10},{10,8},{12,... | collective-permute-start | bytes 3145736 | tf_op jit(solution)/shard_map/ppermute | solution.py:40
  208.0 14.4 %collective-permute-start.21 = (bf16[128,2048]{1,0:T(8,128)(2,1)S(1)}, bf16[128,2048]{1,0:T(8,128)(2,1)S(1)}, u32[]{:S(2)}, u32[]{:S(2)}) collective-permute-start(bf16[128,2048]{1,0:T(8,128)(2,1)S(1)} %slice.487), channel_id=1, source_target_pairs={{0,4},{4,0},{2,6},{6,2},{1,5},{5,1},{3,7},{7,3},{8,12},{12,8},{10,... | collective-permute-start | bytes 1572872 | tf_op jit(solution)/shard_map/ppermute | solution.py:44
  209.6 14.1 %collective-permute-start.22 = (bf16[128,2048]{1,0:T(8,128)(2,1)S(1)}, bf16[128,2048]{1,0:T(8,128)(2,1)S(1)}, u32[]{:S(2)}, u32[]{:S(2)}) collective-permute-start(bf16[128,2048]{1,0:T(8,128)(2,1)S(1)} %slice.488), channel_id=1, source_target_pairs={{0,1},{1,0},{2,3},{3,2},{4,5},{5,4},{6,7},{7,6},{8,9},{9,8},{10,11... | collective-permute-start | bytes 1572872 | tf_op jit(solution)/shard_map/ppermute | solution.py:36
  323.4 388.4 %reduce-scatter.6.cloned.1.call-start = ((), (), s32[]{:S(2)}) async-start(), calls=%async_computation.7 | async-start | bytes 5242880 | tf_op jit(solution)/shard_map/reduce_scatter | solution.py:413
  328.8 21.6 %collective-permute-start.26 = (bf16[256,2048]{1,0:T(8,128)(2,1)S(1)}, bf16[256,2048]{1,0:T(8,128)(2,1)S(1)}, u32[]{:S(2)}, u32[]{:S(2)}) collective-permute-start(bf16[256,2048]{1,0:T(8,128)(2,1)S(1)} %get-tuple-element.65), channel_id=1, source_target_pairs={{0,2},{2,0},{4,6},{6,4},{1,3},{3,1},{5,7},{7,5},{8,10},{10,8},{12,... | collective-permute-start | bytes 3145736 | tf_op jit(solution)/shard_map/ppermute | solution.py:40
  333.4 18.0 %collective-permute-start.27 = (bf16[256,2048]{1,0:T(8,128)(2,1)S(1)}, bf16[256,2048]{1,0:T(8,128)(2,1)S(1)}, u32[]{:S(2)}, u32[]{:S(2)}) collective-permute-start(bf16[256,2048]{1,0:T(8,128)(2,1)S(1)} %get-tuple-element.68), channel_id=1, source_target_pairs={{0,2},{2,0},{4,6},{6,4},{1,3},{3,1},{5,7},{7,5},{8,10},{10,8},{12,... | collective-permute-start | bytes 3145736 | tf_op jit(solution)/shard_map/ppermute | solution.py:40
  333.5 18.0 %collective-permute-start.30 = (bf16[256,2048]{1,0:T(8,128)(2,1)S(1)}, bf16[256,2048]{1,0:T(8,128)(2,1)S(1)}, u32[]{:S(2)}, u32[]{:S(2)}) collective-permute-start(bf16[256,2048]{1,0:T(8,128)(2,1)S(1)} %get-tuple-element.69), channel_id=1, source_target_pairs={{0,2},{2,0},{4,6},{6,4},{1,3},{3,1},{5,7},{7,5},{8,10},{10,8},{12,... | collective-permute-start | bytes 3145736 | tf_op jit(solution)/shard_map/ppermute | solution.py:40
  333.9 87.7 %collective-permute-start.25 = (bf16[256,2048]{1,0:T(8,128)(2,1)S(1)}, bf16[256,2048]{1,0:T(8,128)(2,1)S(1)}, u32[]{:S(2)}, u32[]{:S(2)}) collective-permute-start(bf16[256,2048]{1,0:T(8,128)(2,1)S(1)} %get-tuple-element.64), channel_id=1, source_target_pairs={{0,2},{2,0},{4,6},{6,4},{1,3},{3,1},{5,7},{7,5},{8,10},{10,8},{12,... | collective-permute-start | bytes 3145736 | tf_op jit(solution)/shard_map/ppermute | solution.py:40
  338.0 19.2 %collective-permute-start.38 = (bf16[256,2048]{1,0:T(8,128)(2,1)S(1)}, bf16[256,2048]{1,0:T(8,128)(2,1)S(1)}, u32[]{:S(2)}, u32[]{:S(2)}) collective-permute-start(bf16[256,2048]{1,0:T(8,128)(2,1)S(1)} %get-tuple-element.57), channel_id=1, source_target_pairs={{0,2},{2,0},{4,6},{6,4},{1,3},{3,1},{5,7},{7,5},{8,10},{10,8},{12,... | collective-permute-start | bytes 3145736 | tf_op jit(solution)/shard_map/ppermute | solution.py:40
  351.5 45.2 %collective-permute-start.37 = (bf16[256,2048]{1,0:T(8,128)(2,1)S(1)}, bf16[256,2048]{1,0:T(8,128)(2,1)S(1)}, u32[]{:S(2)}, u32[]{:S(2)}) collective-permute-start(bf16[256,2048]{1,0:T(8,128)(2,1)S(1)} %get-tuple-element.56), channel_id=1, source_target_pairs={{0,2},{2,0},{4,6},{6,4},{1,3},{3,1},{5,7},{7,5},{8,10},{10,8},{12,... | collective-permute-start | bytes 3145736 | tf_op jit(solution)/shard_map/ppermute | solution.py:40
  353.2 40.8 %collective-permute-start.28 = (bf16[128,2048]{1,0:T(8,128)(2,1)S(1)}, bf16[128,2048]{1,0:T(8,128)(2,1)S(1)}, u32[]{:S(2)}, u32[]{:S(2)}) collective-permute-start(bf16[128,2048]{1,0:T(8,128)(2,1)S(1)} %get-tuple-element.89), channel_id=1, source_target_pairs={{0,4},{4,0},{2,6},{6,2},{1,5},{5,1},{3,7},{7,3},{8,12},{12,8},{10,... | collective-permute-start | bytes 1572872 | tf_op jit(solution)/shard_map/ppermute | solution.py:44
  354.9 41.0 %collective-permute-start.31 = (bf16[128,2048]{1,0:T(8,128)(2,1)S(1)}, bf16[128,2048]{1,0:T(8,128)(2,1)S(1)}, u32[]{:S(2)}, u32[]{:S(2)}) collective-permute-start(bf16[128,2048]{1,0:T(8,128)(2,1)S(1)} %get-tuple-element.90), channel_id=1, source_target_pairs={{0,1},{1,0},{2,3},{3,2},{4,5},{5,4},{6,7},{7,6},{8,9},{9,8},{10,11... | collective-permute-start | bytes 1572872 | tf_op jit(solution)/shard_map/ppermute | solution.py:36
  357.3 21.4 %collective-permute-start.40 = (bf16[128,2048]{1,0:T(8,128)(2,1)S(1)}, bf16[128,2048]{1,0:T(8,128)(2,1)S(1)}, u32[]{:S(2)}, u32[]{:S(2)}) collective-permute-start(bf16[128,2048]{1,0:T(8,128)(2,1)S(1)} %get-tuple-element.87), channel_id=1, source_target_pairs={{0,4},{4,0},{2,6},{6,2},{1,5},{5,1},{3,7},{7,3},{8,12},{12,8},{10,... | collective-permute-start | bytes 1572872 | tf_op jit(solution)/shard_map/ppermute | solution.py:44
  392.1 26.1 %collective-permute-start.41 = (bf16[256,2048]{1,0:T(8,128)(2,1)S(1)}, bf16[256,2048]{1,0:T(8,128)(2,1)S(1)}, u32[]{:S(2)}, u32[]{:S(2)}) collective-permute-start(bf16[256,2048]{1,0:T(8,128)(2,1)S(1)} %pad_maximum_fusion.12), channel_id=1, source_target_pairs={{0,1},{1,0},{2,3},{3,2},{4,5},{5,4},{6,7},{7,6},{8,9},{9,8},{10,11... | collective-permute-start | bytes 3145736 | tf_op jit(solution)/shard_map/ppermute | solution.py:36
  394.1 26.2 %collective-permute-start.44 = (bf16[256,2048]{1,0:T(8,128)(2,1)S(1)}, bf16[256,2048]{1,0:T(8,128)(2,1)S(1)}, u32[]{:S(2)}, u32[]{:S(2)}) collective-permute-start(bf16[256,2048]{1,0:T(8,128)(2,1)S(1)} %pad_maximum_fusion.13), channel_id=1, source_target_pairs={{0,4},{4,0},{2,6},{6,2},{1,5},{5,1},{3,7},{7,3},{8,12},{12,8},{10,... | collective-permute-start | bytes 3145736 | tf_op jit(solution)/shard_map/ppermute | solution.py:44
  395.8 42.7 %collective-permute-start.29 = (bf16[256,2048]{1,0:T(8,128)(2,1)S(1)}, bf16[256,2048]{1,0:T(8,128)(2,1)S(1)}, u32[]{:S(2)}, u32[]{:S(2)}) collective-permute-start(bf16[256,2048]{1,0:T(8,128)(2,1)S(1)} %pad_maximum_fusion.10), channel_id=1, source_target_pairs={{0,1},{1,0},{2,3},{3,2},{4,5},{5,4},{6,7},{7,6},{8,9},{9,8},{10,11... | collective-permute-start | bytes 3145736 | tf_op jit(solution)/shard_map/ppermute | solution.py:36
  396.7 43.5 %collective-permute-start.32 = (bf16[256,2048]{1,0:T(8,128)(2,1)S(1)}, bf16[256,2048]{1,0:T(8,128)(2,1)S(1)}, u32[]{:S(2)}, u32[]{:S(2)}) collective-permute-start(bf16[256,2048]{1,0:T(8,128)(2,1)S(1)} %pad_maximum_fusion.11), channel_id=1, source_target_pairs={{0,4},{4,0},{2,6},{6,2},{1,5},{5,1},{3,7},{7,3},{8,12},{12,8},{10,... | collective-permute-start | bytes 3145736 | tf_op jit(solution)/shard_map/ppermute | solution.py:44
  443.7 22.7 %collective-permute-start.45 = (bf16[256,2048]{1,0:T(8,128)(2,1)S(1)}, bf16[256,2048]{1,0:T(8,128)(2,1)S(1)}, u32[]{:S(2)}, u32[]{:S(2)}) collective-permute-start(bf16[256,2048]{1,0:T(8,128)(2,1)S(1)} %get-tuple-element.30), channel_id=1, source_target_pairs={{0,1},{1,0},{2,3},{3,2},{4,5},{5,4},{6,7},{7,6},{8,9},{9,8},{10,11... | collective-permute-start | bytes 3145736 | tf_op jit(solution)/shard_map/ppermute | solution.py:36
  444.1 38.0 %collective-permute-start.48 = (bf16[256,2048]{1,0:T(8,128)(2,1)S(1)}, bf16[256,2048]{1,0:T(8,128)(2,1)S(1)}, u32[]{:S(2)}, u32[]{:S(2)}) collective-permute-start(bf16[256,2048]{1,0:T(8,128)(2,1)S(1)} %get-tuple-element.30), channel_id=1, source_target_pairs={{0,4},{4,0},{2,6},{6,2},{1,5},{5,1},{3,7},{7,3},{8,12},{12,8},{10,... | collective-permute-start | bytes 3145736 | tf_op jit(solution)/shard_map/ppermute | solution.py:44
  445.7 38.7 %collective-permute-start.46 = (bf16[256,2048]{1,0:T(8,128)(2,1)S(1)}, bf16[256,2048]{1,0:T(8,128)(2,1)}, u32[]{:S(2)}, u32[]{:S(2)}) collective-permute-start(bf16[256,2048]{1,0:T(8,128)(2,1)S(1)} %get-tuple-element.30), channel_id=1, source_target_pairs={{0,2},{2,0},{4,6},{6,4},{1,3},{3,1},{5,7},{7,5},{8,10},{10,8},{12,... | collective-permute-start | bytes 3145736 | tf_op jit(solution)/shard_map/ppermute | solution.py:40
  466.4 30.7 %collective-permute-start.47 = (bf16[256,2048]{1,0:T(8,128)(2,1)S(1)}, bf16[256,2048]{1,0:T(8,128)(2,1)}, u32[]{:S(2)}, u32[]{:S(2)}) collective-permute-start(bf16[256,2048]{1,0:T(8,128)(2,1)S(1)} %collective-permute-done.45), channel_id=1, source_target_pairs={{0,2},{2,0},{4,6},{6,4},{1,3},{3,1},{5,7},{7,5},{8,10},{10,8},{12,... | collective-permute-start | bytes 3145736 | tf_op jit(solution)/shard_map/ppermute | solution.py:40
  480.4 272.5 %reduce-scatter.4.cloned.1.call-start = ((), (), s32[]{:S(2)}) async-start(), calls=%async_computation.6 | async-start | bytes 5242880 | tf_op jit(solution)/shard_map/reduce_scatter | solution.py:430
  480.5 14.4 %collective-permute-start.49 = (bf16[128,2048]{1,0:T(8,128)(2,1)S(1)}, bf16[128,2048]{1,0:T(8,128)(2,1)S(1)}, u32[]{:S(2)}, u32[]{:S(2)}) collective-permute-start(bf16[128,2048]{1,0:T(8,128)(2,1)S(1)} %slice.527), channel_id=1, source_target_pairs={{0,4},{4,0},{2,6},{6,2},{1,5},{5,1},{3,7},{7,3},{8,12},{12,8},{10,... | collective-permute-start | bytes 1572872 | tf_op jit(solution)/shard_map/ppermute | solution.py:44
  482.1 14.8 %collective-permute-start.50 = (bf16[128,2048]{1,0:T(8,128)(2,1)S(1)}, bf16[128,2048]{1,0:T(8,128)(2,1)S(1)}, u32[]{:S(2)}, u32[]{:S(2)}) collective-permute-start(bf16[128,2048]{1,0:T(8,128)(2,1)S(1)} %slice.528), channel_id=1, source_target_pairs={{0,1},{1,0},{2,3},{3,2},{4,5},{5,4},{6,7},{7,6},{8,9},{9,8},{10,11... | collective-permute-start | bytes 1572872 | tf_op jit(solution)/shard_map/ppermute | solution.py:36
  482.8 92.9 %collective-permute-start.33 = (bf16[256,2048]{1,0:T(8,128)(2,1)}, bf16[256,2048]{1,0:T(8,128)(2,1)}, u32[]{:S(2)}, u32[]{:S(2)}) collective-permute-start(bf16[256,2048]{1,0:T(8,128)(2,1)} %get-tuple-element.55), channel_id=1, source_target_pairs={{0,1},{1,0},{2,3},{3,2},{4,5},{5,4},{6,7},{7,6},{8,9},{9,8},{10,11... | collective-permute-start | bytes 3145736 | tf_op jit(solution)/shard_map/ppermute | solution.py:36
  484.4 14.2 %collective-permute-start.51 = (bf16[256,2048]{1,0:T(8,128)(2,1)S(1)}, bf16[256,2048]{1,0:T(8,128)(2,1)S(1)}, u32[]{:S(2)}, u32[]{:S(2)}) collective-permute-start(bf16[256,2048]{1,0:T(8,128)(2,1)S(1)} %collective-permute-done.48), channel_id=1, source_target_pairs={{0,2},{2,0},{4,6},{6,4},{1,3},{3,1},{5,7},{7,5},{8,10},{10,8},{12,... | collective-permute-start | bytes 3145736 | tf_op jit(solution)/shard_map/ppermute | solution.py:40
  529.5 27.6 %collective-permute-start.54 = (bf16[256,2048]{1,0:T(8,128)(2,1)}, bf16[256,2048]{1,0:T(8,128)(2,1)}, u32[]{:S(2)}, u32[]{:S(2)}) collective-permute-start(bf16[256,2048]{1,0:T(8,128)(2,1)} %get-tuple-element.50), channel_id=1, source_target_pairs={{0,2},{2,0},{4,6},{6,4},{1,3},{3,1},{5,7},{7,5},{8,10},{10,8},{12,... | collective-permute-start | bytes 3145736 | tf_op jit(solution)/shard_map/ppermute | solution.py:40
  533.2 20.9 %collective-permute-start.55 = (bf16[256,2048]{1,0:T(8,128)(2,1)}, bf16[256,2048]{1,0:T(8,128)(2,1)}, u32[]{:S(2)}, u32[]{:S(2)}) collective-permute-start(bf16[256,2048]{1,0:T(8,128)(2,1)} %get-tuple-element.53), channel_id=1, source_target_pairs={{0,2},{2,0},{4,6},{6,4},{1,3},{3,1},{5,7},{7,5},{8,10},{10,8},{12,... | collective-permute-start | bytes 3145736 | tf_op jit(solution)/shard_map/ppermute | solution.py:40
  533.3 20.9 %collective-permute-start.58 = (bf16[256,2048]{1,0:T(8,128)(2,1)}, bf16[256,2048]{1,0:T(8,128)(2,1)}, u32[]{:S(2)}, u32[]{:S(2)}) collective-permute-start(bf16[256,2048]{1,0:T(8,128)(2,1)} %get-tuple-element.54), channel_id=1, source_target_pairs={{0,2},{2,0},{4,6},{6,4},{1,3},{3,1},{5,7},{7,5},{8,10},{10,8},{12,... | collective-permute-start | bytes 3145736 | tf_op jit(solution)/shard_map/ppermute | solution.py:40
  533.7 118.2 %collective-permute-start.53 = (bf16[256,2048]{1,0:T(8,128)(2,1)}, bf16[256,2048]{1,0:T(8,128)(2,1)}, u32[]{:S(2)}, u32[]{:S(2)}) collective-permute-start(bf16[256,2048]{1,0:T(8,128)(2,1)} %get-tuple-element.49), channel_id=1, source_target_pairs={{0,2},{2,0},{4,6},{6,4},{1,3},{3,1},{5,7},{7,5},{8,10},{10,8},{12,... | collective-permute-start | bytes 3145736 | tf_op jit(solution)/shard_map/ppermute | solution.py:40
  556.5 14.5 %collective-permute-start.56 = (bf16[128,2048]{1,0:T(8,128)(2,1)S(1)}, bf16[128,2048]{1,0:T(8,128)(2,1)S(1)}, u32[]{:S(2)}, u32[]{:S(2)}) collective-permute-start(bf16[128,2048]{1,0:T(8,128)(2,1)S(1)} %get-tuple-element.85), channel_id=1, source_target_pairs={{0,4},{4,0},{2,6},{6,2},{1,5},{5,1},{3,7},{7,3},{8,12},{12,8},{10,... | collective-permute-start | bytes 1572872 | tf_op jit(solution)/shard_map/ppermute | solution.py:44
  558.7 14.1 %collective-permute-start.59 = (bf16[128,2048]{1,0:T(8,128)(2,1)S(1)}, bf16[128,2048]{1,0:T(8,128)(2,1)S(1)}, u32[]{:S(2)}, u32[]{:S(2)}) collective-permute-start(bf16[128,2048]{1,0:T(8,128)(2,1)S(1)} %get-tuple-element.86), channel_id=1, source_target_pairs={{0,1},{1,0},{2,3},{3,2},{4,5},{5,4},{6,7},{7,6},{8,9},{9,8},{10,11... | collective-permute-start | bytes 1572872 | tf_op jit(solution)/shard_map/ppermute | solution.py:36
  572.2 79.7 %collective-permute-start.57 = (bf16[256,2048]{1,0:T(8,128)(2,1)}, bf16[256,2048]{1,0:T(8,128)(2,1)}, u32[]{:S(2)}, u32[]{:S(2)}) collective-permute-start(bf16[256,2048]{1,0:T(8,128)(2,1)} %pad_maximum_fusion.15), channel_id=1, source_target_pairs={{0,1},{1,0},{2,3},{3,2},{4,5},{5,4},{6,7},{7,6},{8,9},{9,8},{10,11... | collective-permute-start | bytes 3145736 | tf_op jit(solution)/shard_map/ppermute | solution.py:36
  574.1 77.9 %collective-permute-start.60 = (bf16[256,2048]{1,0:T(8,128)(2,1)}, bf16[256,2048]{1,0:T(8,128)(2,1)}, u32[]{:S(2)}, u32[]{:S(2)}) collective-permute-start(bf16[256,2048]{1,0:T(8,128)(2,1)} %pad_maximum_fusion.16), channel_id=1, source_target_pairs={{0,4},{4,0},{2,6},{6,2},{1,5},{5,1},{3,7},{7,3},{8,12},{12,8},{10,... | collective-permute-start | bytes 3145736 | tf_op jit(solution)/shard_map/ppermute | solution.py:44
  657.3 72.7 %collective-permute-start.61 = (bf16[256,2048]{1,0:T(8,128)(2,1)S(1)}, bf16[256,2048]{1,0:T(8,128)(2,1)}, u32[]{:S(2)}, u32[]{:S(2)}) collective-permute-start(bf16[256,2048]{1,0:T(8,128)(2,1)S(1)} %add_convert_fusion.3), channel_id=1, source_target_pairs={{0,1},{1,0},{2,3},{3,2},{4,5},{5,4},{6,7},{7,6},{8,9},{9,8},{10,11... | collective-permute-start | bytes 3145736 | tf_op jit(solution)/shard_map/ppermute | solution.py:36
  658.8 70.8 %collective-permute-start.78 = (bf16[1024,512]{0,1:T(8,128)(2,1)}, bf16[1024,512]{0,1:T(8,128)(2,1)}, u32[]{:S(2)}, u32[]{:S(2)}) collective-permute-start(bf16[1024,512]{0,1:T(8,128)(2,1)} %bitcast.119), channel_id=1, source_target_pairs={{0,4},{4,0},{2,6},{6,2},{1,5},{5,1},{3,7},{7,3},{8,12},{12,8},{10,... | collective-permute-start | bytes 3145736 | tf_op jit(solution)/shard_map/ppermute | solution.py:44
  711.8 22.4 %collective-permute-start.77 = (bf16[1024,512]{0,1:T(8,128)(2,1)}, bf16[1024,512]{0,1:T(8,128)(2,1)}, u32[]{:S(2)}, u32[]{:S(2)}) collective-permute-start(bf16[1024,512]{0,1:T(8,128)(2,1)} %bitcast.120), channel_id=1, source_target_pairs={{0,2},{2,0},{4,6},{6,4},{1,3},{3,1},{5,7},{7,5},{8,10},{10,8},{12,... | collective-permute-start | bytes 3145736 | tf_op jit(solution)/shard_map/ppermute | solution.py:40
  711.8 26.4 %collective-permute-start.75 = (bf16[512,1024]{1,0:T(8,128)(2,1)}, bf16[512,1024]{1,0:T(8,128)(2,1)}, u32[]{:S(2)}, u32[]{:S(2)}) collective-permute-start(bf16[512,1024]{1,0:T(8,128)(2,1)} %reduce-scatter.6.cloned.1.call-done), channel_id=1, source_target_pairs={{0,4},{4,0},{2,6},{6,2},{1,5},{5,1},{3,7},{7,3},{8,12},{12,8},{10,... | collective-permute-start | bytes 3145736 | tf_op jit(solution)/shard_map/ppermute | solution.py:44
  715.6 27.2 %collective-permute-start.74 = (bf16[512,1024]{1,0:T(8,128)(2,1)}, bf16[512,1024]{1,0:T(8,128)(2,1)}, u32[]{:S(2)}, u32[]{:S(2)}) collective-permute-start(bf16[512,1024]{1,0:T(8,128)(2,1)} %reduce-scatter.6.cloned.1.call-done), channel_id=1, source_target_pairs={{0,2},{2,0},{4,6},{6,4},{1,3},{3,1},{5,7},{7,5},{8,10},{10,8},{12,... | collective-permute-start | bytes 3145736 | tf_op jit(solution)/shard_map/ppermute | solution.py:40
  729.6 18.8 %collective-permute-start.79 = (bf16[1024,512]{0,1:T(8,128)(2,1)}, bf16[1024,512]{0,1:T(8,128)(2,1)}, u32[]{:S(2)}, u32[]{:S(2)}) collective-permute-start(bf16[1024,512]{0,1:T(8,128)(2,1)} %collective-permute-done.78), channel_id=1, source_target_pairs={{0,2},{2,0},{4,6},{6,4},{1,3},{3,1},{5,7},{7,5},{8,10},{10,8},{12,... | collective-permute-start | bytes 3145736 | tf_op jit(solution)/shard_map/ppermute | solution.py:40
  755.7 13.9 %collective-permute-start.72 = (bf16[256,512]{1,0:T(8,128)(2,1)}, bf16[256,512]{1,0:T(8,128)(2,1)}, u32[]{:S(2)}, u32[]{:S(2)}) collective-permute-start(bf16[256,512]{1,0:T(8,128)(2,1)} %get-tuple-element.78), channel_id=1, source_target_pairs={{0,4},{4,0},{2,6},{6,2},{1,5},{5,1},{3,7},{7,3},{8,12},{12,8},{10,... | collective-permute-start | bytes 786440 | tf_op jit(solution)/shard_map/ppermute | solution.py:44
  757.4 14.0 %collective-permute-start.68 = (bf16[512,256]{0,1:T(8,128)(2,1)}, bf16[512,256]{0,1:T(8,128)(2,1)}, u32[]{:S(2)}, u32[]{:S(2)}) collective-permute-start(bf16[512,256]{0,1:T(8,128)(2,1)} %get-tuple-element.82), channel_id=1, source_target_pairs={{0,2},{2,0},{4,6},{6,4},{1,3},{3,1},{5,7},{7,5},{8,10},{10,8},{12,... | collective-permute-start | bytes 786440 | tf_op jit(solution)/shard_map/ppermute | solution.py:40
  757.4 15.4 %collective-permute-start.69 = (bf16[512,256]{0,1:T(8,128)(2,1)}, bf16[512,256]{0,1:T(8,128)(2,1)}, u32[]{:S(2)}, u32[]{:S(2)}) collective-permute-start(bf16[512,256]{0,1:T(8,128)(2,1)} %get-tuple-element.82), channel_id=1, source_target_pairs={{0,4},{4,0},{2,6},{6,2},{1,5},{5,1},{3,7},{7,3},{8,12},{12,8},{10,... | collective-permute-start | bytes 786440 | tf_op jit(solution)/shard_map/ppermute | solution.py:44
  758.1 19.1 %collective-permute-start.65 = (bf16[512,256]{0,1:T(8,128)(2,1)}, bf16[512,256]{0,1:T(8,128)(2,1)}, u32[]{:S(2)}, u32[]{:S(2)}) collective-permute-start(bf16[512,256]{0,1:T(8,128)(2,1)} %get-tuple-element.83), channel_id=1, source_target_pairs={{0,2},{2,0},{4,6},{6,4},{1,3},{3,1},{5,7},{7,5},{8,10},{10,8},{12,... | collective-permute-start | bytes 786440 | tf_op jit(solution)/shard_map/ppermute | solution.py:40
  772.8 23.4 %collective-permute-start.73 = (bf16[256,512]{1,0:T(8,128)(2,1)}, bf16[256,512]{1,0:T(8,128)(2,1)}, u32[]{:S(2)}, u32[]{:S(2)}) collective-permute-start(bf16[256,512]{1,0:T(8,128)(2,1)} %collective-permute-done.72), channel_id=1, source_target_pairs={{0,2},{2,0},{4,6},{6,4},{1,3},{3,1},{5,7},{7,5},{8,10},{10,8},{12,... | collective-permute-start | bytes 786440 | tf_op jit(solution)/shard_map/ppermute | solution.py:40
  (69 other events, 809.3 us)
Sparse Core Ops, SparseCore 0:
  24.1 79.0 all-gather.3
  105.3 79.2 all-gather.5
  186.8 79.2 all-gather.7
  323.5 75.2 reduce-scatter.7
  480.5 75.1 reduce-scatter.5
  557.9 77.8 reduce-scatter.3

commit v2 on v1

--- a/solution.py
+++ b/solution.py
@@ -44,21 +44,25 @@
     return lax.ppermute(value, "ctx", [(0, 2), (2, 0), (1, 3), (3, 1)])
 
 
+def after(value, *earlier):
+    return lax.optimization_barrier((value,) + earlier)[0]
+
+
 def gather_blocks(own):
     half = own.shape[0] // 2
     across = swap_tp(own)
     along = swap_high(own)
-    corner = jnp.concatenate([swap_high(across[:half]), swap_tp(along[half:])], axis=0)
+    corner_a = swap_high(across[:half])
+    corner_b = swap_tp(along[half:])
     return [
-        own,
-        across,
-        swap_low(own),
-        swap_low(across),
-        along,
-        corner,
-        swap_low(along),
-        swap_low(corner),
+        [own, swap_low(own)],
+        [across, swap_low(across)],
+        [along, swap_low(along)],
+        [corner_a, corner_b, swap_low(corner_a), swap_low(corner_b)],
     ]
+
+
+GROUPS = ((0, 2), (1, 3), (4, 6), (5, 7))
 
 
 def scatter_blocks(parts):
@@ -75,7 +79,7 @@
 def gather_ctx(pair):
     low = swap_low(pair)
     high = swap_high(pair)
-    return jnp.concatenate([pair, low, high, swap_low(high)], axis=0)
+    return [pair, low, high, swap_low(high)]
 
 
 def pair_mask(rows, limits, split):
@@ -253,6 +257,196 @@
         cost_estimate=attention_cost(blocks, rows, heads, 7),
         name="attention_backward",
     )(info, qkv, grad)
+
+
+def grad_matmul_kernel(n_left, spans, *refs):
+    out_ref = refs[-1]
+    total = None
+    for li, lo, ri, ro, size in spans:
+        left = refs[li][pl.ds(lo, size), :]
+        right = refs[n_left + ri][pl.ds(ro, size), :]
+        term = dot_tn(left, right)
+        total = term if total is None else total + term
+    out_ref[...] = total.astype(BF)
+
+
+def row_chunks(pieces, order, rows, chunk):
+    where = {}
+    place = 0
+    spots = []
+    for index, piece in enumerate(pieces):
+        for offset in range(0, piece.shape[0], chunk):
+            spots.append((index, offset))
+    per_block = rows // chunk
+    for block in order:
+        where[block] = spots[place : place + per_block]
+        place += per_block
+    return [spot for block in sorted(where) for spot in where[block]]
+
+
+def grad_matmul(lefts, left_order, rights, right_order, rows, name):
+    chunk = min([rows] + [p.shape[0] for p in list(lefts) + list(rights)])
+    spans = []
+    for left, right in zip(
+        row_chunks(lefts, left_order, rows, chunk), row_chunks(rights, right_order, rows, chunk)
+    ):
+        last = spans[-1] if spans else None
+        if last and left == (last[0], last[1] + last[4]) and right == (last[2], last[3] + last[4]):
+            spans[-1] = last[:4] + (last[4] + chunk,)
+        else:
+            spans.append(left + right + (chunk,))
+    d = lefts[0].shape[1]
+    n = rights[0].shape[1]
+    tile = 256
+    total_rows = sum(p.shape[0] for p in lefts)
+    return pl.pallas_call(
+        partial(grad_matmul_kernel, len(lefts), spans),
+        grid=(d // tile,),
+        in_specs=[pl.BlockSpec((p.shape[0], tile), lambda i: (0, i)) for p in lefts]
+        + [pl.BlockSpec(p.shape, lambda i: (0, 0), pipeline_mode=pl.Buffered(1)) for p in rights],
+        out_specs=pl.BlockSpec((tile, n), lambda i: (i, 0)),
+        out_shape=jax.ShapeDtypeStruct((d, n), BF),
+        compiler_params=pltpu.CompilerParams(vmem_limit_bytes=40 << 20),
+        cost_estimate=pl.CostEstimate(
+            flops=2 * total_rows * d * n,
+            transcendentals=0,
+            bytes_accessed=2 * (total_rows * (d + n) + d * n),
+        ),
+        name=name,
+    )(*lefts, *rights)
+
+
+def assemble_kernel(turn, count, width, ctx_ref, *refs):
+    pieces, outs = refs[:count], refs[count:]
+    step = pl.program_id(0)
+    for k in range(count):
+
+        @pl.when(step == k)
+        def _():
+            for i, out in enumerate(outs):
+                part = pieces[k][:, i * width : (i + 1) * width].astype(F32)
+                out[...] = part.T if turn else part
+
+
+def assemble(ctx, pieces, turn, outputs, name):
+    count = len(pieces)
+    rows, cols = pieces[0].shape
+    width = cols // outputs
+    if turn:
+        block, shape = (width, rows), (width * count, rows)
+        index = lambda k, ctx_ref: (k ^ ctx_ref[0], 0)
+    else:
+        block, shape = (rows, width), (rows, width * count)
+        index = lambda k, ctx_ref: (0, k ^ ctx_ref[0])
+    return pl.pallas_call(
+        partial(assemble_kernel, turn, count, width),
+        grid_spec=pltpu.PrefetchScalarGridSpec(
+            num_scalar_prefetch=1,
+            grid=(count,),
+            in_specs=[
+                pl.BlockSpec((rows, cols), lambda k, ctx_ref: (0, 0), pipeline_mode=pl.Buffered(1))
+                for _ in pieces
+            ],
+            out_specs=[pl.BlockSpec(block, index) for _ in range(outputs)],
+        ),
+        out_shape=[jax.ShapeDtypeStruct(shape, F32) for _ in range(outputs)],
+        compiler_params=pltpu.CompilerParams(vmem_limit_bytes=32 << 20),
+        cost_estimate=pl.CostEstimate(
+            flops=0, transcendentals=0, bytes_accessed=6 * count * rows * cols
+        ),
+        name=name,
+    )(ctx[None].astype(jnp.int32), *pieces)
+
+
+def gelu_and_slope(u):
+    half = 0.5 * (1.0 + lax.erf(u * math.sqrt(0.5)))
+    density = jnp.exp(-0.5 * u * u) * (1.0 / math.sqrt(2.0 * math.pi))
+    return u * half, half + u * density
+
+
+def forward_kernel(pieces, rows, *refs):
+    lefts, (w_ref, bias_ref, hidden_ref, slope_ref) = refs[: len(pieces)], refs[len(pieces) :]
+    for left, (start, size) in zip(lefts, pieces):
+        pre_act = dot_nn(left[...], w_ref[...]) + bias_ref[...]
+        hidden, slope = gelu_and_slope(pre_act)
+        hidden_ref[pl.ds(start, size), :] = hidden.astype(BF)
+        slope_ref[pl.ds(start, size), :] = slope
+
+
+def feed_forward(lefts, starts, weights, bias, units, name):
+    total = sum(p.shape[0] for p in lefts)
+    width = lefts[0].shape[1]
+    tile = 256
+    pieces = [(start, p.shape[0]) for start, p in zip(starts, lefts)]
+    return pl.pallas_call(
+        partial(forward_kernel, pieces, total),
+        grid=(units // tile,),
+        in_specs=[
+            pl.BlockSpec(p.shape, lambda i: (0, 0), pipeline_mode=pl.Buffered(1)) for p in lefts
+        ]
+        + [
+            pl.BlockSpec((width, tile), lambda i: (0, i)),
+            pl.BlockSpec((1, tile), lambda i: (0, i)),
+        ],
+        out_specs=[pl.BlockSpec((total, tile), lambda i: (0, i))] * 2,
+        out_shape=[
+            jax.ShapeDtypeStruct((total, units), BF),
+            jax.ShapeDtypeStruct((total, units), F32),
+        ],
+        compiler_params=pltpu.CompilerParams(vmem_limit_bytes=48 << 20),
+        cost_estimate=pl.CostEstimate(
+            flops=2 * total * width * units,
+            transcendentals=0,
+            bytes_accessed=2 * (total * width + width * units) + 6 * total * units,
+        ),
+        name=name,
+    )(*lefts, weights, bias)
+
+
+def backward_kernel(pieces, *refs):
+    lefts, (w_ref, slope_ref, grad_ref, sum_ref) = refs[: len(pieces)], refs[len(pieces) :]
+    sums = None
+    for left, (start, size) in zip(lefts, pieces):
+        grad = dot_nn(left[...], w_ref[...]) * slope_ref[pl.ds(start, size), :]
+        grad = grad.astype(BF)
+        grad_ref[pl.ds(start, size), :] = grad
+        part = jnp.sum(grad.astype(F32), axis=0, keepdims=True)
+        sums = part if sums is None else sums + part
+    sum_ref[...] = sums
+
+
+def feed_backward(lefts, starts, weights, slope, units, name):
+    total = sum(p.shape[0] for p in lefts)
+    width = lefts[0].shape[1]
+    tile = 256
+    skip = units // tile
+    pieces = [(start, p.shape[0]) for start, p in zip(starts, lefts)]
+    return pl.pallas_call(
+        partial(backward_kernel, pieces),
+        grid=(units // tile,),
+        in_specs=[
+            pl.BlockSpec(p.shape, lambda i: (0, 0), pipeline_mode=pl.Buffered(1)) for p in lefts
+        ]
+        + [
+            pl.BlockSpec((width, tile), lambda i: (0, skip + i)),
+            pl.BlockSpec((total, tile), lambda i: (0, i)),
+        ],
+        out_specs=[
+            pl.BlockSpec((total, tile), lambda i: (0, i)),
+            pl.BlockSpec((1, tile), lambda i: (0, i)),
+        ],
+        out_shape=[
+            jax.ShapeDtypeStruct((total, units), BF),
+            jax.ShapeDtypeStruct((1, units), F32),
+        ],
+        compiler_params=pltpu.CompilerParams(vmem_limit_bytes=48 << 20),
+        cost_estimate=pl.CostEstimate(
+            flops=2 * total * width * units,
+            transcendentals=0,
+            bytes_accessed=2 * (total * width + width * units) + 6 * total * units,
+        ),
+        name=name,
+    )(*lefts, weights, slope)
 
 
 def gather_small(packed, size):
@@ -327,11 +521,13 @@
         ],
         axis=1,
     )
+    feed_shard = jnp.concatenate([cols(up_weight, units), rws(down_weight, units).T], axis=1)
     attn_full = lax.all_gather(attn_shard, "fsdp", axis=0, tiled=True)
     w_qkv = attn_full[:, : 3 * head_width]
     w_out = attn_full[:, 3 * head_width :]
-    w_up = lax.all_gather(cols(up_weight, units), "fsdp", axis=0, tiled=True)
-    w_down = lax.all_gather(rws(down_weight, units).T, "fsdp", axis=0, tiled=True)
+    w_feed = lax.all_gather(feed_shard, "fsdp", axis=0, tiled=True)
+    w_up = w_feed[:, :units]
+    w_down = w_feed[:, units:]
 
     packed = jnp.concatenate(
         [
@@ -346,7 +542,7 @@
             rws(up_bias, unit_rows).reshape(-1),
         ]
     )
-    small = gather_small(packed, fsdp_size).astype(F32)
+    small = gather_small(after(packed, attn_shard), fsdp_size).astype(F32)
     vectors = [small[:, i * d_local : (i + 1) * d_local].reshape(-1) for i in range(6)]
     obias, gain_one, shift_one, gain_two, shift_two, dbias = vectors
     hd_local = HD // fsdp_size
@@ -374,75 +570,105 @@
 
     in_own, in_other = own_pair(prompt_input, continuation_input)
     up_own, up_other = own_pair(prompt_cotangent, continuation_cotangent)
+    up_pair = jnp.concatenate([up_own, up_other], axis=0)
     stacked = jnp.concatenate([in_own, in_other], axis=0).astype(F32)
+    stacked = after(stacked, feed_shard)
     normed_pair, inverse_pair = normalize(stacked)
-    act_pair = (normed_pair * gain_one + shift_one).astype(BF)
-    act_one = gather_ctx(act_pair)
+    act_pieces = gather_ctx((normed_pair * gain_one + shift_one).astype(BF))
+    act_one = jnp.concatenate(act_pieces, axis=0)
     normed_one = normed_pair[:rows]
     inverse_one = inverse_pair[:rows]
     x_own = stacked[:rows]
+    natural = list(range(blocks))
+    grouped = [p for group in GROUPS for p in group]
 
     qkv = (jnp.dot(act_one, w_qkv, preferred_element_type=F32) + qkv_bias).astype(BF)
     qkv = qkv.reshape(blocks, rows, 3 * head_width)
+    up_pieces = gather_ctx(after(up_pair, act_one))
     attended = attention_forward(info, qkv, cont_len)
 
-    def scatter_matmul(left, right):
+    def scatter_parts(lefts, order, right):
         parts = {}
-        for group in ((2, 3), (6, 7), (4, 5), (0, 1)):
-            lhs = left[group[0] : group[0] + 2].reshape(2 * rows, -1)
-            res = dot_nt(lhs, right).astype(BF)
-            parts[group[0]] = res[:rows]
-            parts[group[1]] = res[rows:]
-        return scatter_blocks(parts)
-
-    attn_sum = scatter_matmul(attended, w_out)
+        for left, pair in zip(lefts, order):
+            res = dot_nt(left, right).astype(BF)
+            parts[pair[0]] = res[:rows]
+            parts[pair[1]] = res[rows:]
+        return parts
+
+    def row_pairs(value):
+        flat = value.reshape(total_rows, -1)
+        return [flat[p * rows : (p + 2) * rows] for p in (6, 4, 2, 0)]
+
+    pairs = ((6, 7), (4, 5), (2, 3), (0, 1))
+    attn_sum = scatter_blocks(
+        scatter_parts(row_pairs(attended), pairs, w_out)
+    )
     middle = x_own + (attn_sum + obias)
     normed_two, inverse_two = normalize(middle)
     act_two_own = (normed_two * gain_two + shift_two).astype(BF)
-    act_two = jnp.concatenate(gather_blocks(act_two_own), axis=0)
-    upstream_low = gather_ctx(jnp.concatenate([up_own, up_other], axis=0))
-
-    pre_act = jnp.dot(act_two, w_up, preferred_element_type=F32) + ubias
-    hidden = jax.nn.gelu(pre_act, approximate=False).astype(BF)
-    down_term = dot_tn(upstream_low, hidden).astype(BF)
+    act_two_own, *up_pieces = lax.optimization_barrier((act_two_own, *up_pieces))
+    act_two = gather_blocks(act_two_own)
+
+    act_two_flat = [piece for group in act_two for piece in group]
+    starts = [0, 2, 1, 3, 4, 6, 5, 5.5, 7, 7.5]
+    starts = [int(p * rows) for p in starts]
+    hidden, slope = feed_forward(
+        act_two_flat, starts, w_feed, ubias[None], units, "feed_forward"
+    )
+    down_term = grad_matmul(up_pieces, natural, [hidden], natural, rows, "down_weight_term")
     down_piece = lax.psum_scatter(down_term, "fsdp", scatter_dimension=0, tiled=True)
-    grad_hidden = jnp.dot(upstream_low, w_down, preferred_element_type=F32)
-    gelu_pull = jax.vjp(partial(jax.nn.gelu, approximate=False), pre_act)[1]
-    grad_pre = gelu_pull(grad_hidden)[0].astype(BF)
-    up_term = dot_tn(act_two, grad_pre).astype(BF)
+    pair_starts = [0, 2 * rows, 4 * rows, 6 * rows]
+    slope, down_term = lax.optimization_barrier((slope, down_term))
+    grad_pre, ubias_sum = feed_backward(
+        up_pieces, pair_starts, w_feed, slope, units, "feed_backward"
+    )
+
+    grad_act_two = scatter_blocks(scatter_parts(row_pairs(grad_pre), pairs, w_up))
+    up_term = grad_matmul(act_two_flat, grouped, [grad_pre], natural, rows, "up_weight_term")
     up_piece = lax.psum_scatter(up_term, "fsdp", scatter_dimension=0, tiled=True)
-    grad_act_two = scatter_matmul(grad_pre.reshape(blocks, rows, units), w_up)
+    mlp_parts = scatter_parts(row_pairs(hidden), pairs, w_down)
     grad_middle = up_own.astype(F32) + norm_backward(
-        grad_act_two, normed_two, inverse_two, gain_two
+        after(grad_act_two, up_term), normed_two, inverse_two, gain_two
     )
     middle_low_own = grad_middle.astype(BF)
-    middle_low = jnp.concatenate(gather_blocks(middle_low_own), axis=0)
-
-    mlp_sum = scatter_matmul(hidden.reshape(blocks, rows, units), w_down)
+    middle_low = gather_blocks(middle_low_own)
+
+    grad_attended = []
+    for group in middle_low:
+        lhs = jnp.concatenate(group, axis=0)
+        grad_attended.append(jnp.dot(lhs, w_out, preferred_element_type=F32).astype(BF))
+    by_block = {}
+    for pair, piece in zip(GROUPS, grad_attended):
+        by_block[pair[0]], by_block[pair[1]] = piece[:rows], piece[rows:]
+    grad_attended = jnp.stack([by_block[p] for p in range(blocks)])
+    middle_flat = [piece for group in middle_low for piece in group]
+    grad_attended, mlp_parts, *middle_flat = lax.optimization_barrier(
+        (grad_attended, mlp_parts, *middle_flat)
+    )
+    dqkv = attention_backward(info, qkv, grad_attended, cont_len)
+    dqkv, down_piece = lax.optimization_barrier((dqkv, down_piece))
+    mlp_sum = scatter_blocks(mlp_parts)
+    dqkv_flat = dqkv.reshape(total_rows, 3 * head_width)
+    out_term = grad_matmul(
+        middle_flat, grouped, [attended.reshape(total_rows, head_width)], natural, rows, "output_weight_term"
+    )
+    qkv_term = grad_matmul(act_pieces, natural, [dqkv_flat], natural, rows, "attention_weight_term")
+    attn_term = jnp.concatenate([qkv_term, out_term], axis=1)
+    attn_piece = lax.psum_scatter(attn_term, "fsdp", scatter_dimension=0, tiled=True)
+    dqkv, mlp_sum, attn_term = lax.optimization_barrier((dqkv, mlp_sum, attn_term))
     result = (middle + (mlp_sum + dbias)).astype(BF)
-    result_other = swap_tp(result)
-
-    out_term = dot_tn(middle_low, attended.reshape(total_rows, head_width)).astype(BF)
-    grad_attended = jnp.dot(middle_low, w_out, preferred_element_type=F32).astype(BF)
-    dqkv = attention_backward(info, qkv, grad_attended.reshape(blocks, rows, head_width), cont_len)
-    dqkv_flat = dqkv.reshape(total_rows, 3 * head_width)
-    qkv_term = dot_tn(act_one, dqkv_flat).astype(BF)
-    attn_piece = lax.psum_scatter(
-        jnp.concatenate([qkv_term, out_term], axis=1), "fsdp", scatter_dimension=0, tiled=True
-    )
-    grad_act_one = scatter_matmul(dqkv, w_qkv)
+    grad_act_one = scatter_blocks(
+        scatter_parts(row_pairs(dqkv), pairs, w_qkv)
+    )
     grad_stacked = (
         grad_middle + norm_backward(grad_act_one, normed_one, inverse_one, gain_one)
     ).astype(BF)
-    stacked_other = swap_tp(grad_stacked)
+    result_other = swap_tp(result)
 
     def to_outputs(own, other):
         first = jnp.where(tp == 0, own, other)
         second = jnp.where(tp == 0, other, own)
         return first[None], second.reshape(1, cont_dev, cont_len, width)
-
-    prompt_output, continuation_output = to_outputs(result, result_other)
-    prompt_input_grad, continuation_input_grad = to_outputs(grad_stacked, stacked_other)
 
     def colsum(value):
         return jnp.sum(value, axis=0, dtype=F32)
@@ -457,48 +683,61 @@
             colsum(up_own),
         ]
     )
-    summed = lax.psum(d_vectors, ("fsdp", "ctx", "tp"))
-    summed = lax.dynamic_slice_in_dim(summed, z * d_local, d_local, axis=1)
-    obias_grad, gain_one_grad, shift_one_grad, gain_two_grad, shift_two_grad, dbias_grad = [
-        summed[i] for i in range(6)
-    ]
+    for swap in (swap_tp, swap_low, swap_high):
+        d_vectors = d_vectors + swap(d_vectors)
     colsum_qkv = colsum(dqkv_flat)
     head_terms = jnp.concatenate(
         [
             colsum_qkv[:head_width].reshape(heads, HD),
             colsum_qkv[2 * head_width :].reshape(heads, HD),
-            colsum(grad_pre).reshape(unit_rows, HD),
+            ubias_sum.reshape(unit_rows, HD),
         ]
     )
-    head_slots = jnp.where(
-        lax.broadcasted_iota(jnp.int32, (ctx_size, 1, 1), 0) == ctx, head_terms[None], 0.0
-    )
-    head_sums = lax.psum(head_slots, ("fsdp", "ctx"))
-    head_sums = lax.dynamic_slice_in_dim(head_sums, z * hd_local, hd_local, axis=2)
+
+    def by_owner(value):
+        count = value.shape[0]
+        return value.reshape(count, fsdp_size, -1).transpose(1, 0, 2).reshape(fsdp_size, -1)
+
+    owners = jnp.concatenate([by_owner(d_vectors), by_owner(head_terms)], axis=1)
+    summed = lax.dynamic_slice_in_dim(owners, z, 1, axis=0)
+    for step in range(1, fsdp_size):
+        share = lax.dynamic_slice_in_dim(owners, (z + step) % fsdp_size, 1, axis=0)
+        pairs = [(i, (i + step) % fsdp_size) for i in range(fsdp_size)]
+        summed = summed + lax.ppermute(share, "fsdp", pairs)
+    summed = summed[0]
+    obias_grad, gain_one_grad, shift_one_grad, gain_two_grad, shift_two_grad, dbias_grad = [
+        summed[i * d_local : (i + 1) * d_local] for i in range(6)
+    ]
+    mine = summed[6 * d_local :].reshape(2 * heads + unit_rows, hd_local)
+    mine_high = swap_high(mine)
+    relative = jnp.stack([mine, swap_low(mine), mine_high, swap_low(mine_high)])
+    head_sums = jnp.stack(
+        [lax.dynamic_index_in_dim(relative, ctx ^ i, keepdims=False) for i in range(ctx_size)]
+    )
     qbias_grad = head_sums[:, :heads].reshape(heads_tp, hd_local)
     vbias_grad = head_sums[:, heads : 2 * heads].reshape(heads_tp, hd_local)
     ubias_grad = head_sums[:, 2 * heads :].reshape(ctx_size * unit_rows, hd_local)
 
-    def spread(piece, axis):
-        count = piece.shape[axis]
-        shape = list(piece.shape)
-        shape[axis] = count * ctx_size
-        low = swap_low(piece)
+    def spread(piece):
         high = swap_high(piece)
-        both = swap_low(high)
-        out = jnp.zeros(shape, F32)
-        for offset, part in ((0, piece), (1, low), (2, high), (3, both)):
-            position = [0, 0]
-            position[axis] = (ctx ^ offset) * count
-            out = lax.dynamic_update_slice(out, part.astype(F32), tuple(position))
-        return out
-
-    down_grad = spread(down_piece.T, 0)
-    up_grad = spread(up_piece, 1)
-    query_grad = spread(attn_piece[:, :head_width], 1)
-    key_grad = spread(attn_piece[:, head_width : 2 * head_width], 1)
-    value_grad = spread(attn_piece[:, 2 * head_width : 3 * head_width], 1)
-    output_grad = spread(attn_piece[:, 3 * head_width :].T, 0)
+        return [piece, swap_low(piece), high, swap_low(high)]
+
+    grad_stacked, up_piece, *down_pieces = lax.optimization_barrier(
+        (grad_stacked, up_piece, *spread(down_piece))
+    )
+    stacked_other = swap_tp(grad_stacked)
+    down_grad = assemble(ctx, down_pieces, True, 1, "down_weight_grad")[0]
+    up_grad = assemble(ctx, spread(up_piece), False, 1, "up_weight_grad")[0]
+    prompt_output, continuation_output = to_outputs(result, result_other)
+    prompt_input_grad, continuation_input_grad = to_outputs(grad_stacked, stacked_other)
+    attn_piece, down_grad, up_grad = lax.optimization_barrier((attn_piece, down_grad, up_grad))
+    attn_pieces = spread(attn_piece)
+    query_grad, key_grad, value_grad = assemble(
+        ctx, [p[:, : 3 * head_width] for p in attn_pieces], False, 3, "attention_weight_grads"
+    )
+    output_grad = assemble(
+        ctx, [p[:, 3 * head_width :] for p in attn_pieces], True, 1, "output_weight_grad"
+    )[0]
     return (
         prompt_output,
         continuation_output,

time: 812 us -> 667 us (0.82)
  blocking collectives: 123 us -> 0 us
  Pallas kernels: 32.5 us -> 128 us
  matrix products: 138 us -> 52.8 us
  local copies, waits for them, and re-layouts: 108 us -> 47.2 us
  waiting for transfers between devices: 252 us -> 296 us
  other arithmetic: 76.5 us -> 64.6 us
    psum x2 -> x0, blocking collectives: 123 us -> none  [the longest x1 72.6 us: body(): head_sums = lax.psum(head_slots, ('fsdp', 'ctx'))]
    pallas_call x0 -> x10, Pallas kernels: none -> 95.7 us  [the longest x4 46 us: grad_matmul(): pl.pallas_call(partial(grad_matmul_kernel, len(lefts), spans), grid=(d //...]
    dot_general x7 -> x4, matrix products: 90.1 us -> 2.98 us  [body(): jnp.dot(lhs, w_out, preferred_element_type=F32).astype(BF)]
    ppermute x21 -> x20, waiting for transfers between devices: 109 us -> 167 us  [swap_high(): return lax.ppermute(value, 'ctx', [(0, 2), (2, 0), (1, 3), (3, 1)])]
    convert_element_type x16 -> x0, local copies, waits for them, and re-layouts: 20.7 us -> none  [spread(): out = lax.dynamic_update_slice(out, part.astype(F32), tuple(position))]
    dynamic_update_slice x16 -> x0, local copies, waits for them, and re-layouts: 19 us -> none  [spread(): out = lax.dynamic_update_slice(out, part.astype(F32), tuple(position))]
    dynamic_update_slice x8 -> x0, other arithmetic: 16.1 us -> none  [spread(): out = lax.dynamic_update_slice(out, part.astype(F32), tuple(position))]
    slice x16 -> x26, local copies, waits for them, and re-layouts: 7.84 us -> 18.5 us  [the longest x7 7.89 us: scatter_parts(): parts[pair[1]] = res[rows:]]
  transfers between devices with their start and end apart: 86 -> 87, of which waited for: 26 -> 30; matrix products, arithmetic and copies ran while one was open for 31% -> 21% of each run, Pallas kernels for 4% -> 14%
where the time goes in v2:
time: 667 us; the launch traced here: 661 us
  waiting for transfers between devices  296 us (44%)
  Pallas kernels  128 us (19%)
  other arithmetic  64.6 us (10%)
  starting transfers between devices  55.8 us (8%)
  matrix products  52.8 us (8%)
  local copies, waits for them, and re-layouts  47.2 us (7%)
  between operations  16.6 us (2%)
    ppermute x20, waiting for transfers between devices, swap_high(): return lax.ppermute(value, 'ctx', [(0, 2), (2, 0), (1, 3), (3, 1)])  167 us
    ppermute x15, waiting for transfers between devices, swap_tp(): return lax.ppermute(value, 'tp', [(0, 1), (1, 0)])  101 us
    pallas_call x4, Pallas kernels, grad_matmul(): pl.pallas_call(partial(grad_matmul_kernel, len(lefts), spans), grid=(d //...  46 us
    dot_general x16, matrix products, dot_nt(): lax.dot_general(a, b, (((1,), (1,)), ((), ())), preferred_element_type=F32)  36.9 us
    all_gather x1, waiting for transfers between devices, body(): w_feed = lax.all_gather(feed_shard, 'fsdp', axis=0, tiled=True)  22.1 us
    pallas_call x1, Pallas kernels, attention_backward(): pl.pallas_call(partial(attention_backward_kernel, blocks // 2, rows, cont...  20.9 us
    ppermute x20, starting transfers between devices, swap_high(): return lax.ppermute(value, 'ctx', [(0, 2), (2, 0), (1, 3), (3, 1)])  20.5 us
    unnamed x172, local copies, waits for them, and re-layouts  18.7 us
  transfers between devices with their start and end apart: 87, of which 30 were waited for; matrix products, arithmetic and copies ran while one was open for 21% of the time, Pallas kernels for 14%

profile of v2, /device:TPU:0, one launch (start us, length us, event | category | flops | bytes accessed | tf_op | source)
XLA Modules:
  0.0 660.9 jit_solution(687848644750633679)
XLA Ops:
  12.9 3.0 collective-permute-start.3
  15.9 2.6 collective-permute-start.4
  20.0 3.3 bitcast_select_fusion.3
  28.2 3.8 maximum_convert_fusion
  32.1 2.5 reduce_sum.135
  34.5 2.7 multiply_reduce_fusion
  38.7 5.2 add_convert_fusion.1
  45.5 45.2 %collective-permute-done.7.refs_2_ = bf16[512,2048]{1,0:T(8,128)(2,1)} collective-permute-done((bf16[512,2048]{1,0:T(8,128)(2,1)S(1)}, bf16[512,2048]{1,0:T(8,128)(2,1)}, u32[]{:S(2)}, u32[]{:S(2)}) %collective-permute-start.7) | collective-permute-done | bytes 2097184 | tf_op jit(solution)/shard_map/ppermute | solution.py:44
  99.2 12.9 %add_convert_fusion = bf16[2048,768]{1,0:T(8,128)(2,1)S(1)} fusion(f32[768]{0:T(1024)S(1)} %pad_maximum_fusion.19, bf16[2048,1024]{0,1:T(8,128)(2,1)} %all-gather.3.cloned.1.call-done, bf16[512,2048]{1,0:T(8,128)(2,1)} %collective-permute-done.8.refs_3_, bf16[512,2048]{1,0:T(8,128)(2,1)} %collective-permute-done.7.refs_2_, ...), kind=kOutput, calls=%fused_computation.2 | convolution fusion | flops 6479151104 | bytes 14683136 | tf_op jit(solution)/shard_map/dot_general | solution.py:585
  112.1 10.9 %attention_forward.1 = bf16[8,256,256]{2,1,0:T(8,128)(2,1)S(1)} custom-call(s32[10]{0:T(128)S(1)} %concatenate.86.info_ref, bf16[8,256,768]{2,1,0:T(8,128)(2,1)S(1)} %bitcast.130), custom_call_target="tpu_custom_call" | custom-call | flops 2013265920 | bytes 4194304 | tf_op jit(solution)/shard_map/attention_forward/pallas_call | solution.py:224
  132.6 21.6 %collective-permute-done.12 = bf16[128,2048]{1,0:T(8,128)(2,1)S(1)} collective-permute-done((bf16[128,2048]{1,0:T(8,128)(2,1)S(1)}, bf16[128,2048]{1,0:T(8,128)(2,1)S(1)}, u32[]{:S(2)}, u32[]{:S(2)}) %collective-permute-start.12) | collective-permute-done | bytes 524320 | tf_op jit(solution)/shard_map/ppermute | solution.py:44
  157.4 21.8 %collective-permute-done.13 = bf16[256,2048]{1,0:T(8,128)(2,1)S(1)} collective-permute-done((bf16[256,2048]{1,0:T(8,128)(2,1)S(1)}, bf16[256,2048]{1,0:T(8,128)(2,1)S(1)}, u32[]{:S(2)}, u32[]{:S(2)}) %collective-permute-start.13) | collective-permute-done | bytes 1048608 | tf_op jit(solution)/shard_map/ppermute | solution.py:36
  186.2 22.5 %collective-permute-done.21.refs_2_ = bf16[256,2048]{1,0:T(8,128)(2,1)S(1)} collective-permute-done((bf16[256,2048]{1,0:T(8,128)(2,1)S(1)}, bf16[256,2048]{1,0:T(8,128)(2,1)S(1)}, u32[]{:S(2)}, u32[]{:S(2)}) %collective-permute-start.21) | collective-permute-done | bytes 1048608 | tf_op jit(solution)/shard_map/ppermute | solution.py:36
  212.5 7.8 %collective-permute-done.25.refs_6_ = bf16[128,2048]{1,0:T(8,128)(2,1)} collective-permute-done((bf16[128,2048]{1,0:T(8,128)(2,1)S(1)}, bf16[128,2048]{1,0:T(8,128)(2,1)}, u32[]{:S(2)}, u32[]{:S(2)}) %collective-permute-start.25) | collective-permute-done | bytes 524320 | tf_op jit(solution)/shard_map/ppermute | solution.py:44
  220.4 4.8 collective-permute-done.26.refs_7_
  225.4 2.0 collective-permute-done.28.refs_9_
  227.4 22.1 %all-gather.5.cloned.1.call-done.refs_10_.refs_4_ = bf16[2048,2048]{1,0:T(8,128)(2,1)} async-done(((bf16[512,2048]{1,0:T(8,128)(2,1)}), bf16[2048,2048]{1,0:T(8,128)(2,1)}) %all-gather.5.cloned.1.call-update) | async-done | bytes 8388624 | tf_op jit(solution)/shard_map/all_gather | solution.py:528
  249.5 17.6 %feed_forward.1 = (bf16[2048,1024]{1,0:T(8,128)(2,1)}, f32[2048,1024]{1,0:T(8,128)}) custom-call(bf16[256,2048]{1,0:T(8,128)(2,1)S(1)} %add_convert_fusion.7.refs_0_, bf16[256,2048]{1,0:T(8,128)(2,1)} %collective-permute-done.20.refs_1_, bf16[256,2048]{1,0:T(8,128)(2,1)S(1)} %collective-permute-done.21.refs_2_, ...), custom_call_target="tpu_custom_call" | custom-call | flops 8589934592 | bytes 25165824 | tf_op jit(solution)/shard_map/feed_forward/pallas_call | solution.py:381
  267.1 13.1 %down_weight_term.1 = bf16[2048,1024]{1,0:T(8,128)(2,1)S(1)} custom-call(bf16[512,2048]{1,0:T(8,128)(2,1)} %pad_maximum_fusion.3.refs_0_, bf16[512,2048]{1,0:T(8,128)(2,1)S(1)} %copy-done.29, bf16[512,2048]{1,0:T(8,128)(2,1)} %collective-permute-done.18.refs_2_, bf16[512,2048]{1,0:T(8,128)(2,1)S(1)} %copy-done.32, bf16[2048,1024]{1,0:T(8,128)(2,1)} %get-tuple-element.77.refs_4_), custom_call_target="tpu_custom_call" | custom-call | flops 8589934592 | bytes 16777216 | tf_op jit(solution)/shard_map/down_weight_term/pallas_call | solution.py:302
  280.2 1.9 copy-done.5
  283.8 15.5 %feed_backward.1 = (bf16[2048,1024]{1,0:T(8,128)(2,1)}, f32[1,1024]{1,0:T(1,128)S(1)}) custom-call(bf16[512,2048]{1,0:T(8,128)(2,1)} %pad_maximum_fusion.3.refs_0_, bf16[512,2048]{1,0:T(8,128)(2,1)S(1)} %copy-done.30, bf16[512,2048]{1,0:T(8,128)(2,1)} %collective-permute-done.18.refs_2_, bf16[512,2048]{1,0:T(8,128)(2,1)} %copy-done.31, ...), custom_call_target="tpu_custom_call" | custom-call | flops 8589934592 | bytes 25165824 | tf_op jit(solution)/shard_map/feed_backward/pallas_call | solution.py:424
  299.3 3.6 convolution_convert_fusion.6
  305.5 2.4 convolution_convert_fusion.4
  308.8 2.4 convolution_convert_fusion.7
  311.2 2.4 convolution_convert_fusion.5
  314.1 2.4 convolution_convert_fusion
  316.5 4.1 convolution_convert_fusion.1
  320.6 3.7 convolution_convert_fusion.2
  324.3 3.7 convolution_convert_fusion.3
  332.4 10.8 %collective-permute-done.32 = bf16[128,2048]{1,0:T(8,128)(2,1)S(1)} collective-permute-done((bf16[128,2048]{1,0:T(8,128)(2,1)S(1)}, bf16[128,2048]{1,0:T(8,128)(2,1)S(1)}, u32[]{:S(2)}, u32[]{:S(2)}) %collective-permute-start.32) | collective-permute-done | bytes 524320 | tf_op jit(solution)/shard_map/ppermute | solution.py:44
  350.1 15.7 %up_weight_term.1 = bf16[2048,1024]{1,0:T(8,128)(2,1)S(1)} custom-call(bf16[256,2048]{1,0:T(8,128)(2,1)S(1)} %add_convert_fusion.7.refs_0_, bf16[256,2048]{1,0:T(8,128)(2,1)} %collective-permute-done.20.refs_1_, bf16[256,2048]{1,0:T(8,128)(2,1)S(1)} %collective-permute-done.21.refs_2_, bf16[256,2048]{1,0:T(8,128)(2,1)} %collective-permute-done.22.refs_3_, ...), custom_call_target="tpu_custom_call" | custom-call | flops 8589934592 | bytes 16777216 | tf_op jit(solution)/shard_map/up_weight_term/pallas_call | solution.py:302
  365.7 2.0 copy-done.4
  369.5 2.4 collective-permute-done.36
  371.9 2.9 convert_add_fusion.7
  376.0 2.3 convert_reduce_fusion.2
  383.3 18.6 %collective-permute-done.38.refs_2_ = bf16[256,2048]{1,0:T(8,128)(2,1)S(1)} collective-permute-done((bf16[256,2048]{1,0:T(8,128)(2,1)S(1)}, bf16[256,2048]{1,0:T(8,128)(2,1)S(1)}, u32[]{:S(2)}, u32[]{:S(2)}) %collective-permute-start.38) | collective-permute-done | bytes 1048608 | tf_op jit(solution)/shard_map/ppermute | solution.py:36
  406.7 11.2 %collective-permute-done.42.refs_6_ = bf16[128,2048]{1,0:T(8,128)(2,1)S(1)} collective-permute-done((bf16[128,2048]{1,0:T(8,128)(2,1)S(1)}, bf16[128,2048]{1,0:T(8,128)(2,1)S(1)}, u32[]{:S(2)}, u32[]{:S(2)}) %collective-permute-start.42) | collective-permute-done | bytes 524320 | tf_op jit(solution)/shard_map/ppermute | solution.py:44
  424.6 1.9 collective-permute-done.48
  426.5 2.2 add_convert_fusion.5
  432.3 10.8 %collective-permute-done.49 = bf16[128,2048]{1,0:T(8,128)(2,1)S(1)} collective-permute-done((bf16[128,2048]{1,0:T(8,128)(2,1)S(1)}, bf16[128,2048]{1,0:T(8,128)(2,1)S(1)}, u32[]{:S(2)}, u32[]{:S(2)}) %collective-permute-start.49) | collective-permute-done | bytes 524320 | tf_op jit(solution)/shard_map/ppermute | solution.py:44
  446.9 5.8 output_weight_term.1
  453.7 20.9 %attention_backward.1 = bf16[8,256,768]{2,1,0:T(8,128)(2,1)S(1)} custom-call(s32[10]{0:T(128)S(1)} %concatenate.86.info_ref, bf16[8,256,768]{2,1,0:T(8,128)(2,1)S(1)} %bitcast.131, bf16[8,256,256]{2,1,0:T(8,128)(2,1)S(1)} %copy-done.27), custom_call_target="tpu_custom_call" | custom-call | flops 7046430720 | bytes 7340032 | tf_op jit(solution)/shard_map/attention_backward/pallas_call | solution.py:242
  476.4 2.0 convert_add_fusion.4
  478.4 11.4 %attention_weight_term.1 = bf16[2048,768]{1,0:T(8,128)(2,1)S(1)} custom-call(bf16[512,2048]{1,0:T(8,128)(2,1)S(1)} %copy-done.11, bf16[512,2048]{1,0:T(8,128)(2,1)} %collective-permute-done.6.refs_1_, bf16[512,2048]{1,0:T(8,128)(2,1)} %collective-permute-done.7.refs_2_, bf16[512,2048]{1,0:T(8,128)(2,1)} %collective-permute-done.8.refs_3_, ...), custom_call_target="tpu_custom_call" | custom-call | flops 6442450944 | bytes 14680064 | tf_op jit(solution)/shard_map/attention_weight_term/pallas_call | solution.py:302
  489.8 2.6 pad_maximum_fusion.1
  503.7 4.1 convolution_convert_fusion.15
  507.8 1.8 convolution_convert_fusion.13
  509.6 2.2 add_convert_fusion.3
  516.0 23.3 %collective-permute-done.58 = bf16[128,2048]{1,0:T(8,128)(2,1)S(1)} collective-permute-done((bf16[128,2048]{1,0:T(8,128)(2,1)S(1)}, bf16[128,2048]{1,0:T(8,128)(2,1)S(1)}, u32[]{:S(2)}, u32[]{:S(2)}) %collective-permute-start.58) | collective-permute-done | bytes 524320 | tf_op jit(solution)/shard_map/ppermute | solution.py:44
  541.9 22.0 %collective-permute-done.59 = bf16[256,2048]{1,0:T(8,128)(2,1)S(1)} collective-permute-done((bf16[256,2048]{1,0:T(8,128)(2,1)S(1)}, bf16[256,2048]{1,0:T(8,128)(2,1)S(1)}, u32[]{:S(2)}, u32[]{:S(2)}) %collective-permute-start.59) | collective-permute-done | bytes 1048608 | tf_op jit(solution)/shard_map/ppermute | solution.py:36
  565.0 2.5 multiply_reduce_fusion.2
  570.9 3.7 add_convert_fusion.4
  576.6 2.3 collective-permute-done.73
  579.1 13.6 %collective-permute-done.68.refs_2_ = bf16[512,1024]{1,0:T(8,128)(2,1)} collective-permute-done((bf16[512,1024]{1,0:T(8,128)(2,1)}, bf16[512,1024]{1,0:T(8,128)(2,1)}, u32[]{:S(2)}, u32[]{:S(2)}) %collective-permute-start.68) | collective-permute-done | bytes 1048608 | tf_op jit(solution)/shard_map/ppermute | solution.py:44
  595.1 2.3 collective-permute-done.75
  598.3 3.2 collective-permute-start.78
  601.5 6.4 down_weight_grad.1
  608.9 5.2 up_weight_grad.1
  616.2 3.8 collective-permute-done.54
  620.0 3.0 broadcast_select_fusion.1
  623.0 15.4 %collective-permute-done.80 = f32[12,32]{1,0:T(8,128)S(1)} collective-permute-done((f32[12,32]{1,0:T(8,128)S(1)}, f32[12,32]{1,0:T(8,128)S(1)}, u32[]{:S(2)}, u32[]{:S(2)}) %collective-permute-start.80) | collective-permute-done | bytes 1568 | tf_op jit(solution)/shard_map/ppermute | solution.py:44
  641.8 2.7 broadcast_select_fusion
  647.9 2.1 output_weight_grad.1
  651.2 3.0 attention_weight_grads.1
  (476 shorter events, 131.0 us)
Async XLA Ops:
  7.2 91.9 %all-gather.3.cloned.1.call-start = ((), (), s32[]{:S(2)}) async-start(), calls=%async_computation.3 | async-start | bytes 5242880 | tf_op jit(solution)/shard_map/all_gather | solution.py:525
  12.9 24.6 %collective-permute-start.3 = (bf16[3456]{0:T(1024)(128)(2,1)S(1)}, bf16[3456]{0:T(1024)(128)(2,1)S(1)}, u32[]{:S(2)}, u32[]{:S(2)}) collective-permute-start(bf16[3456]{0:T(1024)(128)(2,1)S(1)} %concatenate.87), channel_id=1, source_target_pairs={{0,8},{8,16},{16,24},{24,0},{1,9},{9,17},{17,25},{25,1},{2,10},{10... | collective-permute-start | bytes 20744 | tf_op jit(solution)/shard_map/ppermute | solution.py:458
  15.9 21.7 %collective-permute-start.4 = (bf16[3456]{0:T(1024)(128)(2,1)S(1)}, bf16[3456]{0:T(1024)(128)(2,1)S(1)}, u32[]{:S(2)}, u32[]{:S(2)}) collective-permute-start(bf16[3456]{0:T(1024)(128)(2,1)S(1)} %concatenate.87), channel_id=1, source_target_pairs={{0,16},{8,24},{16,0},{24,8},{1,17},{9,25},{17,1},{25,9},{2,18},{10... | collective-permute-start | bytes 20744 | tf_op jit(solution)/shard_map/ppermute | solution.py:458
  18.5 19.3 %collective-permute-start.5 = (bf16[3456]{0:T(1024)(128)(2,1)S(1)}, bf16[3456]{0:T(1024)(128)(2,1)S(1)}, u32[]{:S(2)}, u32[]{:S(2)}) collective-permute-start(bf16[3456]{0:T(1024)(128)(2,1)S(1)} %concatenate.87), channel_id=1, source_target_pairs={{0,24},{8,0},{16,8},{24,16},{1,25},{9,1},{17,9},{25,17},{2,26},{10... | collective-permute-start | bytes 20744 | tf_op jit(solution)/shard_map/ppermute | solution.py:458
  19.9 229.6 %all-gather.5.cloned.1.call-start = ((), (), s32[]{:S(2)}) async-start(), calls=%async_computation.4 | async-start | bytes 10485760 | tf_op jit(solution)/shard_map/all_gather | solution.py:528
  43.9 46.8 %collective-permute-start.7 = (bf16[512,2048]{1,0:T(8,128)(2,1)S(1)}, bf16[512,2048]{1,0:T(8,128)(2,1)}, u32[]{:S(2)}, u32[]{:S(2)}) collective-permute-start(bf16[512,2048]{1,0:T(8,128)(2,1)S(1)} %get-tuple-element.133.refs_0_), channel_id=1, source_target_pairs={{0,4},{4,0},{2,6},{6,2},{1,5},{5,1},{3,7},{7,3},{8,12},{12,8},{10,... | collective-permute-start | bytes 6291464 | tf_op jit(solution)/shard_map/ppermute | solution.py:44
  45.5 53.1 %collective-permute-start.6 = (bf16[512,2048]{1,0:T(8,128)(2,1)S(1)}, bf16[512,2048]{1,0:T(8,128)(2,1)}, u32[]{:S(2)}, u32[]{:S(2)}) collective-permute-start(bf16[512,2048]{1,0:T(8,128)(2,1)S(1)} %get-tuple-element.133.refs_0_), channel_id=1, source_target_pairs={{0,2},{2,0},{4,6},{6,4},{1,3},{3,1},{5,7},{7,5},{8,10},{10,8},{12,... | collective-permute-start | bytes 6291464 | tf_op jit(solution)/shard_map/ppermute | solution.py:40
  95.0 61.9 %collective-permute-start.18 = (bf16[512,2048]{1,0:T(8,128)(2,1)}, bf16[512,2048]{1,0:T(8,128)(2,1)}, u32[]{:S(2)}, u32[]{:S(2)}) collective-permute-start(bf16[512,2048]{1,0:T(8,128)(2,1)} %pad_maximum_fusion.3.refs_0_), channel_id=1, source_target_pairs={{0,4},{4,0},{2,6},{6,2},{1,5},{5,1},{3,7},{7,3},{8,12},{12,8},{10,... | collective-permute-start | bytes 6291464 | tf_op jit(solution)/shard_map/ppermute | solution.py:44
  95.6 382.8 %reduce-scatter.4.cloned.1.call-start = ((), (), s32[]{:S(2)}) async-start(), calls=%async_computation.5 | async-start | bytes 5242880 | tf_op jit(solution)/shard_map/reduce_scatter | solution.py:619
  125.7 31.7 %collective-permute-start.9 = (bf16[256,2048]{1,0:T(8,128)(2,1)S(1)}, bf16[256,2048]{1,0:T(8,128)(2,1)S(1)}, u32[]{:S(2)}, u32[]{:S(2)}) collective-permute-start(bf16[256,2048]{1,0:T(8,128)(2,1)S(1)} %get-tuple-element.163), channel_id=1, source_target_pairs={{0,2},{2,0},{4,6},{6,4},{1,3},{3,1},{5,7},{7,5},{8,10},{10,8},{12,... | collective-permute-start | bytes 3145736 | tf_op jit(solution)/shard_map/ppermute | solution.py:40
  129.1 25.2 %collective-permute-start.12 = (bf16[128,2048]{1,0:T(8,128)(2,1)S(1)}, bf16[128,2048]{1,0:T(8,128)(2,1)S(1)}, u32[]{:S(2)}, u32[]{:S(2)}) collective-permute-start(bf16[128,2048]{1,0:T(8,128)(2,1)S(1)} %get-tuple-element.177), channel_id=1, source_target_pairs={{0,4},{4,0},{2,6},{6,2},{1,5},{5,1},{3,7},{7,3},{8,12},{12,8},{10,... | collective-permute-start | bytes 1572872 | tf_op jit(solution)/shard_map/ppermute | solution.py:44
  131.0 25.0 %collective-permute-start.15 = (bf16[128,2048]{1,0:T(8,128)(2,1)S(1)}, bf16[128,2048]{1,0:T(8,128)(2,1)S(1)}, u32[]{:S(2)}, u32[]{:S(2)}) collective-permute-start(bf16[128,2048]{1,0:T(8,128)(2,1)S(1)} %get-tuple-element.178), channel_id=1, source_target_pairs={{0,1},{1,0},{2,3},{3,2},{4,5},{5,4},{6,7},{7,6},{8,9},{9,8},{10,11... | collective-permute-start | bytes 1572872 | tf_op jit(solution)/shard_map/ppermute | solution.py:36
  154.5 24.7 %collective-permute-start.13 = (bf16[256,2048]{1,0:T(8,128)(2,1)S(1)}, bf16[256,2048]{1,0:T(8,128)(2,1)S(1)}, u32[]{:S(2)}, u32[]{:S(2)}) collective-permute-start(bf16[256,2048]{1,0:T(8,128)(2,1)S(1)} %pad_maximum_fusion.5), channel_id=1, source_target_pairs={{0,1},{1,0},{2,3},{3,2},{4,5},{5,4},{6,7},{7,6},{8,9},{9,8},{10,11... | collective-permute-start | bytes 3145736 | tf_op jit(solution)/shard_map/ppermute | solution.py:36
  156.3 24.4 %collective-permute-start.16 = (bf16[256,2048]{1,0:T(8,128)(2,1)S(1)}, bf16[256,2048]{1,0:T(8,128)(2,1)S(1)}, u32[]{:S(2)}, u32[]{:S(2)}) collective-permute-start(bf16[256,2048]{1,0:T(8,128)(2,1)S(1)} %pad_maximum_fusion.6), channel_id=1, source_target_pairs={{0,4},{4,0},{2,6},{6,2},{1,5},{5,1},{3,7},{7,3},{8,12},{12,8},{10,... | collective-permute-start | bytes 3145736 | tf_op jit(solution)/shard_map/ppermute | solution.py:44
  156.8 25.6 %collective-permute-start.17 = (bf16[512,2048]{1,0:T(8,128)(2,1)}, bf16[512,2048]{1,0:T(8,128)(2,1)S(1)}, u32[]{:S(2)}, u32[]{:S(2)}) collective-permute-start(bf16[512,2048]{1,0:T(8,128)(2,1)} %pad_maximum_fusion.3.refs_0_), channel_id=1, source_target_pairs={{0,2},{2,0},{4,6},{6,4},{1,3},{3,1},{5,7},{7,5},{8,10},{10,8},{12,... | collective-permute-start | bytes 6291464 | tf_op jit(solution)/shard_map/ppermute | solution.py:40
  156.8 26.9 %collective-permute-start.19 = (bf16[512,2048]{1,0:T(8,128)(2,1)}, bf16[512,2048]{1,0:T(8,128)(2,1)S(1)}, u32[]{:S(2)}, u32[]{:S(2)}) collective-permute-start(bf16[512,2048]{1,0:T(8,128)(2,1)} %collective-permute-done.18.refs_2_), channel_id=1, source_target_pairs={{0,2},{2,0},{4,6},{6,4},{1,3},{3,1},{5,7},{7,5},{8,10},{10,8},{12,... | collective-permute-start | bytes 6291464 | tf_op jit(solution)/shard_map/ppermute | solution.py:40
  185.1 23.5 %collective-permute-start.21 = (bf16[256,2048]{1,0:T(8,128)(2,1)S(1)}, bf16[256,2048]{1,0:T(8,128)(2,1)S(1)}, u32[]{:S(2)}, u32[]{:S(2)}) collective-permute-start(bf16[256,2048]{1,0:T(8,128)(2,1)S(1)} %add_convert_fusion.7.refs_0_), channel_id=1, source_target_pairs={{0,1},{1,0},{2,3},{3,2},{4,5},{5,4},{6,7},{7,6},{8,9},{9,8},{10,11... | collective-permute-start | bytes 3145736 | tf_op jit(solution)/shard_map/ppermute | solution.py:36
  185.6 23.6 %collective-permute-start.23 = (bf16[256,2048]{1,0:T(8,128)(2,1)S(1)}, bf16[256,2048]{1,0:T(8,128)(2,1)}, u32[]{:S(2)}, u32[]{:S(2)}) collective-permute-start(bf16[256,2048]{1,0:T(8,128)(2,1)S(1)} %add_convert_fusion.7.refs_0_), channel_id=1, source_target_pairs={{0,4},{4,0},{2,6},{6,2},{1,5},{5,1},{3,7},{7,3},{8,12},{12,8},{10,... | collective-permute-start | bytes 3145736 | tf_op jit(solution)/shard_map/ppermute | solution.py:44
  186.2 39.1 %collective-permute-start.20 = (bf16[256,2048]{1,0:T(8,128)(2,1)S(1)}, bf16[256,2048]{1,0:T(8,128)(2,1)}, u32[]{:S(2)}, u32[]{:S(2)}) collective-permute-start(bf16[256,2048]{1,0:T(8,128)(2,1)S(1)} %add_convert_fusion.7.refs_0_), channel_id=1, source_target_pairs={{0,2},{2,0},{4,6},{6,4},{1,3},{3,1},{5,7},{7,5},{8,10},{10,8},{12,... | collective-permute-start | bytes 3145736 | tf_op jit(solution)/shard_map/ppermute | solution.py:40
  209.3 16.1 %collective-permute-start.22 = (bf16[256,2048]{1,0:T(8,128)(2,1)S(1)}, bf16[256,2048]{1,0:T(8,128)(2,1)}, u32[]{:S(2)}, u32[]{:S(2)}) collective-permute-start(bf16[256,2048]{1,0:T(8,128)(2,1)S(1)} %collective-permute-done.21.refs_2_), channel_id=1, source_target_pairs={{0,2},{2,0},{4,6},{6,4},{1,3},{3,1},{5,7},{7,5},{8,10},{10,8},{12,... | collective-permute-start | bytes 3145736 | tf_op jit(solution)/shard_map/ppermute | solution.py:40
  210.4 15.0 %collective-permute-start.24 = (bf16[256,2048]{1,0:T(8,128)(2,1)}, bf16[256,2048]{1,0:T(8,128)(2,1)}, u32[]{:S(2)}, u32[]{:S(2)}) collective-permute-start(bf16[256,2048]{1,0:T(8,128)(2,1)} %collective-permute-done.23.refs_4_), channel_id=1, source_target_pairs={{0,2},{2,0},{4,6},{6,4},{1,3},{3,1},{5,7},{7,5},{8,10},{10,8},{12,... | collective-permute-start | bytes 3145736 | tf_op jit(solution)/shard_map/ppermute | solution.py:40
  210.9 14.2 %collective-permute-start.26 = (bf16[128,2048]{1,0:T(8,128)(2,1)S(1)}, bf16[128,2048]{1,0:T(8,128)(2,1)}, u32[]{:S(2)}, u32[]{:S(2)}) collective-permute-start(bf16[128,2048]{1,0:T(8,128)(2,1)S(1)} %slice.590), channel_id=1, source_target_pairs={{0,1},{1,0},{2,3},{3,2},{4,5},{5,4},{6,7},{7,6},{8,9},{9,8},{10,11... | collective-permute-start | bytes 1572872 | tf_op jit(solution)/shard_map/ppermute | solution.py:36
  282.2 286.9 %reduce-scatter.6.cloned.1.call-start = ((), (), s32[]{:S(2)}) async-start(), calls=%async_computation.6 | async-start | bytes 5242880 | tf_op jit(solution)/shard_map/reduce_scatter | solution.py:628
  304.2 26.2 %collective-permute-start.30 = (bf16[256,2048]{1,0:T(8,128)(2,1)S(1)}, bf16[256,2048]{1,0:T(8,128)(2,1)S(1)}, u32[]{:S(2)}, u32[]{:S(2)}) collective-permute-start(bf16[256,2048]{1,0:T(8,128)(2,1)S(1)} %get-tuple-element.158), channel_id=1, source_target_pairs={{0,2},{2,0},{4,6},{6,4},{1,3},{3,1},{5,7},{7,5},{8,10},{10,8},{12,... | collective-permute-start | bytes 3145736 | tf_op jit(solution)/shard_map/ppermute | solution.py:40
  308.1 19.8 %collective-permute-start.31 = (bf16[256,2048]{1,0:T(8,128)(2,1)S(1)}, bf16[256,2048]{1,0:T(8,128)(2,1)S(1)}, u32[]{:S(2)}, u32[]{:S(2)}) collective-permute-start(bf16[256,2048]{1,0:T(8,128)(2,1)S(1)} %get-tuple-element.161), channel_id=1, source_target_pairs={{0,2},{2,0},{4,6},{6,4},{1,3},{3,1},{5,7},{7,5},{8,10},{10,8},{12,... | collective-permute-start | bytes 3145736 | tf_op jit(solution)/shard_map/ppermute | solution.py:40
  308.2 19.7 %collective-permute-start.34 = (bf16[256,2048]{1,0:T(8,128)(2,1)S(1)}, bf16[256,2048]{1,0:T(8,128)(2,1)S(1)}, u32[]{:S(2)}, u32[]{:S(2)}) collective-permute-start(bf16[256,2048]{1,0:T(8,128)(2,1)S(1)} %get-tuple-element.162), channel_id=1, source_target_pairs={{0,2},{2,0},{4,6},{6,4},{1,3},{3,1},{5,7},{7,5},{8,10},{10,8},{12,... | collective-permute-start | bytes 3145736 | tf_op jit(solution)/shard_map/ppermute | solution.py:40
  308.7 59.1 %collective-permute-start.29 = (bf16[256,2048]{1,0:T(8,128)(2,1)}, bf16[256,2048]{1,0:T(8,128)(2,1)}, u32[]{:S(2)}, u32[]{:S(2)}) collective-permute-start(bf16[256,2048]{1,0:T(8,128)(2,1)} %get-tuple-element.157), channel_id=1, source_target_pairs={{0,2},{2,0},{4,6},{6,4},{1,3},{3,1},{5,7},{7,5},{8,10},{10,8},{12,... | collective-permute-start | bytes 3145736 | tf_op jit(solution)/shard_map/ppermute | solution.py:40
  328.8 14.3 %collective-permute-start.32 = (bf16[128,2048]{1,0:T(8,128)(2,1)S(1)}, bf16[128,2048]{1,0:T(8,128)(2,1)S(1)}, u32[]{:S(2)}, u32[]{:S(2)}) collective-permute-start(bf16[128,2048]{1,0:T(8,128)(2,1)S(1)} %get-tuple-element.175), channel_id=1, source_target_pairs={{0,4},{4,0},{2,6},{6,2},{1,5},{5,1},{3,7},{7,3},{8,12},{12,8},{10,... | collective-permute-start | bytes 1572872 | tf_op jit(solution)/shard_map/ppermute | solution.py:44
  330.8 15.0 %collective-permute-start.35 = (bf16[128,2048]{1,0:T(8,128)(2,1)S(1)}, bf16[128,2048]{1,0:T(8,128)(2,1)S(1)}, u32[]{:S(2)}, u32[]{:S(2)}) collective-permute-start(bf16[128,2048]{1,0:T(8,128)(2,1)S(1)} %get-tuple-element.176), channel_id=1, source_target_pairs={{0,1},{1,0},{2,3},{3,2},{4,5},{5,4},{6,7},{7,6},{8,9},{9,8},{10,11... | collective-permute-start | bytes 1572872 | tf_op jit(solution)/shard_map/ppermute | solution.py:36
  344.4 25.1 %collective-permute-start.33 = (bf16[256,2048]{1,0:T(8,128)(2,1)}, bf16[256,2048]{1,0:T(8,128)(2,1)}, u32[]{:S(2)}, u32[]{:S(2)}) collective-permute-start(bf16[256,2048]{1,0:T(8,128)(2,1)} %pad_maximum_fusion.7), channel_id=1, source_target_pairs={{0,1},{1,0},{2,3},{3,2},{4,5},{5,4},{6,7},{7,6},{8,9},{9,8},{10,11... | collective-permute-start | bytes 3145736 | tf_op jit(solution)/shard_map/ppermute | solution.py:36
  347.0 24.9 %collective-permute-start.36 = (bf16[256,2048]{1,0:T(8,128)(2,1)}, bf16[256,2048]{1,0:T(8,128)(2,1)}, u32[]{:S(2)}, u32[]{:S(2)}) collective-permute-start(bf16[256,2048]{1,0:T(8,128)(2,1)} %pad_maximum_fusion.8), channel_id=1, source_target_pairs={{0,4},{4,0},{2,6},{6,2},{1,5},{5,1},{3,7},{7,3},{8,12},{12,8},{10,... | collective-permute-start | bytes 3145736 | tf_op jit(solution)/shard_map/ppermute | solution.py:44
  378.3 23.6 %collective-permute-start.38 = (bf16[256,2048]{1,0:T(8,128)(2,1)S(1)}, bf16[256,2048]{1,0:T(8,128)(2,1)S(1)}, u32[]{:S(2)}, u32[]{:S(2)}) collective-permute-start(bf16[256,2048]{1,0:T(8,128)(2,1)S(1)} %get-tuple-element.91.refs_0_), channel_id=1, source_target_pairs={{0,1},{1,0},{2,3},{3,2},{4,5},{5,4},{6,7},{7,6},{8,9},{9,8},{10,11... | collective-permute-start | bytes 3145736 | tf_op jit(solution)/shard_map/ppermute | solution.py:36
  380.4 24.6 %collective-permute-start.40 = (bf16[256,2048]{1,0:T(8,128)(2,1)S(1)}, bf16[256,2048]{1,0:T(8,128)(2,1)S(1)}, u32[]{:S(2)}, u32[]{:S(2)}) collective-permute-start(bf16[256,2048]{1,0:T(8,128)(2,1)S(1)} %get-tuple-element.91.refs_0_), channel_id=1, source_target_pairs={{0,4},{4,0},{2,6},{6,2},{1,5},{5,1},{3,7},{7,3},{8,12},{12,8},{10,... | collective-permute-start | bytes 3145736 | tf_op jit(solution)/shard_map/ppermute | solution.py:44
  381.9 23.8 %collective-permute-start.37 = (bf16[256,2048]{1,0:T(8,128)(2,1)S(1)}, bf16[256,2048]{1,0:T(8,128)(2,1)S(1)}, u32[]{:S(2)}, u32[]{:S(2)}) collective-permute-start(bf16[256,2048]{1,0:T(8,128)(2,1)S(1)} %get-tuple-element.91.refs_0_), channel_id=1, source_target_pairs={{0,2},{2,0},{4,6},{6,4},{1,3},{3,1},{5,7},{7,5},{8,10},{10,8},{12,... | collective-permute-start | bytes 3145736 | tf_op jit(solution)/shard_map/ppermute | solution.py:40
  401.9 17.3 %collective-permute-start.39 = (bf16[256,2048]{1,0:T(8,128)(2,1)S(1)}, bf16[256,2048]{1,0:T(8,128)(2,1)S(1)}, u32[]{:S(2)}, u32[]{:S(2)}) collective-permute-start(bf16[256,2048]{1,0:T(8,128)(2,1)S(1)} %collective-permute-done.38.refs_2_), channel_id=1, source_target_pairs={{0,2},{2,0},{4,6},{6,4},{1,3},{3,1},{5,7},{7,5},{8,10},{10,8},{12,... | collective-permute-start | bytes 3145736 | tf_op jit(solution)/shard_map/ppermute | solution.py:40
  403.4 14.4 %collective-permute-start.42 = (bf16[128,2048]{1,0:T(8,128)(2,1)S(1)}, bf16[128,2048]{1,0:T(8,128)(2,1)S(1)}, u32[]{:S(2)}, u32[]{:S(2)}) collective-permute-start(bf16[128,2048]{1,0:T(8,128)(2,1)S(1)} %slice.612), channel_id=1, source_target_pairs={{0,4},{4,0},{2,6},{6,2},{1,5},{5,1},{3,7},{7,3},{8,12},{12,8},{10,... | collective-permute-start | bytes 1572872 | tf_op jit(solution)/shard_map/ppermute | solution.py:44
  405.0 14.1 %collective-permute-start.43 = (bf16[128,2048]{1,0:T(8,128)(2,1)S(1)}, bf16[128,2048]{1,0:T(8,128)(2,1)S(1)}, u32[]{:S(2)}, u32[]{:S(2)}) collective-permute-start(bf16[128,2048]{1,0:T(8,128)(2,1)S(1)} %slice.613), channel_id=1, source_target_pairs={{0,1},{1,0},{2,3},{3,2},{4,5},{5,4},{6,7},{7,6},{8,9},{9,8},{10,11... | collective-permute-start | bytes 1572872 | tf_op jit(solution)/shard_map/ppermute | solution.py:36
  405.7 14.6 %collective-permute-start.41 = (bf16[256,2048]{1,0:T(8,128)(2,1)S(1)}, bf16[256,2048]{1,0:T(8,128)(2,1)S(1)}, u32[]{:S(2)}, u32[]{:S(2)}) collective-permute-start(bf16[256,2048]{1,0:T(8,128)(2,1)S(1)} %collective-permute-done.40.refs_4_), channel_id=1, source_target_pairs={{0,2},{2,0},{4,6},{6,4},{1,3},{3,1},{5,7},{7,5},{8,10},{10,8},{12,... | collective-permute-start | bytes 3145736 | tf_op jit(solution)/shard_map/ppermute | solution.py:40
  424.0 190.1 %reduce-scatter.8.cloned.1.call-start = ((), (), s32[]{:S(2)}) async-start(), calls=%async_computation.7 | async-start | bytes 5242880 | tf_op jit(solution)/shard_map/reduce_scatter | solution.py:657
  424.5 51.8 %collective-permute-start.46 = (bf16[256,2048]{1,0:T(8,128)(2,1)}, bf16[256,2048]{1,0:T(8,128)(2,1)S(1)}, u32[]{:S(2)}, u32[]{:S(2)}) collective-permute-start(bf16[256,2048]{1,0:T(8,128)(2,1)} %get-tuple-element.84), channel_id=1, source_target_pairs={{0,2},{2,0},{4,6},{6,4},{1,3},{3,1},{5,7},{7,5},{8,10},{10,8},{12,... | collective-permute-start | bytes 3145736 | tf_op jit(solution)/shard_map/ppermute | solution.py:40
  428.8 14.2 %collective-permute-start.49 = (bf16[128,2048]{1,0:T(8,128)(2,1)S(1)}, bf16[128,2048]{1,0:T(8,128)(2,1)S(1)}, u32[]{:S(2)}, u32[]{:S(2)}) collective-permute-start(bf16[128,2048]{1,0:T(8,128)(2,1)S(1)} %get-tuple-element.173), channel_id=1, source_target_pairs={{0,4},{4,0},{2,6},{6,2},{1,5},{5,1},{3,7},{7,3},{8,12},{12,8},{10,... | collective-permute-start | bytes 1572872 | tf_op jit(solution)/shard_map/ppermute | solution.py:44
  431.2 14.3 %collective-permute-start.52 = (bf16[128,2048]{1,0:T(8,128)(2,1)S(1)}, bf16[128,2048]{1,0:T(8,128)(2,1)S(1)}, u32[]{:S(2)}, u32[]{:S(2)}) collective-permute-start(bf16[128,2048]{1,0:T(8,128)(2,1)S(1)} %get-tuple-element.174), channel_id=1, source_target_pairs={{0,1},{1,0},{2,3},{3,2},{4,5},{5,4},{6,7},{7,6},{8,9},{9,8},{10,11... | collective-permute-start | bytes 1572872 | tf_op jit(solution)/shard_map/ppermute | solution.py:36
  443.4 33.0 %collective-permute-start.50 = (bf16[256,2048]{1,0:T(8,128)(2,1)S(1)}, bf16[256,2048]{1,0:T(8,128)(2,1)S(1)}, u32[]{:S(2)}, u32[]{:S(2)}) collective-permute-start(bf16[256,2048]{1,0:T(8,128)(2,1)S(1)} %pad_maximum_fusion.9), channel_id=1, source_target_pairs={{0,1},{1,0},{2,3},{3,2},{4,5},{5,4},{6,7},{7,6},{8,9},{9,8},{10,11... | collective-permute-start | bytes 3145736 | tf_op jit(solution)/shard_map/ppermute | solution.py:36
  445.7 30.7 %collective-permute-start.53 = (bf16[256,2048]{1,0:T(8,128)(2,1)S(1)}, bf16[256,2048]{1,0:T(8,128)(2,1)S(1)}, u32[]{:S(2)}, u32[]{:S(2)}) collective-permute-start(bf16[256,2048]{1,0:T(8,128)(2,1)S(1)} %pad_maximum_fusion.10), channel_id=1, source_target_pairs={{0,4},{4,0},{2,6},{6,2},{1,5},{5,1},{3,7},{7,3},{8,12},{12,8},{10,... | collective-permute-start | bytes 3145736 | tf_op jit(solution)/shard_map/ppermute | solution.py:44
  502.3 39.6 %collective-permute-start.55 = (bf16[256,2048]{1,0:T(8,128)(2,1)}, bf16[256,2048]{1,0:T(8,128)(2,1)}, u32[]{:S(2)}, u32[]{:S(2)}) collective-permute-start(bf16[256,2048]{1,0:T(8,128)(2,1)} %get-tuple-element.141), channel_id=1, source_target_pairs={{0,2},{2,0},{4,6},{6,4},{1,3},{3,1},{5,7},{7,5},{8,10},{10,8},{12,... | collective-permute-start | bytes 3145736 | tf_op jit(solution)/shard_map/ppermute | solution.py:40
  502.8 38.6 %collective-permute-start.64 = (bf16[512,1024]{1,0:T(8,128)(2,1)}, bf16[512,1024]{1,0:T(8,128)(2,1)}, u32[]{:S(2)}, u32[]{:S(2)}) collective-permute-start(bf16[512,1024]{1,0:T(8,128)(2,1)} %reduce-scatter.4.cloned.1.call-done.refs_0_), channel_id=1, source_target_pairs={{0,4},{4,0},{2,6},{6,2},{1,5},{5,1},{3,7},{7,3},{8,12},{12,8},{10,... | collective-permute-start | bytes 3145736 | tf_op jit(solution)/shard_map/ppermute | solution.py:44
  512.0 27.3 %collective-permute-start.58 = (bf16[128,2048]{1,0:T(8,128)(2,1)S(1)}, bf16[128,2048]{1,0:T(8,128)(2,1)S(1)}, u32[]{:S(2)}, u32[]{:S(2)}) collective-permute-start(bf16[128,2048]{1,0:T(8,128)(2,1)S(1)} %get-tuple-element.171), channel_id=1, source_target_pairs={{0,4},{4,0},{2,6},{6,2},{1,5},{5,1},{3,7},{7,3},{8,12},{12,8},{10,... | collective-permute-start | bytes 1572872 | tf_op jit(solution)/shard_map/ppermute | solution.py:44
  514.9 25.8 %collective-permute-start.61 = (bf16[128,2048]{1,0:T(8,128)(2,1)S(1)}, bf16[128,2048]{1,0:T(8,128)(2,1)S(1)}, u32[]{:S(2)}, u32[]{:S(2)}) collective-permute-start(bf16[128,2048]{1,0:T(8,128)(2,1)S(1)} %get-tuple-element.172), channel_id=1, source_target_pairs={{0,1},{1,0},{2,3},{3,2},{4,5},{5,4},{6,7},{7,6},{8,9},{9,8},{10,11... | collective-permute-start | bytes 1572872 | tf_op jit(solution)/shard_map/ppermute | solution.py:36
  539.5 24.4 %collective-permute-start.59 = (bf16[256,2048]{1,0:T(8,128)(2,1)S(1)}, bf16[256,2048]{1,0:T(8,128)(2,1)S(1)}, u32[]{:S(2)}, u32[]{:S(2)}) collective-permute-start(bf16[256,2048]{1,0:T(8,128)(2,1)S(1)} %pad_maximum_fusion.11), channel_id=1, source_target_pairs={{0,1},{1,0},{2,3},{3,2},{4,5},{5,4},{6,7},{7,6},{8,9},{9,8},{10,11... | collective-permute-start | bytes 3145736 | tf_op jit(solution)/shard_map/ppermute | solution.py:36
  540.8 24.1 %collective-permute-start.62 = (bf16[256,2048]{1,0:T(8,128)(2,1)S(1)}, bf16[256,2048]{1,0:T(8,128)(2,1)S(1)}, u32[]{:S(2)}, u32[]{:S(2)}) collective-permute-start(bf16[256,2048]{1,0:T(8,128)(2,1)S(1)} %pad_maximum_fusion.12), channel_id=1, source_target_pairs={{0,4},{4,0},{2,6},{6,2},{1,5},{5,1},{3,7},{7,3},{8,12},{12,8},{10,... | collective-permute-start | bytes 3145736 | tf_op jit(solution)/shard_map/ppermute | solution.py:44
  541.4 27.7 %collective-permute-start.63 = (bf16[512,1024]{1,0:T(8,128)(2,1)}, bf16[512,1024]{1,0:T(8,128)(2,1)}, u32[]{:S(2)}, u32[]{:S(2)}) collective-permute-start(bf16[512,1024]{1,0:T(8,128)(2,1)} %reduce-scatter.4.cloned.1.call-done.refs_0_), channel_id=1, source_target_pairs={{0,2},{2,0},{4,6},{6,4},{1,3},{3,1},{5,7},{7,5},{8,10},{10,8},{12,... | collective-permute-start | bytes 3145736 | tf_op jit(solution)/shard_map/ppermute | solution.py:40
  541.4 27.7 %collective-permute-start.65 = (bf16[512,1024]{1,0:T(8,128)(2,1)}, bf16[512,1024]{1,0:T(8,128)(2,1)}, u32[]{:S(2)}, u32[]{:S(2)}) collective-permute-start(bf16[512,1024]{1,0:T(8,128)(2,1)} %collective-permute-done.64.refs_2_), channel_id=1, source_target_pairs={{0,2},{2,0},{4,6},{6,4},{1,3},{3,1},{5,7},{7,5},{8,10},{10,8},{12,... | collective-permute-start | bytes 3145736 | tf_op jit(solution)/shard_map/ppermute | solution.py:40
  569.1 23.6 %collective-permute-start.68 = (bf16[512,1024]{1,0:T(8,128)(2,1)}, bf16[512,1024]{1,0:T(8,128)(2,1)}, u32[]{:S(2)}, u32[]{:S(2)}) collective-permute-start(bf16[512,1024]{1,0:T(8,128)(2,1)} %reduce-scatter.6.cloned.1.call-done.refs_0_), channel_id=1, source_target_pairs={{0,4},{4,0},{2,6},{6,2},{1,5},{5,1},{3,7},{7,3},{8,12},{12,8},{10,... | collective-permute-start | bytes 3145736 | tf_op jit(solution)/shard_map/ppermute | solution.py:44
  576.6 21.7 %collective-permute-start.67 = (bf16[512,1024]{1,0:T(8,128)(2,1)}, bf16[512,1024]{1,0:T(8,128)(2,1)S(1)}, u32[]{:S(2)}, u32[]{:S(2)}) collective-permute-start(bf16[512,1024]{1,0:T(8,128)(2,1)} %reduce-scatter.6.cloned.1.call-done.refs_0_), channel_id=1, source_target_pairs={{0,2},{2,0},{4,6},{6,4},{1,3},{3,1},{5,7},{7,5},{8,10},{10,8},{12,... | collective-permute-start | bytes 3145736 | tf_op jit(solution)/shard_map/ppermute | solution.py:40
  579.0 13.9 %collective-permute-start.74 = (f32[6,2048]{1,0:T(8,128)S(1)}, f32[6,2048]{1,0:T(8,128)S(1)}, u32[]{:S(2)}, u32[]{:S(2)}) collective-permute-start(f32[6,2048]{1,0:T(8,128)S(1)} %add.350), channel_id=1, source_target_pairs={{0,2},{2,0},{4,6},{6,4},{1,3},{3,1},{5,7},{7,5},{8,10},{10,8},{12,... | collective-permute-start | bytes 147464 | tf_op jit(solution)/shard_map/ppermute | solution.py:40
  592.7 15.2 %collective-permute-start.69 = (bf16[512,1024]{1,0:T(8,128)(2,1)}, bf16[512,1024]{1,0:T(8,128)(2,1)S(1)}, u32[]{:S(2)}, u32[]{:S(2)}) collective-permute-start(bf16[512,1024]{1,0:T(8,128)(2,1)} %collective-permute-done.68.refs_2_), channel_id=1, source_target_pairs={{0,2},{2,0},{4,6},{6,4},{1,3},{3,1},{5,7},{7,5},{8,10},{10,8},{12,... | collective-permute-start | bytes 3145736 | tf_op jit(solution)/shard_map/ppermute | solution.py:40
  593.5 26.5 %collective-permute-start.54 = (bf16[256,2048]{1,0:T(8,128)(2,1)}, bf16[256,2048]{1,0:T(8,128)(2,1)}, u32[]{:S(2)}, u32[]{:S(2)}) collective-permute-start(bf16[256,2048]{1,0:T(8,128)(2,1)} %add_convert_fusion.4), channel_id=1, source_target_pairs={{0,1},{1,0},{2,3},{3,2},{4,5},{5,4},{6,7},{7,6},{8,9},{9,8},{10,11... | collective-permute-start | bytes 3145736 | tf_op jit(solution)/shard_map/ppermute | solution.py:36
  597.6 16.5 %collective-permute-start.76 = (f32[1,3456]{1,0:T(1,128)S(1)}, f32[1,3456]{1,0:T(1,128)S(1)}, u32[]{:S(2)}, u32[]{:S(2)}) collective-permute-start(f32[1,3456]{1,0:T(1,128)S(1)} %get-tuple-element.183), channel_id=1, source_target_pairs={{0,8},{8,16},{16,24},{24,0},{1,9},{9,17},{17,25},{25,1},{2,10},{10... | collective-permute-start | bytes 41480 | tf_op jit(solution)/shard_map/ppermute | solution.py:706
  597.6 17.3 %collective-permute-start.77 = (f32[1,3456]{1,0:T(1,128)S(1)}, f32[1,3456]{1,0:T(1,128)S(1)}, u32[]{:S(2)}, u32[]{:S(2)}) collective-permute-start(f32[1,3456]{1,0:T(1,128)S(1)} %get-tuple-element.185), channel_id=1, source_target_pairs={{0,16},{8,24},{16,0},{24,8},{1,17},{9,25},{17,1},{25,9},{2,18},{10... | collective-permute-start | bytes 41480 | tf_op jit(solution)/shard_map/ppermute | solution.py:706
  598.3 16.7 %collective-permute-start.78 = (f32[1,3456]{1,0:T(1,128)S(1)}, f32[1,3456]{1,0:T(1,128)S(1)}, u32[]{:S(2)}, u32[]{:S(2)}) collective-permute-start(f32[1,3456]{1,0:T(1,128)S(1)} %get-tuple-element.184), channel_id=1, source_target_pairs={{0,24},{8,0},{16,8},{24,16},{1,25},{9,1},{17,9},{25,17},{2,26},{10... | collective-permute-start | bytes 41480 | tf_op jit(solution)/shard_map/ppermute | solution.py:706
  607.8 34.0 %collective-permute-start.66 = (bf16[256,2048]{1,0:T(8,128)(2,1)S(1)}, bf16[256,2048]{1,0:T(8,128)(2,1)}, u32[]{:S(2)}, u32[]{:S(2)}) collective-permute-start(bf16[256,2048]{1,0:T(8,128)(2,1)S(1)} %copy-done.42), channel_id=1, source_target_pairs={{0,1},{1,0},{2,3},{3,2},{4,5},{5,4},{6,7},{7,6},{8,9},{9,8},{10,11... | collective-permute-start | bytes 3145736 | tf_op jit(solution)/shard_map/ppermute | solution.py:36
  614.0 24.9 %collective-permute-start.71 = (bf16[512,1024]{1,0:T(8,128)(2,1)}, bf16[512,1024]{1,0:T(8,128)(2,1)S(1)}, u32[]{:S(2)}, u32[]{:S(2)}) collective-permute-start(bf16[512,1024]{1,0:T(8,128)(2,1)} %reduce-scatter.8.cloned.1.call-done), channel_id=1, source_target_pairs={{0,4},{4,0},{2,6},{6,2},{1,5},{5,1},{3,7},{7,3},{8,12},{12,8},{10,... | collective-permute-start | bytes 3145736 | tf_op jit(solution)/shard_map/ppermute | solution.py:44
  615.1 23.3 %collective-permute-start.80 = (f32[12,32]{1,0:T(8,128)S(1)}, f32[12,32]{1,0:T(8,128)S(1)}, u32[]{:S(2)}, u32[]{:S(2)}) collective-permute-start(f32[12,32]{1,0:T(8,128)S(1)} %reshape.221), channel_id=1, source_target_pairs={{0,4},{4,0},{2,6},{6,2},{1,5},{5,1},{3,7},{7,3},{8,12},{12,8},{10,... | collective-permute-start | bytes 4616 | tf_op jit(solution)/shard_map/ppermute | solution.py:44
  623.0 16.6 %collective-permute-start.79 = (f32[12,32]{1,0:T(8,128)S(1)}, f32[12,32]{1,0:T(8,128)S(1)}, u32[]{:S(2)}, u32[]{:S(2)}) collective-permute-start(f32[12,32]{1,0:T(8,128)S(1)} %reshape.221), channel_id=1, source_target_pairs={{0,2},{2,0},{4,6},{6,4},{1,3},{3,1},{5,7},{7,5},{8,10},{10,8},{12,... | collective-permute-start | bytes 4616 | tf_op jit(solution)/shard_map/ppermute | solution.py:40
  (100 other events, 833.6 us)
Sparse Core Ops, SparseCore 0:
  20.0 79.0 all-gather.2
  101.3 148.1 all-gather.4
  282.3 74.9 reduce-scatter.3
  424.1 73.2 reduce-scatter.5
  503.8 74.1 reduce-scatter.7

commit v3 on v2

v3 whole, which is shorter than its diff:
```python
from functools import partial
import math

import jax
import jax.numpy as jnp
from jax import lax
from jax.experimental import pallas as pl
from jax.experimental.pallas import tpu as pltpu
from jax.sharding import PartitionSpec as P

HD = 128
BF = jnp.bfloat16
F32 = jnp.float32
VMEM_BYTES = 62 << 20


norm_epsilon = 1e-05


def normalize(values):
    centre = jnp.mean(values, axis=-1, keepdims=True)
    centered = values - centre
    inverse = lax.rsqrt(jnp.mean(centered * centered, axis=-1, keepdims=True) + norm_epsilon)
    return (centered * inverse, inverse)


def norm_backward(incoming, normed, inverse, gain_vec):
    scaled = incoming * gain_vec
    return inverse * (
        scaled
        - jnp.mean(scaled, axis=-1, keepdims=True)
        - normed * jnp.mean(scaled * normed, axis=-1, keepdims=True)
    )


def swap_tp(value):
    return lax.ppermute(value, "tp", [(0, 1), (1, 0)])


def swap_low(value):
    return lax.ppermute(value, "ctx", [(0, 1), (1, 0), (2, 3), (3, 2)])


def swap_high(value):
    return lax.ppermute(value, "ctx", [(0, 2), (2, 0), (1, 3), (3, 1)])


def stage(*values):
    return lax.optimization_barrier(values)


def swap_any(value, distance):
    return lax.ppermute(value, ("ctx", "tp"), [(i, i ^ distance) for i in range(8)])


GATHERED = (0, 2, 1, 4, 3, 6, 5, 7)


def scatter_first(sums):
    return [swap_tp(sums[2]), swap_high(sums[3])]


def scatter_second(sums, first):
    half = sums[1].shape[0]
    by_tp, by_high = first
    across = sums[1].astype(F32) + by_high[:half].astype(F32)
    along = sums[4].astype(F32) + by_tp[half:].astype(F32)
    return [swap_tp(across.astype(BF)), swap_high(along.astype(BF))]


def scatter_sum(sums, first, second):
    half = sums[1].shape[0]
    by_tp = jnp.concatenate([second[0], first[0][:half]], axis=0)
    by_high = jnp.concatenate([first[1][half:], second[1]], axis=0)
    return sums[0] + by_tp.astype(F32) + by_high.astype(F32)


def pair_mask(rows, limits, split):
    row = lax.broadcasted_iota(jnp.int32, (rows, rows), 0)
    col = lax.broadcasted_iota(jnp.int32, (rows, rows), 1)
    mask = col <= row
    for seq in range(rows // split):
        inside = (row >= seq * split) & (row < (seq + 1) * split)
        limit = jnp.where(inside, limits[seq] + seq * split, 0)
        lower = jnp.where(inside, seq * split, 0)
        ok = (col >= lower) & (col < limit)
        mask = mask & (jnp.logical_not(inside) | ok)
    return mask


def attention_tiles(info_ref, tiles, rows, cont_len):
    me = info_ref[0]
    prompt_len = info_ref[1]
    per_block = rows // cont_len
    col = lax.broadcasted_iota(jnp.int32, (rows, rows), 1)
    row = lax.broadcasted_iota(jnp.int32, (rows, rows), 0)
    plan = []
    for t in range(tiles):
        keys = []
        for j in range(t + 1):
            mask = None
            if j == tiles - 1:
                mask = (col + j * rows) < prompt_len
            if j == t:
                mask = (col <= row) if mask is None else mask & (col <= row)
            keys.append((2 * j, mask))
        plan.append((2 * t, keys))
    for t in range(tiles):
        keys = []
        for j in range(tiles):
            keys.append((2 * j, (col + j * rows) < prompt_len if j == tiles - 1 else None))
        base = 2 + ((2 * t) ^ (me & (2 * tiles - 2))) // 2 * per_block
        limits = [info_ref[base + s] for s in range(per_block)]
        keys.append((2 * t + 1, pair_mask(rows, limits, cont_len)))
        plan.append((2 * t + 1, keys))
    return me, plan


def dot_nt(a, b):
    return lax.dot_general(a, b, (((1,), (1,)), ((), ())), preferred_element_type=F32)


def dot_nn(a, b):
    return lax.dot_general(a, b, (((1,), (0,)), ((), ())), preferred_element_type=F32)


def dot_tn(a, b):
    return lax.dot_general(a, b, (((0,), (0,)), ((), ())), preferred_element_type=F32)


def softmax_tiles(query, keys, scale):
    scores = []
    for key, mask in keys:
        score = dot_nt(query, key) * scale
        scores.append(score if mask is None else jnp.where(mask, score, -1e30))
    top = jnp.max(scores[0], axis=-1, keepdims=True)
    for s in scores[1:]:
        top = jnp.maximum(top, jnp.max(s, axis=-1, keepdims=True))
    weights = [jnp.exp(s - top) for s in scores]
    total = jnp.sum(weights[0], axis=-1, keepdims=True)
    for w in weights[1:]:
        total = total + jnp.sum(w, axis=-1, keepdims=True)
    inverse = 1.0 / total
    return [w * inverse for w in weights]


def attention_forward_kernel(tiles, rows, cont_len, heads, info_ref, qkv_ref, out_ref):
    h = pl.program_id(0)
    scale = 1.0 / math.sqrt(HD)
    me, plan = attention_tiles(info_ref, tiles, rows, cont_len)

    def load(kind, block):
        cols = pl.ds(pl.multiple_of((kind * heads + h) * HD, HD), HD)
        return qkv_ref[block ^ me, :, cols]

    for block, keys in plan:
        query = load(0, block)
        probs = softmax_tiles(query, [(load(1, kb), mask) for kb, mask in keys], scale)
        total = None
        for p, (kb, _) in zip(probs, keys):
            term = dot_nn(p.astype(BF), load(2, kb))
            total = term if total is None else total + term
        cols = pl.ds(pl.multiple_of(h * HD, HD), HD)
        out_ref[block ^ me, :, cols] = total.astype(BF)


def attention_backward_kernel(
    tiles, rows, cont_len, heads, info_ref, qkv_ref, grad_ref, out_ref, dkey_ref, dvalue_ref
):
    h = pl.program_id(0)
    scale = 1.0 / math.sqrt(HD)
    me, plan = attention_tiles(info_ref, tiles, rows, cont_len)

    def columns(kind):
        return pl.ds(pl.multiple_of((kind * heads + h) * HD, HD), HD)

    def load(kind, block):
        return qkv_ref[block ^ me, :, columns(kind)]

    seen = set()
    for block, keys in plan:
        query = load(0, block)
        grad = grad_ref[block ^ me, :, columns(0)]
        probs = softmax_tiles(query, [(load(1, kb), mask) for kb, mask in keys], scale)
        gprobs = [dot_nt(grad, load(2, kb)) for kb, _ in keys]
        delta = jnp.sum(probs[0] * gprobs[0], axis=-1, keepdims=True)
        for p, g in zip(probs[1:], gprobs[1:]):
            delta = delta + jnp.sum(p * g, axis=-1, keepdims=True)
        dquery = None
        for p, g, (kb, _) in zip(probs, gprobs, keys):
            dscore = (p * (g - delta)).astype(BF)
            term = dot_nn(dscore, load(1, kb))
            dquery = term if dquery is None else dquery + term
            dkey = dot_tn(dscore, query)
            dvalue = dot_tn(p.astype(BF), grad)
            if kb in seen:
                dkey_ref[kb] += dkey
                dvalue_ref[kb] += dvalue
            else:
                dkey_ref[kb] = dkey
                dvalue_ref[kb] = dvalue
                seen.add(kb)
        out_ref[block ^ me, :, columns(0)] = (dquery * scale).astype(BF)
    for kb in sorted(seen):
        out_ref[kb ^ me, :, columns(1)] = (dkey_ref[kb] * scale).astype(BF)
        out_ref[kb ^ me, :, columns(2)] = dvalue_ref[kb].astype(BF)


def attention_cost(blocks, rows, heads, matmuls):
    tiles = blocks // 2
    pairs = (tiles * (tiles + 1)) // 2 + tiles * (tiles + 1)
    return pl.CostEstimate(
        flops=2 * matmuls * pairs * heads * rows * rows * HD,
        transcendentals=pairs * heads * rows * rows,
        bytes_accessed=2 * blocks * rows * heads * HD * (4 if matmuls == 2 else 7),
    )


def attention_forward(info, qkv, cont_len):
    blocks, rows, width = qkv.shape
    heads = width // (3 * HD)
    return pl.pallas_call(
        partial(attention_forward_kernel, blocks // 2, rows, cont_len, heads),
        grid=(heads,),
        in_specs=[
            pl.BlockSpec(memory_space=pltpu.SMEM),
            pl.BlockSpec((blocks, rows, width), lambda h: (0, 0, 0)),
        ],
        out_specs=pl.BlockSpec((blocks, rows, heads * HD), lambda h: (0, 0, 0)),
        out_shape=jax.ShapeDtypeStruct((blocks, rows, heads * HD), BF),
        compiler_params=pltpu.CompilerParams(vmem_limit_bytes=32 << 20),
        cost_estimate=attention_cost(blocks, rows, heads, 2),
        name="attention_forward",
    )(info, qkv)


def attention_backward(info, qkv, grad, cont_len):
    blocks, rows, width = qkv.shape
    heads = width // (3 * HD)
    return pl.pallas_call(
        partial(attention_backward_kernel, blocks // 2, rows, cont_len, heads),
        grid=(heads,),
        in_specs=[
            pl.BlockSpec(memory_space=pltpu.SMEM),
            pl.BlockSpec((blocks, rows, width), lambda h: (0, 0, 0)),
            pl.BlockSpec((blocks, rows, heads * HD), lambda h: (0, 0, 0)),
        ],
        out_specs=pl.BlockSpec((blocks, rows, width), lambda h: (0, 0, 0)),
        out_shape=jax.ShapeDtypeStruct((blocks, rows, width), BF),
        scratch_shapes=[
            pltpu.VMEM((blocks, rows, HD), F32),
            pltpu.VMEM((blocks, rows, HD), F32),
        ],
        compiler_params=pltpu.CompilerParams(vmem_limit_bytes=32 << 20),
        cost_estimate=attention_cost(blocks, rows, heads, 7),
        name="attention_backward",
    )(info, qkv, grad)


def grad_matmul_kernel(n_left, spans, widths, *refs):
    total = None
    for li, lo, ri, ro, size in spans:
        left = refs[li][pl.ds(lo, size), :]
        right = refs[n_left + ri][pl.ds(ro, size), :]
        term = dot_tn(left, right)
        total = term if total is None else total + term
    start = 0
    for out_ref, n in zip(refs[len(refs) - len(widths) :], widths):
        out_ref[...] = total[:, start : start + n].astype(BF)
        start += n


def row_chunks(pieces, order, rows, chunk):
    where = {}
    place = 0
    spots = []
    for index, piece in enumerate(pieces):
        for offset in range(0, piece.shape[0], chunk):
            spots.append((index, offset))
    per_block = rows // chunk
    for block in order:
        where[block] = spots[place : place + per_block]
        place += per_block
    return [spot for block in sorted(where) for spot in where[block]]


def matched_spans(lefts, left_order, rights, right_order, rows):
    chunk = min([rows] + [p.shape[0] for p in list(lefts) + list(rights)])
    spans = []
    for left, right in zip(
        row_chunks(lefts, left_order, rows, chunk), row_chunks(rights, right_order, rows, chunk)
    ):
        last = spans[-1] if spans else None
        if last and left == (last[0], last[1] + last[4]) and right == (last[2], last[3] + last[4]):
            spans[-1] = last[:4] + (last[4] + chunk,)
        else:
            spans.append(left + right + (chunk,))
    return spans


def grad_matmul(lefts, left_order, rights, right_order, rows, name, widths=None):
    spans = matched_spans(lefts, left_order, rights, right_order, rows)
    d = lefts[0].shape[1]
    n = rights[0].shape[1]
    widths = widths or [n]
    tile = 512
    total_rows = sum(p.shape[0] for p in lefts)
    return pl.pallas_call(
        partial(grad_matmul_kernel, len(lefts), spans, widths),
        grid=(d // tile,),
        in_specs=[pl.BlockSpec((p.shape[0], tile), lambda i: (0, i)) for p in lefts]
        + [pl.BlockSpec(p.shape, lambda i: (0, 0), pipeline_mode=pl.Buffered(1)) for p in rights],
        out_specs=[pl.BlockSpec((tile, w), lambda i: (i, 0)) for w in widths],
        out_shape=[jax.ShapeDtypeStruct((d, w), BF) for w in widths],
        compiler_params=pltpu.CompilerParams(vmem_limit_bytes=32 << 20),
        cost_estimate=pl.CostEstimate(
            flops=2 * total_rows * d * n,
            transcendentals=0,
            bytes_accessed=2 * (total_rows * (d + n) + d * n),
        ),
        name=name,
    )(*lefts, *rights)


def sent_kernel(rows, low_ref, high_ref, w_ref, out_ref):
    for i, left in enumerate((low_ref, high_ref)):
        out_ref[pl.ds(2 * i * rows, 2 * rows), :] = dot_nt(left[...], w_ref[...]).astype(BF)


def kept_kernel(rows, low_ref, high_ref, w_ref, arrived_ref, own_ref, *outs):
    across_ref, to_tp_ref, to_high_ref, along_ref = outs
    half = rows // 2
    low = dot_nt(low_ref[...], w_ref[...])
    low = low + arrived_ref[pl.ds(0, 2 * rows), :].astype(F32)
    own_ref[...] = low[:rows]
    across_ref[...] = low[rows : rows + half].astype(BF)
    to_tp_ref[pl.ds(0, half), :] = low[rows + half :].astype(BF)
    high = dot_nt(high_ref[...], w_ref[...])
    high = (high + arrived_ref[pl.ds(2 * rows, 2 * rows), :].astype(F32)).astype(BF)
    to_tp_ref[pl.ds(half, half), :] = high[rows + half :]
    to_high_ref[pl.ds(0, half), :] = high[rows : rows + half]
    to_high_ref[pl.ds(half, half), :] = high[:half]
    along_ref[...] = high[half:rows]


def partial_blocks(left, rows, weights, column, arrived, name):
    k = left.shape[1]
    d = weights.shape[0]
    tile = 512
    pair = 2 * rows
    if arrived is None:
        first, kernel, more = 1, sent_kernel, []
        outs = [(4 * rows, BF)]
    else:
        first, kernel, more = 0, kept_kernel, [arrived]
        outs = [(rows, F32), (rows // 2, BF), (rows, BF), (rows, BF), (rows // 2, BF)]
    result = pl.pallas_call(
        partial(kernel, rows),
        grid=(d // tile,),
        in_specs=[
            pl.BlockSpec((pair, k), lambda i: (first, 0), pipeline_mode=pl.Buffered(1)),
            pl.BlockSpec((pair, k), lambda i: (first + 2, 0), pipeline_mode=pl.Buffered(1)),
            pl.BlockSpec((tile, k), lambda i: (i, column)),
        ]
        + [pl.BlockSpec((2 * pair, tile), lambda i: (0, i)) for _ in more],
        out_specs=[pl.BlockSpec((n, tile), lambda i: (0, i)) for n, _ in outs],
        out_shape=[jax.ShapeDtypeStruct((n, d), t) for n, t in outs],
        compiler_params=pltpu.CompilerParams(vmem_limit_bytes=VMEM_BYTES),
        cost_estimate=pl.CostEstimate(
            flops=8 * rows * d * k,
            transcendentals=0,
            bytes_accessed=2 * (4 * rows * (k + d) + d * k),
        ),
        name=name,
    )(left, left, weights, *more)
    return result[0] if arrived is None else result


def block_copies(pieces, rows, total):
    seen, plan = set(), []
    for start in range(0, total, rows):
        need = [
            i
            for i, (begin, size) in enumerate(pieces)
            if begin < start + rows and start < begin + size and i not in seen
        ]
        seen.update(need)
        plan.append(need)
    return plan


def piece_copy(refs, pieces, buffer, sems, i):
    begin, size = pieces[i]
    return pltpu.make_async_copy(refs[i], buffer.at[pl.ds(begin, size), :], sems.at[i])


def project_kernel(pieces, rows, *refs):
    lefts, (w_ref, bias_ref, out_ref, buffer, sems) = refs[: len(pieces)], refs[len(pieces) :]
    total = out_ref.shape[0]
    plan = block_copies(pieces, rows, total)

    def compute(p):
        block = pl.ds(p * rows, rows)
        out_ref[block, :] = (dot_nn(buffer[block, :], w_ref[...]) + bias_ref[...]).astype(BF)

    @pl.when(pl.program_id(0) == 0)
    def _():
        for need in plan:
            for i in need:
                piece_copy(lefts, pieces, buffer, sems, i).start()
        for p, need in enumerate(plan):
            for i in need:
                piece_copy(lefts, pieces, buffer, sems, i).wait()
            compute(p)

    @pl.when(pl.program_id(0) > 0)
    def _():
        for p in range(len(plan)):
            compute(p)


def project(lefts, starts, rows, weights, bias, column, n, name):
    total = sum(p.shape[0] for p in lefts)
    width = lefts[0].shape[1]
    pieces = [(start, p.shape[0]) for start, p in zip(starts, lefts)]
    tile = 256
    skip = column // tile
    return pl.pallas_call(
        partial(project_kernel, pieces, rows),
        grid=(n // tile,),
        in_specs=[pl.BlockSpec(memory_space=pl.ANY) for _ in lefts]
        + [
            pl.BlockSpec((width, tile), lambda i: (0, skip + i)),
            pl.BlockSpec((1, tile), lambda i: (0, i)),
        ],
        out_specs=pl.BlockSpec((total, tile), lambda i: (0, i)),
        out_shape=jax.ShapeDtypeStruct((total, n), BF),
        scratch_shapes=[
            pltpu.VMEM((total, width), BF),
            pltpu.SemaphoreType.DMA((len(lefts),)),
        ],
        compiler_params=pltpu.CompilerParams(vmem_limit_bytes=VMEM_BYTES),
        cost_estimate=pl.CostEstimate(
            flops=2 * total * width * n,
            transcendentals=0,
            bytes_accessed=2 * (total * (width + n) + width * n),
        ),
        name=name,
    )(*lefts, weights, bias)


def middle_kernel(pieces, tile, *refs):
    lefts = refs[: len(pieces)]
    att_ref, w_ref, term_ref, grad_ref, buffer, total_ref, sems = refs[len(pieces) :]
    step = pl.program_id(0)

    @pl.when(step == 0)
    def _():
        for i in range(len(pieces)):
            piece_copy(lefts, pieces, buffer, sems, i).start()
        for i in range(len(pieces)):
            piece_copy(lefts, pieces, buffer, sems, i).wait()

    left = buffer[:, pl.ds(pl.multiple_of(step * tile, tile), tile)]
    term_ref[...] = dot_tn(left, att_ref[...]).astype(BF)
    grad = dot_nn(left, w_ref[...])

    @pl.when(step == 0)
    def _():
        total_ref[...] = grad

    @pl.when(step > 0)
    def _():
        total_ref[...] += grad

    @pl.when(step == pl.num_programs(0) - 1)
    def _():
        grad_ref[...] = total_ref[...].astype(BF)


def middle_terms(lefts, starts, attended, weights, column, name):
    total, n = attended.shape
    d = lefts[0].shape[1]
    tile = 512
    pieces = [(start, p.shape[0]) for start, p in zip(starts, lefts)]
    return pl.pallas_call(
        partial(middle_kernel, pieces, tile),
        grid=(d // tile,),
        in_specs=[pl.BlockSpec(memory_space=pl.ANY) for _ in lefts]
        + [
            pl.BlockSpec((total, n), lambda i: (0, 0), pipeline_mode=pl.Buffered(1)),
            pl.BlockSpec((tile, n), lambda i: (i, column)),
        ],
        out_specs=[
            pl.BlockSpec((tile, n), lambda i: (i, 0)),
            pl.BlockSpec((total, n), lambda i: (0, 0)),
        ],
        out_shape=[
            jax.ShapeDtypeStruct((d, n), BF),
            jax.ShapeDtypeStruct((total, n), BF),
        ],
        scratch_shapes=[
            pltpu.VMEM((total, d), BF),
            pltpu.VMEM((total, n), F32),
            pltpu.SemaphoreType.DMA((len(lefts),)),
        ],
        compiler_params=pltpu.CompilerParams(vmem_limit_bytes=VMEM_BYTES),
        cost_estimate=pl.CostEstimate(
            flops=4 * total * d * n,
            transcendentals=0,
            bytes_accessed=2 * total * (d + 2 * n) + 4 * d * n,
        ),
        name=name,
    )(*lefts, attended, weights)


def shard_kernel(n_cols, ctx_ref, *refs):
    ins, out = refs[:-1], refs[-1]
    start = 0
    for i, ref in enumerate(ins):
        value = ref[...] if i < n_cols else ref[...].T
        out[:, start : start + value.shape[1]] = value
        start += value.shape[1]


def weight_shard(ctx, by_column, by_row, size, name):
    d = by_column[0].shape[0]
    count = len(by_column) + len(by_row)
    return pl.pallas_call(
        partial(shard_kernel, len(by_column)),
        grid_spec=pltpu.PrefetchScalarGridSpec(
            num_scalar_prefetch=1,
            grid=(1,),
            in_specs=[pl.BlockSpec((d, size), lambda i, c: (0, c[0])) for _ in by_column]
            + [pl.BlockSpec((size, d), lambda i, c: (c[0], 0)) for _ in by_row],
            out_specs=pl.BlockSpec((d, count * size), lambda i, c: (0, 0)),
        ),
        out_shape=jax.ShapeDtypeStruct((d, count * size), BF),
        compiler_params=pltpu.CompilerParams(vmem_limit_bytes=VMEM_BYTES),
        cost_estimate=pl.CostEstimate(
            flops=0, transcendentals=0, bytes_accessed=4 * d * count * size
        ),
        name=name,
    )(ctx[None].astype(jnp.int32), *by_column, *by_row)


def assemble_kernel(turn, count, width, ctx_ref, *refs):
    pieces, outs = refs[:count], refs[count:]
    step = pl.program_id(0)
    for k in range(count):

        @pl.when(step == k)
        def _():
            for i, out in enumerate(outs):
                part = pieces[k][:, i * width : (i + 1) * width].astype(F32)
                out[...] = part.T if turn else part


def assemble(ctx, pieces, turn, outputs, name):
    count = len(pieces)
    rows, cols = pieces[0].shape
    width = cols // outputs
    if turn:
        block, shape = (width, rows), (width * count, rows)
        index = lambda k, ctx_ref: (k ^ ctx_ref[0], 0)
    else:
        block, shape = (rows, width), (rows, width * count)
        index = lambda k, ctx_ref: (0, k ^ ctx_ref[0])
    return pl.pallas_call(
        partial(assemble_kernel, turn, count, width),
        grid_spec=pltpu.PrefetchScalarGridSpec(
            num_scalar_prefetch=1,
            grid=(count,),
            in_specs=[
                pl.BlockSpec((rows, cols), lambda k, ctx_ref: (0, 0), pipeline_mode=pl.Buffered(1))
                for _ in pieces
            ],
            out_specs=[pl.BlockSpec(block, index) for _ in range(outputs)],
        ),
        out_shape=[jax.ShapeDtypeStruct(shape, F32) for _ in range(outputs)],
        compiler_params=pltpu.CompilerParams(vmem_limit_bytes=VMEM_BYTES),
        cost_estimate=pl.CostEstimate(
            flops=0, transcendentals=0, bytes_accessed=6 * count * rows * cols
        ),
        name=name,
    )(ctx[None].astype(jnp.int32), *pieces)


def gelu_and_slope(u):
    half = 0.5 * (1.0 + lax.erf(u * math.sqrt(0.5)))
    density = jnp.exp(-0.5 * u * u) * (1.0 / math.sqrt(2.0 * math.pi))
    return u * half, half + u * density


def feed_kernel(act_pieces, up_pieces, rows, *refs):
    count = len(act_pieces)
    acts, ups = refs[:count], refs[count : count + len(up_pieces)]
    (
        w_up_ref,
        w_down_ref,
        bias_ref,
        hidden_ref,
        grad_ref,
        sum_ref,
        act_buffer,
        up_buffer,
        act_sems,
        up_sems,
    ) = refs[count + len(up_pieces) :]
    total = hidden_ref.shape[0]
    act_plan = block_copies(act_pieces, rows, total)
    up_plan = block_copies(up_pieces, rows, total)

    def compute(p):
        block = pl.ds(p * rows, rows)
        pre_act = dot_nn(act_buffer[block, :], w_up_ref[...]) + bias_ref[...]
        grad_hidden = dot_nn(up_buffer[block, :], w_down_ref[...])
        hidden, slope = gelu_and_slope(pre_act)
        hidden_ref[block, :] = hidden.astype(BF)
        grad = (grad_hidden * slope).astype(BF)
        grad_ref[block, :] = grad
        part = jnp.sum(grad.astype(F32), axis=0, keepdims=True)
        if p == 0:
            sum_ref[...] = part
        else:
            sum_ref[...] += part

    def act_copy(i):
        return piece_copy(acts, act_pieces, act_buffer, act_sems, i)

    def up_copy(i):
        return piece_copy(ups, up_pieces, up_buffer, up_sems, i)

    @pl.when(pl.program_id(0) == 0)
    def _():
        for act_need, up_need in zip(act_plan, up_plan):
            for i in act_need:
                act_copy(i).start()
            for i in up_need:
                up_copy(i).start()
        for p, (act_need, up_need) in enumerate(zip(act_plan, up_plan)):
            for i in act_need:
                act_copy(i).wait()
            for i in up_need:
                up_copy(i).wait()
            compute(p)

    @pl.when(pl.program_id(0) > 0)
    def _():
        for p in range(len(act_plan)):
            compute(p)


def feed_both(acts, act_starts, ups, up_starts, rows, weights, bias, units, name):
    total = sum(p.shape[0] for p in acts)
    width = acts[0].shape[1]
    tile = 256
    skip = units // tile
    act_pieces = [(start, p.shape[0]) for start, p in zip(act_starts, acts)]
    up_pieces = [(start, p.shape[0]) for start, p in zip(up_starts, ups)]
    return pl.pallas_call(
        partial(feed_kernel, act_pieces, up_pieces, rows),
        grid=(units // tile,),
        in_specs=[pl.BlockSpec(memory_space=pl.ANY) for _ in acts + ups]
        + [
            pl.BlockSpec((width, tile), lambda i: (0, i)),
            pl.BlockSpec((width, tile), lambda i: (0, skip + i)),
            pl.BlockSpec((1, tile), lambda i: (0, i)),
        ],
        out_specs=[
            pl.BlockSpec((total, tile), lambda i: (0, i)),
            pl.BlockSpec((total, tile), lambda i: (0, i)),
            pl.BlockSpec((1, tile), lambda i: (0, i)),
        ],
        out_shape=[
            jax.ShapeDtypeStruct((total, units), BF),
            jax.ShapeDtypeStruct((total, units), BF),
            jax.ShapeDtypeStruct((1, units), F32),
        ],
        scratch_shapes=[
            pltpu.VMEM((total, width), BF),
            pltpu.VMEM((total, width), BF),
            pltpu.SemaphoreType.DMA((len(acts),)),
            pltpu.SemaphoreType.DMA((len(ups),)),
        ],
        compiler_params=pltpu.CompilerParams(vmem_limit_bytes=VMEM_BYTES),
        cost_estimate=pl.CostEstimate(
            flops=4 * total * width * units,
            transcendentals=0,
            bytes_accessed=4 * (total * width + width * units + total * units),
        ),
        name=name,
    )(*acts, *ups, weights, weights, bias)


def gather_small(packed, size):
    index = lax.axis_index("fsdp")
    out = lax.dynamic_update_slice(
        jnp.zeros((size,) + packed.shape, packed.dtype), packed[None], (index, 0)
    )
    for step in range(1, size):
        moved = lax.ppermute(packed, "fsdp", [(i, (i + step) % size) for i in range(size)])
        out = lax.dynamic_update_slice(out, moved[None], ((index + size - step) % size, 0))
    return out


def body(
    prompt_input,
    continuation_input,
    prompt_lengths,
    continuation_lengths,
    query_weight,
    key_weight,
    value_weight,
    query_bias,
    value_bias,
    output_weight,
    output_bias,
    first_gain,
    first_shift,
    second_gain,
    second_shift,
    up_weight,
    up_bias,
    down_weight,
    down_bias,
    prompt_cotangent,
    continuation_cotangent,
):
    prompt_dev = prompt_input.shape[1]
    cont_dev = continuation_input.shape[1]
    cont_len = continuation_input.shape[2]
    width = prompt_input.shape[2]
    rows = prompt_dev
    fsdp_size = lax.axis_size("fsdp")
    ctx_size = lax.axis_size("ctx")
    tp_size = lax.axis_size("tp")
    assert ctx_size == 4 and tp_size == 2 and cont_dev * cont_len == rows
    blocks = ctx_size * tp_size
    total_rows = blocks * rows
    z = lax.axis_index("fsdp")
    ctx = lax.axis_index("ctx")
    tp = lax.axis_index("tp")
    me = 2 * ctx + tp

    heads_tp = query_bias.shape[0]
    heads = heads_tp // ctx_size
    head_width = heads * HD
    units = up_weight.shape[1] // ctx_size
    unit_rows = units // HD
    d_local = query_weight.shape[0]

    def rws(weight, count):
        return lax.dynamic_slice_in_dim(weight, ctx * count, count, axis=0)

    attn_shard = weight_shard(
        ctx, [query_weight, key_weight, value_weight], [output_weight], head_width, "attention_shard"
    )
    (
        attn_shard,
        prompt_input,
        continuation_input,
        prompt_cotangent,
        continuation_cotangent,
        continuation_lengths,
    ) = stage(
        attn_shard,
        prompt_input,
        continuation_input,
        prompt_cotangent,
        continuation_cotangent,
        continuation_lengths,
    )
    attn_full = lax.all_gather(attn_shard, "fsdp", axis=0, tiled=True)
    w_qkv = attn_full[:, : 3 * head_width]
    def own_pair(first, second):
        a = first[0]
        b = second[0].reshape(rows, width)
        return jnp.where(tp == 0, a, b), jnp.where(tp == 0, b, a)

    in_own, in_other = own_pair(prompt_input, continuation_input)
    up_own, up_other = own_pair(prompt_cotangent, continuation_cotangent)
    stacked = jnp.concatenate([in_own, in_other], axis=0).astype(F32)
    normed_pair, inverse_pair = normalize(stacked)
    (
        output_bias,
        first_gain,
        first_shift,
        second_gain,
        second_shift,
        down_bias,
        query_bias,
        value_bias,
        up_bias,
        up_weight,
        continuation_lengths,
        inverse_pair,
    ) = stage(
        output_bias,
        first_gain,
        first_shift,
        second_gain,
        second_shift,
        down_bias,
        query_bias,
        value_bias,
        up_bias,
        up_weight,
        continuation_lengths,
        inverse_pair,
    )
    packed = jnp.concatenate(
        [
            output_bias,
            first_gain,
            first_shift,
            second_gain,
            second_shift,
            down_bias,
            rws(query_bias, heads).reshape(-1),
            rws(value_bias, heads).reshape(-1),
            rws(up_bias, unit_rows).reshape(-1),
        ]
    )
    feed_shard = weight_shard(ctx, [up_weight], [down_weight], units, "feed_shard")
    small, feed_shard = stage(gather_small(packed, fsdp_size), feed_shard)
    w_feed = lax.all_gather(feed_shard, "fsdp", axis=0, tiled=True)
    small = small.astype(F32)
    vectors = [small[:, i * d_local : (i + 1) * d_local].reshape(-1) for i in range(6)]
    obias, gain_one, shift_one, gain_two, shift_two, dbias = vectors
    hd_local = HD // fsdp_size

    def head_vector(start, count):
        piece = small[:, start : start + count * hd_local].reshape(fsdp_size, count, hd_local)
        return piece.transpose(1, 0, 2).reshape(-1)

    start = 6 * d_local
    qbias = head_vector(start, heads)
    vbias = head_vector(start + heads * hd_local, heads)
    ubias = head_vector(start + 2 * heads * hd_local, unit_rows)
    qkv_bias = jnp.concatenate([qbias, jnp.zeros_like(qbias), vbias])

    lens = continuation_lengths[0]
    lens_high = swap_high(lens)
    info = jnp.concatenate(
        [me[None].astype(jnp.int32), prompt_lengths, lens, swap_low(lens), lens_high, swap_low(lens_high)]
    )

    natural = list(range(blocks))
    up_along = swap_high(up_own)
    act_pair = (normed_pair * gain_one + shift_one).astype(BF)
    act_pair, up_along = stage(act_pair, up_along)
    up_pair = jnp.concatenate([up_own, up_other], axis=0)
    act_high, act_low, up_corner, up_low, up_far = stage(
        swap_high(act_pair), swap_low(act_pair), swap_tp(up_along), swap_low(up_pair), swap_low(up_along)
    )
    act_pieces = [act_pair, act_low, act_high, swap_low(act_high)]
    act_starts = [0, 2 * rows, 4 * rows, 6 * rows]
    up_pieces = [up_pair, up_low, up_along, up_corner, up_far, swap_low(up_corner)]
    up_starts = [0, 2 * rows, 4 * rows, 5 * rows, 6 * rows, 7 * rows]
    act_pieces, up_pieces = stage(act_pieces, up_pieces)
    normed_one = normed_pair[:rows]
    inverse_one = inverse_pair[:rows]
    x_own = stacked[:rows]

    qkv = project(
        act_pieces, act_starts, rows, attn_full, qkv_bias[None], 0, 3 * head_width, "heads"
    ).reshape(blocks, rows, 3 * head_width)
    attended = attention_forward(info, qkv, cont_len).reshape(total_rows, head_width)
    parts = partial_blocks(attended, rows, attn_full, 3, None, "attention_sent")
    parts = swap_low(parts)
    sums = partial_blocks(attended, rows, attn_full, 3, parts, "attention_kept")
    first = stage(*scatter_first(sums))
    second = scatter_second(sums, first)
    middle = x_own + (scatter_sum(sums, first, second) + obias)
    normed_two, inverse_two = normalize(middle)
    act_two_own = (normed_two * gain_two + shift_two).astype(BF)

    def gather_blocks(own, beside=(), between=None):
        half = rows // 2
        across, along, low, *beside = stage(swap_tp(own), swap_high(own), swap_low(own), *beside)
        if between is not None:
            beside = between(*beside)
        corner_a, corner_b, across_low, along_low, *beside = stage(
            swap_high(across[:half]),
            swap_tp(along[half:]),
            swap_low(across),
            swap_low(along),
            *beside,
        )
        pieces = stage(
            own,
            low,
            across,
            along,
            across_low,
            along_low,
            corner_a,
            corner_b,
            swap_low(corner_a),
            swap_low(corner_b),
        )
        return list(pieces), beside

    act_two, _ = gather_blocks(act_two_own)
    starts = []
    for p in GATHERED[:6]:
        starts.append(p * rows)
    for p in GATHERED[6:]:
        starts += [p * rows, p * rows + rows // 2]

    def to_outputs(own, other):
        first = jnp.where(tp == 0, own, other)
        second = jnp.where(tp == 0, other, own)
        return first[None], second.reshape(1, cont_dev, cont_len, width)

    hidden, grad_pre, ubias_sum = feed_both(
        act_two, starts, up_pieces, up_starts, 2 * rows, w_feed, ubias[None], units, "feed_both"
    )
    parts = partial_blocks(grad_pre, rows, w_feed, 0, None, "act_two_sent")
    parts, hidden = stage(parts, hidden)
    (down_term,) = grad_matmul(up_pieces, natural, [hidden], natural, rows, "down_weight_term")
    parts, grad_pre, down_term = stage(swap_low(parts), grad_pre, down_term)
    down_piece = lax.psum_scatter(down_term, "fsdp", scatter_dimension=0, tiled=True)
    sums = partial_blocks(grad_pre, rows, w_feed, 0, parts, "act_two_kept")
    sums, grad_pre = stage(sums, grad_pre)
    (up_term,) = grad_matmul(act_two, GATHERED, [grad_pre], natural, rows, "up_weight_term")
    first, up_term, hidden = stage(scatter_first(sums), up_term, hidden)
    mlp_parts = partial_blocks(hidden, rows, w_feed, 1, None, "feed_sent")
    second, mlp_parts, up_term, hidden = stage(
        scatter_second(sums, first), mlp_parts, up_term, hidden
    )
    up_piece = lax.psum_scatter(up_term, "fsdp", scatter_dimension=0, tiled=True)
    grad_act_two = scatter_sum(sums, first, second)
    grad_middle = up_own.astype(F32) + norm_backward(
        grad_act_two, normed_two, inverse_two, gain_two
    )
    middle_low_own = grad_middle.astype(BF)

    def feed_sums(mlp_parts, hidden, down_piece):
        return partial_blocks(hidden, rows, w_feed, 1, mlp_parts, "feed_kept"), down_piece

    middle_low, (mlp_sums, down_piece) = gather_blocks(
        middle_low_own, (swap_low(mlp_parts), hidden, down_piece), feed_sums
    )

    def colsum(value):
        return jnp.sum(value, axis=0, dtype=F32)

    middle_low, mlp_sums = stage(middle_low, mlp_sums)
    out_term, grad_attended = middle_terms(
        middle_low, starts, attended, attn_full, 3, "middle_terms"
    )
    mlp_first, grad_attended, out_term = stage(
        scatter_first(mlp_sums), grad_attended, out_term
    )
    out_piece = lax.psum_scatter(out_term, "fsdp", scatter_dimension=0, tiled=True)
    dqkv = attention_backward(
        info, qkv, grad_attended.reshape(blocks, rows, head_width), cont_len
    ).reshape(total_rows, 3 * head_width)
    mlp_second, dqkv, up_piece = stage(scatter_second(mlp_sums, mlp_first), dqkv, up_piece)
    parts = partial_blocks(dqkv, rows, attn_full, 0, None, "act_one_sent")
    result = (middle + (scatter_sum(mlp_sums, mlp_first, mlp_second) + dbias)).astype(BF)
    parts, result, dqkv, down_high = stage(parts, result, dqkv, swap_high(down_piece))
    (qkv_term,) = grad_matmul(
        act_pieces, natural, [dqkv], natural, rows, "attention_weight_term"
    )
    qkv_piece = lax.psum_scatter(qkv_term, "fsdp", scatter_dimension=0, tiled=True)
    dqkv, parts, result_other, up_high, out_piece = stage(
        dqkv, swap_low(parts), swap_tp(result), swap_high(up_piece), out_piece
    )
    sums = partial_blocks(dqkv, rows, attn_full, 0, parts, "act_one_kept")
    sums, up_far, down_low, down_far, up_low, out_high = stage(
        sums,
        swap_low(up_high),
        swap_low(down_piece),
        swap_low(down_high),
        swap_low(up_piece),
        swap_high(out_piece),
    )
    (down_grad,) = assemble(
        ctx, [down_piece, down_low, down_high, down_far], True, 1, "down_weight_grad"
    )
    first, down_grad, out_low = stage(scatter_first(sums), down_grad, swap_low(out_piece))
    (up_grad,) = assemble(ctx, [up_piece, up_low, up_high, up_far], False, 1, "up_weight_grad")
    second, up_grad, out_far = stage(scatter_second(sums, first), up_grad, swap_low(out_high))
    grad_act_one = scatter_sum(sums, first, second)
    grad_stacked = (
        grad_middle + norm_backward(grad_act_one, normed_one, inverse_one, gain_one)
    ).astype(BF)
    vectors = jnp.stack(
        [
            colsum(middle_low_own),
            colsum(grad_act_one * normed_one),
            colsum(grad_act_one),
            colsum(grad_act_two * normed_two),
            colsum(grad_act_two),
            colsum(up_own),
        ]
    )
    colsum_qkv = colsum(dqkv)
    head_terms = jnp.concatenate(
        [
            colsum_qkv[:head_width].reshape(heads, HD),
            colsum_qkv[2 * head_width :].reshape(heads, HD),
            ubias_sum.reshape(unit_rows, HD),
        ]
    )
    place = lax.broadcasted_iota(jnp.int32, (blocks, 1, 1), 0)
    places = jnp.where(place == me, head_terms[None], 0.0)

    def by_owner(values):
        flat = values.reshape(-1, fsdp_size, values.shape[-1] // fsdp_size)
        return flat.transpose(1, 0, 2).reshape(fsdp_size, -1)

    small = jnp.concatenate([by_owner(vectors), by_owner(places)], axis=1)
    grad_stacked, small, qkv_piece = stage(grad_stacked, small, qkv_piece)
    small = small + swap_low(small)
    small = small + swap_tp(small)
    (output_grad,) = assemble(
        ctx, [out_piece, out_low, out_high, out_far], True, 1, "output_weight_grad"
    )
    stacked_other, small, qkv_high, qkv_low, output_grad, outputs = stage(
        swap_tp(grad_stacked),
        small,
        swap_high(qkv_piece),
        swap_low(qkv_piece),
        output_grad,
        to_outputs(result, result_other),
    )
    small, qkv_far = stage(small + swap_high(small), swap_low(qkv_high))
    summed = lax.dynamic_slice_in_dim(small, z, 1, axis=0)
    for step in range(1, fsdp_size):
        share = lax.dynamic_slice_in_dim(small, (z + step) % fsdp_size, 1, axis=0)
        pairs = [(i, (i + step) % fsdp_size) for i in range(fsdp_size)]
        summed = summed + lax.ppermute(share, "fsdp", pairs)
    summed = summed[0]
    obias_grad, gain_one_grad, shift_one_grad, gain_two_grad, shift_two_grad, dbias_grad = [
        summed[i * d_local : (i + 1) * d_local] for i in range(6)
    ]
    head_sums = summed[6 * d_local :].reshape(ctx_size, tp_size, 2 * heads + unit_rows, hd_local)
    head_sums = lax.dynamic_index_in_dim(head_sums, tp, axis=1, keepdims=False)
    qbias_grad = head_sums[:, :heads].reshape(heads_tp, hd_local)
    vbias_grad = head_sums[:, heads : 2 * heads].reshape(heads_tp, hd_local)
    ubias_grad = head_sums[:, 2 * heads :].reshape(ctx_size * unit_rows, hd_local)

    prompt_output, continuation_output = outputs
    prompt_input_grad, continuation_input_grad = to_outputs(grad_stacked, stacked_other)
    query_grad, key_grad, value_grad = assemble(
        ctx, [qkv_piece, qkv_low, qkv_high, qkv_far], False, 3, "attention_weight_grads"
    )
    return (
        prompt_output,
        continuation_output,
        prompt_input_grad,
        continuation_input_grad,
        query_grad,
        key_grad,
        value_grad,
        qbias_grad,
        vbias_grad,
        output_grad,
        obias_grad,
        gain_one_grad,
        shift_one_grad,
        gain_two_grad,
        shift_two_grad,
        up_grad,
        ubias_grad,
        down_grad,
        dbias_grad,
    )


def solution(mesh):
    return jax.shard_map(
        body,
        mesh=mesh,
        in_specs=(
            P("fsdp", "ctx", None),
            P("fsdp", "ctx", None, None),
            P("fsdp"),
            P("fsdp", "ctx"),
            P("fsdp", "tp"),
            P("fsdp", "tp"),
            P("fsdp", "tp"),
            P("tp", "fsdp"),
            P("tp", "fsdp"),
            P("tp", "fsdp"),
            P("fsdp"),
            P("fsdp"),
            P("fsdp"),
            P("fsdp"),
            P("fsdp"),
            P("fsdp", "tp"),
            P("tp", "fsdp"),
            P("tp", "fsdp"),
            P("fsdp"),
            P("fsdp", "ctx", None),
            P("fsdp", "ctx", None, None),
        ),
        out_specs=(
            P("fsdp", "ctx", None),
            P("fsdp", "ctx", None, None),
            P("fsdp", "ctx", None),
            P("fsdp", "ctx", None, None),
            P("fsdp", "tp"),
            P("fsdp", "tp"),
            P("fsdp", "tp"),
            P("tp", "fsdp"),
            P("tp", "fsdp"),
            P("tp", "fsdp"),
            P("fsdp"),
            P("fsdp"),
            P("fsdp"),
            P("fsdp"),
            P("fsdp"),
            P("fsdp", "tp"),
            P("tp", "fsdp"),
            P("tp", "fsdp"),
            P("fsdp"),
        ),
        check_vma=False,
    )
```

time: 667 us -> 632 us (0.948)
  Pallas kernels: 128 us -> 206 us
  matrix products: 52.8 us -> 0 us
  waiting for transfers between devices: 296 us -> 244 us
  other arithmetic: 64.6 us -> 55.5 us
    pallas_call x6 -> x16, Pallas kernels: 79 us -> 153 us  [the longest x8 62.2 us: partial_blocks(): pl.pallas_call(partial(kernel, rows), grid=(d // tile,), in_specs=[pl.Blo...]
    ppermute x20, waiting for transfers between devices: 167 us -> 107 us  [swap_high(): return lax.ppermute(value, 'ctx', [(0, 2), (2, 0), (1, 3), (3, 1)])]
    dot_general x21 -> x0, matrix products: 52.8 us -> none  [the longest x16 36.9 us: dot_nt(): lax.dot_general(a, b, (((1,), (1,)), ((), ())), preferred_element_type=F32)]
    unnamed x172 -> x154, local copies, waits for them, and re-layouts: 18.7 us -> 34.6 us
    all_gather x1, waiting for transfers between devices: 22.1 us -> 10.6 us  [body(): w_feed = lax.all_gather(feed_shard, 'fsdp', axis=0, tiled=True)]
    ppermute x41 -> x30, waiting for transfers between devices: 5.8 us -> 17.1 us  [swap_low(): return lax.ppermute(value, 'ctx', [(0, 1), (1, 0), (2, 3), (3, 2)])]
    reduce_sum x4 -> x5, other arithmetic: 6.31 us -> 15.6 us  [colsum(): return jnp.sum(value, axis=0, dtype=F32)]
    add x10 -> x3, other arithmetic: 9.06 us -> 0.08 us  [the longest x1 0.03 us: body(): small = small + swap_low(small)]
  transfers between devices with their start and end apart: 87 -> 78, of which waited for: 30 -> 39; matrix products, arithmetic and copies ran while one was open for 21% -> 11% of each run, Pallas kernels for 14% -> 27%
where the time goes in v3:
time: 632 us; the launch traced here: 626 us
  waiting for transfers between devices  244 us (39%)
  Pallas kernels  206 us (33%)
  other arithmetic  55.5 us (9%)
  starting transfers between devices  54.4 us (9%)
  local copies, waits for them, and re-layouts  50.3 us (8%)
  between operations  16.2 us (3%)
    ppermute x16, waiting for transfers between devices, swap_tp(): return lax.ppermute(value, 'tp', [(0, 1), (1, 0)])  109 us
    ppermute x20, waiting for transfers between devices, swap_high(): return lax.ppermute(value, 'ctx', [(0, 2), (2, 0), (1, 3), (3, 1)])  107 us
    pallas_call x8, Pallas kernels, partial_blocks(): pl.pallas_call(partial(kernel, rows), grid=(d // tile,), in_specs=[pl.Blo...  62.2 us
    unnamed x154, local copies, waits for them, and re-layouts  34.6 us
    pallas_call x3, Pallas kernels, grad_matmul(): pl.pallas_call(partial(grad_matmul_kernel, len(lefts), spans, widths), gr...  33.1 us
    pallas_call x1, Pallas kernels, feed_both(): pl.pallas_call(partial(feed_kernel, act_pieces, up_pieces, rows), grid=(u...  27.7 us
    ppermute x20, starting transfers between devices, swap_high(): return lax.ppermute(value, 'ctx', [(0, 2), (2, 0), (1, 3), (3, 1)])  24 us
    pallas_call x1, Pallas kernels, attention_backward(): pl.pallas_call(partial(attention_backward_kernel, blocks // 2, rows, cont...  21.4 us
  transfers between devices with their start and end apart: 78, of which 39 were waited for; matrix products, arithmetic and copies ran while one was open for 11% of the time, Pallas kernels for 27%

profile of v3, /device:TPU:0, one launch (start us, length us, event | category | flops | bytes accessed | tf_op | source)
XLA Modules:
  0.0 625.8 jit_solution(9110024488831304083)
XLA Ops:
  7.3 2.4 attention_shard.1
  13.6 5.0 collective-permute-start.5
  19.6 2.8 convert_reduce_fusion.2
  24.1 2.9 pad_maximum_fusion.1.refs_10_.refs_0_
  27.1 3.2 feed_shard.1
  31.0 4.5 subtract_multiply_fusion
  35.5 11.2 %collective-permute-done.6.refs_12_.refs_2_ = bf16[256,2048]{1,0:T(8,128)(2,1)S(1)} collective-permute-done((bf16[256,2048]{1,0:T(8,128)(2,1)}, bf16[256,2048]{1,0:T(8,128)(2,1)S(1)}, u32[]{:S(2)}, u32[]{:S(2)}) %collective-permute-start.6) | collective-permute-done | bytes 1048608 | tf_op jit(solution)/shard_map/ppermute | solution.py:45
  49.9 2.4 collective-permute-done.11.refs_14_.refs_4_
  52.3 21.6 %collective-permute-done.9.refs_13_.refs_3_ = bf16[256,2048]{1,0:T(8,128)(2,1)} collective-permute-done((bf16[256,2048]{1,0:T(8,128)(2,1)S(1)}, bf16[256,2048]{1,0:T(8,128)(2,1)}, u32[]{:S(2)}, u32[]{:S(2)}) %collective-permute-start.9) | collective-permute-done | bytes 1048608 | tf_op jit(solution)/shard_map/ppermute | solution.py:37
  73.9 20.8 %collective-permute-done.7.refs_2_ = bf16[512,2048]{1,0:T(8,128)(2,1)S(1)} collective-permute-done((bf16[512,2048]{1,0:T(8,128)(2,1)S(1)}, bf16[512,2048]{1,0:T(8,128)(2,1)S(1)}, u32[]{:S(2)}, u32[]{:S(2)}) %collective-permute-start.7) | collective-permute-done | bytes 2097184 | tf_op jit(solution)/shard_map/ppermute | solution.py:45
  101.5 12.4 %heads.1 = bf16[2048,768]{1,0:T(8,128)(2,1)} custom-call(bf16[512,2048]{1,0:T(8,128)(2,1)} %copy-done.10, bf16[512,2048]{1,0:T(8,128)(2,1)} %copy-done.18, bf16[512,2048]{1,0:T(8,128)(2,1)} %copy-done.20, bf16[512,2048]{1,0:T(8,128)(2,1)} %collective-permute-done.12.refs_3_, bf16[2048,1024]{1,0:T(8,128)(2,1)} %all-gather.3.cloned.1.call-done.refs_4_.w_ref.refs_11_, ...), custom_call_target="tpu_custom_call" | custom-call | flops 6442450944 | bytes 14680064 | tf_op jit(solution)/shard_map/heads/pallas_call | solution.py:428
  115.8 11.0 %attention_forward.1 = bf16[8,256,256]{2,1,0:T(8,128)(2,1)S(1)} custom-call(s32[10]{0:T(128)S(1)} %concatenate.47.info_ref, bf16[8,256,768]{2,1,0:T(8,128)(2,1)S(1)} %bitcast.93), custom_call_target="tpu_custom_call" | custom-call | flops 2013265920 | bytes 4194304 | tf_op jit(solution)/shard_map/attention_forward/pallas_call | solution.py:222
  127.8 5.0 attention_sent.1
  132.9 7.3 %collective-permute-done.14.arrived_ref = bf16[1024,2048]{1,0:T(8,128)(2,1)} collective-permute-done((bf16[1024,2048]{1,0:T(8,128)(2,1)}, bf16[1024,2048]{1,0:T(8,128)(2,1)}, u32[]{:S(2)}, u32[]{:S(2)}) %collective-permute-start.14) | collective-permute-done | bytes 4194336 | tf_op jit(solution)/shard_map/ppermute | solution.py:41
  140.3 6.1 attention_kept.1
  149.3 22.5 %collective-permute-done.15 = bf16[256,2048]{1,0:T(8,128)(2,1)S(1)} collective-permute-done((bf16[256,2048]{1,0:T(8,128)(2,1)}, bf16[256,2048]{1,0:T(8,128)(2,1)S(1)}, u32[]{:S(2)}, u32[]{:S(2)}) %collective-permute-start.15) | collective-permute-done | bytes 1048608 | tf_op jit(solution)/shard_map/ppermute | solution.py:37
  178.2 9.0 %collective-permute-done.18 = bf16[128,2048]{1,0:T(8,128)(2,1)S(1)} collective-permute-done((bf16[128,2048]{1,0:T(8,128)(2,1)S(1)}, bf16[128,2048]{1,0:T(8,128)(2,1)S(1)}, u32[]{:S(2)}, u32[]{:S(2)}) %collective-permute-start.18) | collective-permute-done | bytes 524320 | tf_op jit(solution)/shard_map/ppermute | solution.py:45
  187.2 2.5 collective-permute-done.17
  194.0 22.9 %collective-permute-done.20.refs_3_ = bf16[256,2048]{1,0:T(8,128)(2,1)S(1)} collective-permute-done((bf16[256,2048]{1,0:T(8,128)(2,1)S(1)}, bf16[256,2048]{1,0:T(8,128)(2,1)S(1)}, u32[]{:S(2)}, u32[]{:S(2)}) %collective-permute-start.20) | collective-permute-done | bytes 1048608 | tf_op jit(solution)/shard_map/ppermute | solution.py:45
  220.0 11.8 %collective-permute-done.23.refs_7_ = bf16[128,2048]{1,0:T(8,128)(2,1)S(1)} collective-permute-done((bf16[128,2048]{1,0:T(8,128)(2,1)S(1)}, bf16[128,2048]{1,0:T(8,128)(2,1)S(1)}, u32[]{:S(2)}, u32[]{:S(2)}) %collective-permute-start.23) | collective-permute-done | bytes 524320 | tf_op jit(solution)/shard_map/ppermute | solution.py:37
  235.1 10.6 %all-gather.5.cloned.1.call-done.refs_16_.refs_17_.w_ref = bf16[2048,2048]{1,0:T(8,128)(2,1)} async-done(((bf16[512,2048]{1,0:T(8,128)(2,1)}), bf16[2048,2048]{1,0:T(8,128)(2,1)}) %all-gather.5.cloned.1.call-update) | async-done | bytes 8388624 | tf_op jit(solution)/shard_map/all_gather | solution.py:827
  245.7 27.7 %feed_both.1 = (bf16[2048,1024]{1,0:T(8,128)(2,1)}, bf16[2048,1024]{1,0:T(8,128)(2,1)}, f32[1,1024]{1,0:T(1,128)}) custom-call(bf16[256,2048]{1,0:T(8,128)(2,1)} %copy-done.12, bf16[256,2048]{1,0:T(8,128)(2,1)} %copy-done.26, bf16[256,2048]{1,0:T(8,128)(2,1)} %copy-done.16, bf16[256,2048]{1,0:T(8,128)(2,1)} %copy-done.14, bf16[256,2048]{1,0:T(8,128)(2,1)} %copy-done.28, ...), custom_call_target="tpu_custom_call" | custom-call | flops 17179869184 | bytes 33554432 | tf_op jit(solution)/shard_map/feed_both/pallas_call | solution.py:661
  273.5 8.9 %act_two_sent.1 = bf16[1024,2048]{1,0:T(8,128)(2,1)} custom-call(bf16[2048,1024]{1,0:T(8,128)(2,1)} %get-tuple-element.286.low_ref.high_ref.refs_10_, bf16[2048,1024]{1,0:T(8,128)(2,1)} %get-tuple-element.286.low_ref.high_ref.refs_10_, bf16[2048,2048]{1,0:T(8,128)(2,1)} %all-gather.5.cloned.1.call-done.refs_16_.refs_17_.w_ref), custom_call_target="tpu_custom_call" | custom-call | flops 4294967296 | bytes 10485760 | tf_op jit(solution)/shard_map/act_two_sent/pallas_call | solution.py:357
  282.5 2.2 copy-done.4
  285.9 10.9 %down_weight_term.1 = bf16[2048,1024]{1,0:T(8,128)(2,1)S(1)} custom-call(bf16[512,2048]{1,0:T(8,128)(2,1)} %pad_maximum_fusion.1.refs_10_.refs_0_, bf16[512,2048]{1,0:T(8,128)(2,1)} %collective-permute-done.10.refs_11_.refs_1_, bf16[256,2048]{1,0:T(8,128)(2,1)S(1)} %copy-done.23, bf16[256,2048]{1,0:T(8,128)(2,1)} %collective-permute-done.9.refs_13_.refs_3_, ...), custom_call_target="tpu_custom_call" | custom-call | flops 8589934592 | bytes 16777216 | tf_op jit(solution)/shard_map/down_weight_term/pallas_call | solution.py:308
  296.8 2.0 copy-done.8
  299.0 9.7 %act_two_kept.1 = (f32[256,2048]{1,0:T(8,128)}, bf16[128,2048]{1,0:T(8,128)(2,1)}, bf16[256,2048]{1,0:T(8,128)(2,1)}, bf16[256,2048]{1,0:T(8,128)(2,1)}, bf16[128,2048]{1,0:T(8,128)(2,1)}) custom-call(bf16[2048,1024]{1,0:T(8,128)(2,1)} %get-tuple-element.286.low_ref.high_ref.refs_10_, bf16[2048,1024]{1,0:T(8,128)(2,1)} %get-tuple-element.286.low_ref.high_ref.refs_10_, ...), custom_call_target="tpu_custom_call" | custom-call | flops 4294967296 | bytes 10485760 | tf_op jit(solution)/shard_map/act_two_kept/pallas_call | solution.py:357
  311.7 2.3 copy-done.5
  322.2 13.0 %up_weight_term.1 = bf16[2048,1024]{1,0:T(8,128)(2,1)S(1)} custom-call(bf16[256,2048]{1,0:T(8,128)(2,1)S(1)} %copy-done.13, bf16[256,2048]{1,0:T(8,128)(2,1)S(1)} %copy-done.27, bf16[256,2048]{1,0:T(8,128)(2,1)S(1)} %copy-done.17, bf16[256,2048]{1,0:T(8,128)(2,1)S(1)} %copy-done.15, bf16[256,2048]{1,0:T(8,128)(2,1)S(1)} %copy-done.29, ...), custom_call_target="tpu_custom_call" | custom-call | flops 8589934592 | bytes 16777216 | tf_op jit(solution)/shard_map/up_weight_term/pallas_call | solution.py:308
  342.0 8.4 %feed_sent.1 = bf16[1024,2048]{1,0:T(8,128)(2,1)} custom-call(bf16[2048,1024]{1,0:T(8,128)(2,1)} %get-tuple-element.301.refs_6_.low_ref.high_ref, bf16[2048,1024]{1,0:T(8,128)(2,1)} %get-tuple-element.301.refs_6_.low_ref.high_ref, bf16[2048,2048]{1,0:T(8,128)(2,1)} %all-gather.5.cloned.1.call-done.refs_16_.refs_17_.w_ref), custom_call_target="tpu_custom_call" | custom-call | flops 4294967296 | bytes 10485760 | tf_op jit(solution)/shard_map/feed_sent/pallas_call | solution.py:357
  350.4 2.3 collective-permute-done.32
  352.7 2.4 collective-permute-done.31
  358.0 2.9 multiply_reduce_fusion.1
  360.9 3.7 convert_reduce_fusion.3
  367.3 22.9 %collective-permute-done.34.refs_3_ = bf16[256,2048]{1,0:T(8,128)(2,1)} collective-permute-done((bf16[256,2048]{1,0:T(8,128)(2,1)S(1)}, bf16[256,2048]{1,0:T(8,128)(2,1)}, u32[]{:S(2)}, u32[]{:S(2)}) %collective-permute-start.34) | collective-permute-done | bytes 1048608 | tf_op jit(solution)/shard_map/ppermute | solution.py:45
  396.1 8.8 %feed_kept.1 = (f32[256,2048]{1,0:T(8,128)}, bf16[128,2048]{1,0:T(8,128)(2,1)}, bf16[256,2048]{1,0:T(8,128)(2,1)}, bf16[256,2048]{1,0:T(8,128)(2,1)}, bf16[128,2048]{1,0:T(8,128)(2,1)}) custom-call(bf16[2048,1024]{1,0:T(8,128)(2,1)} %get-tuple-element.301.refs_6_.low_ref.high_ref, bf16[2048,1024]{1,0:T(8,128)(2,1)} %get-tuple-element.301.refs_6_.low_ref.high_ref, ...), custom_call_target="tpu_custom_call" | custom-call | flops 4294967296 | bytes 10485760 | tf_op jit(solution)/shard_map/feed_kept/pallas_call | solution.py:357
  404.9 4.4 collective-permute-done.38.refs_7_
  415.8 12.0 %middle_terms.1 = (bf16[2048,256]{1,0:T(8,128)(2,1)}, bf16[2048,256]{1,0:T(8,128)(2,1)}) custom-call(bf16[256,2048]{1,0:T(8,128)(2,1)} %copy-done.56, bf16[256,2048]{1,0:T(8,128)(2,1)} %copy-done.70, bf16[256,2048]{1,0:T(8,128)(2,1)} %collective-permute-done.33.refs_2_, bf16[256,2048]{1,0:T(8,128)(2,1)} %collective-permute-done.34.refs_3_, ...), custom_call_target="tpu_custom_call" | custom-call | flops 4294967296 | bytes 12582912 | tf_op jit(solution)/shard_map/middle_terms/pallas_call | solution.py:486
  427.8 10.0 %collective-permute-done.43 = bf16[256,2048]{1,0:T(8,128)(2,1)} collective-permute-done((bf16[256,2048]{1,0:T(8,128)(2,1)}, bf16[256,2048]{1,0:T(8,128)(2,1)}, u32[]{:S(2)}, u32[]{:S(2)}) %collective-permute-start.43) | collective-permute-done | bytes 1048608 | tf_op jit(solution)/shard_map/ppermute | solution.py:37
  437.8 2.3 collective-permute-done.44
  440.1 2.1 add_convert_fusion.6
  442.7 2.1 add_convert_fusion.7
  446.7 21.4 %attention_backward.1 = bf16[8,256,768]{2,1,0:T(8,128)(2,1)S(1)} custom-call(s32[10]{0:T(128)S(1)} %concatenate.47.info_ref, bf16[8,256,768]{2,1,0:T(8,128)(2,1)S(1)} %bitcast.94, bf16[8,256,256]{2,1,0:T(8,128)(2,1)S(1)} %bitcast.95), custom_call_target="tpu_custom_call" | custom-call | flops 7046430720 | bytes 7340032 | tf_op jit(solution)/shard_map/attention_backward/pallas_call | solution.py:240
  473.5 7.2 %act_one_sent.1 = bf16[1024,2048]{1,0:T(8,128)(2,1)} custom-call(bf16[2048,768]{1,0:T(8,128)(2,1)} %bitcast.82, bf16[2048,768]{1,0:T(8,128)(2,1)} %bitcast.83, bf16[2048,1024]{1,0:T(8,128)(2,1)} %all-gather.3.cloned.1.call-done.refs_4_.w_ref.refs_11_), custom_call_target="tpu_custom_call" | custom-call | flops 3221225472 | bytes 8912896 | tf_op jit(solution)/shard_map/act_one_sent/pallas_call | solution.py:357
  480.8 4.5 add_convert_fusion.2
  493.3 9.1 %attention_weight_term.1 = bf16[2048,768]{1,0:T(8,128)(2,1)S(1)} custom-call(bf16[512,2048]{1,0:T(8,128)(2,1)S(1)} %copy-done.11, bf16[512,2048]{1,0:T(8,128)(2,1)S(1)} %copy-done.19, bf16[512,2048]{1,0:T(8,128)(2,1)S(1)} %copy-done.21, bf16[512,2048]{1,0:T(8,128)(2,1)} %collective-permute-done.12.refs_3_, bf16[2048,768]{1,0:T(8,128)(2,1)S(1)} %bitcast.87), custom_call_target="tpu_custom_call" | custom-call | flops 6442450944 | bytes 14680064 | tf_op jit(solution)/shard_map/attention_weight_term/pallas_call | solution.py:308
  505.3 6.0 collective-permute-done.50.refs_2_
  513.4 8.1 %act_one_kept.1 = (f32[256,2048]{1,0:T(8,128)}, bf16[128,2048]{1,0:T(8,128)(2,1)}, bf16[256,2048]{1,0:T(8,128)(2,1)}, bf16[256,2048]{1,0:T(8,128)(2,1)}, bf16[128,2048]{1,0:T(8,128)(2,1)}) custom-call(bf16[2048,768]{1,0:T(8,128)(2,1)} %bitcast.84, bf16[2048,768]{1,0:T(8,128)(2,1)} %bitcast.85, ...), custom_call_target="tpu_custom_call" | custom-call | flops 3221225472 | bytes 8912896 | tf_op jit(solution)/shard_map/act_one_kept/pallas_call | solution.py:357
  524.6 2.5 convert_reduce_fusion
  527.1 6.4 %down_weight_grad.1 = f32[4096,512]{1,0:T(8,128)} custom-call(s32[1]{0:T(128)} %bitcast.ctx_ref, bf16[512,1024]{1,0:T(8,128)(2,1)} %reduce-scatter.5.cloned.1.call-done.refs_0_, bf16[512,1024]{1,0:T(8,128)(2,1)} %collective-permute-done.52.refs_1_, bf16[512,1024]{1,0:T(8,128)(2,1)} %collective-permute-done.47.refs_2_, ...), custom_call_target="tpu_custom_call" | custom-call | bytes 12582912 | tf_op jit(solution)/shard_map/down_weight_grad/pallas_call | solution.py:569
  533.5 13.3 %collective-permute-done.56 = bf16[256,2048]{1,0:T(8,128)(2,1)S(1)} collective-permute-done((bf16[256,2048]{1,0:T(8,128)(2,1)}, bf16[256,2048]{1,0:T(8,128)(2,1)S(1)}, u32[]{:S(2)}, u32[]{:S(2)}) %collective-permute-start.56) | collective-permute-done | bytes 1048608 | tf_op jit(solution)/shard_map/ppermute | solution.py:37
  548.1 2.0 add_convert_fusion.4
  551.7 2.0 add_convert_fusion.5
  554.8 5.8 up_weight_grad.1
  563.1 3.4 collective-permute-done.59
  566.4 3.8 multiply_reduce_fusion.2
  570.4 2.9 add_convert_fusion.1
  578.0 3.0 broadcast_select_fusion.1
  581.0 3.2 output_weight_grad.1
  584.2 14.8 %collective-permute-done.64 = f32[4,6144]{1,0:T(4,128)S(1)} collective-permute-done((f32[4,6144]{1,0:T(4,128)S(1)}, f32[4,6144]{1,0:T(4,128)S(1)}, u32[]{:S(2)}, u32[]{:S(2)}) %collective-permute-start.64) | collective-permute-done | bytes 98336 | tf_op jit(solution)/shard_map/ppermute | solution.py:37
  600.7 3.7 collective-permute-done.67
  605.7 2.6 collective-permute-start.71
  609.2 2.7 broadcast_select_fusion
  611.9 4.8 attention_weight_grads.1
  (377 shorter events, 117.4 us)
Async XLA Ops:
  7.2 94.3 %all-gather.3.cloned.1.call-start = ((), (), s32[]{:S(2)}) async-start(), calls=%async_computation.4 | async-start | bytes 5242880 | tf_op jit(solution)/shard_map/all_gather | solution.py:774
  9.7 236.0 %all-gather.5.cloned.1.call-start = ((), (), s32[]{:S(2)}) async-start(), calls=%async_computation.5 | async-start | bytes 10485760 | tf_op jit(solution)/shard_map/all_gather | solution.py:827
  13.6 17.2 %collective-permute-start.5 = (bf16[3456]{0:T(1024)(128)(2,1)S(1)}, bf16[3456]{0:T(1024)(128)(2,1)S(1)}, u32[]{:S(2)}, u32[]{:S(2)}) collective-permute-start(bf16[3456]{0:T(1024)(128)(2,1)S(1)} %concatenate.48), channel_id=1, source_target_pairs={{0,24},{8,0},{16,8},{24,16},{1,25},{9,1},{17,9},{25,17},{2,26},{10... | collective-permute-start | bytes 20744 | tf_op jit(solution)/shard_map/ppermute | solution.py:702
  18.6 12.0 %collective-permute-start.4 = (bf16[3456]{0:T(1024)(128)(2,1)S(1)}, bf16[3456]{0:T(1024)(128)(2,1)S(1)}, u32[]{:S(2)}, u32[]{:S(2)}) collective-permute-start(bf16[3456]{0:T(1024)(128)(2,1)S(1)} %concatenate.48), channel_id=1, source_target_pairs={{0,16},{8,24},{16,0},{24,8},{1,17},{9,25},{17,1},{25,9},{2,18},{10... | collective-permute-start | bytes 20744 | tf_op jit(solution)/shard_map/ppermute | solution.py:702
  18.6 11.8 %collective-permute-start.3 = (bf16[3456]{0:T(1024)(128)(2,1)S(1)}, bf16[3456]{0:T(1024)(128)(2,1)S(1)}, u32[]{:S(2)}, u32[]{:S(2)}) collective-permute-start(bf16[3456]{0:T(1024)(128)(2,1)S(1)} %concatenate.48), channel_id=1, source_target_pairs={{0,8},{8,16},{16,24},{24,0},{1,9},{9,17},{17,25},{25,1},{2,10},{10... | collective-permute-start | bytes 20744 | tf_op jit(solution)/shard_map/ppermute | solution.py:702
  22.4 24.3 %collective-permute-start.6 = (bf16[256,2048]{1,0:T(8,128)(2,1)}, bf16[256,2048]{1,0:T(8,128)(2,1)S(1)}, u32[]{:S(2)}, u32[]{:S(2)}) collective-permute-start(bf16[256,2048]{1,0:T(8,128)(2,1)} %get-tuple-element.412), channel_id=1, source_target_pairs={{0,4},{4,0},{2,6},{6,2},{1,5},{5,1},{3,7},{7,3},{8,12},{12,8},{10,... | collective-permute-start | bytes 3145736 | tf_op jit(solution)/shard_map/ppermute | solution.py:45
  27.0 22.9 %collective-permute-start.10 = (bf16[512,2048]{1,0:T(8,128)(2,1)}, bf16[512,2048]{1,0:T(8,128)(2,1)}, u32[]{:S(2)}, u32[]{:S(2)}) collective-permute-start(bf16[512,2048]{1,0:T(8,128)(2,1)} %pad_maximum_fusion.1.refs_10_.refs_0_), channel_id=1, source_target_pairs={{0,2},{2,0},{4,6},{6,4},{1,3},{3,1},{5,7},{7,5},{8,10},{10,8},{12,... | collective-permute-start | bytes 6291464 | tf_op jit(solution)/shard_map/ppermute | solution.py:41
  46.7 27.2 %collective-permute-start.8 = (bf16[512,2048]{1,0:T(8,128)(2,1)S(1)}, bf16[512,2048]{1,0:T(8,128)(2,1)S(1)}, u32[]{:S(2)}, u32[]{:S(2)}) collective-permute-start(bf16[512,2048]{1,0:T(8,128)(2,1)S(1)} %get-tuple-element.235.refs_0_), channel_id=1, source_target_pairs={{0,2},{2,0},{4,6},{6,4},{1,3},{3,1},{5,7},{7,5},{8,10},{10,8},{12,... | collective-permute-start | bytes 6291464 | tf_op jit(solution)/shard_map/ppermute | solution.py:41
  46.7 48.0 %collective-permute-start.7 = (bf16[512,2048]{1,0:T(8,128)(2,1)S(1)}, bf16[512,2048]{1,0:T(8,128)(2,1)S(1)}, u32[]{:S(2)}, u32[]{:S(2)}) collective-permute-start(bf16[512,2048]{1,0:T(8,128)(2,1)S(1)} %get-tuple-element.235.refs_0_), channel_id=1, source_target_pairs={{0,4},{4,0},{2,6},{6,2},{1,5},{5,1},{3,7},{7,3},{8,12},{12,8},{10,... | collective-permute-start | bytes 6291464 | tf_op jit(solution)/shard_map/ppermute | solution.py:45
  48.4 25.5 %collective-permute-start.9 = (bf16[256,2048]{1,0:T(8,128)(2,1)S(1)}, bf16[256,2048]{1,0:T(8,128)(2,1)}, u32[]{:S(2)}, u32[]{:S(2)}) collective-permute-start(bf16[256,2048]{1,0:T(8,128)(2,1)S(1)} %collective-permute-done.6.refs_12_.refs_2_), channel_id=1, source_target_pairs={{0,1},{1,0},{2,3},{3,2},{4,5},{5,4},{6,7},{7,6},{8,9},{9,8},{10,11... | collective-permute-start | bytes 3145736 | tf_op jit(solution)/shard_map/ppermute | solution.py:37
  94.7 6.7 %collective-permute-start.12 = (bf16[512,2048]{1,0:T(8,128)(2,1)S(1)}, bf16[512,2048]{1,0:T(8,128)(2,1)}, u32[]{:S(2)}, u32[]{:S(2)}) collective-permute-start(bf16[512,2048]{1,0:T(8,128)(2,1)S(1)} %collective-permute-done.7.refs_2_), channel_id=1, source_target_pairs={{0,2},{2,0},{4,6},{6,4},{1,3},{3,1},{5,7},{7,5},{8,10},{10,8},{12,... | collective-permute-start | bytes 6291464 | tf_op jit(solution)/shard_map/ppermute | solution.py:41
  95.3 296.2 %reduce-scatter.5.cloned.1.call-start = ((), (), s32[]{:S(2)}) async-start(), calls=%async_computation.6 | async-start | bytes 5242880 | tf_op jit(solution)/shard_map/reduce_scatter | solution.py:924
  132.8 7.5 %collective-permute-start.14 = (bf16[1024,2048]{1,0:T(8,128)(2,1)}, bf16[1024,2048]{1,0:T(8,128)(2,1)}, u32[]{:S(2)}, u32[]{:S(2)}) collective-permute-start(bf16[1024,2048]{1,0:T(8,128)(2,1)} %attention_sent.1), channel_id=1, source_target_pairs={{0,2},{2,0},{4,6},{6,4},{1,3},{3,1},{5,7},{7,5},{8,10},{10,8},{12,... | collective-permute-start | bytes 12582920 | tf_op jit(solution)/shard_map/ppermute | solution.py:41
  146.4 25.5 %collective-permute-start.15 = (bf16[256,2048]{1,0:T(8,128)(2,1)}, bf16[256,2048]{1,0:T(8,128)(2,1)S(1)}, u32[]{:S(2)}, u32[]{:S(2)}) collective-permute-start(bf16[256,2048]{1,0:T(8,128)(2,1)} %get-tuple-element.242), channel_id=1, source_target_pairs={{0,1},{1,0},{2,3},{3,2},{4,5},{5,4},{6,7},{7,6},{8,9},{9,8},{10,11... | collective-permute-start | bytes 3145736 | tf_op jit(solution)/shard_map/ppermute | solution.py:37
  147.8 25.2 %collective-permute-start.16 = (bf16[256,2048]{1,0:T(8,128)(2,1)}, bf16[256,2048]{1,0:T(8,128)(2,1)S(1)}, u32[]{:S(2)}, u32[]{:S(2)}) collective-permute-start(bf16[256,2048]{1,0:T(8,128)(2,1)} %get-tuple-element.243), channel_id=1, source_target_pairs={{0,4},{4,0},{2,6},{6,2},{1,5},{5,1},{3,7},{7,3},{8,12},{12,8},{10,... | collective-permute-start | bytes 3145736 | tf_op jit(solution)/shard_map/ppermute | solution.py:45
  174.2 13.1 %collective-permute-start.18 = (bf16[128,2048]{1,0:T(8,128)(2,1)S(1)}, bf16[128,2048]{1,0:T(8,128)(2,1)S(1)}, u32[]{:S(2)}, u32[]{:S(2)}) collective-permute-start(bf16[128,2048]{1,0:T(8,128)(2,1)S(1)} %add_convert_fusion.10), channel_id=1, source_target_pairs={{0,4},{4,0},{2,6},{6,2},{1,5},{5,1},{3,7},{7,3},{8,12},{12,8},{10,... | collective-permute-start | bytes 1572872 | tf_op jit(solution)/shard_map/ppermute | solution.py:45
  176.9 12.8 %collective-permute-start.17 = (bf16[128,2048]{1,0:T(8,128)(2,1)S(1)}, bf16[128,2048]{1,0:T(8,128)(2,1)S(1)}, u32[]{:S(2)}, u32[]{:S(2)}) collective-permute-start(bf16[128,2048]{1,0:T(8,128)(2,1)S(1)} %add_convert_fusion.11), channel_id=1, source_target_pairs={{0,1},{1,0},{2,3},{3,2},{4,5},{5,4},{6,7},{7,6},{8,9},{9,8},{10,11... | collective-permute-start | bytes 1572872 | tf_op jit(solution)/shard_map/ppermute | solution.py:37
  191.3 25.6 %collective-permute-start.20 = (bf16[256,2048]{1,0:T(8,128)(2,1)S(1)}, bf16[256,2048]{1,0:T(8,128)(2,1)S(1)}, u32[]{:S(2)}, u32[]{:S(2)}) collective-permute-start(bf16[256,2048]{1,0:T(8,128)(2,1)S(1)} %add_convert_fusion.3.refs_0_), channel_id=1, source_target_pairs={{0,4},{4,0},{2,6},{6,2},{1,5},{5,1},{3,7},{7,3},{8,12},{12,8},{10,... | collective-permute-start | bytes 3145736 | tf_op jit(solution)/shard_map/ppermute | solution.py:45
  191.9 25.2 %collective-permute-start.19 = (bf16[256,2048]{1,0:T(8,128)(2,1)S(1)}, bf16[256,2048]{1,0:T(8,128)(2,1)S(1)}, u32[]{:S(2)}, u32[]{:S(2)}) collective-permute-start(bf16[256,2048]{1,0:T(8,128)(2,1)S(1)} %add_convert_fusion.3.refs_0_), channel_id=1, source_target_pairs={{0,1},{1,0},{2,3},{3,2},{4,5},{5,4},{6,7},{7,6},{8,9},{9,8},{10,11... | collective-permute-start | bytes 3145736 | tf_op jit(solution)/shard_map/ppermute | solution.py:37
  217.1 14.9 %collective-permute-start.24 = (bf16[256,2048]{1,0:T(8,128)(2,1)S(1)}, bf16[256,2048]{1,0:T(8,128)(2,1)S(1)}, u32[]{:S(2)}, u32[]{:S(2)}) collective-permute-start(bf16[256,2048]{1,0:T(8,128)(2,1)S(1)} %collective-permute-done.19.refs_2_), channel_id=1, source_target_pairs={{0,2},{2,0},{4,6},{6,4},{1,3},{3,1},{5,7},{7,5},{8,10},{10,8},{12,... | collective-permute-start | bytes 3145736 | tf_op jit(solution)/shard_map/ppermute | solution.py:41
  217.1 14.9 %collective-permute-start.25 = (bf16[256,2048]{1,0:T(8,128)(2,1)S(1)}, bf16[256,2048]{1,0:T(8,128)(2,1)S(1)}, u32[]{:S(2)}, u32[]{:S(2)}) collective-permute-start(bf16[256,2048]{1,0:T(8,128)(2,1)S(1)} %collective-permute-done.20.refs_3_), channel_id=1, source_target_pairs={{0,2},{2,0},{4,6},{6,4},{1,3},{3,1},{5,7},{7,5},{8,10},{10,8},{12,... | collective-permute-start | bytes 3145736 | tf_op jit(solution)/shard_map/ppermute | solution.py:41
  218.0 13.7 %collective-permute-start.23 = (bf16[128,2048]{1,0:T(8,128)(2,1)S(1)}, bf16[128,2048]{1,0:T(8,128)(2,1)S(1)}, u32[]{:S(2)}, u32[]{:S(2)}) collective-permute-start(bf16[128,2048]{1,0:T(8,128)(2,1)S(1)} %slice.184), channel_id=1, source_target_pairs={{0,1},{1,0},{2,3},{3,2},{4,5},{5,4},{6,7},{7,6},{8,9},{9,8},{10,11... | collective-permute-start | bytes 1572872 | tf_op jit(solution)/shard_map/ppermute | solution.py:37
  218.6 13.4 %collective-permute-start.22 = (bf16[128,2048]{1,0:T(8,128)(2,1)S(1)}, bf16[128,2048]{1,0:T(8,128)(2,1)S(1)}, u32[]{:S(2)}, u32[]{:S(2)}) collective-permute-start(bf16[128,2048]{1,0:T(8,128)(2,1)S(1)} %slice.183), channel_id=1, source_target_pairs={{0,4},{4,0},{2,6},{6,2},{1,5},{5,1},{3,7},{7,3},{8,12},{12,8},{10,... | collective-permute-start | bytes 1572872 | tf_op jit(solution)/shard_map/ppermute | solution.py:45
  282.4 16.5 %collective-permute-start.28 = (bf16[1024,2048]{1,0:T(8,128)(2,1)}, bf16[1024,2048]{1,0:T(8,128)(2,1)}, u32[]{:S(2)}, u32[]{:S(2)}) collective-permute-start(bf16[1024,2048]{1,0:T(8,128)(2,1)} %act_two_sent.1), channel_id=1, source_target_pairs={{0,2},{2,0},{4,6},{6,4},{1,3},{3,1},{5,7},{7,5},{8,10},{10,8},{12,... | collective-permute-start | bytes 12582920 | tf_op jit(solution)/shard_map/ppermute | solution.py:41
  298.9 174.6 %reduce-scatter.7.cloned.1.call-start = ((), (), s32[]{:S(2)}) async-start(), calls=%async_computation.7 | async-start | bytes 5242880 | tf_op jit(solution)/shard_map/reduce_scatter | solution.py:933
  308.6 28.6 %collective-permute-start.29 = (bf16[256,2048]{1,0:T(8,128)(2,1)}, bf16[256,2048]{1,0:T(8,128)(2,1)}, u32[]{:S(2)}, u32[]{:S(2)}) collective-permute-start(bf16[256,2048]{1,0:T(8,128)(2,1)} %get-tuple-element.284), channel_id=1, source_target_pairs={{0,1},{1,0},{2,3},{3,2},{4,5},{5,4},{6,7},{7,6},{8,9},{9,8},{10,11... | collective-permute-start | bytes 3145736 | tf_op jit(solution)/shard_map/ppermute | solution.py:37
  310.2 27.0 %collective-permute-start.30 = (bf16[256,2048]{1,0:T(8,128)(2,1)}, bf16[256,2048]{1,0:T(8,128)(2,1)S(1)}, u32[]{:S(2)}, u32[]{:S(2)}) collective-permute-start(bf16[256,2048]{1,0:T(8,128)(2,1)} %get-tuple-element.285), channel_id=1, source_target_pairs={{0,4},{4,0},{2,6},{6,2},{1,5},{5,1},{3,7},{7,3},{8,12},{12,8},{10,... | collective-permute-start | bytes 3145736 | tf_op jit(solution)/shard_map/ppermute | solution.py:45
  339.0 13.8 %collective-permute-start.32 = (bf16[128,2048]{1,0:T(8,128)(2,1)S(1)}, bf16[128,2048]{1,0:T(8,128)(2,1)S(1)}, u32[]{:S(2)}, u32[]{:S(2)}) collective-permute-start(bf16[128,2048]{1,0:T(8,128)(2,1)S(1)} %add_convert_fusion.8), channel_id=1, source_target_pairs={{0,4},{4,0},{2,6},{6,2},{1,5},{5,1},{3,7},{7,3},{8,12},{12,8},{10,... | collective-permute-start | bytes 1572872 | tf_op jit(solution)/shard_map/ppermute | solution.py:45
  341.5 13.6 %collective-permute-start.31 = (bf16[128,2048]{1,0:T(8,128)(2,1)}, bf16[128,2048]{1,0:T(8,128)(2,1)S(1)}, u32[]{:S(2)}, u32[]{:S(2)}) collective-permute-start(bf16[128,2048]{1,0:T(8,128)(2,1)} %add_convert_fusion.9), channel_id=1, source_target_pairs={{0,1},{1,0},{2,3},{3,2},{4,5},{5,4},{6,7},{7,6},{8,9},{9,8},{10,11... | collective-permute-start | bytes 1572872 | tf_op jit(solution)/shard_map/ppermute | solution.py:37
  355.9 35.6 %collective-permute-start.36 = (bf16[1024,2048]{1,0:T(8,128)(2,1)}, bf16[1024,2048]{1,0:T(8,128)(2,1)}, u32[]{:S(2)}, u32[]{:S(2)}) collective-permute-start(bf16[1024,2048]{1,0:T(8,128)(2,1)} %feed_sent.1), channel_id=1, source_target_pairs={{0,2},{2,0},{4,6},{6,4},{1,3},{3,1},{5,7},{7,5},{8,10},{10,8},{12,... | collective-permute-start | bytes 12582920 | tf_op jit(solution)/shard_map/ppermute | solution.py:41
  356.0 156.6 %reduce-scatter.9.cloned.1.call-start = ((), (), s32[]{:S(2)}) async-start(), calls=%async_computation.8 | async-start | bytes 1310720 | tf_op jit(solution)/shard_map/reduce_scatter | solution.py:957
  365.0 25.2 %collective-permute-start.34 = (bf16[256,2048]{1,0:T(8,128)(2,1)S(1)}, bf16[256,2048]{1,0:T(8,128)(2,1)}, u32[]{:S(2)}, u32[]{:S(2)}) collective-permute-start(bf16[256,2048]{1,0:T(8,128)(2,1)S(1)} %get-tuple-element.331.refs_0_), channel_id=1, source_target_pairs={{0,4},{4,0},{2,6},{6,2},{1,5},{5,1},{3,7},{7,3},{8,12},{12,8},{10,... | collective-permute-start | bytes 3145736 | tf_op jit(solution)/shard_map/ppermute | solution.py:45
  366.6 24.9 %collective-permute-start.33 = (bf16[256,2048]{1,0:T(8,128)(2,1)S(1)}, bf16[256,2048]{1,0:T(8,128)(2,1)}, u32[]{:S(2)}, u32[]{:S(2)}) collective-permute-start(bf16[256,2048]{1,0:T(8,128)(2,1)S(1)} %get-tuple-element.331.refs_0_), channel_id=1, source_target_pairs={{0,1},{1,0},{2,3},{3,2},{4,5},{5,4},{6,7},{7,6},{8,9},{9,8},{10,11... | collective-permute-start | bytes 3145736 | tf_op jit(solution)/shard_map/ppermute | solution.py:37
  391.5 17.8 %collective-permute-start.39 = (bf16[256,2048]{1,0:T(8,128)(2,1)}, bf16[256,2048]{1,0:T(8,128)(2,1)}, u32[]{:S(2)}, u32[]{:S(2)}) collective-permute-start(bf16[256,2048]{1,0:T(8,128)(2,1)} %collective-permute-done.33.refs_2_), channel_id=1, source_target_pairs={{0,2},{2,0},{4,6},{6,4},{1,3},{3,1},{5,7},{7,5},{8,10},{10,8},{12,... | collective-permute-start | bytes 3145736 | tf_op jit(solution)/shard_map/ppermute | solution.py:41
  391.6 17.7 %collective-permute-start.40 = (bf16[256,2048]{1,0:T(8,128)(2,1)}, bf16[256,2048]{1,0:T(8,128)(2,1)}, u32[]{:S(2)}, u32[]{:S(2)}) collective-permute-start(bf16[256,2048]{1,0:T(8,128)(2,1)} %collective-permute-done.34.refs_3_), channel_id=1, source_target_pairs={{0,2},{2,0},{4,6},{6,4},{1,3},{3,1},{5,7},{7,5},{8,10},{10,8},{12,... | collective-permute-start | bytes 3145736 | tf_op jit(solution)/shard_map/ppermute | solution.py:41
  395.1 14.2 %collective-permute-start.38 = (bf16[128,2048]{1,0:T(8,128)(2,1)}, bf16[128,2048]{1,0:T(8,128)(2,1)}, u32[]{:S(2)}, u32[]{:S(2)}) collective-permute-start(bf16[128,2048]{1,0:T(8,128)(2,1)} %slice.192), channel_id=1, source_target_pairs={{0,1},{1,0},{2,3},{3,2},{4,5},{5,4},{6,7},{7,6},{8,9},{9,8},{10,11... | collective-permute-start | bytes 1572872 | tf_op jit(solution)/shard_map/ppermute | solution.py:37
  395.6 13.7 %collective-permute-start.37 = (bf16[128,2048]{1,0:T(8,128)(2,1)S(1)}, bf16[128,2048]{1,0:T(8,128)(2,1)}, u32[]{:S(2)}, u32[]{:S(2)}) collective-permute-start(bf16[128,2048]{1,0:T(8,128)(2,1)S(1)} %slice.191), channel_id=1, source_target_pairs={{0,4},{4,0},{2,6},{6,2},{1,5},{5,1},{3,7},{7,3},{8,12},{12,8},{10,... | collective-permute-start | bytes 1572872 | tf_op jit(solution)/shard_map/ppermute | solution.py:45
  412.3 25.5 %collective-permute-start.43 = (bf16[256,2048]{1,0:T(8,128)(2,1)}, bf16[256,2048]{1,0:T(8,128)(2,1)}, u32[]{:S(2)}, u32[]{:S(2)}) collective-permute-start(bf16[256,2048]{1,0:T(8,128)(2,1)} %get-tuple-element.329), channel_id=1, source_target_pairs={{0,1},{1,0},{2,3},{3,2},{4,5},{5,4},{6,7},{7,6},{8,9},{9,8},{10,11... | collective-permute-start | bytes 3145736 | tf_op jit(solution)/shard_map/ppermute | solution.py:37
  413.7 26.4 %collective-permute-start.44 = (bf16[256,2048]{1,0:T(8,128)(2,1)}, bf16[256,2048]{1,0:T(8,128)(2,1)}, u32[]{:S(2)}, u32[]{:S(2)}) collective-permute-start(bf16[256,2048]{1,0:T(8,128)(2,1)} %get-tuple-element.330), channel_id=1, source_target_pairs={{0,4},{4,0},{2,6},{6,2},{1,5},{5,1},{3,7},{7,3},{8,12},{12,8},{10,... | collective-permute-start | bytes 3145736 | tf_op jit(solution)/shard_map/ppermute | solution.py:45
  414.2 71.0 %collective-permute-start.47 = (bf16[512,1024]{1,0:T(8,128)(2,1)}, bf16[512,1024]{1,0:T(8,128)(2,1)}, u32[]{:S(2)}, u32[]{:S(2)}) collective-permute-start(bf16[512,1024]{1,0:T(8,128)(2,1)} %reduce-scatter.5.cloned.1.call-done.refs_0_), channel_id=1, source_target_pairs={{0,4},{4,0},{2,6},{6,2},{1,5},{5,1},{3,7},{7,3},{8,12},{12,8},{10,... | collective-permute-start | bytes 3145736 | tf_op jit(solution)/shard_map/ppermute | solution.py:45
  442.2 31.3 %collective-permute-start.46 = (bf16[128,2048]{1,0:T(8,128)(2,1)}, bf16[128,2048]{1,0:T(8,128)(2,1)}, u32[]{:S(2)}, u32[]{:S(2)}) collective-permute-start(bf16[128,2048]{1,0:T(8,128)(2,1)} %add_convert_fusion.6), channel_id=1, source_target_pairs={{0,4},{4,0},{2,6},{6,2},{1,5},{5,1},{3,7},{7,3},{8,12},{12,8},{10,... | collective-permute-start | bytes 1572872 | tf_op jit(solution)/shard_map/ppermute | solution.py:45
  444.8 28.7 %collective-permute-start.45 = (bf16[128,2048]{1,0:T(8,128)(2,1)}, bf16[128,2048]{1,0:T(8,128)(2,1)}, u32[]{:S(2)}, u32[]{:S(2)}) collective-permute-start(bf16[128,2048]{1,0:T(8,128)(2,1)} %add_convert_fusion.7), channel_id=1, source_target_pairs={{0,1},{1,0},{2,3},{3,2},{4,5},{5,4},{6,7},{7,6},{8,9},{9,8},{10,11... | collective-permute-start | bytes 1572872 | tf_op jit(solution)/shard_map/ppermute | solution.py:37
  485.3 27.3 %collective-permute-start.48 = (bf16[1024,2048]{1,0:T(8,128)(2,1)}, bf16[1024,2048]{1,0:T(8,128)(2,1)}, u32[]{:S(2)}, u32[]{:S(2)}) collective-permute-start(bf16[1024,2048]{1,0:T(8,128)(2,1)} %act_one_sent.1), channel_id=1, source_target_pairs={{0,2},{2,0},{4,6},{6,4},{1,3},{3,1},{5,7},{7,5},{8,10},{10,8},{12,... | collective-permute-start | bytes 12582920 | tf_op jit(solution)/shard_map/ppermute | solution.py:41
  485.3 88.0 %reduce-scatter.11.cloned.1.call-start = ((), (), s32[]{:S(2)}) async-start(), calls=%async_computation.9 | async-start | bytes 3932160 | tf_op jit(solution)/shard_map/reduce_scatter | solution.py:968
  485.4 25.9 %collective-permute-start.50 = (bf16[512,1024]{1,0:T(8,128)(2,1)}, bf16[512,1024]{1,0:T(8,128)(2,1)}, u32[]{:S(2)}, u32[]{:S(2)}) collective-permute-start(bf16[512,1024]{1,0:T(8,128)(2,1)} %reduce-scatter.7.cloned.1.call-done.refs_0_), channel_id=1, source_target_pairs={{0,4},{4,0},{2,6},{6,2},{1,5},{5,1},{3,7},{7,3},{8,12},{12,8},{10,... | collective-permute-start | bytes 3145736 | tf_op jit(solution)/shard_map/ppermute | solution.py:45
  487.0 25.6 %collective-permute-start.49 = (bf16[256,2048]{1,0:T(8,128)(2,1)}, bf16[256,2048]{1,0:T(8,128)(2,1)}, u32[]{:S(2)}, u32[]{:S(2)}) collective-permute-start(bf16[256,2048]{1,0:T(8,128)(2,1)} %add_convert_fusion.2), channel_id=1, source_target_pairs={{0,1},{1,0},{2,3},{3,2},{4,5},{5,4},{6,7},{7,6},{8,9},{9,8},{10,11... | collective-permute-start | bytes 3145736 | tf_op jit(solution)/shard_map/ppermute | solution.py:37
  504.1 17.4 %collective-permute-start.52 = (bf16[512,1024]{1,0:T(8,128)(2,1)}, bf16[512,1024]{1,0:T(8,128)(2,1)}, u32[]{:S(2)}, u32[]{:S(2)}) collective-permute-start(bf16[512,1024]{1,0:T(8,128)(2,1)} %reduce-scatter.5.cloned.1.call-done.refs_0_), channel_id=1, source_target_pairs={{0,2},{2,0},{4,6},{6,4},{1,3},{3,1},{5,7},{7,5},{8,10},{10,8},{12,... | collective-permute-start | bytes 3145736 | tf_op jit(solution)/shard_map/ppermute | solution.py:41
  505.3 16.2 %collective-permute-start.54 = (bf16[512,1024]{1,0:T(8,128)(2,1)S(1)}, bf16[512,1024]{1,0:T(8,128)(2,1)}, u32[]{:S(2)}, u32[]{:S(2)}) collective-permute-start(bf16[512,1024]{1,0:T(8,128)(2,1)S(1)} %copy-done.55), channel_id=1, source_target_pairs={{0,2},{2,0},{4,6},{6,4},{1,3},{3,1},{5,7},{7,5},{8,10},{10,8},{12,... | collective-permute-start | bytes 3145736 | tf_op jit(solution)/shard_map/ppermute | solution.py:41
  511.3 10.3 %collective-permute-start.53 = (bf16[512,1024]{1,0:T(8,128)(2,1)}, bf16[512,1024]{1,0:T(8,128)(2,1)}, u32[]{:S(2)}, u32[]{:S(2)}) collective-permute-start(bf16[512,1024]{1,0:T(8,128)(2,1)} %collective-permute-done.47.refs_2_), channel_id=1, source_target_pairs={{0,2},{2,0},{4,6},{6,4},{1,3},{3,1},{5,7},{7,5},{8,10},{10,8},{12,... | collective-permute-start | bytes 3145736 | tf_op jit(solution)/shard_map/ppermute | solution.py:41
  512.6 9.1 %collective-permute-start.51 = (bf16[512,1024]{1,0:T(8,128)(2,1)}, bf16[512,1024]{1,0:T(8,128)(2,1)}, u32[]{:S(2)}, u32[]{:S(2)}) collective-permute-start(bf16[512,1024]{1,0:T(8,128)(2,1)} %collective-permute-done.50.refs_2_), channel_id=1, source_target_pairs={{0,2},{2,0},{4,6},{6,4},{1,3},{3,1},{5,7},{7,5},{8,10},{10,8},{12,... | collective-permute-start | bytes 3145736 | tf_op jit(solution)/shard_map/ppermute | solution.py:41
  512.7 9.0 %collective-permute-start.55 = (bf16[512,256]{1,0:T(8,128)(2,1)}, bf16[512,256]{1,0:T(8,128)(2,1)}, u32[]{:S(2)}, u32[]{:S(2)}) collective-permute-start(bf16[512,256]{1,0:T(8,128)(2,1)} %reduce-scatter.9.cloned.1.call-done.refs_0_), channel_id=1, source_target_pairs={{0,4},{4,0},{2,6},{6,2},{1,5},{5,1},{3,7},{7,3},{8,12},{12,8},{10,... | collective-permute-start | bytes 786440 | tf_op jit(solution)/shard_map/ppermute | solution.py:45
  521.7 25.1 %collective-permute-start.56 = (bf16[256,2048]{1,0:T(8,128)(2,1)}, bf16[256,2048]{1,0:T(8,128)(2,1)S(1)}, u32[]{:S(2)}, u32[]{:S(2)}) collective-permute-start(bf16[256,2048]{1,0:T(8,128)(2,1)} %get-tuple-element.370), channel_id=1, source_target_pairs={{0,1},{1,0},{2,3},{3,2},{4,5},{5,4},{6,7},{7,6},{8,9},{9,8},{10,11... | collective-permute-start | bytes 3145736 | tf_op jit(solution)/shard_map/ppermute | solution.py:37
  523.1 25.0 %collective-permute-start.57 = (bf16[256,2048]{1,0:T(8,128)(2,1)}, bf16[256,2048]{1,0:T(8,128)(2,1)}, u32[]{:S(2)}, u32[]{:S(2)}) collective-permute-start(bf16[256,2048]{1,0:T(8,128)(2,1)} %get-tuple-element.371), channel_id=1, source_target_pairs={{0,4},{4,0},{2,6},{6,2},{1,5},{5,1},{3,7},{7,3},{8,12},{12,8},{10,... | collective-permute-start | bytes 3145736 | tf_op jit(solution)/shard_map/ppermute | solution.py:45
  524.5 8.9 %collective-permute-start.58 = (bf16[512,256]{1,0:T(8,128)(2,1)S(1)}, bf16[512,256]{1,0:T(8,128)(2,1)}, u32[]{:S(2)}, u32[]{:S(2)}) collective-permute-start(bf16[512,256]{1,0:T(8,128)(2,1)S(1)} %copy-done.60), channel_id=1, source_target_pairs={{0,2},{2,0},{4,6},{6,4},{1,3},{3,1},{5,7},{7,5},{8,10},{10,8},{12,... | collective-permute-start | bytes 786440 | tf_op jit(solution)/shard_map/ppermute | solution.py:41
  550.1 12.9 %collective-permute-start.60 = (bf16[128,2048]{1,0:T(8,128)(2,1)}, bf16[128,2048]{1,0:T(8,128)(2,1)}, u32[]{:S(2)}, u32[]{:S(2)}) collective-permute-start(bf16[128,2048]{1,0:T(8,128)(2,1)} %add_convert_fusion.4), channel_id=1, source_target_pairs={{0,4},{4,0},{2,6},{6,2},{1,5},{5,1},{3,7},{7,3},{8,12},{12,8},{10,... | collective-permute-start | bytes 1572872 | tf_op jit(solution)/shard_map/ppermute | solution.py:45
  553.7 12.8 %collective-permute-start.59 = (bf16[128,2048]{1,0:T(8,128)(2,1)}, bf16[128,2048]{1,0:T(8,128)(2,1)S(1)}, u32[]{:S(2)}, u32[]{:S(2)}) collective-permute-start(bf16[128,2048]{1,0:T(8,128)(2,1)} %add_convert_fusion.5), channel_id=1, source_target_pairs={{0,1},{1,0},{2,3},{3,2},{4,5},{5,4},{6,7},{7,6},{8,9},{9,8},{10,11... | collective-permute-start | bytes 1572872 | tf_op jit(solution)/shard_map/ppermute | solution.py:37
  554.3 7.6 %collective-permute-start.61 = (bf16[512,256]{1,0:T(8,128)(2,1)}, bf16[512,256]{1,0:T(8,128)(2,1)S(1)}, u32[]{:S(2)}, u32[]{:S(2)}) collective-permute-start(bf16[512,256]{1,0:T(8,128)(2,1)} %collective-permute-done.55.refs_2_), channel_id=1, source_target_pairs={{0,2},{2,0},{4,6},{6,4},{1,3},{3,1},{5,7},{7,5},{8,10},{10,8},{12,... | collective-permute-start | bytes 786440 | tf_op jit(solution)/shard_map/ppermute | solution.py:41
  573.4 25.7 %collective-permute-start.62 = (bf16[256,2048]{1,0:T(8,128)(2,1)S(1)}, bf16[256,2048]{1,0:T(8,128)(2,1)}, u32[]{:S(2)}, u32[]{:S(2)}) collective-permute-start(bf16[256,2048]{1,0:T(8,128)(2,1)S(1)} %add_convert_fusion.1), channel_id=1, source_target_pairs={{0,1},{1,0},{2,3},{3,2},{4,5},{5,4},{6,7},{7,6},{8,9},{9,8},{10,11... | collective-permute-start | bytes 3145736 | tf_op jit(solution)/shard_map/ppermute | solution.py:37
  573.9 25.1 %collective-permute-start.66 = (bf16[512,768]{1,0:T(8,128)(2,1)}, bf16[512,768]{1,0:T(8,128)(2,1)}, u32[]{:S(2)}, u32[]{:S(2)}) collective-permute-start(bf16[512,768]{1,0:T(8,128)(2,1)} %reduce-scatter.11.cloned.1.call-done.refs_0_), channel_id=1, source_target_pairs={{0,2},{2,0},{4,6},{6,4},{1,3},{3,1},{5,7},{7,5},{8,10},{10,8},{12,... | collective-permute-start | bytes 2359304 | tf_op jit(solution)/shard_map/ppermute | solution.py:41
  573.9 25.1 %collective-permute-start.65 = (bf16[512,768]{1,0:T(8,128)(2,1)}, bf16[512,768]{1,0:T(8,128)(2,1)}, u32[]{:S(2)}, u32[]{:S(2)}) collective-permute-start(bf16[512,768]{1,0:T(8,128)(2,1)} %reduce-scatter.11.cloned.1.call-done.refs_0_), channel_id=1, source_target_pairs={{0,4},{4,0},{2,6},{6,2},{1,5},{5,1},{3,7},{7,3},{8,12},{12,8},{10,... | collective-permute-start | bytes 2359304 | tf_op jit(solution)/shard_map/ppermute | solution.py:45
  576.4 22.6 %collective-permute-start.64 = (f32[4,6144]{1,0:T(4,128)S(1)}, f32[4,6144]{1,0:T(4,128)S(1)}, u32[]{:S(2)}, u32[]{:S(2)}) collective-permute-start(f32[4,6144]{1,0:T(4,128)S(1)} %add.257), channel_id=1, source_target_pairs={{0,1},{1,0},{2,3},{3,2},{4,5},{5,4},{6,7},{7,6},{8,9},{9,8},{10,11... | collective-permute-start | bytes 294920 | tf_op jit(solution)/shard_map/ppermute | solution.py:37
  604.5 12.2 %collective-permute-start.69 = (f32[1,6144]{1,0:T(1,128)S(1)}, f32[1,6144]{1,0:T(1,128)S(1)}, u32[]{:S(2)}, u32[]{:S(2)}) collective-permute-start(f32[1,6144]{1,0:T(1,128)S(1)} %get-tuple-element.428), channel_id=1, source_target_pairs={{0,8},{8,16},{16,24},{24,0},{1,9},{9,17},{17,25},{25,1},{2,10},{10... | collective-permute-start | bytes 73736 | tf_op jit(solution)/shard_map/ppermute | solution.py:1036
  605.7 11.0 %collective-permute-start.71 = (f32[1,6144]{1,0:T(1,128)S(1)}, f32[1,6144]{1,0:T(1,128)S(1)}, u32[]{:S(2)}, u32[]{:S(2)}) collective-permute-start(f32[1,6144]{1,0:T(1,128)S(1)} %get-tuple-element.429), channel_id=1, source_target_pairs={{0,24},{8,0},{16,8},{24,16},{1,25},{9,1},{17,9},{25,17},{2,26},{10... | collective-permute-start | bytes 73736 | tf_op jit(solution)/shard_map/ppermute | solution.py:1036
  608.4 8.4 %collective-permute-start.70 = (f32[1,6144]{1,0:T(1,128)S(1)}, f32[1,6144]{1,0:T(1,128)S(1)}, u32[]{:S(2)}, u32[]{:S(2)}) collective-permute-start(f32[1,6144]{1,0:T(1,128)S(1)} %get-tuple-element.430), channel_id=1, source_target_pairs={{0,16},{8,24},{16,0},{24,8},{1,17},{9,25},{17,1},{25,9},{2,18},{10... | collective-permute-start | bytes 73736 | tf_op jit(solution)/shard_map/ppermute | solution.py:1036
  (88 other events, 809.1 us)
Sparse Core Ops, SparseCore 0:
  10.2 83.4 all-gather.2
  95.8 149.8 all-gather.4
  299.0 75.0 reduce-scatter.4
  376.4 77.2 reduce-scatter.6
  485.4 25.4 reduce-scatter.8
  513.2 58.8 reduce-scatter.10

commit v4 on v3

--- a/solution.py
+++ b/solution.py
@@ -257,69 +257,81 @@
     )(info, qkv, grad)
 
 
-def grad_matmul_kernel(n_left, spans, widths, *refs):
-    total = None
-    for li, lo, ri, ro, size in spans:
-        left = refs[li][pl.ds(lo, size), :]
-        right = refs[n_left + ri][pl.ds(ro, size), :]
-        term = dot_tn(left, right)
-        total = term if total is None else total + term
-    start = 0
-    for out_ref, n in zip(refs[len(refs) - len(widths) :], widths):
-        out_ref[...] = total[:, start : start + n].astype(BF)
-        start += n
-
-
-def row_chunks(pieces, order, rows, chunk):
-    where = {}
-    place = 0
-    spots = []
-    for index, piece in enumerate(pieces):
-        for offset in range(0, piece.shape[0], chunk):
-            spots.append((index, offset))
-    per_block = rows // chunk
-    for block in order:
-        where[block] = spots[place : place + per_block]
-        place += per_block
-    return [spot for block in sorted(where) for spot in where[block]]
-
-
-def matched_spans(lefts, left_order, rights, right_order, rows):
-    chunk = min([rows] + [p.shape[0] for p in list(lefts) + list(rights)])
-    spans = []
-    for left, right in zip(
-        row_chunks(lefts, left_order, rows, chunk), row_chunks(rights, right_order, rows, chunk)
-    ):
-        last = spans[-1] if spans else None
-        if last and left == (last[0], last[1] + last[4]) and right == (last[2], last[3] + last[4]):
-            spans[-1] = last[:4] + (last[4] + chunk,)
-        else:
-            spans.append(left + right + (chunk,))
-    return spans
-
-
-def grad_matmul(lefts, left_order, rights, right_order, rows, name, widths=None):
-    spans = matched_spans(lefts, left_order, rights, right_order, rows)
+def block_copies(pieces, rows, total):
+    seen, plan = set(), []
+    for start in range(0, total, rows):
+        need = [
+            i
+            for i, (begin, size) in enumerate(pieces)
+            if begin < start + rows and start < begin + size and i not in seen
+        ]
+        seen.update(need)
+        plan.append(need)
+    return plan
+
+
+def piece_copy(refs, pieces, buffer, sems, i):
+    begin, size = pieces[i]
+    return pltpu.make_async_copy(refs[i], buffer.at[pl.ds(begin, size), :], sems.at[i])
+
+
+def grad_matmul_kernel(pieces, rows, tile, *refs):
+    lefts = refs[: len(pieces)]
+    right_hbm, out_ref, buffer, right_ref, sems, right_sems = refs[len(pieces) :]
+    step = pl.program_id(0)
+    plan = block_copies(pieces, rows, right_ref.shape[0])
+    columns = pl.ds(pl.multiple_of(step * tile, tile), tile)
+
+    def right_copy(p):
+        block = pl.ds(p * rows, rows)
+        return pltpu.make_async_copy(right_hbm.at[block], right_ref.at[block], right_sems.at[p])
+
+    @pl.when(step == 0)
+    def _():
+        for p, need in enumerate(plan):
+            right_copy(p).start()
+            for i in need:
+                piece_copy(lefts, pieces, buffer, sems, i).start()
+        total = None
+        for p, need in enumerate(plan):
+            right_copy(p).wait()
+            for i in need:
+                piece_copy(lefts, pieces, buffer, sems, i).wait()
+            block = pl.ds(p * rows, rows)
+            term = dot_tn(buffer[block, columns], right_ref[block, :])
+            total = term if total is None else total + term
+        out_ref[...] = total.astype(BF)
+
+    @pl.when(step > 0)
+    def _():
+        out_ref[...] = dot_tn(buffer[:, columns], right_ref[...]).astype(BF)
+
+
+def grad_matmul(lefts, starts, right, rows, name):
     d = lefts[0].shape[1]
-    n = rights[0].shape[1]
-    widths = widths or [n]
+    total_rows, n = right.shape
     tile = 512
-    total_rows = sum(p.shape[0] for p in lefts)
+    pieces = [(start, p.shape[0]) for start, p in zip(starts, lefts)]
     return pl.pallas_call(
-        partial(grad_matmul_kernel, len(lefts), spans, widths),
+        partial(grad_matmul_kernel, pieces, rows, tile),
         grid=(d // tile,),
-        in_specs=[pl.BlockSpec((p.shape[0], tile), lambda i: (0, i)) for p in lefts]
-        + [pl.BlockSpec(p.shape, lambda i: (0, 0), pipeline_mode=pl.Buffered(1)) for p in rights],
-        out_specs=[pl.BlockSpec((tile, w), lambda i: (i, 0)) for w in widths],
-        out_shape=[jax.ShapeDtypeStruct((d, w), BF) for w in widths],
-        compiler_params=pltpu.CompilerParams(vmem_limit_bytes=32 << 20),
+        in_specs=[pl.BlockSpec(memory_space=pl.ANY) for _ in range(len(lefts) + 1)],
+        out_specs=pl.BlockSpec((tile, n), lambda i: (i, 0)),
+        out_shape=jax.ShapeDtypeStruct((d, n), BF),
+        scratch_shapes=[
+            pltpu.VMEM((total_rows, d), BF),
+            pltpu.VMEM((total_rows, n), BF),
+            pltpu.SemaphoreType.DMA((len(lefts),)),
+            pltpu.SemaphoreType.DMA((total_rows // rows,)),
+        ],
+        compiler_params=pltpu.CompilerParams(vmem_limit_bytes=VMEM_BYTES),
         cost_estimate=pl.CostEstimate(
             flops=2 * total_rows * d * n,
             transcendentals=0,
             bytes_accessed=2 * (total_rows * (d + n) + d * n),
         ),
         name=name,
-    )(*lefts, *rights)
+    )(*lefts, right)
 
 
 def sent_kernel(rows, low_ref, high_ref, w_ref, out_ref):
@@ -374,24 +386,6 @@
         name=name,
     )(left, left, weights, *more)
     return result[0] if arrived is None else result
-
-
-def block_copies(pieces, rows, total):
-    seen, plan = set(), []
-    for start in range(0, total, rows):
-        need = [
-            i
-            for i, (begin, size) in enumerate(pieces)
-            if begin < start + rows and start < begin + size and i not in seen
-        ]
-        seen.update(need)
-        plan.append(need)
-    return plan
-
-
-def piece_copy(refs, pieces, buffer, sems, i):
-    begin, size = pieces[i]
-    return pltpu.make_async_copy(refs[i], buffer.at[pl.ds(begin, size), :], sems.at[i])
 
 
 def project_kernel(pieces, rows, *refs):
@@ -846,7 +840,6 @@
         [me[None].astype(jnp.int32), prompt_lengths, lens, swap_low(lens), lens_high, swap_low(lens_high)]
     )
 
-    natural = list(range(blocks))
     up_along = swap_high(up_own)
     act_pair = (normed_pair * gain_one + shift_one).astype(BF)
     act_pair, up_along = stage(act_pair, up_along)
@@ -876,17 +869,11 @@
     normed_two, inverse_two = normalize(middle)
     act_two_own = (normed_two * gain_two + shift_two).astype(BF)
 
-    def gather_blocks(own, beside=(), between=None):
+    def gather_blocks(own, beside=()):
         half = rows // 2
         across, along, low, *beside = stage(swap_tp(own), swap_high(own), swap_low(own), *beside)
-        if between is not None:
-            beside = between(*beside)
-        corner_a, corner_b, across_low, along_low, *beside = stage(
-            swap_high(across[:half]),
-            swap_tp(along[half:]),
-            swap_low(across),
-            swap_low(along),
-            *beside,
+        corner_a, corner_b, across_low, along_low = stage(
+            swap_high(across[:half]), swap_tp(along[half:]), swap_low(across), swap_low(along)
         )
         pieces = stage(
             own,
@@ -919,30 +906,31 @@
     )
     parts = partial_blocks(grad_pre, rows, w_feed, 0, None, "act_two_sent")
     parts, hidden = stage(parts, hidden)
-    (down_term,) = grad_matmul(up_pieces, natural, [hidden], natural, rows, "down_weight_term")
+    down_term = grad_matmul(up_pieces, up_starts, hidden, 2 * rows, "down_weight_term")
     parts, grad_pre, down_term = stage(swap_low(parts), grad_pre, down_term)
     down_piece = lax.psum_scatter(down_term, "fsdp", scatter_dimension=0, tiled=True)
     sums = partial_blocks(grad_pre, rows, w_feed, 0, parts, "act_two_kept")
-    sums, grad_pre = stage(sums, grad_pre)
-    (up_term,) = grad_matmul(act_two, GATHERED, [grad_pre], natural, rows, "up_weight_term")
-    first, up_term, hidden = stage(scatter_first(sums), up_term, hidden)
+    sums, grad_pre, hidden = stage(sums, grad_pre, hidden)
     mlp_parts = partial_blocks(hidden, rows, w_feed, 1, None, "feed_sent")
-    second, mlp_parts, up_term, hidden = stage(
-        scatter_second(sums, first), mlp_parts, up_term, hidden
-    )
-    up_piece = lax.psum_scatter(up_term, "fsdp", scatter_dimension=0, tiled=True)
+    first, mlp_parts, hidden, grad_pre = stage(scatter_first(sums), mlp_parts, hidden, grad_pre)
+    second, mlp_parts, hidden, grad_pre = stage(
+        scatter_second(sums, first), swap_low(mlp_parts), hidden, grad_pre
+    )
     grad_act_two = scatter_sum(sums, first, second)
     grad_middle = up_own.astype(F32) + norm_backward(
         grad_act_two, normed_two, inverse_two, gain_two
     )
     middle_low_own = grad_middle.astype(BF)
 
-    def feed_sums(mlp_parts, hidden, down_piece):
-        return partial_blocks(hidden, rows, w_feed, 1, mlp_parts, "feed_kept"), down_piece
-
-    middle_low, (mlp_sums, down_piece) = gather_blocks(
-        middle_low_own, (swap_low(mlp_parts), hidden, down_piece), feed_sums
-    )
+    middle_low_own, mlp_parts, hidden, grad_pre = stage(
+        middle_low_own, mlp_parts, hidden, grad_pre
+    )
+    up_term = grad_matmul(act_two, starts, grad_pre, 2 * rows, "up_weight_term")
+    mlp_sums = partial_blocks(hidden, rows, w_feed, 1, mlp_parts, "feed_kept")
+    middle_low, (mlp_sums, up_term, down_piece) = gather_blocks(
+        middle_low_own, (mlp_sums, up_term, down_piece)
+    )
+    up_piece = lax.psum_scatter(up_term, "fsdp", scatter_dimension=0, tiled=True)
 
     def colsum(value):
         return jnp.sum(value, axis=0, dtype=F32)
@@ -962,9 +950,7 @@
     parts = partial_blocks(dqkv, rows, attn_full, 0, None, "act_one_sent")
     result = (middle + (scatter_sum(mlp_sums, mlp_first, mlp_second) + dbias)).astype(BF)
     parts, result, dqkv, down_high = stage(parts, result, dqkv, swap_high(down_piece))
-    (qkv_term,) = grad_matmul(
-        act_pieces, natural, [dqkv], natural, rows, "attention_weight_term"
-    )
+    qkv_term = grad_matmul(act_pieces, act_starts, dqkv, 2 * rows, "attention_weight_term")
     qkv_piece = lax.psum_scatter(qkv_term, "fsdp", scatter_dimension=0, tiled=True)
     dqkv, parts, result_other, up_high, out_piece = stage(
         dqkv, swap_low(parts), swap_tp(result), swap_high(up_piece), out_piece
@@ -978,12 +964,18 @@
         swap_low(up_piece),
         swap_high(out_piece),
     )
+    out_low = swap_low(out_piece)
     (down_grad,) = assemble(
         ctx, [down_piece, down_low, down_high, down_far], True, 1, "down_weight_grad"
     )
-    first, down_grad, out_low = stage(scatter_first(sums), down_grad, swap_low(out_piece))
+    (output_grad,) = assemble(
+        ctx, [out_piece, out_low, out_high, swap_low(out_high)], True, 1, "output_weight_grad"
+    )
+    first, down_grad, output_grad, outputs = stage(
+        scatter_first(sums), down_grad, output_grad, to_outputs(result, result_other)
+    )
     (up_grad,) = assemble(ctx, [up_piece, up_low, up_high, up_far], False, 1, "up_weight_grad")
-    second, up_grad, out_far = stage(scatter_second(sums, first), up_grad, swap_low(out_high))
+    second, up_grad = stage(scatter_second(sums, first), up_grad)
     grad_act_one = scatter_sum(sums, first, second)
     grad_stacked = (
         grad_middle + norm_backward(grad_act_one, normed_one, inverse_one, gain_one)
@@ -1015,20 +1007,12 @@
 
     small = jnp.concatenate([by_owner(vectors), by_owner(places)], axis=1)
     grad_stacked, small, qkv_piece = stage(grad_stacked, small, qkv_piece)
-    small = small + swap_low(small)
-    small = small + swap_tp(small)
-    (output_grad,) = assemble(
-        ctx, [out_piece, out_low, out_high, out_far], True, 1, "output_weight_grad"
-    )
-    stacked_other, small, qkv_high, qkv_low, output_grad, outputs = stage(
-        swap_tp(grad_stacked),
-        small,
-        swap_high(qkv_piece),
-        swap_low(qkv_piece),
-        output_grad,
-        to_outputs(result, result_other),
-    )
-    small, qkv_far = stage(small + swap_high(small), swap_low(qkv_high))
+    for swap in (swap_low, swap_high, swap_tp):
+        small = small + swap(small)
+    stacked_other, small, qkv_high, qkv_low = stage(
+        swap_tp(grad_stacked), small, swap_high(qkv_piece), swap_low(qkv_piece)
+    )
+    qkv_far = swap_low(qkv_high)
     summed = lax.dynamic_slice_in_dim(small, z, 1, axis=0)
     for step in range(1, fsdp_size):
         share = lax.dynamic_slice_in_dim(small, (z + step) % fsdp_size, 1, axis=0)

time: 632 us -> 618 us (0.978)
  local copies, waits for them, and re-layouts: 50.3 us -> 22.6 us
  waiting for transfers between devices: 244 us -> 259 us
  other arithmetic: 55.5 us -> 46.8 us
  Pallas kernels: 206 us -> 214 us
    unnamed x154 -> x120, local copies, waits for them, and re-layouts: 34.6 us -> 9.66 us
    ppermute x20, waiting for transfers between devices: 107 us -> 115 us  [swap_high(): return lax.ppermute(value, 'ctx', [(0, 2), (2, 0), (1, 3), (3, 1)])]
    pallas_call x3, Pallas kernels: 33.1 us -> 40.7 us  [grad_matmul(): pl.pallas_call(partial(grad_matmul_kernel, pieces, rows, tile), grid=(d /...]
    reduce_sum x5, other arithmetic: 15.6 us -> 9.01 us  [colsum(): return jnp.sum(value, axis=0, dtype=F32)]
  transfers between devices with their start and end apart: 78 -> 78, of which waited for: 39 -> 43; matrix products, arithmetic and copies ran while one was open for 11% -> 10% of each run, Pallas kernels for 27% -> 28%
where the time goes in v4:
time: 618 us; the launch traced here: 613 us
  waiting for transfers between devices  259 us (42%)
  Pallas kernels  214 us (35%)
  starting transfers between devices  54.7 us (9%)
  other arithmetic  46.8 us (8%)
  local copies, waits for them, and re-layouts  22.6 us (4%)
  between operations  16.1 us (3%)
    ppermute x20, waiting for transfers between devices, swap_high(): return lax.ppermute(value, 'ctx', [(0, 2), (2, 0), (1, 3), (3, 1)])  115 us
    ppermute x16, waiting for transfers between devices, swap_tp(): return lax.ppermute(value, 'tp', [(0, 1), (1, 0)])  114 us
    pallas_call x8, Pallas kernels, partial_blocks(): pl.pallas_call(partial(kernel, rows), grid=(d // tile,), in_specs=[pl.Blo...  62.2 us
    pallas_call x3, Pallas kernels, grad_matmul(): pl.pallas_call(partial(grad_matmul_kernel, pieces, rows, tile), grid=(d /...  40.7 us
    pallas_call x1, Pallas kernels, feed_both(): pl.pallas_call(partial(feed_kernel, act_pieces, up_pieces, rows), grid=(u...  27.7 us
    ppermute x20, starting transfers between devices, swap_high(): return lax.ppermute(value, 'ctx', [(0, 2), (2, 0), (1, 3), (3, 1)])  24.8 us
    pallas_call x1, Pallas kernels, attention_backward(): pl.pallas_call(partial(attention_backward_kernel, blocks // 2, rows, cont...  21.6 us
    pallas_call x4, Pallas kernels, assemble(): pl.pallas_call(partial(assemble_kernel, turn, count, width), grid_spec=pl...  20.3 us
  transfers between devices with their start and end apart: 78, of which 43 were waited for; matrix products, arithmetic and copies ran while one was open for 10% of the time, Pallas kernels for 28%

profile of v4, /device:TPU:0, one launch (start us, length us, event | category | flops | bytes accessed | tf_op | source)
XLA Modules:
  0.0 612.6 jit_solution(5580100078979987680)
XLA Ops:
  7.3 2.3 attention_shard.1
  9.7 1.7 bitcast_select_fusion.1
  13.7 5.0 collective-permute-start.5
  19.8 3.1 convert_reduce_fusion.2
  25.8 2.9 pad_maximum_fusion.1.refs_10_.refs_0_
  28.7 3.2 feed_shard.1
  32.7 4.2 subtract_multiply_fusion
  36.9 10.3 %collective-permute-done.6.refs_12_.refs_2_ = bf16[256,2048]{1,0:T(8,128)(2,1)} collective-permute-done((bf16[256,2048]{1,0:T(8,128)(2,1)}, bf16[256,2048]{1,0:T(8,128)(2,1)}, u32[]{:S(2)}, u32[]{:S(2)}) %collective-permute-start.6) | collective-permute-done | bytes 1048608 | tf_op jit(solution)/shard_map/ppermute | solution.py:45
  50.5 2.6 collective-permute-done.11.refs_14_.refs_4_
  53.1 21.4 %collective-permute-done.9.refs_13_.refs_3_ = bf16[256,2048]{1,0:T(8,128)(2,1)S(1)} collective-permute-done((bf16[256,2048]{1,0:T(8,128)(2,1)}, bf16[256,2048]{1,0:T(8,128)(2,1)S(1)}, u32[]{:S(2)}, u32[]{:S(2)}) %collective-permute-start.9) | collective-permute-done | bytes 1048608 | tf_op jit(solution)/shard_map/ppermute | solution.py:37
  74.5 20.8 %collective-permute-done.7.refs_2_ = bf16[512,2048]{1,0:T(8,128)(2,1)} collective-permute-done((bf16[512,2048]{1,0:T(8,128)(2,1)S(1)}, bf16[512,2048]{1,0:T(8,128)(2,1)}, u32[]{:S(2)}, u32[]{:S(2)}) %collective-permute-start.7) | collective-permute-done | bytes 2097184 | tf_op jit(solution)/shard_map/ppermute | solution.py:45
  102.2 12.4 %heads.1 = bf16[2048,768]{1,0:T(8,128)(2,1)} custom-call(bf16[512,2048]{1,0:T(8,128)(2,1)} %copy-done.19, bf16[512,2048]{1,0:T(8,128)(2,1)} %copy-done.42, bf16[512,2048]{1,0:T(8,128)(2,1)} %collective-permute-done.7.refs_2_, bf16[512,2048]{1,0:T(8,128)(2,1)} %collective-permute-done.12.refs_3_, ...), custom_call_target="tpu_custom_call" | custom-call | flops 6442450944 | bytes 14680064 | tf_op jit(solution)/shard_map/heads/pallas_call | solution.py:422
  114.6 1.9 copy-done.5
  116.5 11.0 %attention_forward.1 = bf16[8,256,256]{2,1,0:T(8,128)(2,1)S(1)} custom-call(s32[10]{0:T(128)S(1)} %concatenate.47.info_ref, bf16[8,256,768]{2,1,0:T(8,128)(2,1)S(1)} %bitcast.93), custom_call_target="tpu_custom_call" | custom-call | flops 2013265920 | bytes 4194304 | tf_op jit(solution)/shard_map/attention_forward/pallas_call | solution.py:222
  128.4 5.0 attention_sent.1
  133.6 7.3 %collective-permute-done.14.arrived_ref = bf16[1024,2048]{1,0:T(8,128)(2,1)} collective-permute-done((bf16[1024,2048]{1,0:T(8,128)(2,1)}, bf16[1024,2048]{1,0:T(8,128)(2,1)}, u32[]{:S(2)}, u32[]{:S(2)}) %collective-permute-start.14) | collective-permute-done | bytes 4194336 | tf_op jit(solution)/shard_map/ppermute | solution.py:41
  140.9 6.2 %attention_kept.1 = (f32[256,2048]{1,0:T(8,128)}, bf16[128,2048]{1,0:T(8,128)(2,1)}, bf16[256,2048]{1,0:T(8,128)(2,1)}, bf16[256,2048]{1,0:T(8,128)(2,1)}, bf16[128,2048]{1,0:T(8,128)(2,1)}) custom-call(bf16[2048,256]{1,0:T(8,128)(2,1)} %bitcast.90, bf16[2048,256]{1,0:T(8,128)(2,1)} %bitcast.91, ...), custom_call_target="tpu_custom_call" | custom-call | flops 1073741824 | bytes 5767168 | tf_op jit(solution)/shard_map/attention_kept/pallas_call | solution.py:369
  148.6 1.6 collective-permute-start.16
  150.2 22.5 %collective-permute-done.15 = bf16[256,2048]{1,0:T(8,128)(2,1)S(1)} collective-permute-done((bf16[256,2048]{1,0:T(8,128)(2,1)}, bf16[256,2048]{1,0:T(8,128)(2,1)S(1)}, u32[]{:S(2)}, u32[]{:S(2)}) %collective-permute-start.15) | collective-permute-done | bytes 1048608 | tf_op jit(solution)/shard_map/ppermute | solution.py:37
  175.0 1.6 collective-permute-start.18
  179.1 9.1 %collective-permute-done.18 = bf16[128,2048]{1,0:T(8,128)(2,1)S(1)} collective-permute-done((bf16[128,2048]{1,0:T(8,128)(2,1)S(1)}, bf16[128,2048]{1,0:T(8,128)(2,1)S(1)}, u32[]{:S(2)}, u32[]{:S(2)}) %collective-permute-start.18) | collective-permute-done | bytes 524320 | tf_op jit(solution)/shard_map/ppermute | solution.py:45
  188.1 2.4 collective-permute-done.17
  195.3 22.9 %collective-permute-done.20.refs_3_ = bf16[256,2048]{1,0:T(8,128)(2,1)S(1)} collective-permute-done((bf16[256,2048]{1,0:T(8,128)(2,1)S(1)}, bf16[256,2048]{1,0:T(8,128)(2,1)S(1)}, u32[]{:S(2)}, u32[]{:S(2)}) %collective-permute-start.20) | collective-permute-done | bytes 1048608 | tf_op jit(solution)/shard_map/ppermute | solution.py:45
  221.2 11.8 %collective-permute-done.23.refs_7_ = bf16[128,2048]{1,0:T(8,128)(2,1)S(1)} collective-permute-done((bf16[128,2048]{1,0:T(8,128)(2,1)S(1)}, bf16[128,2048]{1,0:T(8,128)(2,1)S(1)}, u32[]{:S(2)}, u32[]{:S(2)}) %collective-permute-start.23) | collective-permute-done | bytes 524320 | tf_op jit(solution)/shard_map/ppermute | solution.py:37
  236.3 10.1 %all-gather.5.cloned.1.call-done.refs_16_.refs_17_.w_ref = bf16[2048,2048]{1,0:T(8,128)(2,1)} async-done(((bf16[512,2048]{1,0:T(8,128)(2,1)}), bf16[2048,2048]{1,0:T(8,128)(2,1)}) %all-gather.5.cloned.1.call-update) | async-done | bytes 8388624 | tf_op jit(solution)/shard_map/all_gather | solution.py:821
  246.4 27.7 %feed_both.1 = (bf16[2048,1024]{1,0:T(8,128)(2,1)}, bf16[2048,1024]{1,0:T(8,128)(2,1)}, f32[1,1024]{1,0:T(1,128)}) custom-call(bf16[256,2048]{1,0:T(8,128)(2,1)} %copy-done.21, bf16[256,2048]{1,0:T(8,128)(2,1)} %copy-done.45, bf16[256,2048]{1,0:T(8,128)(2,1)} %copy-done.30, bf16[256,2048]{1,0:T(8,128)(2,1)} %copy-done.29, bf16[256,2048]{1,0:T(8,128)(2,1)} %copy-done.46, ...), custom_call_target="tpu_custom_call" | custom-call | flops 17179869184 | bytes 33554432 | tf_op jit(solution)/shard_map/feed_both/pallas_call | solution.py:655
  274.1 8.5 %act_two_sent.1 = bf16[1024,2048]{1,0:T(8,128)(2,1)} custom-call(bf16[2048,1024]{1,0:T(8,128)(2,1)} %get-tuple-element.307.low_ref.high_ref.refs_10_, bf16[2048,1024]{1,0:T(8,128)(2,1)} %get-tuple-element.307.low_ref.high_ref.refs_10_, bf16[2048,2048]{1,0:T(8,128)(2,1)} %all-gather.5.cloned.1.call-done.refs_16_.refs_17_.w_ref), custom_call_target="tpu_custom_call" | custom-call | flops 4294967296 | bytes 10485760 | tf_op jit(solution)/shard_map/act_two_sent/pallas_call | solution.py:369
  282.6 14.0 %down_weight_term.1 = bf16[2048,1024]{1,0:T(8,128)(2,1)} custom-call(bf16[512,2048]{1,0:T(8,128)(2,1)} %pad_maximum_fusion.1.refs_10_.refs_0_, bf16[512,2048]{1,0:T(8,128)(2,1)} %collective-permute-done.10.refs_11_.refs_1_, bf16[256,2048]{1,0:T(8,128)(2,1)} %collective-permute-done.6.refs_12_.refs_2_, bf16[256,2048]{1,0:T(8,128)(2,1)} %copy-done.44, ...), custom_call_target="tpu_custom_call" | custom-call | flops 8589934592 | bytes 16777216 | tf_op jit(solution)/shard_map/down_weight_term/pallas_call | solution.py:315
  296.7 9.8 %act_two_kept.1 = (f32[256,2048]{1,0:T(8,128)}, bf16[128,2048]{1,0:T(8,128)(2,1)}, bf16[256,2048]{1,0:T(8,128)(2,1)}, bf16[256,2048]{1,0:T(8,128)(2,1)}, bf16[128,2048]{1,0:T(8,128)(2,1)}) custom-call(bf16[2048,1024]{1,0:T(8,128)(2,1)} %get-tuple-element.307.low_ref.high_ref.refs_10_, bf16[2048,1024]{1,0:T(8,128)(2,1)} %get-tuple-element.307.low_ref.high_ref.refs_10_, ...), custom_call_target="tpu_custom_call" | custom-call | flops 4294967296 | bytes 10485760 | tf_op jit(solution)/shard_map/act_two_kept/pallas_call | solution.py:369
  309.5 8.5 %feed_sent.1 = bf16[1024,2048]{1,0:T(8,128)(2,1)} custom-call(bf16[2048,1024]{1,0:T(8,128)(2,1)} %get-tuple-element.300.refs_6_.low_ref.high_ref, bf16[2048,1024]{1,0:T(8,128)(2,1)} %get-tuple-element.300.refs_6_.low_ref.high_ref, bf16[2048,2048]{1,0:T(8,128)(2,1)} %all-gather.5.cloned.1.call-done.refs_16_.refs_17_.w_ref), custom_call_target="tpu_custom_call" | custom-call | flops 4294967296 | bytes 10485760 | tf_op jit(solution)/shard_map/feed_sent/pallas_call | solution.py:369
  318.0 14.2 %collective-permute-done.29 = bf16[256,2048]{1,0:T(8,128)(2,1)S(1)} collective-permute-done((bf16[256,2048]{1,0:T(8,128)(2,1)}, bf16[256,2048]{1,0:T(8,128)(2,1)S(1)}, u32[]{:S(2)}, u32[]{:S(2)}) %collective-permute-start.29) | collective-permute-done | bytes 1048608 | tf_op jit(solution)/shard_map/ppermute | solution.py:37
  339.5 9.9 %collective-permute-done.32 = bf16[128,2048]{1,0:T(8,128)(2,1)S(1)} collective-permute-done((bf16[128,2048]{1,0:T(8,128)(2,1)S(1)}, bf16[128,2048]{1,0:T(8,128)(2,1)S(1)}, u32[]{:S(2)}, u32[]{:S(2)}) %collective-permute-start.32) | collective-permute-done | bytes 524320 | tf_op jit(solution)/shard_map/ppermute | solution.py:45
  349.4 2.5 collective-permute-done.31
  353.1 3.5 fusion.1
  357.9 8.8 %feed_kept.1 = (f32[256,2048]{1,0:T(8,128)}, bf16[128,2048]{1,0:T(8,128)(2,1)}, bf16[256,2048]{1,0:T(8,128)(2,1)}, bf16[256,2048]{1,0:T(8,128)(2,1)}, bf16[128,2048]{1,0:T(8,128)(2,1)}) custom-call(bf16[2048,1024]{1,0:T(8,128)(2,1)} %get-tuple-element.300.refs_6_.low_ref.high_ref, bf16[2048,1024]{1,0:T(8,128)(2,1)} %get-tuple-element.300.refs_6_.low_ref.high_ref, ...), custom_call_target="tpu_custom_call" | custom-call | flops 4294967296 | bytes 10485760 | tf_op jit(solution)/shard_map/feed_kept/pallas_call | solution.py:369
  366.7 14.3 %up_weight_term.1 = bf16[2048,1024]{1,0:T(8,128)(2,1)} custom-call(bf16[256,2048]{1,0:T(8,128)(2,1)} %copy-done.21, bf16[256,2048]{1,0:T(8,128)(2,1)} %copy-done.45, bf16[256,2048]{1,0:T(8,128)(2,1)} %copy-done.30, bf16[256,2048]{1,0:T(8,128)(2,1)} %copy-done.29, bf16[256,2048]{1,0:T(8,128)(2,1)} %copy-done.46, bf16[256,2048]{1,0:T(8,128)(2,1)} %copy-done.47, ...), custom_call_target="tpu_custom_call" | custom-call | flops 8589934592 | bytes 16777216 | tf_op jit(solution)/shard_map/up_weight_term/pallas_call | solution.py:315
  387.5 12.1 %collective-permute-done.38.refs_7_ = bf16[128,2048]{1,0:T(8,128)(2,1)S(1)} collective-permute-done((bf16[128,2048]{1,0:T(8,128)(2,1)S(1)}, bf16[128,2048]{1,0:T(8,128)(2,1)S(1)}, u32[]{:S(2)}, u32[]{:S(2)}) %collective-permute-start.38) | collective-permute-done | bytes 524320 | tf_op jit(solution)/shard_map/ppermute | solution.py:37
  402.5 1.6 collective-permute-start.43
  406.2 12.0 %middle_terms.1 = (bf16[2048,256]{1,0:T(8,128)(2,1)}, bf16[2048,256]{1,0:T(8,128)(2,1)}) custom-call(bf16[256,2048]{1,0:T(8,128)(2,1)} %copy-done.13, bf16[256,2048]{1,0:T(8,128)(2,1)} %collective-permute-done.36.refs_1_, bf16[256,2048]{1,0:T(8,128)(2,1)} %collective-permute-done.34.refs_2_, bf16[256,2048]{1,0:T(8,128)(2,1)} %collective-permute-done.35.refs_3_, ...), custom_call_target="tpu_custom_call" | custom-call | flops 4294967296 | bytes 12582912 | tf_op jit(solution)/shard_map/middle_terms/pallas_call | solution.py:480
  418.2 9.8 %collective-permute-done.43 = bf16[256,2048]{1,0:T(8,128)(2,1)} collective-permute-done((bf16[256,2048]{1,0:T(8,128)(2,1)}, bf16[256,2048]{1,0:T(8,128)(2,1)}, u32[]{:S(2)}, u32[]{:S(2)}) %collective-permute-start.43) | collective-permute-done | bytes 1048608 | tf_op jit(solution)/shard_map/ppermute | solution.py:37
  428.0 2.3 collective-permute-done.44
  430.4 1.8 add_convert_fusion.6
  435.4 21.6 %attention_backward.1 = bf16[8,256,768]{2,1,0:T(8,128)(2,1)S(1)} custom-call(s32[10]{0:T(128)S(1)} %concatenate.47.info_ref, bf16[8,256,768]{2,1,0:T(8,128)(2,1)S(1)} %bitcast.94, bf16[8,256,256]{2,1,0:T(8,128)(2,1)S(1)} %bitcast.95), custom_call_target="tpu_custom_call" | custom-call | flops 7046430720 | bytes 7340032 | tf_op jit(solution)/shard_map/attention_backward/pallas_call | solution.py:240
  457.0 1.7 copy-done.2
  459.8 3.3 collective-permute-done.46
  463.1 7.3 %act_one_sent.1 = bf16[1024,2048]{1,0:T(8,128)(2,1)} custom-call(bf16[2048,768]{1,0:T(8,128)(2,1)} %bitcast.82, bf16[2048,768]{1,0:T(8,128)(2,1)} %bitcast.83, bf16[2048,1024]{1,0:T(8,128)(2,1)} %all-gather.3.cloned.1.call-done.refs_4_.w_ref.refs_11_), custom_call_target="tpu_custom_call" | custom-call | flops 3221225472 | bytes 8912896 | tf_op jit(solution)/shard_map/act_one_sent/pallas_call | solution.py:369
  470.3 4.0 add_convert_fusion.2
  476.2 12.4 %attention_weight_term.1 = bf16[2048,768]{1,0:T(8,128)(2,1)} custom-call(bf16[512,2048]{1,0:T(8,128)(2,1)} %copy-done.19, bf16[512,2048]{1,0:T(8,128)(2,1)} %copy-done.42, bf16[512,2048]{1,0:T(8,128)(2,1)} %collective-permute-done.7.refs_2_, bf16[512,2048]{1,0:T(8,128)(2,1)} %collective-permute-done.12.refs_3_, bf16[2048,768]{1,0:T(8,128)(2,1)} %bitcast.84), custom_call_target="tpu_custom_call" | custom-call | flops 6442450944 | bytes 14680064 | tf_op jit(solution)/shard_map/attention_weight_term/pallas_call | solution.py:315
  489.3 11.1 %collective-permute-done.50.refs_2_ = bf16[512,1024]{1,0:T(8,128)(2,1)} collective-permute-done((bf16[512,1024]{1,0:T(8,128)(2,1)}, bf16[512,1024]{1,0:T(8,128)(2,1)}, u32[]{:S(2)}, u32[]{:S(2)}) %collective-permute-start.50) | collective-permute-done | bytes 1048608 | tf_op jit(solution)/shard_map/ppermute | solution.py:45
  502.2 8.2 %act_one_kept.1 = (f32[256,2048]{1,0:T(8,128)}, bf16[128,2048]{1,0:T(8,128)(2,1)}, bf16[256,2048]{1,0:T(8,128)(2,1)}, bf16[256,2048]{1,0:T(8,128)(2,1)}, bf16[128,2048]{1,0:T(8,128)(2,1)}) custom-call(bf16[2048,768]{1,0:T(8,128)(2,1)} %bitcast.85, bf16[2048,768]{1,0:T(8,128)(2,1)} %bitcast.86, ...), custom_call_target="tpu_custom_call" | custom-call | flops 3221225472 | bytes 8912896 | tf_op jit(solution)/shard_map/act_one_kept/pallas_call | solution.py:369
  512.5 3.2 broadcast_select_fusion.1
  516.6 6.4 %down_weight_grad.1 = f32[4096,512]{1,0:T(8,128)} custom-call(s32[1]{0:T(128)} %bitcast.ctx_ref, bf16[512,1024]{1,0:T(8,128)(2,1)} %reduce-scatter.5.cloned.1.call-done.refs_0_, bf16[512,1024]{1,0:T(8,128)(2,1)} %collective-permute-done.52.refs_1_, bf16[512,1024]{1,0:T(8,128)(2,1)} %collective-permute-done.47.refs_2_, ...), custom_call_target="tpu_custom_call" | custom-call | bytes 12582912 | tf_op jit(solution)/shard_map/down_weight_grad/pallas_call | solution.py:563
  523.8 3.2 output_weight_grad.1
  527.0 9.0 %collective-permute-done.56 = bf16[256,2048]{1,0:T(8,128)(2,1)} collective-permute-done((bf16[256,2048]{1,0:T(8,128)(2,1)}, bf16[256,2048]{1,0:T(8,128)(2,1)}, u32[]{:S(2)}, u32[]{:S(2)}) %collective-permute-start.56) | collective-permute-done | bytes 1048608 | tf_op jit(solution)/shard_map/ppermute | solution.py:37
  540.0 1.7 collective-permute-start.60
  542.1 5.8 up_weight_grad.1
  550.7 2.2 collective-permute-done.60
  553.6 3.9 multiply_reduce_fusion.2
  557.7 2.8 add_convert_fusion.1
  565.5 18.8 %collective-permute-done.64 = f32[4,6144]{1,0:T(4,128)S(1)} collective-permute-done((f32[4,6144]{1,0:T(4,128)S(1)}, f32[4,6144]{1,0:T(4,128)S(1)}, u32[]{:S(2)}, u32[]{:S(2)}) %collective-permute-start.64) | collective-permute-done | bytes 98336 | tf_op jit(solution)/shard_map/ppermute | solution.py:45
  585.1 4.0 collective-permute-done.65
  589.7 3.4 collective-permute-start.71
  595.0 2.8 collective-permute-done.70
  600.8 4.8 attention_weight_grads.1
  (344 shorter events, 90.0 us)
Async XLA Ops:
  7.2 94.9 %all-gather.3.cloned.1.call-start = ((), (), s32[]{:S(2)}) async-start(), calls=%async_computation.4 | async-start | bytes 5242880 | tf_op jit(solution)/shard_map/all_gather | solution.py:768
  9.6 236.8 %all-gather.5.cloned.1.call-start = ((), (), s32[]{:S(2)}) async-start(), calls=%async_computation.5 | async-start | bytes 10485760 | tf_op jit(solution)/shard_map/all_gather | solution.py:821
  13.7 18.8 %collective-permute-start.5 = (bf16[3456]{0:T(1024)(128)(2,1)S(1)}, bf16[3456]{0:T(1024)(128)(2,1)S(1)}, u32[]{:S(2)}, u32[]{:S(2)}) collective-permute-start(bf16[3456]{0:T(1024)(128)(2,1)S(1)} %concatenate.48), channel_id=1, source_target_pairs={{0,24},{8,0},{16,8},{24,16},{1,25},{9,1},{17,9},{25,17},{2,26},{10... | collective-permute-start | bytes 20744 | tf_op jit(solution)/shard_map/ppermute | solution.py:696
  18.7 13.6 %collective-permute-start.4 = (bf16[3456]{0:T(1024)(128)(2,1)S(1)}, bf16[3456]{0:T(1024)(128)(2,1)S(1)}, u32[]{:S(2)}, u32[]{:S(2)}) collective-permute-start(bf16[3456]{0:T(1024)(128)(2,1)S(1)} %concatenate.48), channel_id=1, source_target_pairs={{0,16},{8,24},{16,0},{24,8},{1,17},{9,25},{17,1},{25,9},{2,18},{10... | collective-permute-start | bytes 20744 | tf_op jit(solution)/shard_map/ppermute | solution.py:696
  18.7 13.4 %collective-permute-start.3 = (bf16[3456]{0:T(1024)(128)(2,1)S(1)}, bf16[3456]{0:T(1024)(128)(2,1)S(1)}, u32[]{:S(2)}, u32[]{:S(2)}) collective-permute-start(bf16[3456]{0:T(1024)(128)(2,1)S(1)} %concatenate.48), channel_id=1, source_target_pairs={{0,8},{8,16},{16,24},{24,0},{1,9},{9,17},{17,25},{25,1},{2,10},{10... | collective-permute-start | bytes 20744 | tf_op jit(solution)/shard_map/ppermute | solution.py:696
  22.9 24.3 %collective-permute-start.6 = (bf16[256,2048]{1,0:T(8,128)(2,1)}, bf16[256,2048]{1,0:T(8,128)(2,1)}, u32[]{:S(2)}, u32[]{:S(2)}) collective-permute-start(bf16[256,2048]{1,0:T(8,128)(2,1)} %get-tuple-element.412), channel_id=1, source_target_pairs={{0,4},{4,0},{2,6},{6,2},{1,5},{5,1},{3,7},{7,3},{8,12},{12,8},{10,... | collective-permute-start | bytes 3145736 | tf_op jit(solution)/shard_map/ppermute | solution.py:45
  28.7 21.8 %collective-permute-start.10 = (bf16[512,2048]{1,0:T(8,128)(2,1)}, bf16[512,2048]{1,0:T(8,128)(2,1)}, u32[]{:S(2)}, u32[]{:S(2)}) collective-permute-start(bf16[512,2048]{1,0:T(8,128)(2,1)} %pad_maximum_fusion.1.refs_10_.refs_0_), channel_id=1, source_target_pairs={{0,2},{2,0},{4,6},{6,4},{1,3},{3,1},{5,7},{7,5},{8,10},{10,8},{12,... | collective-permute-start | bytes 6291464 | tf_op jit(solution)/shard_map/ppermute | solution.py:41
  47.2 27.3 %collective-permute-start.8 = (bf16[512,2048]{1,0:T(8,128)(2,1)S(1)}, bf16[512,2048]{1,0:T(8,128)(2,1)S(1)}, u32[]{:S(2)}, u32[]{:S(2)}) collective-permute-start(bf16[512,2048]{1,0:T(8,128)(2,1)S(1)} %get-tuple-element.235.refs_0_), channel_id=1, source_target_pairs={{0,2},{2,0},{4,6},{6,4},{1,3},{3,1},{5,7},{7,5},{8,10},{10,8},{12,... | collective-permute-start | bytes 6291464 | tf_op jit(solution)/shard_map/ppermute | solution.py:41
  47.2 48.1 %collective-permute-start.7 = (bf16[512,2048]{1,0:T(8,128)(2,1)S(1)}, bf16[512,2048]{1,0:T(8,128)(2,1)}, u32[]{:S(2)}, u32[]{:S(2)}) collective-permute-start(bf16[512,2048]{1,0:T(8,128)(2,1)S(1)} %get-tuple-element.235.refs_0_), channel_id=1, source_target_pairs={{0,4},{4,0},{2,6},{6,2},{1,5},{5,1},{3,7},{7,3},{8,12},{12,8},{10,... | collective-permute-start | bytes 6291464 | tf_op jit(solution)/shard_map/ppermute | solution.py:45
  49.0 25.6 %collective-permute-start.9 = (bf16[256,2048]{1,0:T(8,128)(2,1)}, bf16[256,2048]{1,0:T(8,128)(2,1)S(1)}, u32[]{:S(2)}, u32[]{:S(2)}) collective-permute-start(bf16[256,2048]{1,0:T(8,128)(2,1)} %collective-permute-done.6.refs_12_.refs_2_), channel_id=1, source_target_pairs={{0,1},{1,0},{2,3},{3,2},{4,5},{5,4},{6,7},{7,6},{8,9},{9,8},{10,11... | collective-permute-start | bytes 3145736 | tf_op jit(solution)/shard_map/ppermute | solution.py:37
  95.4 6.7 %collective-permute-start.12 = (bf16[512,2048]{1,0:T(8,128)(2,1)}, bf16[512,2048]{1,0:T(8,128)(2,1)}, u32[]{:S(2)}, u32[]{:S(2)}) collective-permute-start(bf16[512,2048]{1,0:T(8,128)(2,1)} %collective-permute-done.7.refs_2_), channel_id=1, source_target_pairs={{0,2},{2,0},{4,6},{6,4},{1,3},{3,1},{5,7},{7,5},{8,10},{10,8},{12,... | collective-permute-start | bytes 6291464 | tf_op jit(solution)/shard_map/ppermute | solution.py:41
  95.4 6.7 %collective-permute-start.13 = (bf16[256,2048]{1,0:T(8,128)(2,1)S(1)}, bf16[256,2048]{1,0:T(8,128)(2,1)}, u32[]{:S(2)}, u32[]{:S(2)}) collective-permute-start(bf16[256,2048]{1,0:T(8,128)(2,1)S(1)} %collective-permute-done.9.refs_13_.refs_3_), channel_id=1, source_target_pairs={{0,2},{2,0},{4,6},{6,4},{1,3},{3,1},{5,7},{7,5},{8,10},{10,8},{12,... | collective-permute-start | bytes 3145736 | tf_op jit(solution)/shard_map/ppermute | solution.py:41
  95.9 286.9 %reduce-scatter.5.cloned.1.call-start = ((), (), s32[]{:S(2)}) async-start(), calls=%async_computation.6 | async-start | bytes 5242880 | tf_op jit(solution)/shard_map/reduce_scatter | solution.py:911
  133.4 7.5 %collective-permute-start.14 = (bf16[1024,2048]{1,0:T(8,128)(2,1)}, bf16[1024,2048]{1,0:T(8,128)(2,1)}, u32[]{:S(2)}, u32[]{:S(2)}) collective-permute-start(bf16[1024,2048]{1,0:T(8,128)(2,1)} %attention_sent.1), channel_id=1, source_target_pairs={{0,2},{2,0},{4,6},{6,4},{1,3},{3,1},{5,7},{7,5},{8,10},{10,8},{12,... | collective-permute-start | bytes 12582920 | tf_op jit(solution)/shard_map/ppermute | solution.py:41
  147.2 25.5 %collective-permute-start.15 = (bf16[256,2048]{1,0:T(8,128)(2,1)}, bf16[256,2048]{1,0:T(8,128)(2,1)S(1)}, u32[]{:S(2)}, u32[]{:S(2)}) collective-permute-start(bf16[256,2048]{1,0:T(8,128)(2,1)} %get-tuple-element.242), channel_id=1, source_target_pairs={{0,1},{1,0},{2,3},{3,2},{4,5},{5,4},{6,7},{7,6},{8,9},{9,8},{10,11... | collective-permute-start | bytes 3145736 | tf_op jit(solution)/shard_map/ppermute | solution.py:37
  148.6 25.2 %collective-permute-start.16 = (bf16[256,2048]{1,0:T(8,128)(2,1)}, bf16[256,2048]{1,0:T(8,128)(2,1)S(1)}, u32[]{:S(2)}, u32[]{:S(2)}) collective-permute-start(bf16[256,2048]{1,0:T(8,128)(2,1)} %get-tuple-element.243), channel_id=1, source_target_pairs={{0,4},{4,0},{2,6},{6,2},{1,5},{5,1},{3,7},{7,3},{8,12},{12,8},{10,... | collective-permute-start | bytes 3145736 | tf_op jit(solution)/shard_map/ppermute | solution.py:45
  175.0 13.1 %collective-permute-start.18 = (bf16[128,2048]{1,0:T(8,128)(2,1)S(1)}, bf16[128,2048]{1,0:T(8,128)(2,1)S(1)}, u32[]{:S(2)}, u32[]{:S(2)}) collective-permute-start(bf16[128,2048]{1,0:T(8,128)(2,1)S(1)} %add_convert_fusion.10), channel_id=1, source_target_pairs={{0,4},{4,0},{2,6},{6,2},{1,5},{5,1},{3,7},{7,3},{8,12},{12,8},{10,... | collective-permute-start | bytes 1572872 | tf_op jit(solution)/shard_map/ppermute | solution.py:45
  177.8 12.8 %collective-permute-start.17 = (bf16[128,2048]{1,0:T(8,128)(2,1)S(1)}, bf16[128,2048]{1,0:T(8,128)(2,1)S(1)}, u32[]{:S(2)}, u32[]{:S(2)}) collective-permute-start(bf16[128,2048]{1,0:T(8,128)(2,1)S(1)} %add_convert_fusion.11), channel_id=1, source_target_pairs={{0,1},{1,0},{2,3},{3,2},{4,5},{5,4},{6,7},{7,6},{8,9},{9,8},{10,11... | collective-permute-start | bytes 1572872 | tf_op jit(solution)/shard_map/ppermute | solution.py:37
  192.6 25.6 %collective-permute-start.20 = (bf16[256,2048]{1,0:T(8,128)(2,1)S(1)}, bf16[256,2048]{1,0:T(8,128)(2,1)S(1)}, u32[]{:S(2)}, u32[]{:S(2)}) collective-permute-start(bf16[256,2048]{1,0:T(8,128)(2,1)S(1)} %add_convert_fusion.3.refs_0_), channel_id=1, source_target_pairs={{0,4},{4,0},{2,6},{6,2},{1,5},{5,1},{3,7},{7,3},{8,12},{12,8},{10,... | collective-permute-start | bytes 3145736 | tf_op jit(solution)/shard_map/ppermute | solution.py:45
  193.1 25.3 %collective-permute-start.19 = (bf16[256,2048]{1,0:T(8,128)(2,1)S(1)}, bf16[256,2048]{1,0:T(8,128)(2,1)S(1)}, u32[]{:S(2)}, u32[]{:S(2)}) collective-permute-start(bf16[256,2048]{1,0:T(8,128)(2,1)S(1)} %add_convert_fusion.3.refs_0_), channel_id=1, source_target_pairs={{0,1},{1,0},{2,3},{3,2},{4,5},{5,4},{6,7},{7,6},{8,9},{9,8},{10,11... | collective-permute-start | bytes 3145736 | tf_op jit(solution)/shard_map/ppermute | solution.py:37
  218.4 14.9 %collective-permute-start.24 = (bf16[256,2048]{1,0:T(8,128)(2,1)S(1)}, bf16[256,2048]{1,0:T(8,128)(2,1)S(1)}, u32[]{:S(2)}, u32[]{:S(2)}) collective-permute-start(bf16[256,2048]{1,0:T(8,128)(2,1)S(1)} %collective-permute-done.19.refs_2_), channel_id=1, source_target_pairs={{0,2},{2,0},{4,6},{6,4},{1,3},{3,1},{5,7},{7,5},{8,10},{10,8},{12,... | collective-permute-start | bytes 3145736 | tf_op jit(solution)/shard_map/ppermute | solution.py:41
  218.5 14.9 %collective-permute-start.25 = (bf16[256,2048]{1,0:T(8,128)(2,1)S(1)}, bf16[256,2048]{1,0:T(8,128)(2,1)S(1)}, u32[]{:S(2)}, u32[]{:S(2)}) collective-permute-start(bf16[256,2048]{1,0:T(8,128)(2,1)S(1)} %collective-permute-done.20.refs_3_), channel_id=1, source_target_pairs={{0,2},{2,0},{4,6},{6,4},{1,3},{3,1},{5,7},{7,5},{8,10},{10,8},{12,... | collective-permute-start | bytes 3145736 | tf_op jit(solution)/shard_map/ppermute | solution.py:41
  219.1 14.0 %collective-permute-start.23 = (bf16[128,2048]{1,0:T(8,128)(2,1)S(1)}, bf16[128,2048]{1,0:T(8,128)(2,1)S(1)}, u32[]{:S(2)}, u32[]{:S(2)}) collective-permute-start(bf16[128,2048]{1,0:T(8,128)(2,1)S(1)} %slice.184), channel_id=1, source_target_pairs={{0,1},{1,0},{2,3},{3,2},{4,5},{5,4},{6,7},{7,6},{8,9},{9,8},{10,11... | collective-permute-start | bytes 1572872 | tf_op jit(solution)/shard_map/ppermute | solution.py:37
  219.7 13.6 %collective-permute-start.22 = (bf16[128,2048]{1,0:T(8,128)(2,1)S(1)}, bf16[128,2048]{1,0:T(8,128)(2,1)S(1)}, u32[]{:S(2)}, u32[]{:S(2)}) collective-permute-start(bf16[128,2048]{1,0:T(8,128)(2,1)S(1)} %slice.183), channel_id=1, source_target_pairs={{0,4},{4,0},{2,6},{6,2},{1,5},{5,1},{3,7},{7,3},{8,12},{12,8},{10,... | collective-permute-start | bytes 1572872 | tf_op jit(solution)/shard_map/ppermute | solution.py:45
  282.6 14.0 %collective-permute-start.28 = (bf16[1024,2048]{1,0:T(8,128)(2,1)}, bf16[1024,2048]{1,0:T(8,128)(2,1)}, u32[]{:S(2)}, u32[]{:S(2)}) collective-permute-start(bf16[1024,2048]{1,0:T(8,128)(2,1)} %act_two_sent.1), channel_id=1, source_target_pairs={{0,2},{2,0},{4,6},{6,4},{1,3},{3,1},{5,7},{7,5},{8,10},{10,8},{12,... | collective-permute-start | bytes 12582920 | tf_op jit(solution)/shard_map/ppermute | solution.py:41
  296.7 166.4 %reduce-scatter.7.cloned.1.call-start = ((), (), s32[]{:S(2)}) async-start(), calls=%async_computation.7 | async-start | bytes 5242880 | tf_op jit(solution)/shard_map/reduce_scatter | solution.py:933
  306.5 25.8 %collective-permute-start.29 = (bf16[256,2048]{1,0:T(8,128)(2,1)}, bf16[256,2048]{1,0:T(8,128)(2,1)S(1)}, u32[]{:S(2)}, u32[]{:S(2)}) collective-permute-start(bf16[256,2048]{1,0:T(8,128)(2,1)} %get-tuple-element.284), channel_id=1, source_target_pairs={{0,1},{1,0},{2,3},{3,2},{4,5},{5,4},{6,7},{7,6},{8,9},{9,8},{10,11... | collective-permute-start | bytes 3145736 | tf_op jit(solution)/shard_map/ppermute | solution.py:37
  308.0 25.5 %collective-permute-start.30 = (bf16[256,2048]{1,0:T(8,128)(2,1)}, bf16[256,2048]{1,0:T(8,128)(2,1)}, u32[]{:S(2)}, u32[]{:S(2)}) collective-permute-start(bf16[256,2048]{1,0:T(8,128)(2,1)} %get-tuple-element.285), channel_id=1, source_target_pairs={{0,4},{4,0},{2,6},{6,2},{1,5},{5,1},{3,7},{7,3},{8,12},{12,8},{10,... | collective-permute-start | bytes 3145736 | tf_op jit(solution)/shard_map/ppermute | solution.py:45
  333.6 18.3 %collective-permute-start.33 = (bf16[1024,2048]{1,0:T(8,128)(2,1)}, bf16[1024,2048]{1,0:T(8,128)(2,1)}, u32[]{:S(2)}, u32[]{:S(2)}) collective-permute-start(bf16[1024,2048]{1,0:T(8,128)(2,1)} %feed_sent.1), channel_id=1, source_target_pairs={{0,2},{2,0},{4,6},{6,4},{1,3},{3,1},{5,7},{7,5},{8,10},{10,8},{12,... | collective-permute-start | bytes 12582920 | tf_op jit(solution)/shard_map/ppermute | solution.py:41
  335.0 14.4 %collective-permute-start.32 = (bf16[128,2048]{1,0:T(8,128)(2,1)S(1)}, bf16[128,2048]{1,0:T(8,128)(2,1)S(1)}, u32[]{:S(2)}, u32[]{:S(2)}) collective-permute-start(bf16[128,2048]{1,0:T(8,128)(2,1)S(1)} %add_convert_fusion.8), channel_id=1, source_target_pairs={{0,4},{4,0},{2,6},{6,2},{1,5},{5,1},{3,7},{7,3},{8,12},{12,8},{10,... | collective-permute-start | bytes 1572872 | tf_op jit(solution)/shard_map/ppermute | solution.py:45
  337.7 14.1 %collective-permute-start.31 = (bf16[128,2048]{1,0:T(8,128)(2,1)S(1)}, bf16[128,2048]{1,0:T(8,128)(2,1)S(1)}, u32[]{:S(2)}, u32[]{:S(2)}) collective-permute-start(bf16[128,2048]{1,0:T(8,128)(2,1)S(1)} %add_convert_fusion.9), channel_id=1, source_target_pairs={{0,1},{1,0},{2,3},{3,2},{4,5},{5,4},{6,7},{7,6},{8,9},{9,8},{10,11... | collective-permute-start | bytes 1572872 | tf_op jit(solution)/shard_map/ppermute | solution.py:37
  356.6 24.4 %collective-permute-start.36 = (bf16[256,2048]{1,0:T(8,128)(2,1)S(1)}, bf16[256,2048]{1,0:T(8,128)(2,1)}, u32[]{:S(2)}, u32[]{:S(2)}) collective-permute-start(bf16[256,2048]{1,0:T(8,128)(2,1)S(1)} %get-tuple-element.334.refs_0_), channel_id=1, source_target_pairs={{0,2},{2,0},{4,6},{6,4},{1,3},{3,1},{5,7},{7,5},{8,10},{10,8},{12,... | collective-permute-start | bytes 3145736 | tf_op jit(solution)/shard_map/ppermute | solution.py:41
  356.6 25.7 %collective-permute-start.35 = (bf16[256,2048]{1,0:T(8,128)(2,1)S(1)}, bf16[256,2048]{1,0:T(8,128)(2,1)}, u32[]{:S(2)}, u32[]{:S(2)}) collective-permute-start(bf16[256,2048]{1,0:T(8,128)(2,1)S(1)} %get-tuple-element.334.refs_0_), channel_id=1, source_target_pairs={{0,4},{4,0},{2,6},{6,2},{1,5},{5,1},{3,7},{7,3},{8,12},{12,8},{10,... | collective-permute-start | bytes 3145736 | tf_op jit(solution)/shard_map/ppermute | solution.py:45
  357.4 25.4 %collective-permute-start.34 = (bf16[256,2048]{1,0:T(8,128)(2,1)S(1)}, bf16[256,2048]{1,0:T(8,128)(2,1)}, u32[]{:S(2)}, u32[]{:S(2)}) collective-permute-start(bf16[256,2048]{1,0:T(8,128)(2,1)S(1)} %get-tuple-element.334.refs_0_), channel_id=1, source_target_pairs={{0,1},{1,0},{2,3},{3,2},{4,5},{5,4},{6,7},{7,6},{8,9},{9,8},{10,11... | collective-permute-start | bytes 3145736 | tf_op jit(solution)/shard_map/ppermute | solution.py:37
  382.8 117.5 %reduce-scatter.9.cloned.1.call-start = ((), (), s32[]{:S(2)}) async-start(), calls=%async_computation.8 | async-start | bytes 1310720 | tf_op jit(solution)/shard_map/reduce_scatter | solution.py:945
  382.9 16.9 %collective-permute-start.39 = (bf16[256,2048]{1,0:T(8,128)(2,1)}, bf16[256,2048]{1,0:T(8,128)(2,1)S(1)}, u32[]{:S(2)}, u32[]{:S(2)}) collective-permute-start(bf16[256,2048]{1,0:T(8,128)(2,1)} %collective-permute-done.34.refs_2_), channel_id=1, source_target_pairs={{0,2},{2,0},{4,6},{6,4},{1,3},{3,1},{5,7},{7,5},{8,10},{10,8},{12,... | collective-permute-start | bytes 3145736 | tf_op jit(solution)/shard_map/ppermute | solution.py:41
  383.0 16.8 %collective-permute-start.40 = (bf16[256,2048]{1,0:T(8,128)(2,1)}, bf16[256,2048]{1,0:T(8,128)(2,1)S(1)}, u32[]{:S(2)}, u32[]{:S(2)}) collective-permute-start(bf16[256,2048]{1,0:T(8,128)(2,1)} %collective-permute-done.35.refs_3_), channel_id=1, source_target_pairs={{0,2},{2,0},{4,6},{6,4},{1,3},{3,1},{5,7},{7,5},{8,10},{10,8},{12,... | collective-permute-start | bytes 3145736 | tf_op jit(solution)/shard_map/ppermute | solution.py:41
  385.6 14.0 %collective-permute-start.38 = (bf16[128,2048]{1,0:T(8,128)(2,1)S(1)}, bf16[128,2048]{1,0:T(8,128)(2,1)S(1)}, u32[]{:S(2)}, u32[]{:S(2)}) collective-permute-start(bf16[128,2048]{1,0:T(8,128)(2,1)S(1)} %slice.191), channel_id=1, source_target_pairs={{0,1},{1,0},{2,3},{3,2},{4,5},{5,4},{6,7},{7,6},{8,9},{9,8},{10,11... | collective-permute-start | bytes 1572872 | tf_op jit(solution)/shard_map/ppermute | solution.py:37
  386.1 13.6 %collective-permute-start.37 = (bf16[128,2048]{1,0:T(8,128)(2,1)S(1)}, bf16[128,2048]{1,0:T(8,128)(2,1)S(1)}, u32[]{:S(2)}, u32[]{:S(2)}) collective-permute-start(bf16[128,2048]{1,0:T(8,128)(2,1)S(1)} %slice.190), channel_id=1, source_target_pairs={{0,4},{4,0},{2,6},{6,2},{1,5},{5,1},{3,7},{7,3},{8,12},{12,8},{10,... | collective-permute-start | bytes 1572872 | tf_op jit(solution)/shard_map/ppermute | solution.py:45
  402.5 25.5 %collective-permute-start.43 = (bf16[256,2048]{1,0:T(8,128)(2,1)}, bf16[256,2048]{1,0:T(8,128)(2,1)}, u32[]{:S(2)}, u32[]{:S(2)}) collective-permute-start(bf16[256,2048]{1,0:T(8,128)(2,1)} %get-tuple-element.332), channel_id=1, source_target_pairs={{0,1},{1,0},{2,3},{3,2},{4,5},{5,4},{6,7},{7,6},{8,9},{9,8},{10,11... | collective-permute-start | bytes 3145736 | tf_op jit(solution)/shard_map/ppermute | solution.py:37
  404.1 26.3 %collective-permute-start.44 = (bf16[256,2048]{1,0:T(8,128)(2,1)}, bf16[256,2048]{1,0:T(8,128)(2,1)S(1)}, u32[]{:S(2)}, u32[]{:S(2)}) collective-permute-start(bf16[256,2048]{1,0:T(8,128)(2,1)} %get-tuple-element.333), channel_id=1, source_target_pairs={{0,4},{4,0},{2,6},{6,2},{1,5},{5,1},{3,7},{7,3},{8,12},{12,8},{10,... | collective-permute-start | bytes 3145736 | tf_op jit(solution)/shard_map/ppermute | solution.py:45
  405.4 69.0 %collective-permute-start.47 = (bf16[512,1024]{1,0:T(8,128)(2,1)}, bf16[512,1024]{1,0:T(8,128)(2,1)}, u32[]{:S(2)}, u32[]{:S(2)}) collective-permute-start(bf16[512,1024]{1,0:T(8,128)(2,1)} %reduce-scatter.5.cloned.1.call-done.refs_0_), channel_id=1, source_target_pairs={{0,4},{4,0},{2,6},{6,2},{1,5},{5,1},{3,7},{7,3},{8,12},{12,8},{10,... | collective-permute-start | bytes 3145736 | tf_op jit(solution)/shard_map/ppermute | solution.py:45
  432.1 30.9 %collective-permute-start.46 = (bf16[128,2048]{1,0:T(8,128)(2,1)S(1)}, bf16[128,2048]{1,0:T(8,128)(2,1)}, u32[]{:S(2)}, u32[]{:S(2)}) collective-permute-start(bf16[128,2048]{1,0:T(8,128)(2,1)S(1)} %add_convert_fusion.6), channel_id=1, source_target_pairs={{0,4},{4,0},{2,6},{6,2},{1,5},{5,1},{3,7},{7,3},{8,12},{12,8},{10,... | collective-permute-start | bytes 1572872 | tf_op jit(solution)/shard_map/ppermute | solution.py:45
  433.5 29.5 %collective-permute-start.45 = (bf16[128,2048]{1,0:T(8,128)(2,1)S(1)}, bf16[128,2048]{1,0:T(8,128)(2,1)S(1)}, u32[]{:S(2)}, u32[]{:S(2)}) collective-permute-start(bf16[128,2048]{1,0:T(8,128)(2,1)S(1)} %add_convert_fusion.7), channel_id=1, source_target_pairs={{0,1},{1,0},{2,3},{3,2},{4,5},{5,4},{6,7},{7,6},{8,9},{9,8},{10,11... | collective-permute-start | bytes 1572872 | tf_op jit(solution)/shard_map/ppermute | solution.py:37
  474.3 27.0 %collective-permute-start.48 = (bf16[1024,2048]{1,0:T(8,128)(2,1)}, bf16[1024,2048]{1,0:T(8,128)(2,1)}, u32[]{:S(2)}, u32[]{:S(2)}) collective-permute-start(bf16[1024,2048]{1,0:T(8,128)(2,1)} %act_one_sent.1), channel_id=1, source_target_pairs={{0,2},{2,0},{4,6},{6,4},{1,3},{3,1},{5,7},{7,5},{8,10},{10,8},{12,... | collective-permute-start | bytes 12582920 | tf_op jit(solution)/shard_map/ppermute | solution.py:41
  474.4 86.2 %reduce-scatter.11.cloned.1.call-start = ((), (), s32[]{:S(2)}) async-start(), calls=%async_computation.9 | async-start | bytes 3932160 | tf_op jit(solution)/shard_map/reduce_scatter | solution.py:954
  474.4 26.0 %collective-permute-start.50 = (bf16[512,1024]{1,0:T(8,128)(2,1)}, bf16[512,1024]{1,0:T(8,128)(2,1)}, u32[]{:S(2)}, u32[]{:S(2)}) collective-permute-start(bf16[512,1024]{1,0:T(8,128)(2,1)} %reduce-scatter.7.cloned.1.call-done.refs_0_), channel_id=1, source_target_pairs={{0,4},{4,0},{2,6},{6,2},{1,5},{5,1},{3,7},{7,3},{8,12},{12,8},{10,... | collective-permute-start | bytes 3145736 | tf_op jit(solution)/shard_map/ppermute | solution.py:45
  475.7 25.6 %collective-permute-start.49 = (bf16[256,2048]{1,0:T(8,128)(2,1)}, bf16[256,2048]{1,0:T(8,128)(2,1)}, u32[]{:S(2)}, u32[]{:S(2)}) collective-permute-start(bf16[256,2048]{1,0:T(8,128)(2,1)} %add_convert_fusion.2), channel_id=1, source_target_pairs={{0,1},{1,0},{2,3},{3,2},{4,5},{5,4},{6,7},{7,6},{8,9},{9,8},{10,11... | collective-permute-start | bytes 3145736 | tf_op jit(solution)/shard_map/ppermute | solution.py:37
  488.7 21.6 %collective-permute-start.52 = (bf16[512,1024]{1,0:T(8,128)(2,1)}, bf16[512,1024]{1,0:T(8,128)(2,1)}, u32[]{:S(2)}, u32[]{:S(2)}) collective-permute-start(bf16[512,1024]{1,0:T(8,128)(2,1)} %reduce-scatter.5.cloned.1.call-done.refs_0_), channel_id=1, source_target_pairs={{0,2},{2,0},{4,6},{6,4},{1,3},{3,1},{5,7},{7,5},{8,10},{10,8},{12,... | collective-permute-start | bytes 3145736 | tf_op jit(solution)/shard_map/ppermute | solution.py:41
  488.8 21.6 %collective-permute-start.54 = (bf16[512,1024]{1,0:T(8,128)(2,1)}, bf16[512,1024]{1,0:T(8,128)(2,1)}, u32[]{:S(2)}, u32[]{:S(2)}) collective-permute-start(bf16[512,1024]{1,0:T(8,128)(2,1)} %reduce-scatter.7.cloned.1.call-done.refs_0_), channel_id=1, source_target_pairs={{0,2},{2,0},{4,6},{6,4},{1,3},{3,1},{5,7},{7,5},{8,10},{10,8},{12,... | collective-permute-start | bytes 3145736 | tf_op jit(solution)/shard_map/ppermute | solution.py:41
  500.4 10.0 %collective-permute-start.53 = (bf16[512,1024]{1,0:T(8,128)(2,1)}, bf16[512,1024]{1,0:T(8,128)(2,1)}, u32[]{:S(2)}, u32[]{:S(2)}) collective-permute-start(bf16[512,1024]{1,0:T(8,128)(2,1)} %collective-permute-done.47.refs_2_), channel_id=1, source_target_pairs={{0,2},{2,0},{4,6},{6,4},{1,3},{3,1},{5,7},{7,5},{8,10},{10,8},{12,... | collective-permute-start | bytes 3145736 | tf_op jit(solution)/shard_map/ppermute | solution.py:41
  501.3 9.1 %collective-permute-start.51 = (bf16[512,1024]{1,0:T(8,128)(2,1)}, bf16[512,1024]{1,0:T(8,128)(2,1)}, u32[]{:S(2)}, u32[]{:S(2)}) collective-permute-start(bf16[512,1024]{1,0:T(8,128)(2,1)} %collective-permute-done.50.refs_2_), channel_id=1, source_target_pairs={{0,2},{2,0},{4,6},{6,4},{1,3},{3,1},{5,7},{7,5},{8,10},{10,8},{12,... | collective-permute-start | bytes 3145736 | tf_op jit(solution)/shard_map/ppermute | solution.py:41
  501.3 9.1 %collective-permute-start.55 = (bf16[512,256]{1,0:T(8,128)(2,1)}, bf16[512,256]{1,0:T(8,128)(2,1)S(1)}, u32[]{:S(2)}, u32[]{:S(2)}) collective-permute-start(bf16[512,256]{1,0:T(8,128)(2,1)} %reduce-scatter.9.cloned.1.call-done.refs_0_), channel_id=1, source_target_pairs={{0,4},{4,0},{2,6},{6,2},{1,5},{5,1},{3,7},{7,3},{8,12},{12,8},{10,... | collective-permute-start | bytes 786440 | tf_op jit(solution)/shard_map/ppermute | solution.py:45
  510.4 25.7 %collective-permute-start.56 = (bf16[256,2048]{1,0:T(8,128)(2,1)}, bf16[256,2048]{1,0:T(8,128)(2,1)}, u32[]{:S(2)}, u32[]{:S(2)}) collective-permute-start(bf16[256,2048]{1,0:T(8,128)(2,1)} %get-tuple-element.371), channel_id=1, source_target_pairs={{0,1},{1,0},{2,3},{3,2},{4,5},{5,4},{6,7},{7,6},{8,9},{9,8},{10,11... | collective-permute-start | bytes 3145736 | tf_op jit(solution)/shard_map/ppermute | solution.py:37
  510.9 25.3 %collective-permute-start.57 = (bf16[256,2048]{1,0:T(8,128)(2,1)}, bf16[256,2048]{1,0:T(8,128)(2,1)}, u32[]{:S(2)}, u32[]{:S(2)}) collective-permute-start(bf16[256,2048]{1,0:T(8,128)(2,1)} %get-tuple-element.372), channel_id=1, source_target_pairs={{0,4},{4,0},{2,6},{6,2},{1,5},{5,1},{3,7},{7,3},{8,12},{12,8},{10,... | collective-permute-start | bytes 3145736 | tf_op jit(solution)/shard_map/ppermute | solution.py:45
  512.5 10.6 %collective-permute-start.58 = (bf16[512,256]{1,0:T(8,128)(2,1)S(1)}, bf16[512,256]{1,0:T(8,128)(2,1)S(1)}, u32[]{:S(2)}, u32[]{:S(2)}) collective-permute-start(bf16[512,256]{1,0:T(8,128)(2,1)S(1)} %copy-done.31), channel_id=1, source_target_pairs={{0,2},{2,0},{4,6},{6,4},{1,3},{3,1},{5,7},{7,5},{8,10},{10,8},{12,... | collective-permute-start | bytes 786440 | tf_op jit(solution)/shard_map/ppermute | solution.py:41
  515.7 7.3 %collective-permute-start.59 = (bf16[512,256]{1,0:T(8,128)(2,1)S(1)}, bf16[512,256]{1,0:T(8,128)(2,1)}, u32[]{:S(2)}, u32[]{:S(2)}) collective-permute-start(bf16[512,256]{1,0:T(8,128)(2,1)S(1)} %collective-permute-done.55.refs_2_), channel_id=1, source_target_pairs={{0,2},{2,0},{4,6},{6,4},{1,3},{3,1},{5,7},{7,5},{8,10},{10,8},{12,... | collective-permute-start | bytes 786440 | tf_op jit(solution)/shard_map/ppermute | solution.py:41
  537.4 13.3 %collective-permute-start.61 = (bf16[128,2048]{1,0:T(8,128)(2,1)S(1)}, bf16[128,2048]{1,0:T(8,128)(2,1)}, u32[]{:S(2)}, u32[]{:S(2)}) collective-permute-start(bf16[128,2048]{1,0:T(8,128)(2,1)S(1)} %add_convert_fusion.4), channel_id=1, source_target_pairs={{0,4},{4,0},{2,6},{6,2},{1,5},{5,1},{3,7},{7,3},{8,12},{12,8},{10,... | collective-permute-start | bytes 1572872 | tf_op jit(solution)/shard_map/ppermute | solution.py:45
  540.0 12.9 %collective-permute-start.60 = (bf16[128,2048]{1,0:T(8,128)(2,1)S(1)}, bf16[128,2048]{1,0:T(8,128)(2,1)S(1)}, u32[]{:S(2)}, u32[]{:S(2)}) collective-permute-start(bf16[128,2048]{1,0:T(8,128)(2,1)S(1)} %add_convert_fusion.5), channel_id=1, source_target_pairs={{0,1},{1,0},{2,3},{3,2},{4,5},{5,4},{6,7},{7,6},{8,9},{9,8},{10,11... | collective-permute-start | bytes 1572872 | tf_op jit(solution)/shard_map/ppermute | solution.py:37
  560.6 28.5 %collective-permute-start.62 = (bf16[256,2048]{1,0:T(8,128)(2,1)S(1)}, bf16[256,2048]{1,0:T(8,128)(2,1)S(1)}, u32[]{:S(2)}, u32[]{:S(2)}) collective-permute-start(bf16[256,2048]{1,0:T(8,128)(2,1)S(1)} %add_convert_fusion.1), channel_id=1, source_target_pairs={{0,1},{1,0},{2,3},{3,2},{4,5},{5,4},{6,7},{7,6},{8,9},{9,8},{10,11... | collective-permute-start | bytes 3145736 | tf_op jit(solution)/shard_map/ppermute | solution.py:37
  562.1 27.0 %collective-permute-start.67 = (bf16[512,768]{1,0:T(8,128)(2,1)}, bf16[512,768]{1,0:T(8,128)(2,1)S(1)}, u32[]{:S(2)}, u32[]{:S(2)}) collective-permute-start(bf16[512,768]{1,0:T(8,128)(2,1)} %reduce-scatter.11.cloned.1.call-done.refs_0_), channel_id=1, source_target_pairs={{0,2},{2,0},{4,6},{6,4},{1,3},{3,1},{5,7},{7,5},{8,10},{10,8},{12,... | collective-permute-start | bytes 2359304 | tf_op jit(solution)/shard_map/ppermute | solution.py:41
  562.1 27.0 %collective-permute-start.66 = (bf16[512,768]{1,0:T(8,128)(2,1)}, bf16[512,768]{1,0:T(8,128)(2,1)}, u32[]{:S(2)}, u32[]{:S(2)}) collective-permute-start(bf16[512,768]{1,0:T(8,128)(2,1)} %reduce-scatter.11.cloned.1.call-done.refs_0_), channel_id=1, source_target_pairs={{0,4},{4,0},{2,6},{6,2},{1,5},{5,1},{3,7},{7,3},{8,12},{12,8},{10,... | collective-permute-start | bytes 2359304 | tf_op jit(solution)/shard_map/ppermute | solution.py:45
  564.6 19.8 %collective-permute-start.64 = (f32[4,6144]{1,0:T(4,128)S(1)}, f32[4,6144]{1,0:T(4,128)S(1)}, u32[]{:S(2)}, u32[]{:S(2)}) collective-permute-start(f32[4,6144]{1,0:T(4,128)S(1)} %add.257), channel_id=1, source_target_pairs={{0,4},{4,0},{2,6},{6,2},{1,5},{5,1},{3,7},{7,3},{8,12},{12,8},{10,... | collective-permute-start | bytes 294920 | tf_op jit(solution)/shard_map/ppermute | solution.py:45
  589.2 5.8 collective-permute-start.69
  (71 other events, 691.3 us)
Sparse Core Ops, SparseCore 0:
  10.2 83.4 all-gather.2
  96.0 150.2 all-gather.4
  296.8 75.0 reduce-scatter.4
  383.0 73.7 reduce-scatter.6
  474.5 24.2 reduce-scatter.8
  501.1 58.8 reduce-scatter.10

commit v5 on v4

--- a/solution.py
+++ b/solution.py
@@ -648,7 +648,7 @@
 def feed_both(acts, act_starts, ups, up_starts, rows, weights, bias, units, name):
     total = sum(p.shape[0] for p in acts)
     width = acts[0].shape[1]
-    tile = 256
+    tile = 512
     skip = units // tile
     act_pieces = [(start, p.shape[0]) for start, p in zip(act_starts, acts)]
     up_pieces = [(start, p.shape[0]) for start, p in zip(up_starts, ups)]
@@ -1014,11 +1014,26 @@
     )
     qkv_far = swap_low(qkv_high)
     summed = lax.dynamic_slice_in_dim(small, z, 1, axis=0)
+    shares = []
     for step in range(1, fsdp_size):
         share = lax.dynamic_slice_in_dim(small, (z + step) % fsdp_size, 1, axis=0)
         pairs = [(i, (i + step) % fsdp_size) for i in range(fsdp_size)]
-        summed = summed + lax.ppermute(share, "fsdp", pairs)
-    summed = summed[0]
+        shares.append(lax.ppermute(share, "fsdp", pairs))
+    query_grad, key_grad, value_grad = assemble(
+        ctx, [qkv_piece, qkv_low, qkv_high, qkv_far], False, 3, "attention_weight_grads"
+    )
+    prompt_input_grad, continuation_input_grad = to_outputs(grad_stacked, stacked_other)
+    (
+        shares,
+        query_grad,
+        key_grad,
+        value_grad,
+        prompt_input_grad,
+        continuation_input_grad,
+    ) = stage(
+        shares, query_grad, key_grad, value_grad, prompt_input_grad, continuation_input_grad
+    )
+    summed = (summed + sum(shares))[0]
     obias_grad, gain_one_grad, shift_one_grad, gain_two_grad, shift_two_grad, dbias_grad = [
         summed[i * d_local : (i + 1) * d_local] for i in range(6)
     ]
@@ -1029,10 +1044,6 @@
     ubias_grad = head_sums[:, 2 * heads :].reshape(ctx_size * unit_rows, hd_local)
 
     prompt_output, continuation_output = outputs
-    prompt_input_grad, continuation_input_grad = to_outputs(grad_stacked, stacked_other)
-    query_grad, key_grad, value_grad = assemble(
-        ctx, [qkv_piece, qkv_low, qkv_high, qkv_far], False, 3, "attention_weight_grads"
-    )
     return (
         prompt_output,
         continuation_output,

time: 618 us -> 613 us (level)
  transfers between devices with their start and end apart: 78 -> 78, of which waited for: 43 -> 41; matrix products, arithmetic and copies ran while one was open for 10% -> 10% of each run, Pallas kernels for 28% -> 29%
where the time goes in v5:
time: 613 us; the launch traced here: 608 us
  waiting for transfers between devices  256 us (42%)
  Pallas kernels  212 us (35%)
  starting transfers between devices  54.9 us (9%)
  other arithmetic  46.9 us (8%)
  local copies, waits for them, and re-layouts  21.7 us (4%)
  between operations  16.1 us (3%)
    ppermute x20, waiting for transfers between devices, swap_high(): return lax.ppermute(value, 'ctx', [(0, 2), (2, 0), (1, 3), (3, 1)])  114 us
    ppermute x16, waiting for transfers between devices, swap_tp(): return lax.ppermute(value, 'tp', [(0, 1), (1, 0)])  114 us
    pallas_call x8, Pallas kernels, partial_blocks(): pl.pallas_call(partial(kernel, rows), grid=(d // tile,), in_specs=[pl.Blo...  61.6 us
    pallas_call x3, Pallas kernels, grad_matmul(): pl.pallas_call(partial(grad_matmul_kernel, pieces, rows, tile), grid=(d /...  40.7 us
    pallas_call x1, Pallas kernels, feed_both(): pl.pallas_call(partial(feed_kernel, act_pieces, up_pieces, rows), grid=(u...  26.9 us
    ppermute x20, starting transfers between devices, swap_high(): return lax.ppermute(value, 'ctx', [(0, 2), (2, 0), (1, 3), (3, 1)])  24.9 us
    pallas_call x1, Pallas kernels, attention_backward(): pl.pallas_call(partial(attention_backward_kernel, blocks // 2, rows, cont...  21.6 us
    pallas_call x4, Pallas kernels, assemble(): pl.pallas_call(partial(assemble_kernel, turn, count, width), grid_spec=pl...  20.3 us
  transfers between devices with their start and end apart: 78, of which 41 were waited for; matrix products, arithmetic and copies ran while one was open for 10% of the time, Pallas kernels for 29%

profile of v5, /device:TPU:0, one launch (start us, length us, event | category | flops | bytes accessed | tf_op | source)
XLA Modules:
  0.0 607.7 jit_solution(4307915466603213869)
XLA Ops:
  7.3 2.3 attention_shard.1
  9.7 1.7 bitcast_select_fusion.1
  13.7 5.0 collective-permute-start.5
  19.8 3.2 convert_reduce_fusion.2
  25.8 2.9 pad_maximum_fusion.1.refs_10_.refs_0_
  28.7 3.2 feed_shard.1
  32.7 4.2 subtract_multiply_fusion
  36.9 10.3 %collective-permute-done.6.refs_12_.refs_2_ = bf16[256,2048]{1,0:T(8,128)(2,1)} collective-permute-done((bf16[256,2048]{1,0:T(8,128)(2,1)}, bf16[256,2048]{1,0:T(8,128)(2,1)}, u32[]{:S(2)}, u32[]{:S(2)}) %collective-permute-start.6) | collective-permute-done | bytes 1048608 | tf_op jit(solution)/shard_map/ppermute | solution.py:45
  50.5 2.6 collective-permute-done.11.refs_14_.refs_4_
  53.1 21.4 %collective-permute-done.9.refs_13_.refs_3_ = bf16[256,2048]{1,0:T(8,128)(2,1)S(1)} collective-permute-done((bf16[256,2048]{1,0:T(8,128)(2,1)}, bf16[256,2048]{1,0:T(8,128)(2,1)S(1)}, u32[]{:S(2)}, u32[]{:S(2)}) %collective-permute-start.9) | collective-permute-done | bytes 1048608 | tf_op jit(solution)/shard_map/ppermute | solution.py:37
  74.5 20.8 %collective-permute-done.7.refs_2_ = bf16[512,2048]{1,0:T(8,128)(2,1)} collective-permute-done((bf16[512,2048]{1,0:T(8,128)(2,1)S(1)}, bf16[512,2048]{1,0:T(8,128)(2,1)}, u32[]{:S(2)}, u32[]{:S(2)}) %collective-permute-start.7) | collective-permute-done | bytes 2097184 | tf_op jit(solution)/shard_map/ppermute | solution.py:45
  96.2 1.6 collective-permute-start.1
  102.2 12.4 %heads.1 = bf16[2048,768]{1,0:T(8,128)(2,1)} custom-call(bf16[512,2048]{1,0:T(8,128)(2,1)} %copy-done.19, bf16[512,2048]{1,0:T(8,128)(2,1)} %copy-done.41, bf16[512,2048]{1,0:T(8,128)(2,1)} %collective-permute-done.7.refs_2_, bf16[512,2048]{1,0:T(8,128)(2,1)} %collective-permute-done.12.refs_3_, ...), custom_call_target="tpu_custom_call" | custom-call | flops 6442450944 | bytes 14680064 | tf_op jit(solution)/shard_map/heads/pallas_call | solution.py:422
  114.6 1.9 copy-done.5
  116.5 11.0 %attention_forward.1 = bf16[8,256,256]{2,1,0:T(8,128)(2,1)S(1)} custom-call(s32[10]{0:T(128)S(1)} %concatenate.47.info_ref, bf16[8,256,768]{2,1,0:T(8,128)(2,1)S(1)} %bitcast.93), custom_call_target="tpu_custom_call" | custom-call | flops 2013265920 | bytes 4194304 | tf_op jit(solution)/shard_map/attention_forward/pallas_call | solution.py:222
  128.5 5.0 attention_sent.1
  133.6 7.3 %collective-permute-done.14.arrived_ref = bf16[1024,2048]{1,0:T(8,128)(2,1)} collective-permute-done((bf16[1024,2048]{1,0:T(8,128)(2,1)}, bf16[1024,2048]{1,0:T(8,128)(2,1)}, u32[]{:S(2)}, u32[]{:S(2)}) %collective-permute-start.14) | collective-permute-done | bytes 4194336 | tf_op jit(solution)/shard_map/ppermute | solution.py:41
  140.9 5.9 attention_kept.1
  149.8 22.5 %collective-permute-done.15 = bf16[256,2048]{1,0:T(8,128)(2,1)S(1)} collective-permute-done((bf16[256,2048]{1,0:T(8,128)(2,1)}, bf16[256,2048]{1,0:T(8,128)(2,1)S(1)}, u32[]{:S(2)}, u32[]{:S(2)}) %collective-permute-start.15) | collective-permute-done | bytes 1048608 | tf_op jit(solution)/shard_map/ppermute | solution.py:37
  174.6 1.6 collective-permute-start.18
  178.7 9.0 %collective-permute-done.18 = bf16[128,2048]{1,0:T(8,128)(2,1)S(1)} collective-permute-done((bf16[128,2048]{1,0:T(8,128)(2,1)S(1)}, bf16[128,2048]{1,0:T(8,128)(2,1)S(1)}, u32[]{:S(2)}, u32[]{:S(2)}) %collective-permute-start.18) | collective-permute-done | bytes 524320 | tf_op jit(solution)/shard_map/ppermute | solution.py:45
  187.7 2.5 collective-permute-done.17
  194.9 22.9 %collective-permute-done.20.refs_3_ = bf16[256,2048]{1,0:T(8,128)(2,1)S(1)} collective-permute-done((bf16[256,2048]{1,0:T(8,128)(2,1)S(1)}, bf16[256,2048]{1,0:T(8,128)(2,1)S(1)}, u32[]{:S(2)}, u32[]{:S(2)}) %collective-permute-start.20) | collective-permute-done | bytes 1048608 | tf_op jit(solution)/shard_map/ppermute | solution.py:45
  220.8 11.7 %collective-permute-done.23.refs_7_ = bf16[128,2048]{1,0:T(8,128)(2,1)S(1)} collective-permute-done((bf16[128,2048]{1,0:T(8,128)(2,1)S(1)}, bf16[128,2048]{1,0:T(8,128)(2,1)S(1)}, u32[]{:S(2)}, u32[]{:S(2)}) %collective-permute-start.23) | collective-permute-done | bytes 524320 | tf_op jit(solution)/shard_map/ppermute | solution.py:37
  235.8 10.6 %all-gather.5.cloned.1.call-done.refs_16_.refs_17_.w_ref = bf16[2048,2048]{1,0:T(8,128)(2,1)} async-done(((bf16[512,2048]{1,0:T(8,128)(2,1)}), bf16[2048,2048]{1,0:T(8,128)(2,1)}) %all-gather.5.cloned.1.call-update) | async-done | bytes 8388624 | tf_op jit(solution)/shard_map/all_gather | solution.py:821
  246.4 26.9 %feed_both.1 = (bf16[2048,1024]{1,0:T(8,128)(2,1)}, bf16[2048,1024]{1,0:T(8,128)(2,1)}, f32[1,1024]{1,0:T(1,128)}) custom-call(bf16[256,2048]{1,0:T(8,128)(2,1)} %copy-done.21, bf16[256,2048]{1,0:T(8,128)(2,1)} %copy-done.44, bf16[256,2048]{1,0:T(8,128)(2,1)} %copy-done.29, bf16[256,2048]{1,0:T(8,128)(2,1)} %copy-done.28, bf16[256,2048]{1,0:T(8,128)(2,1)} %copy-done.45, ...), custom_call_target="tpu_custom_call" | custom-call | flops 17179869184 | bytes 33554432 | tf_op jit(solution)/shard_map/feed_both/pallas_call | solution.py:655
  273.3 8.5 %act_two_sent.1 = bf16[1024,2048]{1,0:T(8,128)(2,1)} custom-call(bf16[2048,1024]{1,0:T(8,128)(2,1)} %get-tuple-element.315.low_ref.high_ref.refs_10_, bf16[2048,1024]{1,0:T(8,128)(2,1)} %get-tuple-element.315.low_ref.high_ref.refs_10_, bf16[2048,2048]{1,0:T(8,128)(2,1)} %all-gather.5.cloned.1.call-done.refs_16_.refs_17_.w_ref), custom_call_target="tpu_custom_call" | custom-call | flops 4294967296 | bytes 10485760 | tf_op jit(solution)/shard_map/act_two_sent/pallas_call | solution.py:369
  281.9 14.0 %down_weight_term.1 = bf16[2048,1024]{1,0:T(8,128)(2,1)} custom-call(bf16[512,2048]{1,0:T(8,128)(2,1)} %pad_maximum_fusion.1.refs_10_.refs_0_, bf16[512,2048]{1,0:T(8,128)(2,1)} %collective-permute-done.10.refs_11_.refs_1_, bf16[256,2048]{1,0:T(8,128)(2,1)} %collective-permute-done.6.refs_12_.refs_2_, bf16[256,2048]{1,0:T(8,128)(2,1)} %copy-done.43, ...), custom_call_target="tpu_custom_call" | custom-call | flops 8589934592 | bytes 16777216 | tf_op jit(solution)/shard_map/down_weight_term/pallas_call | solution.py:315
  295.9 9.6 %act_two_kept.1 = (f32[256,2048]{1,0:T(8,128)}, bf16[128,2048]{1,0:T(8,128)(2,1)}, bf16[256,2048]{1,0:T(8,128)(2,1)}, bf16[256,2048]{1,0:T(8,128)(2,1)}, bf16[128,2048]{1,0:T(8,128)(2,1)}) custom-call(bf16[2048,1024]{1,0:T(8,128)(2,1)} %get-tuple-element.315.low_ref.high_ref.refs_10_, bf16[2048,1024]{1,0:T(8,128)(2,1)} %get-tuple-element.315.low_ref.high_ref.refs_10_, ...), custom_call_target="tpu_custom_call" | custom-call | flops 4294967296 | bytes 10485760 | tf_op jit(solution)/shard_map/act_two_kept/pallas_call | solution.py:369
  308.5 8.5 %feed_sent.1 = bf16[1024,2048]{1,0:T(8,128)(2,1)} custom-call(bf16[2048,1024]{1,0:T(8,128)(2,1)} %get-tuple-element.308.refs_6_.low_ref.high_ref, bf16[2048,1024]{1,0:T(8,128)(2,1)} %get-tuple-element.308.refs_6_.low_ref.high_ref, bf16[2048,2048]{1,0:T(8,128)(2,1)} %all-gather.5.cloned.1.call-done.refs_16_.refs_17_.w_ref), custom_call_target="tpu_custom_call" | custom-call | flops 4294967296 | bytes 10485760 | tf_op jit(solution)/shard_map/feed_sent/pallas_call | solution.py:369
  317.1 14.2 %collective-permute-done.29 = bf16[256,2048]{1,0:T(8,128)(2,1)S(1)} collective-permute-done((bf16[256,2048]{1,0:T(8,128)(2,1)}, bf16[256,2048]{1,0:T(8,128)(2,1)S(1)}, u32[]{:S(2)}, u32[]{:S(2)}) %collective-permute-start.29) | collective-permute-done | bytes 1048608 | tf_op jit(solution)/shard_map/ppermute | solution.py:37
  338.5 9.9 %collective-permute-done.32 = bf16[128,2048]{1,0:T(8,128)(2,1)S(1)} collective-permute-done((bf16[128,2048]{1,0:T(8,128)(2,1)S(1)}, bf16[128,2048]{1,0:T(8,128)(2,1)S(1)}, u32[]{:S(2)}, u32[]{:S(2)}) %collective-permute-start.32) | collective-permute-done | bytes 524320 | tf_op jit(solution)/shard_map/ppermute | solution.py:45
  348.4 2.5 collective-permute-done.31
  352.2 3.5 fusion.1
  356.9 8.8 %feed_kept.1 = (f32[256,2048]{1,0:T(8,128)}, bf16[128,2048]{1,0:T(8,128)(2,1)}, bf16[256,2048]{1,0:T(8,128)(2,1)}, bf16[256,2048]{1,0:T(8,128)(2,1)}, bf16[128,2048]{1,0:T(8,128)(2,1)}) custom-call(bf16[2048,1024]{1,0:T(8,128)(2,1)} %get-tuple-element.308.refs_6_.low_ref.high_ref, bf16[2048,1024]{1,0:T(8,128)(2,1)} %get-tuple-element.308.refs_6_.low_ref.high_ref, ...), custom_call_target="tpu_custom_call" | custom-call | flops 4294967296 | bytes 10485760 | tf_op jit(solution)/shard_map/feed_kept/pallas_call | solution.py:369
  365.7 14.3 %up_weight_term.1 = bf16[2048,1024]{1,0:T(8,128)(2,1)} custom-call(bf16[256,2048]{1,0:T(8,128)(2,1)} %copy-done.21, bf16[256,2048]{1,0:T(8,128)(2,1)} %copy-done.44, bf16[256,2048]{1,0:T(8,128)(2,1)} %copy-done.29, bf16[256,2048]{1,0:T(8,128)(2,1)} %copy-done.28, bf16[256,2048]{1,0:T(8,128)(2,1)} %copy-done.45, bf16[256,2048]{1,0:T(8,128)(2,1)} %copy-done.46, ...), custom_call_target="tpu_custom_call" | custom-call | flops 8589934592 | bytes 16777216 | tf_op jit(solution)/shard_map/up_weight_term/pallas_call | solution.py:315
  386.5 12.1 %collective-permute-done.38.refs_7_ = bf16[128,2048]{1,0:T(8,128)(2,1)S(1)} collective-permute-done((bf16[128,2048]{1,0:T(8,128)(2,1)S(1)}, bf16[128,2048]{1,0:T(8,128)(2,1)S(1)}, u32[]{:S(2)}, u32[]{:S(2)}) %collective-permute-start.38) | collective-permute-done | bytes 524320 | tf_op jit(solution)/shard_map/ppermute | solution.py:37
  401.5 1.6 collective-permute-start.43
  405.3 12.0 %middle_terms.1 = (bf16[2048,256]{1,0:T(8,128)(2,1)}, bf16[2048,256]{1,0:T(8,128)(2,1)}) custom-call(bf16[256,2048]{1,0:T(8,128)(2,1)} %copy-done.13, bf16[256,2048]{1,0:T(8,128)(2,1)} %collective-permute-done.36.refs_1_, bf16[256,2048]{1,0:T(8,128)(2,1)} %collective-permute-done.34.refs_2_, bf16[256,2048]{1,0:T(8,128)(2,1)} %collective-permute-done.35.refs_3_, ...), custom_call_target="tpu_custom_call" | custom-call | flops 4294967296 | bytes 12582912 | tf_op jit(solution)/shard_map/middle_terms/pallas_call | solution.py:480
  417.3 9.8 %collective-permute-done.43 = bf16[256,2048]{1,0:T(8,128)(2,1)} collective-permute-done((bf16[256,2048]{1,0:T(8,128)(2,1)}, bf16[256,2048]{1,0:T(8,128)(2,1)}, u32[]{:S(2)}, u32[]{:S(2)}) %collective-permute-start.43) | collective-permute-done | bytes 1048608 | tf_op jit(solution)/shard_map/ppermute | solution.py:37
  427.1 2.3 collective-permute-done.44
  429.4 1.8 add_convert_fusion.6
  434.4 21.6 %attention_backward.1 = bf16[8,256,768]{2,1,0:T(8,128)(2,1)S(1)} custom-call(s32[10]{0:T(128)S(1)} %concatenate.47.info_ref, bf16[8,256,768]{2,1,0:T(8,128)(2,1)S(1)} %bitcast.94, bf16[8,256,256]{2,1,0:T(8,128)(2,1)S(1)} %bitcast.95), custom_call_target="tpu_custom_call" | custom-call | flops 7046430720 | bytes 7340032 | tf_op jit(solution)/shard_map/attention_backward/pallas_call | solution.py:240
  456.1 1.7 copy-done.2
  458.8 3.2 collective-permute-done.46
  462.1 7.3 %act_one_sent.1 = bf16[1024,2048]{1,0:T(8,128)(2,1)} custom-call(bf16[2048,768]{1,0:T(8,128)(2,1)} %bitcast.82, bf16[2048,768]{1,0:T(8,128)(2,1)} %bitcast.83, bf16[2048,1024]{1,0:T(8,128)(2,1)} %all-gather.3.cloned.1.call-done.refs_4_.w_ref.refs_11_), custom_call_target="tpu_custom_call" | custom-call | flops 3221225472 | bytes 8912896 | tf_op jit(solution)/shard_map/act_one_sent/pallas_call | solution.py:369
  469.4 4.0 add_convert_fusion.2
  475.3 12.4 %attention_weight_term.1 = bf16[2048,768]{1,0:T(8,128)(2,1)} custom-call(bf16[512,2048]{1,0:T(8,128)(2,1)} %copy-done.19, bf16[512,2048]{1,0:T(8,128)(2,1)} %copy-done.41, bf16[512,2048]{1,0:T(8,128)(2,1)} %collective-permute-done.7.refs_2_, bf16[512,2048]{1,0:T(8,128)(2,1)} %collective-permute-done.12.refs_3_, bf16[2048,768]{1,0:T(8,128)(2,1)} %bitcast.84), custom_call_target="tpu_custom_call" | custom-call | flops 6442450944 | bytes 14680064 | tf_op jit(solution)/shard_map/attention_weight_term/pallas_call | solution.py:315
  488.3 11.1 %collective-permute-done.50.refs_2_ = bf16[512,1024]{1,0:T(8,128)(2,1)} collective-permute-done((bf16[512,1024]{1,0:T(8,128)(2,1)}, bf16[512,1024]{1,0:T(8,128)(2,1)}, u32[]{:S(2)}, u32[]{:S(2)}) %collective-permute-start.50) | collective-permute-done | bytes 1048608 | tf_op jit(solution)/shard_map/ppermute | solution.py:45
  501.2 8.2 %act_one_kept.1 = (f32[256,2048]{1,0:T(8,128)}, bf16[128,2048]{1,0:T(8,128)(2,1)}, bf16[256,2048]{1,0:T(8,128)(2,1)}, bf16[256,2048]{1,0:T(8,128)(2,1)}, bf16[128,2048]{1,0:T(8,128)(2,1)}) custom-call(bf16[2048,768]{1,0:T(8,128)(2,1)} %bitcast.85, bf16[2048,768]{1,0:T(8,128)(2,1)} %bitcast.86, ...), custom_call_target="tpu_custom_call" | custom-call | flops 3221225472 | bytes 8912896 | tf_op jit(solution)/shard_map/act_one_kept/pallas_call | solution.py:369
  511.6 3.2 broadcast_select_fusion.1
  515.7 6.4 %down_weight_grad.1 = f32[4096,512]{1,0:T(8,128)} custom-call(s32[1]{0:T(128)} %bitcast.ctx_ref, bf16[512,1024]{1,0:T(8,128)(2,1)} %reduce-scatter.5.cloned.1.call-done.refs_0_, bf16[512,1024]{1,0:T(8,128)(2,1)} %collective-permute-done.52.refs_1_, bf16[512,1024]{1,0:T(8,128)(2,1)} %collective-permute-done.47.refs_2_, ...), custom_call_target="tpu_custom_call" | custom-call | bytes 12582912 | tf_op jit(solution)/shard_map/down_weight_grad/pallas_call | solution.py:563
  522.8 3.2 output_weight_grad.1
  526.0 9.0 %collective-permute-done.56 = bf16[256,2048]{1,0:T(8,128)(2,1)} collective-permute-done((bf16[256,2048]{1,0:T(8,128)(2,1)}, bf16[256,2048]{1,0:T(8,128)(2,1)}, u32[]{:S(2)}, u32[]{:S(2)}) %collective-permute-start.56) | collective-permute-done | bytes 1048608 | tf_op jit(solution)/shard_map/ppermute | solution.py:37
  539.0 1.7 collective-permute-start.60
  541.2 5.8 up_weight_grad.1
  549.7 2.2 collective-permute-done.60
  552.7 3.9 multiply_reduce_fusion.2
  556.8 2.8 add_convert_fusion.1
  564.5 18.8 %collective-permute-done.64 = f32[4,6144]{1,0:T(4,128)S(1)} collective-permute-done((f32[4,6144]{1,0:T(4,128)S(1)}, f32[4,6144]{1,0:T(4,128)S(1)}, u32[]{:S(2)}, u32[]{:S(2)}) %collective-permute-start.64) | collective-permute-done | bytes 98336 | tf_op jit(solution)/shard_map/ppermute | solution.py:45
  584.1 4.0 collective-permute-done.65
  588.3 1.8 collective-permute-start.70
  590.3 1.9 collective-permute-start.68
  593.7 4.9 attention_weight_grads.1
  (342 shorter events, 88.6 us)
Async XLA Ops:
  7.2 94.9 %all-gather.3.cloned.1.call-start = ((), (), s32[]{:S(2)}) async-start(), calls=%async_computation.4 | async-start | bytes 5242880 | tf_op jit(solution)/shard_map/all_gather | solution.py:768
  9.6 236.8 %all-gather.5.cloned.1.call-start = ((), (), s32[]{:S(2)}) async-start(), calls=%async_computation.5 | async-start | bytes 10485760 | tf_op jit(solution)/shard_map/all_gather | solution.py:821
  13.7 18.8 %collective-permute-start.5 = (bf16[3456]{0:T(1024)(128)(2,1)S(1)}, bf16[3456]{0:T(1024)(128)(2,1)S(1)}, u32[]{:S(2)}, u32[]{:S(2)}) collective-permute-start(bf16[3456]{0:T(1024)(128)(2,1)S(1)} %concatenate.48), channel_id=1, source_target_pairs={{0,24},{8,0},{16,8},{24,16},{1,25},{9,1},{17,9},{25,17},{2,26},{10... | collective-permute-start | bytes 20744 | tf_op jit(solution)/shard_map/ppermute | solution.py:696
  18.7 13.6 %collective-permute-start.4 = (bf16[3456]{0:T(1024)(128)(2,1)S(1)}, bf16[3456]{0:T(1024)(128)(2,1)S(1)}, u32[]{:S(2)}, u32[]{:S(2)}) collective-permute-start(bf16[3456]{0:T(1024)(128)(2,1)S(1)} %concatenate.48), channel_id=1, source_target_pairs={{0,16},{8,24},{16,0},{24,8},{1,17},{9,25},{17,1},{25,9},{2,18},{10... | collective-permute-start | bytes 20744 | tf_op jit(solution)/shard_map/ppermute | solution.py:696
  18.7 13.4 %collective-permute-start.3 = (bf16[3456]{0:T(1024)(128)(2,1)S(1)}, bf16[3456]{0:T(1024)(128)(2,1)S(1)}, u32[]{:S(2)}, u32[]{:S(2)}) collective-permute-start(bf16[3456]{0:T(1024)(128)(2,1)S(1)} %concatenate.48), channel_id=1, source_target_pairs={{0,8},{8,16},{16,24},{24,0},{1,9},{9,17},{17,25},{25,1},{2,10},{10... | collective-permute-start | bytes 20744 | tf_op jit(solution)/shard_map/ppermute | solution.py:696
  22.9 24.3 %collective-permute-start.6 = (bf16[256,2048]{1,0:T(8,128)(2,1)}, bf16[256,2048]{1,0:T(8,128)(2,1)}, u32[]{:S(2)}, u32[]{:S(2)}) collective-permute-start(bf16[256,2048]{1,0:T(8,128)(2,1)} %get-tuple-element.428), channel_id=1, source_target_pairs={{0,4},{4,0},{2,6},{6,2},{1,5},{5,1},{3,7},{7,3},{8,12},{12,8},{10,... | collective-permute-start | bytes 3145736 | tf_op jit(solution)/shard_map/ppermute | solution.py:45
  28.7 21.8 %collective-permute-start.10 = (bf16[512,2048]{1,0:T(8,128)(2,1)}, bf16[512,2048]{1,0:T(8,128)(2,1)}, u32[]{:S(2)}, u32[]{:S(2)}) collective-permute-start(bf16[512,2048]{1,0:T(8,128)(2,1)} %pad_maximum_fusion.1.refs_10_.refs_0_), channel_id=1, source_target_pairs={{0,2},{2,0},{4,6},{6,4},{1,3},{3,1},{5,7},{7,5},{8,10},{10,8},{12,... | collective-permute-start | bytes 6291464 | tf_op jit(solution)/shard_map/ppermute | solution.py:41
  47.2 27.3 %collective-permute-start.8 = (bf16[512,2048]{1,0:T(8,128)(2,1)S(1)}, bf16[512,2048]{1,0:T(8,128)(2,1)S(1)}, u32[]{:S(2)}, u32[]{:S(2)}) collective-permute-start(bf16[512,2048]{1,0:T(8,128)(2,1)S(1)} %get-tuple-element.243.refs_0_), channel_id=1, source_target_pairs={{0,2},{2,0},{4,6},{6,4},{1,3},{3,1},{5,7},{7,5},{8,10},{10,8},{12,... | collective-permute-start | bytes 6291464 | tf_op jit(solution)/shard_map/ppermute | solution.py:41
  47.2 48.1 %collective-permute-start.7 = (bf16[512,2048]{1,0:T(8,128)(2,1)S(1)}, bf16[512,2048]{1,0:T(8,128)(2,1)}, u32[]{:S(2)}, u32[]{:S(2)}) collective-permute-start(bf16[512,2048]{1,0:T(8,128)(2,1)S(1)} %get-tuple-element.243.refs_0_), channel_id=1, source_target_pairs={{0,4},{4,0},{2,6},{6,2},{1,5},{5,1},{3,7},{7,3},{8,12},{12,8},{10,... | collective-permute-start | bytes 6291464 | tf_op jit(solution)/shard_map/ppermute | solution.py:45
  49.0 25.6 %collective-permute-start.9 = (bf16[256,2048]{1,0:T(8,128)(2,1)}, bf16[256,2048]{1,0:T(8,128)(2,1)S(1)}, u32[]{:S(2)}, u32[]{:S(2)}) collective-permute-start(bf16[256,2048]{1,0:T(8,128)(2,1)} %collective-permute-done.6.refs_12_.refs_2_), channel_id=1, source_target_pairs={{0,1},{1,0},{2,3},{3,2},{4,5},{5,4},{6,7},{7,6},{8,9},{9,8},{10,11... | collective-permute-start | bytes 3145736 | tf_op jit(solution)/shard_map/ppermute | solution.py:37
  95.9 285.9 %reduce-scatter.5.cloned.1.call-start = ((), (), s32[]{:S(2)}) async-start(), calls=%async_computation.6 | async-start | bytes 5242880 | tf_op jit(solution)/shard_map/reduce_scatter | solution.py:911
  133.4 7.5 %collective-permute-start.14 = (bf16[1024,2048]{1,0:T(8,128)(2,1)}, bf16[1024,2048]{1,0:T(8,128)(2,1)}, u32[]{:S(2)}, u32[]{:S(2)}) collective-permute-start(bf16[1024,2048]{1,0:T(8,128)(2,1)} %attention_sent.1), channel_id=1, source_target_pairs={{0,2},{2,0},{4,6},{6,4},{1,3},{3,1},{5,7},{7,5},{8,10},{10,8},{12,... | collective-permute-start | bytes 12582920 | tf_op jit(solution)/shard_map/ppermute | solution.py:41
  146.8 25.5 %collective-permute-start.15 = (bf16[256,2048]{1,0:T(8,128)(2,1)}, bf16[256,2048]{1,0:T(8,128)(2,1)S(1)}, u32[]{:S(2)}, u32[]{:S(2)}) collective-permute-start(bf16[256,2048]{1,0:T(8,128)(2,1)} %get-tuple-element.250), channel_id=1, source_target_pairs={{0,1},{1,0},{2,3},{3,2},{4,5},{5,4},{6,7},{7,6},{8,9},{9,8},{10,11... | collective-permute-start | bytes 3145736 | tf_op jit(solution)/shard_map/ppermute | solution.py:37
  148.3 25.2 %collective-permute-start.16 = (bf16[256,2048]{1,0:T(8,128)(2,1)}, bf16[256,2048]{1,0:T(8,128)(2,1)S(1)}, u32[]{:S(2)}, u32[]{:S(2)}) collective-permute-start(bf16[256,2048]{1,0:T(8,128)(2,1)} %get-tuple-element.251), channel_id=1, source_target_pairs={{0,4},{4,0},{2,6},{6,2},{1,5},{5,1},{3,7},{7,3},{8,12},{12,8},{10,... | collective-permute-start | bytes 3145736 | tf_op jit(solution)/shard_map/ppermute | solution.py:45
  174.6 13.0 %collective-permute-start.18 = (bf16[128,2048]{1,0:T(8,128)(2,1)S(1)}, bf16[128,2048]{1,0:T(8,128)(2,1)S(1)}, u32[]{:S(2)}, u32[]{:S(2)}) collective-permute-start(bf16[128,2048]{1,0:T(8,128)(2,1)S(1)} %add_convert_fusion.10), channel_id=1, source_target_pairs={{0,4},{4,0},{2,6},{6,2},{1,5},{5,1},{3,7},{7,3},{8,12},{12,8},{10,... | collective-permute-start | bytes 1572872 | tf_op jit(solution)/shard_map/ppermute | solution.py:45
  177.4 12.8 %collective-permute-start.17 = (bf16[128,2048]{1,0:T(8,128)(2,1)S(1)}, bf16[128,2048]{1,0:T(8,128)(2,1)S(1)}, u32[]{:S(2)}, u32[]{:S(2)}) collective-permute-start(bf16[128,2048]{1,0:T(8,128)(2,1)S(1)} %add_convert_fusion.11), channel_id=1, source_target_pairs={{0,1},{1,0},{2,3},{3,2},{4,5},{5,4},{6,7},{7,6},{8,9},{9,8},{10,11... | collective-permute-start | bytes 1572872 | tf_op jit(solution)/shard_map/ppermute | solution.py:37
  192.2 25.6 %collective-permute-start.20 = (bf16[256,2048]{1,0:T(8,128)(2,1)S(1)}, bf16[256,2048]{1,0:T(8,128)(2,1)S(1)}, u32[]{:S(2)}, u32[]{:S(2)}) collective-permute-start(bf16[256,2048]{1,0:T(8,128)(2,1)S(1)} %add_convert_fusion.3.refs_0_), channel_id=1, source_target_pairs={{0,4},{4,0},{2,6},{6,2},{1,5},{5,1},{3,7},{7,3},{8,12},{12,8},{10,... | collective-permute-start | bytes 3145736 | tf_op jit(solution)/shard_map/ppermute | solution.py:45
  192.7 25.3 %collective-permute-start.19 = (bf16[256,2048]{1,0:T(8,128)(2,1)S(1)}, bf16[256,2048]{1,0:T(8,128)(2,1)S(1)}, u32[]{:S(2)}, u32[]{:S(2)}) collective-permute-start(bf16[256,2048]{1,0:T(8,128)(2,1)S(1)} %add_convert_fusion.3.refs_0_), channel_id=1, source_target_pairs={{0,1},{1,0},{2,3},{3,2},{4,5},{5,4},{6,7},{7,6},{8,9},{9,8},{10,11... | collective-permute-start | bytes 3145736 | tf_op jit(solution)/shard_map/ppermute | solution.py:37
  218.0 14.9 %collective-permute-start.24 = (bf16[256,2048]{1,0:T(8,128)(2,1)S(1)}, bf16[256,2048]{1,0:T(8,128)(2,1)S(1)}, u32[]{:S(2)}, u32[]{:S(2)}) collective-permute-start(bf16[256,2048]{1,0:T(8,128)(2,1)S(1)} %collective-permute-done.19.refs_2_), channel_id=1, source_target_pairs={{0,2},{2,0},{4,6},{6,4},{1,3},{3,1},{5,7},{7,5},{8,10},{10,8},{12,... | collective-permute-start | bytes 3145736 | tf_op jit(solution)/shard_map/ppermute | solution.py:41
  218.0 14.9 %collective-permute-start.25 = (bf16[256,2048]{1,0:T(8,128)(2,1)S(1)}, bf16[256,2048]{1,0:T(8,128)(2,1)S(1)}, u32[]{:S(2)}, u32[]{:S(2)}) collective-permute-start(bf16[256,2048]{1,0:T(8,128)(2,1)S(1)} %collective-permute-done.20.refs_3_), channel_id=1, source_target_pairs={{0,2},{2,0},{4,6},{6,4},{1,3},{3,1},{5,7},{7,5},{8,10},{10,8},{12,... | collective-permute-start | bytes 3145736 | tf_op jit(solution)/shard_map/ppermute | solution.py:41
  218.6 14.0 %collective-permute-start.23 = (bf16[128,2048]{1,0:T(8,128)(2,1)S(1)}, bf16[128,2048]{1,0:T(8,128)(2,1)S(1)}, u32[]{:S(2)}, u32[]{:S(2)}) collective-permute-start(bf16[128,2048]{1,0:T(8,128)(2,1)S(1)} %slice.184), channel_id=1, source_target_pairs={{0,1},{1,0},{2,3},{3,2},{4,5},{5,4},{6,7},{7,6},{8,9},{9,8},{10,11... | collective-permute-start | bytes 1572872 | tf_op jit(solution)/shard_map/ppermute | solution.py:37
  219.3 13.6 %collective-permute-start.22 = (bf16[128,2048]{1,0:T(8,128)(2,1)S(1)}, bf16[128,2048]{1,0:T(8,128)(2,1)S(1)}, u32[]{:S(2)}, u32[]{:S(2)}) collective-permute-start(bf16[128,2048]{1,0:T(8,128)(2,1)S(1)} %slice.183), channel_id=1, source_target_pairs={{0,4},{4,0},{2,6},{6,2},{1,5},{5,1},{3,7},{7,3},{8,12},{12,8},{10,... | collective-permute-start | bytes 1572872 | tf_op jit(solution)/shard_map/ppermute | solution.py:45
  281.8 14.1 %collective-permute-start.28 = (bf16[1024,2048]{1,0:T(8,128)(2,1)}, bf16[1024,2048]{1,0:T(8,128)(2,1)}, u32[]{:S(2)}, u32[]{:S(2)}) collective-permute-start(bf16[1024,2048]{1,0:T(8,128)(2,1)} %act_two_sent.1), channel_id=1, source_target_pairs={{0,2},{2,0},{4,6},{6,4},{1,3},{3,1},{5,7},{7,5},{8,10},{10,8},{12,... | collective-permute-start | bytes 12582920 | tf_op jit(solution)/shard_map/ppermute | solution.py:41
  295.9 166.2 %reduce-scatter.7.cloned.1.call-start = ((), (), s32[]{:S(2)}) async-start(), calls=%async_computation.7 | async-start | bytes 5242880 | tf_op jit(solution)/shard_map/reduce_scatter | solution.py:933
  305.5 25.8 %collective-permute-start.29 = (bf16[256,2048]{1,0:T(8,128)(2,1)}, bf16[256,2048]{1,0:T(8,128)(2,1)S(1)}, u32[]{:S(2)}, u32[]{:S(2)}) collective-permute-start(bf16[256,2048]{1,0:T(8,128)(2,1)} %get-tuple-element.292), channel_id=1, source_target_pairs={{0,1},{1,0},{2,3},{3,2},{4,5},{5,4},{6,7},{7,6},{8,9},{9,8},{10,11... | collective-permute-start | bytes 3145736 | tf_op jit(solution)/shard_map/ppermute | solution.py:37
  307.0 25.6 %collective-permute-start.30 = (bf16[256,2048]{1,0:T(8,128)(2,1)}, bf16[256,2048]{1,0:T(8,128)(2,1)}, u32[]{:S(2)}, u32[]{:S(2)}) collective-permute-start(bf16[256,2048]{1,0:T(8,128)(2,1)} %get-tuple-element.293), channel_id=1, source_target_pairs={{0,4},{4,0},{2,6},{6,2},{1,5},{5,1},{3,7},{7,3},{8,12},{12,8},{10,... | collective-permute-start | bytes 3145736 | tf_op jit(solution)/shard_map/ppermute | solution.py:45
  332.6 18.3 %collective-permute-start.33 = (bf16[1024,2048]{1,0:T(8,128)(2,1)}, bf16[1024,2048]{1,0:T(8,128)(2,1)}, u32[]{:S(2)}, u32[]{:S(2)}) collective-permute-start(bf16[1024,2048]{1,0:T(8,128)(2,1)} %feed_sent.1), channel_id=1, source_target_pairs={{0,2},{2,0},{4,6},{6,4},{1,3},{3,1},{5,7},{7,5},{8,10},{10,8},{12,... | collective-permute-start | bytes 12582920 | tf_op jit(solution)/shard_map/ppermute | solution.py:41
  334.0 14.4 %collective-permute-start.32 = (bf16[128,2048]{1,0:T(8,128)(2,1)S(1)}, bf16[128,2048]{1,0:T(8,128)(2,1)S(1)}, u32[]{:S(2)}, u32[]{:S(2)}) collective-permute-start(bf16[128,2048]{1,0:T(8,128)(2,1)S(1)} %add_convert_fusion.8), channel_id=1, source_target_pairs={{0,4},{4,0},{2,6},{6,2},{1,5},{5,1},{3,7},{7,3},{8,12},{12,8},{10,... | collective-permute-start | bytes 1572872 | tf_op jit(solution)/shard_map/ppermute | solution.py:45
  336.8 14.1 %collective-permute-start.31 = (bf16[128,2048]{1,0:T(8,128)(2,1)S(1)}, bf16[128,2048]{1,0:T(8,128)(2,1)S(1)}, u32[]{:S(2)}, u32[]{:S(2)}) collective-permute-start(bf16[128,2048]{1,0:T(8,128)(2,1)S(1)} %add_convert_fusion.9), channel_id=1, source_target_pairs={{0,1},{1,0},{2,3},{3,2},{4,5},{5,4},{6,7},{7,6},{8,9},{9,8},{10,11... | collective-permute-start | bytes 1572872 | tf_op jit(solution)/shard_map/ppermute | solution.py:37
  355.6 24.4 %collective-permute-start.36 = (bf16[256,2048]{1,0:T(8,128)(2,1)S(1)}, bf16[256,2048]{1,0:T(8,128)(2,1)}, u32[]{:S(2)}, u32[]{:S(2)}) collective-permute-start(bf16[256,2048]{1,0:T(8,128)(2,1)S(1)} %get-tuple-element.342.refs_0_), channel_id=1, source_target_pairs={{0,2},{2,0},{4,6},{6,4},{1,3},{3,1},{5,7},{7,5},{8,10},{10,8},{12,... | collective-permute-start | bytes 3145736 | tf_op jit(solution)/shard_map/ppermute | solution.py:41
  355.6 25.7 %collective-permute-start.35 = (bf16[256,2048]{1,0:T(8,128)(2,1)S(1)}, bf16[256,2048]{1,0:T(8,128)(2,1)}, u32[]{:S(2)}, u32[]{:S(2)}) collective-permute-start(bf16[256,2048]{1,0:T(8,128)(2,1)S(1)} %get-tuple-element.342.refs_0_), channel_id=1, source_target_pairs={{0,4},{4,0},{2,6},{6,2},{1,5},{5,1},{3,7},{7,3},{8,12},{12,8},{10,... | collective-permute-start | bytes 3145736 | tf_op jit(solution)/shard_map/ppermute | solution.py:45
  356.4 25.4 %collective-permute-start.34 = (bf16[256,2048]{1,0:T(8,128)(2,1)S(1)}, bf16[256,2048]{1,0:T(8,128)(2,1)}, u32[]{:S(2)}, u32[]{:S(2)}) collective-permute-start(bf16[256,2048]{1,0:T(8,128)(2,1)S(1)} %get-tuple-element.342.refs_0_), channel_id=1, source_target_pairs={{0,1},{1,0},{2,3},{3,2},{4,5},{5,4},{6,7},{7,6},{8,9},{9,8},{10,11... | collective-permute-start | bytes 3145736 | tf_op jit(solution)/shard_map/ppermute | solution.py:37
  381.9 117.5 %reduce-scatter.9.cloned.1.call-start = ((), (), s32[]{:S(2)}) async-start(), calls=%async_computation.8 | async-start | bytes 1310720 | tf_op jit(solution)/shard_map/reduce_scatter | solution.py:945
  381.9 16.9 %collective-permute-start.39 = (bf16[256,2048]{1,0:T(8,128)(2,1)}, bf16[256,2048]{1,0:T(8,128)(2,1)S(1)}, u32[]{:S(2)}, u32[]{:S(2)}) collective-permute-start(bf16[256,2048]{1,0:T(8,128)(2,1)} %collective-permute-done.34.refs_2_), channel_id=1, source_target_pairs={{0,2},{2,0},{4,6},{6,4},{1,3},{3,1},{5,7},{7,5},{8,10},{10,8},{12,... | collective-permute-start | bytes 3145736 | tf_op jit(solution)/shard_map/ppermute | solution.py:41
  382.0 16.8 %collective-permute-start.40 = (bf16[256,2048]{1,0:T(8,128)(2,1)}, bf16[256,2048]{1,0:T(8,128)(2,1)S(1)}, u32[]{:S(2)}, u32[]{:S(2)}) collective-permute-start(bf16[256,2048]{1,0:T(8,128)(2,1)} %collective-permute-done.35.refs_3_), channel_id=1, source_target_pairs={{0,2},{2,0},{4,6},{6,4},{1,3},{3,1},{5,7},{7,5},{8,10},{10,8},{12,... | collective-permute-start | bytes 3145736 | tf_op jit(solution)/shard_map/ppermute | solution.py:41
  384.6 14.0 %collective-permute-start.38 = (bf16[128,2048]{1,0:T(8,128)(2,1)S(1)}, bf16[128,2048]{1,0:T(8,128)(2,1)S(1)}, u32[]{:S(2)}, u32[]{:S(2)}) collective-permute-start(bf16[128,2048]{1,0:T(8,128)(2,1)S(1)} %slice.191), channel_id=1, source_target_pairs={{0,1},{1,0},{2,3},{3,2},{4,5},{5,4},{6,7},{7,6},{8,9},{9,8},{10,11... | collective-permute-start | bytes 1572872 | tf_op jit(solution)/shard_map/ppermute | solution.py:37
  385.2 13.6 %collective-permute-start.37 = (bf16[128,2048]{1,0:T(8,128)(2,1)S(1)}, bf16[128,2048]{1,0:T(8,128)(2,1)S(1)}, u32[]{:S(2)}, u32[]{:S(2)}) collective-permute-start(bf16[128,2048]{1,0:T(8,128)(2,1)S(1)} %slice.190), channel_id=1, source_target_pairs={{0,4},{4,0},{2,6},{6,2},{1,5},{5,1},{3,7},{7,3},{8,12},{12,8},{10,... | collective-permute-start | bytes 1572872 | tf_op jit(solution)/shard_map/ppermute | solution.py:45
  401.5 25.5 %collective-permute-start.43 = (bf16[256,2048]{1,0:T(8,128)(2,1)}, bf16[256,2048]{1,0:T(8,128)(2,1)}, u32[]{:S(2)}, u32[]{:S(2)}) collective-permute-start(bf16[256,2048]{1,0:T(8,128)(2,1)} %get-tuple-element.340), channel_id=1, source_target_pairs={{0,1},{1,0},{2,3},{3,2},{4,5},{5,4},{6,7},{7,6},{8,9},{9,8},{10,11... | collective-permute-start | bytes 3145736 | tf_op jit(solution)/shard_map/ppermute | solution.py:37
  403.1 26.3 %collective-permute-start.44 = (bf16[256,2048]{1,0:T(8,128)(2,1)}, bf16[256,2048]{1,0:T(8,128)(2,1)S(1)}, u32[]{:S(2)}, u32[]{:S(2)}) collective-permute-start(bf16[256,2048]{1,0:T(8,128)(2,1)} %get-tuple-element.341), channel_id=1, source_target_pairs={{0,4},{4,0},{2,6},{6,2},{1,5},{5,1},{3,7},{7,3},{8,12},{12,8},{10,... | collective-permute-start | bytes 3145736 | tf_op jit(solution)/shard_map/ppermute | solution.py:45
  404.4 69.0 %collective-permute-start.47 = (bf16[512,1024]{1,0:T(8,128)(2,1)}, bf16[512,1024]{1,0:T(8,128)(2,1)}, u32[]{:S(2)}, u32[]{:S(2)}) collective-permute-start(bf16[512,1024]{1,0:T(8,128)(2,1)} %reduce-scatter.5.cloned.1.call-done.refs_0_), channel_id=1, source_target_pairs={{0,4},{4,0},{2,6},{6,2},{1,5},{5,1},{3,7},{7,3},{8,12},{12,8},{10,... | collective-permute-start | bytes 3145736 | tf_op jit(solution)/shard_map/ppermute | solution.py:45
  431.1 30.9 %collective-permute-start.46 = (bf16[128,2048]{1,0:T(8,128)(2,1)S(1)}, bf16[128,2048]{1,0:T(8,128)(2,1)}, u32[]{:S(2)}, u32[]{:S(2)}) collective-permute-start(bf16[128,2048]{1,0:T(8,128)(2,1)S(1)} %add_convert_fusion.6), channel_id=1, source_target_pairs={{0,4},{4,0},{2,6},{6,2},{1,5},{5,1},{3,7},{7,3},{8,12},{12,8},{10,... | collective-permute-start | bytes 1572872 | tf_op jit(solution)/shard_map/ppermute | solution.py:45
  432.6 29.5 %collective-permute-start.45 = (bf16[128,2048]{1,0:T(8,128)(2,1)S(1)}, bf16[128,2048]{1,0:T(8,128)(2,1)S(1)}, u32[]{:S(2)}, u32[]{:S(2)}) collective-permute-start(bf16[128,2048]{1,0:T(8,128)(2,1)S(1)} %add_convert_fusion.7), channel_id=1, source_target_pairs={{0,1},{1,0},{2,3},{3,2},{4,5},{5,4},{6,7},{7,6},{8,9},{9,8},{10,11... | collective-permute-start | bytes 1572872 | tf_op jit(solution)/shard_map/ppermute | solution.py:37
  473.4 27.0 %collective-permute-start.48 = (bf16[1024,2048]{1,0:T(8,128)(2,1)}, bf16[1024,2048]{1,0:T(8,128)(2,1)}, u32[]{:S(2)}, u32[]{:S(2)}) collective-permute-start(bf16[1024,2048]{1,0:T(8,128)(2,1)} %act_one_sent.1), channel_id=1, source_target_pairs={{0,2},{2,0},{4,6},{6,4},{1,3},{3,1},{5,7},{7,5},{8,10},{10,8},{12,... | collective-permute-start | bytes 12582920 | tf_op jit(solution)/shard_map/ppermute | solution.py:41
  473.4 86.2 %reduce-scatter.11.cloned.1.call-start = ((), (), s32[]{:S(2)}) async-start(), calls=%async_computation.9 | async-start | bytes 3932160 | tf_op jit(solution)/shard_map/reduce_scatter | solution.py:954
  473.4 26.0 %collective-permute-start.50 = (bf16[512,1024]{1,0:T(8,128)(2,1)}, bf16[512,1024]{1,0:T(8,128)(2,1)}, u32[]{:S(2)}, u32[]{:S(2)}) collective-permute-start(bf16[512,1024]{1,0:T(8,128)(2,1)} %reduce-scatter.7.cloned.1.call-done.refs_0_), channel_id=1, source_target_pairs={{0,4},{4,0},{2,6},{6,2},{1,5},{5,1},{3,7},{7,3},{8,12},{12,8},{10,... | collective-permute-start | bytes 3145736 | tf_op jit(solution)/shard_map/ppermute | solution.py:45
  474.7 25.6 %collective-permute-start.49 = (bf16[256,2048]{1,0:T(8,128)(2,1)}, bf16[256,2048]{1,0:T(8,128)(2,1)}, u32[]{:S(2)}, u32[]{:S(2)}) collective-permute-start(bf16[256,2048]{1,0:T(8,128)(2,1)} %add_convert_fusion.2), channel_id=1, source_target_pairs={{0,1},{1,0},{2,3},{3,2},{4,5},{5,4},{6,7},{7,6},{8,9},{9,8},{10,11... | collective-permute-start | bytes 3145736 | tf_op jit(solution)/shard_map/ppermute | solution.py:37
  487.7 21.6 %collective-permute-start.52 = (bf16[512,1024]{1,0:T(8,128)(2,1)}, bf16[512,1024]{1,0:T(8,128)(2,1)}, u32[]{:S(2)}, u32[]{:S(2)}) collective-permute-start(bf16[512,1024]{1,0:T(8,128)(2,1)} %reduce-scatter.5.cloned.1.call-done.refs_0_), channel_id=1, source_target_pairs={{0,2},{2,0},{4,6},{6,4},{1,3},{3,1},{5,7},{7,5},{8,10},{10,8},{12,... | collective-permute-start | bytes 3145736 | tf_op jit(solution)/shard_map/ppermute | solution.py:41
  487.8 21.6 %collective-permute-start.54 = (bf16[512,1024]{1,0:T(8,128)(2,1)}, bf16[512,1024]{1,0:T(8,128)(2,1)}, u32[]{:S(2)}, u32[]{:S(2)}) collective-permute-start(bf16[512,1024]{1,0:T(8,128)(2,1)} %reduce-scatter.7.cloned.1.call-done.refs_0_), channel_id=1, source_target_pairs={{0,2},{2,0},{4,6},{6,4},{1,3},{3,1},{5,7},{7,5},{8,10},{10,8},{12,... | collective-permute-start | bytes 3145736 | tf_op jit(solution)/shard_map/ppermute | solution.py:41
  499.4 10.0 %collective-permute-start.53 = (bf16[512,1024]{1,0:T(8,128)(2,1)}, bf16[512,1024]{1,0:T(8,128)(2,1)}, u32[]{:S(2)}, u32[]{:S(2)}) collective-permute-start(bf16[512,1024]{1,0:T(8,128)(2,1)} %collective-permute-done.47.refs_2_), channel_id=1, source_target_pairs={{0,2},{2,0},{4,6},{6,4},{1,3},{3,1},{5,7},{7,5},{8,10},{10,8},{12,... | collective-permute-start | bytes 3145736 | tf_op jit(solution)/shard_map/ppermute | solution.py:41
  500.3 9.1 %collective-permute-start.51 = (bf16[512,1024]{1,0:T(8,128)(2,1)}, bf16[512,1024]{1,0:T(8,128)(2,1)}, u32[]{:S(2)}, u32[]{:S(2)}) collective-permute-start(bf16[512,1024]{1,0:T(8,128)(2,1)} %collective-permute-done.50.refs_2_), channel_id=1, source_target_pairs={{0,2},{2,0},{4,6},{6,4},{1,3},{3,1},{5,7},{7,5},{8,10},{10,8},{12,... | collective-permute-start | bytes 3145736 | tf_op jit(solution)/shard_map/ppermute | solution.py:41
  500.3 9.1 %collective-permute-start.55 = (bf16[512,256]{1,0:T(8,128)(2,1)}, bf16[512,256]{1,0:T(8,128)(2,1)S(1)}, u32[]{:S(2)}, u32[]{:S(2)}) collective-permute-start(bf16[512,256]{1,0:T(8,128)(2,1)} %reduce-scatter.9.cloned.1.call-done.refs_0_), channel_id=1, source_target_pairs={{0,4},{4,0},{2,6},{6,2},{1,5},{5,1},{3,7},{7,3},{8,12},{12,8},{10,... | collective-permute-start | bytes 786440 | tf_op jit(solution)/shard_map/ppermute | solution.py:45
  509.4 25.6 %collective-permute-start.56 = (bf16[256,2048]{1,0:T(8,128)(2,1)}, bf16[256,2048]{1,0:T(8,128)(2,1)}, u32[]{:S(2)}, u32[]{:S(2)}) collective-permute-start(bf16[256,2048]{1,0:T(8,128)(2,1)} %get-tuple-element.379), channel_id=1, source_target_pairs={{0,1},{1,0},{2,3},{3,2},{4,5},{5,4},{6,7},{7,6},{8,9},{9,8},{10,11... | collective-permute-start | bytes 3145736 | tf_op jit(solution)/shard_map/ppermute | solution.py:37
  509.9 25.2 %collective-permute-start.57 = (bf16[256,2048]{1,0:T(8,128)(2,1)}, bf16[256,2048]{1,0:T(8,128)(2,1)}, u32[]{:S(2)}, u32[]{:S(2)}) collective-permute-start(bf16[256,2048]{1,0:T(8,128)(2,1)} %get-tuple-element.380), channel_id=1, source_target_pairs={{0,4},{4,0},{2,6},{6,2},{1,5},{5,1},{3,7},{7,3},{8,12},{12,8},{10,... | collective-permute-start | bytes 3145736 | tf_op jit(solution)/shard_map/ppermute | solution.py:45
  511.5 10.6 %collective-permute-start.58 = (bf16[512,256]{1,0:T(8,128)(2,1)S(1)}, bf16[512,256]{1,0:T(8,128)(2,1)S(1)}, u32[]{:S(2)}, u32[]{:S(2)}) collective-permute-start(bf16[512,256]{1,0:T(8,128)(2,1)S(1)} %copy-done.30), channel_id=1, source_target_pairs={{0,2},{2,0},{4,6},{6,4},{1,3},{3,1},{5,7},{7,5},{8,10},{10,8},{12,... | collective-permute-start | bytes 786440 | tf_op jit(solution)/shard_map/ppermute | solution.py:41
  514.8 7.3 %collective-permute-start.59 = (bf16[512,256]{1,0:T(8,128)(2,1)S(1)}, bf16[512,256]{1,0:T(8,128)(2,1)}, u32[]{:S(2)}, u32[]{:S(2)}) collective-permute-start(bf16[512,256]{1,0:T(8,128)(2,1)S(1)} %collective-permute-done.55.refs_2_), channel_id=1, source_target_pairs={{0,2},{2,0},{4,6},{6,4},{1,3},{3,1},{5,7},{7,5},{8,10},{10,8},{12,... | collective-permute-start | bytes 786440 | tf_op jit(solution)/shard_map/ppermute | solution.py:41
  536.4 13.3 %collective-permute-start.61 = (bf16[128,2048]{1,0:T(8,128)(2,1)S(1)}, bf16[128,2048]{1,0:T(8,128)(2,1)}, u32[]{:S(2)}, u32[]{:S(2)}) collective-permute-start(bf16[128,2048]{1,0:T(8,128)(2,1)S(1)} %add_convert_fusion.4), channel_id=1, source_target_pairs={{0,4},{4,0},{2,6},{6,2},{1,5},{5,1},{3,7},{7,3},{8,12},{12,8},{10,... | collective-permute-start | bytes 1572872 | tf_op jit(solution)/shard_map/ppermute | solution.py:45
  539.0 12.9 %collective-permute-start.60 = (bf16[128,2048]{1,0:T(8,128)(2,1)S(1)}, bf16[128,2048]{1,0:T(8,128)(2,1)S(1)}, u32[]{:S(2)}, u32[]{:S(2)}) collective-permute-start(bf16[128,2048]{1,0:T(8,128)(2,1)S(1)} %add_convert_fusion.5), channel_id=1, source_target_pairs={{0,1},{1,0},{2,3},{3,2},{4,5},{5,4},{6,7},{7,6},{8,9},{9,8},{10,11... | collective-permute-start | bytes 1572872 | tf_op jit(solution)/shard_map/ppermute | solution.py:37
  559.6 28.5 %collective-permute-start.62 = (bf16[256,2048]{1,0:T(8,128)(2,1)S(1)}, bf16[256,2048]{1,0:T(8,128)(2,1)S(1)}, u32[]{:S(2)}, u32[]{:S(2)}) collective-permute-start(bf16[256,2048]{1,0:T(8,128)(2,1)S(1)} %add_convert_fusion.1), channel_id=1, source_target_pairs={{0,1},{1,0},{2,3},{3,2},{4,5},{5,4},{6,7},{7,6},{8,9},{9,8},{10,11... | collective-permute-start | bytes 3145736 | tf_op jit(solution)/shard_map/ppermute | solution.py:37
  561.1 27.0 %collective-permute-start.67 = (bf16[512,768]{1,0:T(8,128)(2,1)}, bf16[512,768]{1,0:T(8,128)(2,1)S(1)}, u32[]{:S(2)}, u32[]{:S(2)}) collective-permute-start(bf16[512,768]{1,0:T(8,128)(2,1)} %reduce-scatter.11.cloned.1.call-done.refs_0_), channel_id=1, source_target_pairs={{0,2},{2,0},{4,6},{6,4},{1,3},{3,1},{5,7},{7,5},{8,10},{10,8},{12,... | collective-permute-start | bytes 2359304 | tf_op jit(solution)/shard_map/ppermute | solution.py:41
  561.1 27.0 %collective-permute-start.66 = (bf16[512,768]{1,0:T(8,128)(2,1)}, bf16[512,768]{1,0:T(8,128)(2,1)}, u32[]{:S(2)}, u32[]{:S(2)}) collective-permute-start(bf16[512,768]{1,0:T(8,128)(2,1)} %reduce-scatter.11.cloned.1.call-done.refs_0_), channel_id=1, source_target_pairs={{0,4},{4,0},{2,6},{6,2},{1,5},{5,1},{3,7},{7,3},{8,12},{12,8},{10,... | collective-permute-start | bytes 2359304 | tf_op jit(solution)/shard_map/ppermute | solution.py:45
  563.6 19.8 %collective-permute-start.64 = (f32[4,6144]{1,0:T(4,128)S(1)}, f32[4,6144]{1,0:T(4,128)S(1)}, u32[]{:S(2)}, u32[]{:S(2)}) collective-permute-start(f32[4,6144]{1,0:T(4,128)S(1)} %add.257), channel_id=1, source_target_pairs={{0,4},{4,0},{2,6},{6,2},{1,5},{5,1},{3,7},{7,3},{8,12},{12,8},{10,... | collective-permute-start | bytes 294920 | tf_op jit(solution)/shard_map/ppermute | solution.py:45
  588.3 10.3 %collective-permute-start.70 = (f32[1,6144]{1,0:T(1,128)S(1)}, f32[1,6144]{1,0:T(1,128)S(1)}, u32[]{:S(2)}, u32[]{:S(2)}) collective-permute-start(f32[1,6144]{1,0:T(1,128)S(1)} %get-tuple-element.443), channel_id=1, source_target_pairs={{0,24},{8,0},{16,8},{24,16},{1,25},{9,1},{17,9},{25,17},{2,26},{10... | collective-permute-start | bytes 73736 | tf_op jit(solution)/shard_map/ppermute | solution.py:1021
  590.1 8.5 %collective-permute-start.69 = (f32[1,6144]{1,0:T(1,128)S(1)}, f32[1,6144]{1,0:T(1,128)S(1)}, u32[]{:S(2)}, u32[]{:S(2)}) collective-permute-start(f32[1,6144]{1,0:T(1,128)S(1)} %get-tuple-element.444), channel_id=1, source_target_pairs={{0,16},{8,24},{16,0},{24,8},{1,17},{9,25},{17,1},{25,9},{2,18},{10... | collective-permute-start | bytes 73736 | tf_op jit(solution)/shard_map/ppermute | solution.py:1021
  590.3 8.3 %collective-permute-start.68 = (f32[1,6144]{1,0:T(1,128)S(1)}, f32[1,6144]{1,0:T(1,128)S(1)}, u32[]{:S(2)}, u32[]{:S(2)}) collective-permute-start(f32[1,6144]{1,0:T(1,128)S(1)} %get-tuple-element.445), channel_id=1, source_target_pairs={{0,8},{8,16},{16,24},{24,0},{1,9},{9,17},{17,25},{25,1},{2,10},{10... | collective-permute-start | bytes 73736 | tf_op jit(solution)/shard_map/ppermute | solution.py:1021
  (70 other events, 690.3 us)
Sparse Core Ops, SparseCore 0:
  10.2 83.4 all-gather.2
  96.0 150.2 all-gather.4
  296.0 75.0 reduce-scatter.4
  382.0 73.7 reduce-scatter.6
  473.5 24.3 reduce-scatter.8
  500.1 58.8 reduce-scatter.10

commit v6 on v5

--- a/solution.py
+++ b/solution.py
@@ -310,7 +310,7 @@
 def grad_matmul(lefts, starts, right, rows, name):
     d = lefts[0].shape[1]
     total_rows, n = right.shape
-    tile = 512
+    tile = 1024
     pieces = [(start, p.shape[0]) for start, p in zip(starts, lefts)]
     return pl.pallas_call(
         partial(grad_matmul_kernel, pieces, rows, tile),
@@ -358,7 +358,7 @@
 def partial_blocks(left, rows, weights, column, arrived, name):
     k = left.shape[1]
     d = weights.shape[0]
-    tile = 512
+    tile = 1024
     pair = 2 * rows
     if arrived is None:
         first, kernel, more = 1, sent_kernel, []
@@ -951,10 +951,10 @@
     result = (middle + (scatter_sum(mlp_sums, mlp_first, mlp_second) + dbias)).astype(BF)
     parts, result, dqkv, down_high = stage(parts, result, dqkv, swap_high(down_piece))
     qkv_term = grad_matmul(act_pieces, act_starts, dqkv, 2 * rows, "attention_weight_term")
+    dqkv, parts, result_other, up_high, out_piece, qkv_term = stage(
+        dqkv, swap_low(parts), swap_tp(result), swap_high(up_piece), out_piece, qkv_term
+    )
     qkv_piece = lax.psum_scatter(qkv_term, "fsdp", scatter_dimension=0, tiled=True)
-    dqkv, parts, result_other, up_high, out_piece = stage(
-        dqkv, swap_low(parts), swap_tp(result), swap_high(up_piece), out_piece
-    )
     sums = partial_blocks(dqkv, rows, attn_full, 0, parts, "act_one_kept")
     sums, up_far, down_low, down_far, up_low, out_high = stage(
         sums,

time: 613 us -> 611 us (level)
    ppermute x20, waiting for transfers between devices: 114 us -> 104 us  [swap_high(): return lax.ppermute(value, 'ctx', [(0, 2), (2, 0), (1, 3), (3, 1)])]
    reduce_scatter x1, waiting for transfers between devices: 0.01 us -> 9.51 us  [body(): lax.psum_scatter(out_term, 'fsdp', scatter_dimension=0, tiled=True)]
  transfers between devices with their start and end apart: 78 -> 78, of which waited for: 41 -> 43; matrix products, arithmetic and copies ran while one was open for 10% -> 10% of each run, Pallas kernels for 29% -> 28%
where the time goes in v6:
time: 611 us; the launch traced here: 606 us
  waiting for transfers between devices  255 us (42%)
  Pallas kernels  209 us (34%)
  starting transfers between devices  57.4 us (9%)
  other arithmetic  46.1 us (8%)
  local copies, waits for them, and re-layouts  22.5 us (4%)
  between operations  16.1 us (3%)
    ppermute x16, waiting for transfers between devices, swap_tp(): return lax.ppermute(value, 'tp', [(0, 1), (1, 0)])  113 us
    ppermute x20, waiting for transfers between devices, swap_high(): return lax.ppermute(value, 'ctx', [(0, 2), (2, 0), (1, 3), (3, 1)])  104 us
    pallas_call x8, Pallas kernels, partial_blocks(): pl.pallas_call(partial(kernel, rows), grid=(d // tile,), in_specs=[pl.Blo...  57.4 us
    pallas_call x3, Pallas kernels, grad_matmul(): pl.pallas_call(partial(grad_matmul_kernel, pieces, rows, tile), grid=(d /...  41.7 us
    pallas_call x1, Pallas kernels, feed_both(): pl.pallas_call(partial(feed_kernel, act_pieces, up_pieces, rows), grid=(u...  26.7 us
    ppermute x20, starting transfers between devices, swap_high(): return lax.ppermute(value, 'ctx', [(0, 2), (2, 0), (1, 3), (3, 1)])  25.4 us
    pallas_call x1, Pallas kernels, attention_backward(): pl.pallas_call(partial(attention_backward_kernel, blocks // 2, rows, cont...  21.4 us
    pallas_call x4, Pallas kernels, assemble(): pl.pallas_call(partial(assemble_kernel, turn, count, width), grid_spec=pl...  20.5 us
  transfers between devices with their start and end apart: 78, of which 43 were waited for; matrix products, arithmetic and copies ran while one was open for 10% of the time, Pallas kernels for 28%

profile of v6, /device:TPU:0, one launch (start us, length us, event | category | flops | bytes accessed | tf_op | source)
XLA Modules:
  0.0 606.2 jit_solution(15981217116414166516)
XLA Ops:
  7.3 2.3 attention_shard.1
  9.7 1.7 bitcast_select_fusion.1
  13.7 5.0 collective-permute-start.5
  19.8 3.1 convert_reduce_fusion.2
  25.8 2.9 pad_maximum_fusion.1.refs_10_.refs_0_
  28.7 3.2 feed_shard.1
  32.7 4.2 subtract_multiply_fusion
  36.9 10.3 %collective-permute-done.6.refs_12_.refs_2_ = bf16[256,2048]{1,0:T(8,128)(2,1)} collective-permute-done((bf16[256,2048]{1,0:T(8,128)(2,1)}, bf16[256,2048]{1,0:T(8,128)(2,1)}, u32[]{:S(2)}, u32[]{:S(2)}) %collective-permute-start.6) | collective-permute-done | bytes 1048608 | tf_op jit(solution)/shard_map/ppermute | solution.py:45
  50.5 2.6 collective-permute-done.11.refs_14_.refs_4_
  53.1 21.4 %collective-permute-done.9.refs_13_.refs_3_ = bf16[256,2048]{1,0:T(8,128)(2,1)S(1)} collective-permute-done((bf16[256,2048]{1,0:T(8,128)(2,1)}, bf16[256,2048]{1,0:T(8,128)(2,1)S(1)}, u32[]{:S(2)}, u32[]{:S(2)}) %collective-permute-start.9) | collective-permute-done | bytes 1048608 | tf_op jit(solution)/shard_map/ppermute | solution.py:37
  74.5 20.8 %collective-permute-done.7.refs_2_ = bf16[512,2048]{1,0:T(8,128)(2,1)} collective-permute-done((bf16[512,2048]{1,0:T(8,128)(2,1)S(1)}, bf16[512,2048]{1,0:T(8,128)(2,1)}, u32[]{:S(2)}, u32[]{:S(2)}) %collective-permute-start.7) | collective-permute-done | bytes 2097184 | tf_op jit(solution)/shard_map/ppermute | solution.py:45
  102.4 12.4 %heads.1 = bf16[2048,768]{1,0:T(8,128)(2,1)} custom-call(bf16[512,2048]{1,0:T(8,128)(2,1)} %copy-done.20, bf16[512,2048]{1,0:T(8,128)(2,1)} %copy-done.42, bf16[512,2048]{1,0:T(8,128)(2,1)} %collective-permute-done.7.refs_2_, bf16[512,2048]{1,0:T(8,128)(2,1)} %collective-permute-done.12.refs_3_, ...), custom_call_target="tpu_custom_call" | custom-call | flops 6442450944 | bytes 14680064 | tf_op jit(solution)/shard_map/heads/pallas_call | solution.py:422
  114.8 1.9 copy-done.5
  116.7 11.0 %attention_forward.1 = bf16[8,256,256]{2,1,0:T(8,128)(2,1)S(1)} custom-call(s32[10]{0:T(128)S(1)} %concatenate.47.info_ref, bf16[8,256,768]{2,1,0:T(8,128)(2,1)S(1)} %bitcast.93), custom_call_target="tpu_custom_call" | custom-call | flops 2013265920 | bytes 4194304 | tf_op jit(solution)/shard_map/attention_forward/pallas_call | solution.py:222
  128.6 4.0 attention_sent.1
  133.0 7.2 %collective-permute-done.14.arrived_ref = bf16[1024,2048]{1,0:T(8,128)(2,1)} collective-permute-done((bf16[1024,2048]{1,0:T(8,128)(2,1)}, bf16[1024,2048]{1,0:T(8,128)(2,1)}, u32[]{:S(2)}, u32[]{:S(2)}) %collective-permute-start.14) | collective-permute-done | bytes 4194336 | tf_op jit(solution)/shard_map/ppermute | solution.py:41
  140.2 4.7 attention_kept.1
  144.8 1.6 collective-permute-start.15
  148.0 22.5 %collective-permute-done.15 = bf16[256,2048]{1,0:T(8,128)(2,1)S(1)} collective-permute-done((bf16[256,2048]{1,0:T(8,128)(2,1)}, bf16[256,2048]{1,0:T(8,128)(2,1)S(1)}, u32[]{:S(2)}, u32[]{:S(2)}) %collective-permute-start.15) | collective-permute-done | bytes 1048608 | tf_op jit(solution)/shard_map/ppermute | solution.py:37
  172.8 1.6 collective-permute-start.18
  176.9 9.0 %collective-permute-done.18 = bf16[128,2048]{1,0:T(8,128)(2,1)S(1)} collective-permute-done((bf16[128,2048]{1,0:T(8,128)(2,1)S(1)}, bf16[128,2048]{1,0:T(8,128)(2,1)S(1)}, u32[]{:S(2)}, u32[]{:S(2)}) %collective-permute-start.18) | collective-permute-done | bytes 524320 | tf_op jit(solution)/shard_map/ppermute | solution.py:45
  185.9 2.5 collective-permute-done.17
  193.1 22.9 %collective-permute-done.20.refs_3_ = bf16[256,2048]{1,0:T(8,128)(2,1)S(1)} collective-permute-done((bf16[256,2048]{1,0:T(8,128)(2,1)S(1)}, bf16[256,2048]{1,0:T(8,128)(2,1)S(1)}, u32[]{:S(2)}, u32[]{:S(2)}) %collective-permute-start.20) | collective-permute-done | bytes 1048608 | tf_op jit(solution)/shard_map/ppermute | solution.py:45
  219.1 11.7 %collective-permute-done.23.refs_7_ = bf16[128,2048]{1,0:T(8,128)(2,1)S(1)} collective-permute-done((bf16[128,2048]{1,0:T(8,128)(2,1)S(1)}, bf16[128,2048]{1,0:T(8,128)(2,1)S(1)}, u32[]{:S(2)}, u32[]{:S(2)}) %collective-permute-start.23) | collective-permute-done | bytes 524320 | tf_op jit(solution)/shard_map/ppermute | solution.py:37
  234.1 12.3 %all-gather.5.cloned.1.call-done.refs_16_.refs_17_.w_ref = bf16[2048,2048]{1,0:T(8,128)(2,1)} async-done(((bf16[512,2048]{1,0:T(8,128)(2,1)}), bf16[2048,2048]{1,0:T(8,128)(2,1)}) %all-gather.5.cloned.1.call-update) | async-done | bytes 8388624 | tf_op jit(solution)/shard_map/all_gather | solution.py:821
  246.4 26.7 %feed_both.1 = (bf16[2048,1024]{1,0:T(8,128)(2,1)}, bf16[2048,1024]{1,0:T(8,128)(2,1)}, f32[1,1024]{1,0:T(1,128)}) custom-call(bf16[256,2048]{1,0:T(8,128)(2,1)} %copy-done.22, bf16[256,2048]{1,0:T(8,128)(2,1)} %copy-done.45, bf16[256,2048]{1,0:T(8,128)(2,1)} %copy-done.30, bf16[256,2048]{1,0:T(8,128)(2,1)} %copy-done.29, bf16[256,2048]{1,0:T(8,128)(2,1)} %copy-done.46, ...), custom_call_target="tpu_custom_call" | custom-call | flops 17179869184 | bytes 33554432 | tf_op jit(solution)/shard_map/feed_both/pallas_call | solution.py:655
  273.1 8.3 %act_two_sent.1 = bf16[1024,2048]{1,0:T(8,128)(2,1)} custom-call(bf16[2048,1024]{1,0:T(8,128)(2,1)} %get-tuple-element.316.low_ref.high_ref.refs_10_, bf16[2048,1024]{1,0:T(8,128)(2,1)} %get-tuple-element.316.low_ref.high_ref.refs_10_, bf16[2048,2048]{1,0:T(8,128)(2,1)} %all-gather.5.cloned.1.call-done.refs_16_.refs_17_.w_ref), custom_call_target="tpu_custom_call" | custom-call | flops 4294967296 | bytes 10485760 | tf_op jit(solution)/shard_map/act_two_sent/pallas_call | solution.py:369
  281.5 14.3 %down_weight_term.1 = bf16[2048,1024]{1,0:T(8,128)(2,1)} custom-call(bf16[512,2048]{1,0:T(8,128)(2,1)} %pad_maximum_fusion.1.refs_10_.refs_0_, bf16[512,2048]{1,0:T(8,128)(2,1)} %collective-permute-done.10.refs_11_.refs_1_, bf16[256,2048]{1,0:T(8,128)(2,1)} %collective-permute-done.6.refs_12_.refs_2_, bf16[256,2048]{1,0:T(8,128)(2,1)} %copy-done.44, ...), custom_call_target="tpu_custom_call" | custom-call | flops 8589934592 | bytes 16777216 | tf_op jit(solution)/shard_map/down_weight_term/pallas_call | solution.py:315
  295.8 9.1 %act_two_kept.1 = (f32[256,2048]{1,0:T(8,128)}, bf16[128,2048]{1,0:T(8,128)(2,1)}, bf16[256,2048]{1,0:T(8,128)(2,1)}, bf16[256,2048]{1,0:T(8,128)(2,1)}, bf16[128,2048]{1,0:T(8,128)(2,1)}) custom-call(bf16[2048,1024]{1,0:T(8,128)(2,1)} %get-tuple-element.316.low_ref.high_ref.refs_10_, bf16[2048,1024]{1,0:T(8,128)(2,1)} %get-tuple-element.316.low_ref.high_ref.refs_10_, ...), custom_call_target="tpu_custom_call" | custom-call | flops 4294967296 | bytes 10485760 | tf_op jit(solution)/shard_map/act_two_kept/pallas_call | solution.py:369
  308.0 8.3 %feed_sent.1 = bf16[1024,2048]{1,0:T(8,128)(2,1)} custom-call(bf16[2048,1024]{1,0:T(8,128)(2,1)} %get-tuple-element.309.refs_6_.low_ref.high_ref, bf16[2048,1024]{1,0:T(8,128)(2,1)} %get-tuple-element.309.refs_6_.low_ref.high_ref, bf16[2048,2048]{1,0:T(8,128)(2,1)} %all-gather.5.cloned.1.call-done.refs_16_.refs_17_.w_ref), custom_call_target="tpu_custom_call" | custom-call | flops 4294967296 | bytes 10485760 | tf_op jit(solution)/shard_map/feed_sent/pallas_call | solution.py:369
  316.3 14.5 %collective-permute-done.29 = bf16[256,2048]{1,0:T(8,128)(2,1)S(1)} collective-permute-done((bf16[256,2048]{1,0:T(8,128)(2,1)}, bf16[256,2048]{1,0:T(8,128)(2,1)S(1)}, u32[]{:S(2)}, u32[]{:S(2)}) %collective-permute-start.29) | collective-permute-done | bytes 1048608 | tf_op jit(solution)/shard_map/ppermute | solution.py:37
  337.9 9.9 %collective-permute-done.32 = bf16[128,2048]{1,0:T(8,128)(2,1)S(1)} collective-permute-done((bf16[128,2048]{1,0:T(8,128)(2,1)S(1)}, bf16[128,2048]{1,0:T(8,128)(2,1)S(1)}, u32[]{:S(2)}, u32[]{:S(2)}) %collective-permute-start.32) | collective-permute-done | bytes 524320 | tf_op jit(solution)/shard_map/ppermute | solution.py:45
  347.8 2.5 collective-permute-done.31
  351.6 3.5 fusion.1
  356.4 8.7 %feed_kept.1 = (f32[256,2048]{1,0:T(8,128)}, bf16[128,2048]{1,0:T(8,128)(2,1)}, bf16[256,2048]{1,0:T(8,128)(2,1)}, bf16[256,2048]{1,0:T(8,128)(2,1)}, bf16[128,2048]{1,0:T(8,128)(2,1)}) custom-call(bf16[2048,1024]{1,0:T(8,128)(2,1)} %get-tuple-element.309.refs_6_.low_ref.high_ref, bf16[2048,1024]{1,0:T(8,128)(2,1)} %get-tuple-element.309.refs_6_.low_ref.high_ref, ...), custom_call_target="tpu_custom_call" | custom-call | flops 4294967296 | bytes 10485760 | tf_op jit(solution)/shard_map/feed_kept/pallas_call | solution.py:369
  365.1 14.8 %up_weight_term.1 = bf16[2048,1024]{1,0:T(8,128)(2,1)} custom-call(bf16[256,2048]{1,0:T(8,128)(2,1)} %copy-done.22, bf16[256,2048]{1,0:T(8,128)(2,1)} %copy-done.45, bf16[256,2048]{1,0:T(8,128)(2,1)} %copy-done.30, bf16[256,2048]{1,0:T(8,128)(2,1)} %copy-done.29, bf16[256,2048]{1,0:T(8,128)(2,1)} %copy-done.46, bf16[256,2048]{1,0:T(8,128)(2,1)} %copy-done.47, ...), custom_call_target="tpu_custom_call" | custom-call | flops 8589934592 | bytes 16777216 | tf_op jit(solution)/shard_map/up_weight_term/pallas_call | solution.py:315
  385.9 12.1 %collective-permute-done.38.refs_7_ = bf16[128,2048]{1,0:T(8,128)(2,1)S(1)} collective-permute-done((bf16[128,2048]{1,0:T(8,128)(2,1)S(1)}, bf16[128,2048]{1,0:T(8,128)(2,1)S(1)}, u32[]{:S(2)}, u32[]{:S(2)}) %collective-permute-start.38) | collective-permute-done | bytes 524320 | tf_op jit(solution)/shard_map/ppermute | solution.py:37
  404.7 12.0 %middle_terms.1 = (bf16[2048,256]{1,0:T(8,128)(2,1)}, bf16[2048,256]{1,0:T(8,128)(2,1)}) custom-call(bf16[256,2048]{1,0:T(8,128)(2,1)} %copy-done.13, bf16[256,2048]{1,0:T(8,128)(2,1)} %collective-permute-done.36.refs_1_, bf16[256,2048]{1,0:T(8,128)(2,1)} %collective-permute-done.34.refs_2_, bf16[256,2048]{1,0:T(8,128)(2,1)} %collective-permute-done.35.refs_3_, ...), custom_call_target="tpu_custom_call" | custom-call | flops 4294967296 | bytes 12582912 | tf_op jit(solution)/shard_map/middle_terms/pallas_call | solution.py:480
  416.7 9.9 %collective-permute-done.43 = bf16[256,2048]{1,0:T(8,128)(2,1)} collective-permute-done((bf16[256,2048]{1,0:T(8,128)(2,1)}, bf16[256,2048]{1,0:T(8,128)(2,1)}, u32[]{:S(2)}, u32[]{:S(2)}) %collective-permute-start.43) | collective-permute-done | bytes 1048608 | tf_op jit(solution)/shard_map/ppermute | solution.py:37
  426.6 2.2 collective-permute-done.44
  428.8 1.8 add_convert_fusion.6
  433.8 21.4 %attention_backward.1 = bf16[8,256,768]{2,1,0:T(8,128)(2,1)S(1)} custom-call(s32[10]{0:T(128)S(1)} %concatenate.47.info_ref, bf16[8,256,768]{2,1,0:T(8,128)(2,1)S(1)} %bitcast.94, bf16[8,256,256]{2,1,0:T(8,128)(2,1)S(1)} %bitcast.95), custom_call_target="tpu_custom_call" | custom-call | flops 7046430720 | bytes 7340032 | tf_op jit(solution)/shard_map/attention_backward/pallas_call | solution.py:240
  455.3 1.7 copy-done.2
  457.0 1.9 slice.194
  458.9 2.6 collective-permute-done.46
  461.5 6.9 %act_one_sent.1 = bf16[1024,2048]{1,0:T(8,128)(2,1)} custom-call(bf16[2048,768]{1,0:T(8,128)(2,1)} %bitcast.82, bf16[2048,768]{1,0:T(8,128)(2,1)} %bitcast.83, bf16[2048,1024]{1,0:T(8,128)(2,1)} %all-gather.3.cloned.1.call-done.refs_4_.w_ref.refs_11_), custom_call_target="tpu_custom_call" | custom-call | flops 3221225472 | bytes 8912896 | tf_op jit(solution)/shard_map/act_one_sent/pallas_call | solution.py:369
  468.4 3.3 add_convert_fusion.2
  474.1 12.7 %attention_weight_term.1 = bf16[2048,768]{1,0:T(8,128)(2,1)} custom-call(bf16[512,2048]{1,0:T(8,128)(2,1)} %copy-done.20, bf16[512,2048]{1,0:T(8,128)(2,1)} %copy-done.42, bf16[512,2048]{1,0:T(8,128)(2,1)} %collective-permute-done.7.refs_2_, bf16[512,2048]{1,0:T(8,128)(2,1)} %collective-permute-done.12.refs_3_, bf16[2048,768]{1,0:T(8,128)(2,1)} %bitcast.84), custom_call_target="tpu_custom_call" | custom-call | flops 6442450944 | bytes 14680064 | tf_op jit(solution)/shard_map/attention_weight_term/pallas_call | solution.py:315
  486.8 9.5 %reduce-scatter.9.cloned.1.call-done.refs_0_ = bf16[512,256]{1,0:T(8,128)(2,1)} async-done(((bf16[2048,256]{1,0:T(8,128)(2,1)}), bf16[512,256]{1,0:T(8,128)(2,1)}) %reduce-scatter.9.cloned.1.call-update) | async-done | bytes 262160 | tf_op jit(solution)/shard_map/reduce_scatter | solution.py:945
  496.3 1.9 collective-permute-done.50.refs_2_
  500.9 7.4 %act_one_kept.1 = (f32[256,2048]{1,0:T(8,128)}, bf16[128,2048]{1,0:T(8,128)(2,1)}, bf16[256,2048]{1,0:T(8,128)(2,1)}, bf16[256,2048]{1,0:T(8,128)(2,1)}, bf16[128,2048]{1,0:T(8,128)(2,1)}) custom-call(bf16[2048,768]{1,0:T(8,128)(2,1)} %bitcast.85, bf16[2048,768]{1,0:T(8,128)(2,1)} %bitcast.86, ...), custom_call_target="tpu_custom_call" | custom-call | flops 3221225472 | bytes 8912896 | tf_op jit(solution)/shard_map/act_one_kept/pallas_call | solution.py:369
  510.5 3.2 broadcast_select_fusion.1
  514.5 6.4 %down_weight_grad.1 = f32[4096,512]{1,0:T(8,128)} custom-call(s32[1]{0:T(128)} %bitcast.ctx_ref, bf16[512,1024]{1,0:T(8,128)(2,1)} %reduce-scatter.5.cloned.1.call-done.refs_0_, bf16[512,1024]{1,0:T(8,128)(2,1)} %collective-permute-done.52.refs_1_, bf16[512,1024]{1,0:T(8,128)(2,1)} %collective-permute-done.47.refs_2_, ...), custom_call_target="tpu_custom_call" | custom-call | bytes 12582912 | tf_op jit(solution)/shard_map/down_weight_grad/pallas_call | solution.py:563
  521.6 3.4 output_weight_grad.1
  525.0 8.4 %collective-permute-done.56 = bf16[256,2048]{1,0:T(8,128)(2,1)} collective-permute-done((bf16[256,2048]{1,0:T(8,128)(2,1)}, bf16[256,2048]{1,0:T(8,128)(2,1)}, u32[]{:S(2)}, u32[]{:S(2)}) %collective-permute-start.56) | collective-permute-done | bytes 1048608 | tf_op jit(solution)/shard_map/ppermute | solution.py:37
  539.5 5.8 up_weight_grad.1
  547.6 2.1 collective-permute-done.60
  550.5 3.9 multiply_reduce_fusion.2
  554.6 2.8 add_convert_fusion.1
  563.0 18.3 %collective-permute-done.64 = f32[4,6144]{1,0:T(4,128)S(1)} collective-permute-done((f32[4,6144]{1,0:T(4,128)S(1)}, f32[4,6144]{1,0:T(4,128)S(1)}, u32[]{:S(2)}, u32[]{:S(2)}) %collective-permute-start.64) | collective-permute-done | bytes 98336 | tf_op jit(solution)/shard_map/ppermute | solution.py:45
  581.9 4.1 collective-permute-done.65
  586.2 2.4 collective-permute-start.70
  588.8 1.9 collective-permute-start.68
  592.2 4.9 attention_weight_grads.1
  (344 shorter events, 91.8 us)
Async XLA Ops:
  7.2 95.2 %all-gather.3.cloned.1.call-start = ((), (), s32[]{:S(2)}) async-start(), calls=%async_computation.4 | async-start | bytes 5242880 | tf_op jit(solution)/shard_map/all_gather | solution.py:768
  9.6 236.8 %all-gather.5.cloned.1.call-start = ((), (), s32[]{:S(2)}) async-start(), calls=%async_computation.5 | async-start | bytes 10485760 | tf_op jit(solution)/shard_map/all_gather | solution.py:821
  13.7 18.8 %collective-permute-start.5 = (bf16[3456]{0:T(1024)(128)(2,1)S(1)}, bf16[3456]{0:T(1024)(128)(2,1)S(1)}, u32[]{:S(2)}, u32[]{:S(2)}) collective-permute-start(bf16[3456]{0:T(1024)(128)(2,1)S(1)} %concatenate.48), channel_id=1, source_target_pairs={{0,24},{8,0},{16,8},{24,16},{1,25},{9,1},{17,9},{25,17},{2,26},{10... | collective-permute-start | bytes 20744 | tf_op jit(solution)/shard_map/ppermute | solution.py:696
  18.7 13.6 %collective-permute-start.4 = (bf16[3456]{0:T(1024)(128)(2,1)S(1)}, bf16[3456]{0:T(1024)(128)(2,1)S(1)}, u32[]{:S(2)}, u32[]{:S(2)}) collective-permute-start(bf16[3456]{0:T(1024)(128)(2,1)S(1)} %concatenate.48), channel_id=1, source_target_pairs={{0,16},{8,24},{16,0},{24,8},{1,17},{9,25},{17,1},{25,9},{2,18},{10... | collective-permute-start | bytes 20744 | tf_op jit(solution)/shard_map/ppermute | solution.py:696
  18.7 13.4 %collective-permute-start.3 = (bf16[3456]{0:T(1024)(128)(2,1)S(1)}, bf16[3456]{0:T(1024)(128)(2,1)S(1)}, u32[]{:S(2)}, u32[]{:S(2)}) collective-permute-start(bf16[3456]{0:T(1024)(128)(2,1)S(1)} %concatenate.48), channel_id=1, source_target_pairs={{0,8},{8,16},{16,24},{24,0},{1,9},{9,17},{17,25},{25,1},{2,10},{10... | collective-permute-start | bytes 20744 | tf_op jit(solution)/shard_map/ppermute | solution.py:696
  22.9 24.3 %collective-permute-start.6 = (bf16[256,2048]{1,0:T(8,128)(2,1)}, bf16[256,2048]{1,0:T(8,128)(2,1)}, u32[]{:S(2)}, u32[]{:S(2)}) collective-permute-start(bf16[256,2048]{1,0:T(8,128)(2,1)} %get-tuple-element.430), channel_id=1, source_target_pairs={{0,4},{4,0},{2,6},{6,2},{1,5},{5,1},{3,7},{7,3},{8,12},{12,8},{10,... | collective-permute-start | bytes 3145736 | tf_op jit(solution)/shard_map/ppermute | solution.py:45
  28.7 21.8 %collective-permute-start.10 = (bf16[512,2048]{1,0:T(8,128)(2,1)}, bf16[512,2048]{1,0:T(8,128)(2,1)}, u32[]{:S(2)}, u32[]{:S(2)}) collective-permute-start(bf16[512,2048]{1,0:T(8,128)(2,1)} %pad_maximum_fusion.1.refs_10_.refs_0_), channel_id=1, source_target_pairs={{0,2},{2,0},{4,6},{6,4},{1,3},{3,1},{5,7},{7,5},{8,10},{10,8},{12,... | collective-permute-start | bytes 6291464 | tf_op jit(solution)/shard_map/ppermute | solution.py:41
  47.2 27.3 %collective-permute-start.8 = (bf16[512,2048]{1,0:T(8,128)(2,1)S(1)}, bf16[512,2048]{1,0:T(8,128)(2,1)S(1)}, u32[]{:S(2)}, u32[]{:S(2)}) collective-permute-start(bf16[512,2048]{1,0:T(8,128)(2,1)S(1)} %get-tuple-element.244.refs_0_), channel_id=1, source_target_pairs={{0,2},{2,0},{4,6},{6,4},{1,3},{3,1},{5,7},{7,5},{8,10},{10,8},{12,... | collective-permute-start | bytes 6291464 | tf_op jit(solution)/shard_map/ppermute | solution.py:41
  47.2 48.1 %collective-permute-start.7 = (bf16[512,2048]{1,0:T(8,128)(2,1)S(1)}, bf16[512,2048]{1,0:T(8,128)(2,1)}, u32[]{:S(2)}, u32[]{:S(2)}) collective-permute-start(bf16[512,2048]{1,0:T(8,128)(2,1)S(1)} %get-tuple-element.244.refs_0_), channel_id=1, source_target_pairs={{0,4},{4,0},{2,6},{6,2},{1,5},{5,1},{3,7},{7,3},{8,12},{12,8},{10,... | collective-permute-start | bytes 6291464 | tf_op jit(solution)/shard_map/ppermute | solution.py:45
  49.0 25.6 %collective-permute-start.9 = (bf16[256,2048]{1,0:T(8,128)(2,1)}, bf16[256,2048]{1,0:T(8,128)(2,1)S(1)}, u32[]{:S(2)}, u32[]{:S(2)}) collective-permute-start(bf16[256,2048]{1,0:T(8,128)(2,1)} %collective-permute-done.6.refs_12_.refs_2_), channel_id=1, source_target_pairs={{0,1},{1,0},{2,3},{3,2},{4,5},{5,4},{6,7},{7,6},{8,9},{9,8},{10,11... | collective-permute-start | bytes 3145736 | tf_op jit(solution)/shard_map/ppermute | solution.py:37
  95.9 285.3 %reduce-scatter.5.cloned.1.call-start = ((), (), s32[]{:S(2)}) async-start(), calls=%async_computation.6 | async-start | bytes 5242880 | tf_op jit(solution)/shard_map/reduce_scatter | solution.py:911
  132.7 7.5 %collective-permute-start.14 = (bf16[1024,2048]{1,0:T(8,128)(2,1)}, bf16[1024,2048]{1,0:T(8,128)(2,1)}, u32[]{:S(2)}, u32[]{:S(2)}) collective-permute-start(bf16[1024,2048]{1,0:T(8,128)(2,1)} %attention_sent.1), channel_id=1, source_target_pairs={{0,2},{2,0},{4,6},{6,4},{1,3},{3,1},{5,7},{7,5},{8,10},{10,8},{12,... | collective-permute-start | bytes 12582920 | tf_op jit(solution)/shard_map/ppermute | solution.py:41
  144.8 25.6 %collective-permute-start.15 = (bf16[256,2048]{1,0:T(8,128)(2,1)}, bf16[256,2048]{1,0:T(8,128)(2,1)S(1)}, u32[]{:S(2)}, u32[]{:S(2)}) collective-permute-start(bf16[256,2048]{1,0:T(8,128)(2,1)} %get-tuple-element.251), channel_id=1, source_target_pairs={{0,1},{1,0},{2,3},{3,2},{4,5},{5,4},{6,7},{7,6},{8,9},{9,8},{10,11... | collective-permute-start | bytes 3145736 | tf_op jit(solution)/shard_map/ppermute | solution.py:37
  146.4 25.2 %collective-permute-start.16 = (bf16[256,2048]{1,0:T(8,128)(2,1)}, bf16[256,2048]{1,0:T(8,128)(2,1)S(1)}, u32[]{:S(2)}, u32[]{:S(2)}) collective-permute-start(bf16[256,2048]{1,0:T(8,128)(2,1)} %get-tuple-element.252), channel_id=1, source_target_pairs={{0,4},{4,0},{2,6},{6,2},{1,5},{5,1},{3,7},{7,3},{8,12},{12,8},{10,... | collective-permute-start | bytes 3145736 | tf_op jit(solution)/shard_map/ppermute | solution.py:45
  172.8 13.1 %collective-permute-start.18 = (bf16[128,2048]{1,0:T(8,128)(2,1)S(1)}, bf16[128,2048]{1,0:T(8,128)(2,1)S(1)}, u32[]{:S(2)}, u32[]{:S(2)}) collective-permute-start(bf16[128,2048]{1,0:T(8,128)(2,1)S(1)} %add_convert_fusion.10), channel_id=1, source_target_pairs={{0,4},{4,0},{2,6},{6,2},{1,5},{5,1},{3,7},{7,3},{8,12},{12,8},{10,... | collective-permute-start | bytes 1572872 | tf_op jit(solution)/shard_map/ppermute | solution.py:45
  175.6 12.8 %collective-permute-start.17 = (bf16[128,2048]{1,0:T(8,128)(2,1)S(1)}, bf16[128,2048]{1,0:T(8,128)(2,1)S(1)}, u32[]{:S(2)}, u32[]{:S(2)}) collective-permute-start(bf16[128,2048]{1,0:T(8,128)(2,1)S(1)} %add_convert_fusion.11), channel_id=1, source_target_pairs={{0,1},{1,0},{2,3},{3,2},{4,5},{5,4},{6,7},{7,6},{8,9},{9,8},{10,11... | collective-permute-start | bytes 1572872 | tf_op jit(solution)/shard_map/ppermute | solution.py:37
  190.4 25.6 %collective-permute-start.20 = (bf16[256,2048]{1,0:T(8,128)(2,1)S(1)}, bf16[256,2048]{1,0:T(8,128)(2,1)S(1)}, u32[]{:S(2)}, u32[]{:S(2)}) collective-permute-start(bf16[256,2048]{1,0:T(8,128)(2,1)S(1)} %add_convert_fusion.3.refs_0_), channel_id=1, source_target_pairs={{0,4},{4,0},{2,6},{6,2},{1,5},{5,1},{3,7},{7,3},{8,12},{12,8},{10,... | collective-permute-start | bytes 3145736 | tf_op jit(solution)/shard_map/ppermute | solution.py:45
  190.9 25.3 %collective-permute-start.19 = (bf16[256,2048]{1,0:T(8,128)(2,1)S(1)}, bf16[256,2048]{1,0:T(8,128)(2,1)S(1)}, u32[]{:S(2)}, u32[]{:S(2)}) collective-permute-start(bf16[256,2048]{1,0:T(8,128)(2,1)S(1)} %add_convert_fusion.3.refs_0_), channel_id=1, source_target_pairs={{0,1},{1,0},{2,3},{3,2},{4,5},{5,4},{6,7},{7,6},{8,9},{9,8},{10,11... | collective-permute-start | bytes 3145736 | tf_op jit(solution)/shard_map/ppermute | solution.py:37
  216.2 15.0 %collective-permute-start.24 = (bf16[256,2048]{1,0:T(8,128)(2,1)S(1)}, bf16[256,2048]{1,0:T(8,128)(2,1)S(1)}, u32[]{:S(2)}, u32[]{:S(2)}) collective-permute-start(bf16[256,2048]{1,0:T(8,128)(2,1)S(1)} %collective-permute-done.19.refs_2_), channel_id=1, source_target_pairs={{0,2},{2,0},{4,6},{6,4},{1,3},{3,1},{5,7},{7,5},{8,10},{10,8},{12,... | collective-permute-start | bytes 3145736 | tf_op jit(solution)/shard_map/ppermute | solution.py:41
  216.2 15.0 %collective-permute-start.25 = (bf16[256,2048]{1,0:T(8,128)(2,1)S(1)}, bf16[256,2048]{1,0:T(8,128)(2,1)S(1)}, u32[]{:S(2)}, u32[]{:S(2)}) collective-permute-start(bf16[256,2048]{1,0:T(8,128)(2,1)S(1)} %collective-permute-done.20.refs_3_), channel_id=1, source_target_pairs={{0,2},{2,0},{4,6},{6,4},{1,3},{3,1},{5,7},{7,5},{8,10},{10,8},{12,... | collective-permute-start | bytes 3145736 | tf_op jit(solution)/shard_map/ppermute | solution.py:41
  216.8 14.0 %collective-permute-start.23 = (bf16[128,2048]{1,0:T(8,128)(2,1)S(1)}, bf16[128,2048]{1,0:T(8,128)(2,1)S(1)}, u32[]{:S(2)}, u32[]{:S(2)}) collective-permute-start(bf16[128,2048]{1,0:T(8,128)(2,1)S(1)} %slice.184), channel_id=1, source_target_pairs={{0,1},{1,0},{2,3},{3,2},{4,5},{5,4},{6,7},{7,6},{8,9},{9,8},{10,11... | collective-permute-start | bytes 1572872 | tf_op jit(solution)/shard_map/ppermute | solution.py:37
  217.5 13.6 %collective-permute-start.22 = (bf16[128,2048]{1,0:T(8,128)(2,1)S(1)}, bf16[128,2048]{1,0:T(8,128)(2,1)S(1)}, u32[]{:S(2)}, u32[]{:S(2)}) collective-permute-start(bf16[128,2048]{1,0:T(8,128)(2,1)S(1)} %slice.183), channel_id=1, source_target_pairs={{0,4},{4,0},{2,6},{6,2},{1,5},{5,1},{3,7},{7,3},{8,12},{12,8},{10,... | collective-permute-start | bytes 1572872 | tf_op jit(solution)/shard_map/ppermute | solution.py:45
  281.4 14.3 %collective-permute-start.28 = (bf16[1024,2048]{1,0:T(8,128)(2,1)}, bf16[1024,2048]{1,0:T(8,128)(2,1)}, u32[]{:S(2)}, u32[]{:S(2)}) collective-permute-start(bf16[1024,2048]{1,0:T(8,128)(2,1)} %act_two_sent.1), channel_id=1, source_target_pairs={{0,2},{2,0},{4,6},{6,4},{1,3},{3,1},{5,7},{7,5},{8,10},{10,8},{12,... | collective-permute-start | bytes 12582920 | tf_op jit(solution)/shard_map/ppermute | solution.py:41
  295.8 165.7 %reduce-scatter.7.cloned.1.call-start = ((), (), s32[]{:S(2)}) async-start(), calls=%async_computation.7 | async-start | bytes 5242880 | tf_op jit(solution)/shard_map/reduce_scatter | solution.py:933
  304.9 25.8 %collective-permute-start.29 = (bf16[256,2048]{1,0:T(8,128)(2,1)}, bf16[256,2048]{1,0:T(8,128)(2,1)S(1)}, u32[]{:S(2)}, u32[]{:S(2)}) collective-permute-start(bf16[256,2048]{1,0:T(8,128)(2,1)} %get-tuple-element.293), channel_id=1, source_target_pairs={{0,1},{1,0},{2,3},{3,2},{4,5},{5,4},{6,7},{7,6},{8,9},{9,8},{10,11... | collective-permute-start | bytes 3145736 | tf_op jit(solution)/shard_map/ppermute | solution.py:37
  306.5 25.6 %collective-permute-start.30 = (bf16[256,2048]{1,0:T(8,128)(2,1)}, bf16[256,2048]{1,0:T(8,128)(2,1)}, u32[]{:S(2)}, u32[]{:S(2)}) collective-permute-start(bf16[256,2048]{1,0:T(8,128)(2,1)} %get-tuple-element.294), channel_id=1, source_target_pairs={{0,4},{4,0},{2,6},{6,2},{1,5},{5,1},{3,7},{7,3},{8,12},{12,8},{10,... | collective-permute-start | bytes 3145736 | tf_op jit(solution)/shard_map/ppermute | solution.py:45
  332.0 18.3 %collective-permute-start.33 = (bf16[1024,2048]{1,0:T(8,128)(2,1)}, bf16[1024,2048]{1,0:T(8,128)(2,1)}, u32[]{:S(2)}, u32[]{:S(2)}) collective-permute-start(bf16[1024,2048]{1,0:T(8,128)(2,1)} %feed_sent.1), channel_id=1, source_target_pairs={{0,2},{2,0},{4,6},{6,4},{1,3},{3,1},{5,7},{7,5},{8,10},{10,8},{12,... | collective-permute-start | bytes 12582920 | tf_op jit(solution)/shard_map/ppermute | solution.py:41
  333.4 14.4 %collective-permute-start.32 = (bf16[128,2048]{1,0:T(8,128)(2,1)S(1)}, bf16[128,2048]{1,0:T(8,128)(2,1)S(1)}, u32[]{:S(2)}, u32[]{:S(2)}) collective-permute-start(bf16[128,2048]{1,0:T(8,128)(2,1)S(1)} %add_convert_fusion.8), channel_id=1, source_target_pairs={{0,4},{4,0},{2,6},{6,2},{1,5},{5,1},{3,7},{7,3},{8,12},{12,8},{10,... | collective-permute-start | bytes 1572872 | tf_op jit(solution)/shard_map/ppermute | solution.py:45
  336.2 14.1 %collective-permute-start.31 = (bf16[128,2048]{1,0:T(8,128)(2,1)S(1)}, bf16[128,2048]{1,0:T(8,128)(2,1)S(1)}, u32[]{:S(2)}, u32[]{:S(2)}) collective-permute-start(bf16[128,2048]{1,0:T(8,128)(2,1)S(1)} %add_convert_fusion.9), channel_id=1, source_target_pairs={{0,1},{1,0},{2,3},{3,2},{4,5},{5,4},{6,7},{7,6},{8,9},{9,8},{10,11... | collective-permute-start | bytes 1572872 | tf_op jit(solution)/shard_map/ppermute | solution.py:37
  355.1 24.8 %collective-permute-start.36 = (bf16[256,2048]{1,0:T(8,128)(2,1)S(1)}, bf16[256,2048]{1,0:T(8,128)(2,1)}, u32[]{:S(2)}, u32[]{:S(2)}) collective-permute-start(bf16[256,2048]{1,0:T(8,128)(2,1)S(1)} %get-tuple-element.343.refs_0_), channel_id=1, source_target_pairs={{0,2},{2,0},{4,6},{6,4},{1,3},{3,1},{5,7},{7,5},{8,10},{10,8},{12,... | collective-permute-start | bytes 3145736 | tf_op jit(solution)/shard_map/ppermute | solution.py:41
  355.1 25.7 %collective-permute-start.35 = (bf16[256,2048]{1,0:T(8,128)(2,1)S(1)}, bf16[256,2048]{1,0:T(8,128)(2,1)}, u32[]{:S(2)}, u32[]{:S(2)}) collective-permute-start(bf16[256,2048]{1,0:T(8,128)(2,1)S(1)} %get-tuple-element.343.refs_0_), channel_id=1, source_target_pairs={{0,4},{4,0},{2,6},{6,2},{1,5},{5,1},{3,7},{7,3},{8,12},{12,8},{10,... | collective-permute-start | bytes 3145736 | tf_op jit(solution)/shard_map/ppermute | solution.py:45
  355.8 25.4 %collective-permute-start.34 = (bf16[256,2048]{1,0:T(8,128)(2,1)S(1)}, bf16[256,2048]{1,0:T(8,128)(2,1)}, u32[]{:S(2)}, u32[]{:S(2)}) collective-permute-start(bf16[256,2048]{1,0:T(8,128)(2,1)S(1)} %get-tuple-element.343.refs_0_), channel_id=1, source_target_pairs={{0,1},{1,0},{2,3},{3,2},{4,5},{5,4},{6,7},{7,6},{8,9},{9,8},{10,11... | collective-permute-start | bytes 3145736 | tf_op jit(solution)/shard_map/ppermute | solution.py:37
  381.3 115.1 %reduce-scatter.9.cloned.1.call-start = ((), (), s32[]{:S(2)}) async-start(), calls=%async_computation.8 | async-start | bytes 1310720 | tf_op jit(solution)/shard_map/reduce_scatter | solution.py:945
  381.3 17.0 %collective-permute-start.39 = (bf16[256,2048]{1,0:T(8,128)(2,1)}, bf16[256,2048]{1,0:T(8,128)(2,1)S(1)}, u32[]{:S(2)}, u32[]{:S(2)}) collective-permute-start(bf16[256,2048]{1,0:T(8,128)(2,1)} %collective-permute-done.34.refs_2_), channel_id=1, source_target_pairs={{0,2},{2,0},{4,6},{6,4},{1,3},{3,1},{5,7},{7,5},{8,10},{10,8},{12,... | collective-permute-start | bytes 3145736 | tf_op jit(solution)/shard_map/ppermute | solution.py:41
  381.4 16.9 %collective-permute-start.40 = (bf16[256,2048]{1,0:T(8,128)(2,1)}, bf16[256,2048]{1,0:T(8,128)(2,1)S(1)}, u32[]{:S(2)}, u32[]{:S(2)}) collective-permute-start(bf16[256,2048]{1,0:T(8,128)(2,1)} %collective-permute-done.35.refs_3_), channel_id=1, source_target_pairs={{0,2},{2,0},{4,6},{6,4},{1,3},{3,1},{5,7},{7,5},{8,10},{10,8},{12,... | collective-permute-start | bytes 3145736 | tf_op jit(solution)/shard_map/ppermute | solution.py:41
  384.0 14.0 %collective-permute-start.38 = (bf16[128,2048]{1,0:T(8,128)(2,1)S(1)}, bf16[128,2048]{1,0:T(8,128)(2,1)S(1)}, u32[]{:S(2)}, u32[]{:S(2)}) collective-permute-start(bf16[128,2048]{1,0:T(8,128)(2,1)S(1)} %slice.191), channel_id=1, source_target_pairs={{0,1},{1,0},{2,3},{3,2},{4,5},{5,4},{6,7},{7,6},{8,9},{9,8},{10,11... | collective-permute-start | bytes 1572872 | tf_op jit(solution)/shard_map/ppermute | solution.py:37
  384.7 13.6 %collective-permute-start.37 = (bf16[128,2048]{1,0:T(8,128)(2,1)S(1)}, bf16[128,2048]{1,0:T(8,128)(2,1)S(1)}, u32[]{:S(2)}, u32[]{:S(2)}) collective-permute-start(bf16[128,2048]{1,0:T(8,128)(2,1)S(1)} %slice.190), channel_id=1, source_target_pairs={{0,4},{4,0},{2,6},{6,2},{1,5},{5,1},{3,7},{7,3},{8,12},{12,8},{10,... | collective-permute-start | bytes 1572872 | tf_op jit(solution)/shard_map/ppermute | solution.py:45
  401.0 25.5 %collective-permute-start.43 = (bf16[256,2048]{1,0:T(8,128)(2,1)}, bf16[256,2048]{1,0:T(8,128)(2,1)}, u32[]{:S(2)}, u32[]{:S(2)}) collective-permute-start(bf16[256,2048]{1,0:T(8,128)(2,1)} %get-tuple-element.341), channel_id=1, source_target_pairs={{0,1},{1,0},{2,3},{3,2},{4,5},{5,4},{6,7},{7,6},{8,9},{9,8},{10,11... | collective-permute-start | bytes 3145736 | tf_op jit(solution)/shard_map/ppermute | solution.py:37
  402.5 26.3 %collective-permute-start.44 = (bf16[256,2048]{1,0:T(8,128)(2,1)}, bf16[256,2048]{1,0:T(8,128)(2,1)S(1)}, u32[]{:S(2)}, u32[]{:S(2)}) collective-permute-start(bf16[256,2048]{1,0:T(8,128)(2,1)} %get-tuple-element.342), channel_id=1, source_target_pairs={{0,4},{4,0},{2,6},{6,2},{1,5},{5,1},{3,7},{7,3},{8,12},{12,8},{10,... | collective-permute-start | bytes 3145736 | tf_op jit(solution)/shard_map/ppermute | solution.py:45
  403.8 67.9 %collective-permute-start.47 = (bf16[512,1024]{1,0:T(8,128)(2,1)}, bf16[512,1024]{1,0:T(8,128)(2,1)}, u32[]{:S(2)}, u32[]{:S(2)}) collective-permute-start(bf16[512,1024]{1,0:T(8,128)(2,1)} %reduce-scatter.5.cloned.1.call-done.refs_0_), channel_id=1, source_target_pairs={{0,4},{4,0},{2,6},{6,2},{1,5},{5,1},{3,7},{7,3},{8,12},{12,8},{10,... | collective-permute-start | bytes 3145736 | tf_op jit(solution)/shard_map/ppermute | solution.py:45
  430.5 30.9 %collective-permute-start.46 = (bf16[128,2048]{1,0:T(8,128)(2,1)S(1)}, bf16[128,2048]{1,0:T(8,128)(2,1)}, u32[]{:S(2)}, u32[]{:S(2)}) collective-permute-start(bf16[128,2048]{1,0:T(8,128)(2,1)S(1)} %add_convert_fusion.6), channel_id=1, source_target_pairs={{0,4},{4,0},{2,6},{6,2},{1,5},{5,1},{3,7},{7,3},{8,12},{12,8},{10,... | collective-permute-start | bytes 1572872 | tf_op jit(solution)/shard_map/ppermute | solution.py:45
  432.0 29.5 %collective-permute-start.45 = (bf16[128,2048]{1,0:T(8,128)(2,1)S(1)}, bf16[128,2048]{1,0:T(8,128)(2,1)}, u32[]{:S(2)}, u32[]{:S(2)}) collective-permute-start(bf16[128,2048]{1,0:T(8,128)(2,1)S(1)} %add_convert_fusion.7), channel_id=1, source_target_pairs={{0,1},{1,0},{2,3},{3,2},{4,5},{5,4},{6,7},{7,6},{8,9},{9,8},{10,11... | collective-permute-start | bytes 1572872 | tf_op jit(solution)/shard_map/ppermute | solution.py:37
  471.7 27.3 %collective-permute-start.48 = (bf16[1024,2048]{1,0:T(8,128)(2,1)}, bf16[1024,2048]{1,0:T(8,128)(2,1)}, u32[]{:S(2)}, u32[]{:S(2)}) collective-permute-start(bf16[1024,2048]{1,0:T(8,128)(2,1)} %act_one_sent.1), channel_id=1, source_target_pairs={{0,2},{2,0},{4,6},{6,4},{1,3},{3,1},{5,7},{7,5},{8,10},{10,8},{12,... | collective-permute-start | bytes 12582920 | tf_op jit(solution)/shard_map/ppermute | solution.py:41
  471.8 85.7 %reduce-scatter.11.cloned.1.call-start = ((), (), s32[]{:S(2)}) async-start(), calls=%async_computation.9 | async-start | bytes 3932160 | tf_op jit(solution)/shard_map/reduce_scatter | solution.py:957
  472.3 25.9 %collective-permute-start.50 = (bf16[512,1024]{1,0:T(8,128)(2,1)}, bf16[512,1024]{1,0:T(8,128)(2,1)}, u32[]{:S(2)}, u32[]{:S(2)}) collective-permute-start(bf16[512,1024]{1,0:T(8,128)(2,1)} %reduce-scatter.7.cloned.1.call-done.refs_0_), channel_id=1, source_target_pairs={{0,4},{4,0},{2,6},{6,2},{1,5},{5,1},{3,7},{7,3},{8,12},{12,8},{10,... | collective-permute-start | bytes 3145736 | tf_op jit(solution)/shard_map/ppermute | solution.py:45
  473.6 25.4 %collective-permute-start.49 = (bf16[256,2048]{1,0:T(8,128)(2,1)S(1)}, bf16[256,2048]{1,0:T(8,128)(2,1)}, u32[]{:S(2)}, u32[]{:S(2)}) collective-permute-start(bf16[256,2048]{1,0:T(8,128)(2,1)S(1)} %add_convert_fusion.2), channel_id=1, source_target_pairs={{0,1},{1,0},{2,3},{3,2},{4,5},{5,4},{6,7},{7,6},{8,9},{9,8},{10,11... | collective-permute-start | bytes 3145736 | tf_op jit(solution)/shard_map/ppermute | solution.py:37
  499.0 9.2 %collective-permute-start.52 = (bf16[512,1024]{1,0:T(8,128)(2,1)}, bf16[512,1024]{1,0:T(8,128)(2,1)}, u32[]{:S(2)}, u32[]{:S(2)}) collective-permute-start(bf16[512,1024]{1,0:T(8,128)(2,1)} %reduce-scatter.5.cloned.1.call-done.refs_0_), channel_id=1, source_target_pairs={{0,2},{2,0},{4,6},{6,4},{1,3},{3,1},{5,7},{7,5},{8,10},{10,8},{12,... | collective-permute-start | bytes 3145736 | tf_op jit(solution)/shard_map/ppermute | solution.py:41
  499.1 9.2 %collective-permute-start.54 = (bf16[512,1024]{1,0:T(8,128)(2,1)}, bf16[512,1024]{1,0:T(8,128)(2,1)}, u32[]{:S(2)}, u32[]{:S(2)}) collective-permute-start(bf16[512,1024]{1,0:T(8,128)(2,1)} %reduce-scatter.7.cloned.1.call-done.refs_0_), channel_id=1, source_target_pairs={{0,2},{2,0},{4,6},{6,4},{1,3},{3,1},{5,7},{7,5},{8,10},{10,8},{12,... | collective-permute-start | bytes 3145736 | tf_op jit(solution)/shard_map/ppermute | solution.py:41
  499.6 8.7 %collective-permute-start.53 = (bf16[512,1024]{1,0:T(8,128)(2,1)}, bf16[512,1024]{1,0:T(8,128)(2,1)}, u32[]{:S(2)}, u32[]{:S(2)}) collective-permute-start(bf16[512,1024]{1,0:T(8,128)(2,1)} %collective-permute-done.47.refs_2_), channel_id=1, source_target_pairs={{0,2},{2,0},{4,6},{6,4},{1,3},{3,1},{5,7},{7,5},{8,10},{10,8},{12,... | collective-permute-start | bytes 3145736 | tf_op jit(solution)/shard_map/ppermute | solution.py:41
  499.6 8.7 %collective-permute-start.51 = (bf16[512,1024]{1,0:T(8,128)(2,1)}, bf16[512,1024]{1,0:T(8,128)(2,1)}, u32[]{:S(2)}, u32[]{:S(2)}) collective-permute-start(bf16[512,1024]{1,0:T(8,128)(2,1)} %collective-permute-done.50.refs_2_), channel_id=1, source_target_pairs={{0,2},{2,0},{4,6},{6,4},{1,3},{3,1},{5,7},{7,5},{8,10},{10,8},{12,... | collective-permute-start | bytes 3145736 | tf_op jit(solution)/shard_map/ppermute | solution.py:41
  500.1 8.3 %collective-permute-start.55 = (bf16[512,256]{1,0:T(8,128)(2,1)S(1)}, bf16[512,256]{1,0:T(8,128)(2,1)S(1)}, u32[]{:S(2)}, u32[]{:S(2)}) collective-permute-start(bf16[512,256]{1,0:T(8,128)(2,1)S(1)} %copy-done.31), channel_id=1, source_target_pairs={{0,4},{4,0},{2,6},{6,2},{1,5},{5,1},{3,7},{7,3},{8,12},{12,8},{10,... | collective-permute-start | bytes 786440 | tf_op jit(solution)/shard_map/ppermute | solution.py:45
  508.4 25.0 %collective-permute-start.56 = (bf16[256,2048]{1,0:T(8,128)(2,1)}, bf16[256,2048]{1,0:T(8,128)(2,1)}, u32[]{:S(2)}, u32[]{:S(2)}) collective-permute-start(bf16[256,2048]{1,0:T(8,128)(2,1)} %get-tuple-element.380), channel_id=1, source_target_pairs={{0,1},{1,0},{2,3},{3,2},{4,5},{5,4},{6,7},{7,6},{8,9},{9,8},{10,11... | collective-permute-start | bytes 3145736 | tf_op jit(solution)/shard_map/ppermute | solution.py:37
  508.9 24.7 %collective-permute-start.57 = (bf16[256,2048]{1,0:T(8,128)(2,1)}, bf16[256,2048]{1,0:T(8,128)(2,1)}, u32[]{:S(2)}, u32[]{:S(2)}) collective-permute-start(bf16[256,2048]{1,0:T(8,128)(2,1)} %get-tuple-element.381), channel_id=1, source_target_pairs={{0,4},{4,0},{2,6},{6,2},{1,5},{5,1},{3,7},{7,3},{8,12},{12,8},{10,... | collective-permute-start | bytes 3145736 | tf_op jit(solution)/shard_map/ppermute | solution.py:45
  510.4 10.5 %collective-permute-start.58 = (bf16[512,256]{1,0:T(8,128)(2,1)S(1)}, bf16[512,256]{1,0:T(8,128)(2,1)S(1)}, u32[]{:S(2)}, u32[]{:S(2)}) collective-permute-start(bf16[512,256]{1,0:T(8,128)(2,1)S(1)} %copy-done.31), channel_id=1, source_target_pairs={{0,2},{2,0},{4,6},{6,4},{1,3},{3,1},{5,7},{7,5},{8,10},{10,8},{12,... | collective-permute-start | bytes 786440 | tf_op jit(solution)/shard_map/ppermute | solution.py:41
  513.6 7.2 %collective-permute-start.59 = (bf16[512,256]{1,0:T(8,128)(2,1)S(1)}, bf16[512,256]{1,0:T(8,128)(2,1)}, u32[]{:S(2)}, u32[]{:S(2)}) collective-permute-start(bf16[512,256]{1,0:T(8,128)(2,1)S(1)} %collective-permute-done.55.refs_2_), channel_id=1, source_target_pairs={{0,2},{2,0},{4,6},{6,4},{1,3},{3,1},{5,7},{7,5},{8,10},{10,8},{12,... | collective-permute-start | bytes 786440 | tf_op jit(solution)/shard_map/ppermute | solution.py:41
  534.9 12.7 %collective-permute-start.61 = (bf16[128,2048]{1,0:T(8,128)(2,1)S(1)}, bf16[128,2048]{1,0:T(8,128)(2,1)}, u32[]{:S(2)}, u32[]{:S(2)}) collective-permute-start(bf16[128,2048]{1,0:T(8,128)(2,1)S(1)} %add_convert_fusion.4), channel_id=1, source_target_pairs={{0,4},{4,0},{2,6},{6,2},{1,5},{5,1},{3,7},{7,3},{8,12},{12,8},{10,... | collective-permute-start | bytes 1572872 | tf_op jit(solution)/shard_map/ppermute | solution.py:45
  537.4 12.2 %collective-permute-start.60 = (bf16[128,2048]{1,0:T(8,128)(2,1)S(1)}, bf16[128,2048]{1,0:T(8,128)(2,1)S(1)}, u32[]{:S(2)}, u32[]{:S(2)}) collective-permute-start(bf16[128,2048]{1,0:T(8,128)(2,1)S(1)} %add_convert_fusion.5), channel_id=1, source_target_pairs={{0,1},{1,0},{2,3},{3,2},{4,5},{5,4},{6,7},{7,6},{8,9},{9,8},{10,11... | collective-permute-start | bytes 1572872 | tf_op jit(solution)/shard_map/ppermute | solution.py:37
  557.5 28.5 %collective-permute-start.62 = (bf16[256,2048]{1,0:T(8,128)(2,1)S(1)}, bf16[256,2048]{1,0:T(8,128)(2,1)S(1)}, u32[]{:S(2)}, u32[]{:S(2)}) collective-permute-start(bf16[256,2048]{1,0:T(8,128)(2,1)S(1)} %add_convert_fusion.1), channel_id=1, source_target_pairs={{0,1},{1,0},{2,3},{3,2},{4,5},{5,4},{6,7},{7,6},{8,9},{9,8},{10,11... | collective-permute-start | bytes 3145736 | tf_op jit(solution)/shard_map/ppermute | solution.py:37
  559.0 27.0 %collective-permute-start.67 = (bf16[512,768]{1,0:T(8,128)(2,1)}, bf16[512,768]{1,0:T(8,128)(2,1)S(1)}, u32[]{:S(2)}, u32[]{:S(2)}) collective-permute-start(bf16[512,768]{1,0:T(8,128)(2,1)} %reduce-scatter.11.cloned.1.call-done.refs_0_), channel_id=1, source_target_pairs={{0,2},{2,0},{4,6},{6,4},{1,3},{3,1},{5,7},{7,5},{8,10},{10,8},{12,... | collective-permute-start | bytes 2359304 | tf_op jit(solution)/shard_map/ppermute | solution.py:41
  559.0 27.0 %collective-permute-start.66 = (bf16[512,768]{1,0:T(8,128)(2,1)}, bf16[512,768]{1,0:T(8,128)(2,1)}, u32[]{:S(2)}, u32[]{:S(2)}) collective-permute-start(bf16[512,768]{1,0:T(8,128)(2,1)} %reduce-scatter.11.cloned.1.call-done.refs_0_), channel_id=1, source_target_pairs={{0,4},{4,0},{2,6},{6,2},{1,5},{5,1},{3,7},{7,3},{8,12},{12,8},{10,... | collective-permute-start | bytes 2359304 | tf_op jit(solution)/shard_map/ppermute | solution.py:45
  561.8 19.5 %collective-permute-start.64 = (f32[4,6144]{1,0:T(4,128)S(1)}, f32[4,6144]{1,0:T(4,128)S(1)}, u32[]{:S(2)}, u32[]{:S(2)}) collective-permute-start(f32[4,6144]{1,0:T(4,128)S(1)} %add.257), channel_id=1, source_target_pairs={{0,4},{4,0},{2,6},{6,2},{1,5},{5,1},{3,7},{7,3},{8,12},{12,8},{10,... | collective-permute-start | bytes 294920 | tf_op jit(solution)/shard_map/ppermute | solution.py:45
  586.2 10.9 %collective-permute-start.70 = (f32[1,6144]{1,0:T(1,128)S(1)}, f32[1,6144]{1,0:T(1,128)S(1)}, u32[]{:S(2)}, u32[]{:S(2)}) collective-permute-start(f32[1,6144]{1,0:T(1,128)S(1)} %get-tuple-element.445), channel_id=1, source_target_pairs={{0,24},{8,0},{16,8},{24,16},{1,25},{9,1},{17,9},{25,17},{2,26},{10... | collective-permute-start | bytes 73736 | tf_op jit(solution)/shard_map/ppermute | solution.py:1021
  588.6 8.5 %collective-permute-start.69 = (f32[1,6144]{1,0:T(1,128)S(1)}, f32[1,6144]{1,0:T(1,128)S(1)}, u32[]{:S(2)}, u32[]{:S(2)}) collective-permute-start(f32[1,6144]{1,0:T(1,128)S(1)} %get-tuple-element.446), channel_id=1, source_target_pairs={{0,16},{8,24},{16,0},{24,8},{1,17},{9,25},{17,1},{25,9},{2,18},{10... | collective-permute-start | bytes 73736 | tf_op jit(solution)/shard_map/ppermute | solution.py:1021
  588.8 8.3 %collective-permute-start.68 = (f32[1,6144]{1,0:T(1,128)S(1)}, f32[1,6144]{1,0:T(1,128)S(1)}, u32[]{:S(2)}, u32[]{:S(2)}) collective-permute-start(f32[1,6144]{1,0:T(1,128)S(1)} %get-tuple-element.447), channel_id=1, source_target_pairs={{0,8},{8,16},{16,24},{24,0},{1,9},{9,17},{17,25},{25,1},{2,10},{10... | collective-permute-start | bytes 73736 | tf_op jit(solution)/shard_map/ppermute | solution.py:1021
  (71 other events, 685.5 us)
Sparse Core Ops, SparseCore 0:
  10.2 83.4 all-gather.2
  96.0 150.2 all-gather.4
  295.9 75.0 reduce-scatter.4
  381.4 73.8 reduce-scatter.6
  471.9 24.3 reduce-scatter.8
  499.1 58.3 reduce-scatter.10
